TPU v7x, 32 devices: a whole 2x2x4 slice. The times are simulated.
32 devices in a mesh: dp: 2 (over y), gx: 4 (over x, core), gy: 4 (over z).
Axes of the slice: x: 2, y: 2, z: 4, core: 2. Of those that a mesh axis runs over, the one named last changes fastest.
Arguments:
- tokens: bfloat16 [2, 11664, 1152], P(None, ('dp', 'gy'), 'gx'), may hold values from -6 to 6
- cotangent: bfloat16 [2, 11664, 1152], P(None, ('dp', 'gy'), 'gx'), may hold values from -6 to 6
- ln1_gain: bfloat16 [1152], P('gx'), may hold values from 0.25 to 1.75
- ln1_bias: bfloat16 [1152], P('gx'), may hold values from -3 to 3
- qkv_weight: bfloat16 [1152, 3, 1152], P('gx', None, 'gy'), may hold values from -0.1875 to 0.1875
- qv_bias: bfloat16 [2, 1152], P(None, 'gy'), may hold values from -3 to 3
- out_weight: bfloat16 [1152, 1152], P('gy', 'gx'), may hold values from -1.5 to 1.5
- out_bias: bfloat16 [1152], P('gx'), may hold values from -3 to 3
- ln2_gain: bfloat16 [1152], P('gx'), may hold values from 0.25 to 1.75
- ln2_bias: bfloat16 [1152], P('gx'), may hold values from -3 to 3
- fc1_weight: bfloat16 [1152, 4304], P('gx', 'gy'), may hold values from -0.1875 to 0.1875
- fc1_bias: bfloat16 [4304], P('gy'), may hold values from -3 to 3
- fc2_weight: bfloat16 [4304, 1152], P('gy', 'gx'), may hold values from -0.09375 to 0.09375
- fc2_bias: bfloat16 [1152], P('gx'), may hold values from -3 to 3
Outputs:
- layer_out: bfloat16 [2, 11664, 1152], P(None, ('dp', 'gy'), 'gx')
- tokens_grad: bfloat16 [2, 11664, 1152], P(None, ('dp', 'gy'), 'gx')
- ln1_gain_grad: float32 [1152], P('gx')
- ln1_bias_grad: float32 [1152], P('gx')
- qkv_weight_grad: float32 [1152, 3, 1152], P('gx', None, 'gy')
- qv_bias_grad: float32 [2, 1152], P(None, 'gy')
- out_weight_grad: float32 [1152, 1152], P('gy', 'gx')
- out_bias_grad: float32 [1152], P('gx')
- ln2_gain_grad: float32 [1152], P('gx')
- ln2_bias_grad: float32 [1152], P('gx')
- fc1_weight_grad: float32 [1152, 4304], P('gx', 'gy')
- fc1_bias_grad: float32 [4304], P('gy')
- fc2_weight_grad: float32 [4304, 1152], P('gy', 'gx')
- fc2_bias_grad: float32 [1152], P('gx')
All inputs are finite; a program needn't handle non-finite values.
Results may differ from a plain program's by a relative error of at most 0.013.
The roundings to bfloat16 on the way count: a program that leaves them out, or rounds other values in their place, can miss the bound.
Values may be sent and summed in bfloat16 or wider, within the bound.
No kernel may reach another device: no remote copies, remote signals or barrier semaphores. Data moves between devices by JAX's collectives and lax.ppermute only.
A program may use at most 384 MiB of HBM per device.

v0:
```python
import jax
import jax.numpy as jnp
from jax import lax
from jax.sharding import PartitionSpec as P

HEAD_DIM = 72
SEQ = 729
MICRO = 2


epsilon = 1e-06


def contract_rows(left_side, right_side):
    return lax.dot_general(
        left_side, right_side, (((0,), (0,)), ((), ())), preferred_element_type=jnp.float32
    )


def contract_cols(left_side, right_side):
    return lax.dot_general(
        left_side, right_side, (((1,), (1,)), ((), ())), preferred_element_type=jnp.float32
    )


def apply_weight(rows, weight, backward):
    if backward:
        return contract_cols(rows, weight)
    return jnp.dot(rows, weight, preferred_element_type=jnp.float32)


def gelu_tanh(values):
    return jax.nn.gelu(values, approximate=True)


def row_pair_sums(first_terms, second_terms):
    return lax.psum((jnp.sum(first_terms, axis=1), jnp.sum(second_terms, axis=1)), "gx")


def norm_forward(values):
    row_sum, row_square = row_pair_sums(values, values * values)
    full_width = values.shape[1] * lax.axis_size("gx")
    center = row_sum / full_width
    spread = row_square / full_width - center * center
    inverse = lax.rsqrt(spread + epsilon)
    return ((values - center[:, None]) * inverse[:, None], inverse)


def norm_backward(grad_norm, normed, inverse, norm_gain):
    grad_hat = grad_norm * norm_gain
    row_sum, row_cross = row_pair_sums(grad_hat, grad_hat * normed)
    full_width = grad_norm.shape[1] * lax.axis_size("gx")
    return inverse[:, None] * (
        grad_hat - row_sum[:, None] / full_width - normed * (row_cross[:, None] / full_width)
    )


def spread(row_block, weight, backward):
    gathered = lax.all_gather(row_block, "gy", axis=0, tiled=True)
    full_rows = lax.all_to_all(gathered, "gx", split_axis=0, concat_axis=1, tiled=True)
    if backward:
        whole_weight = lax.all_gather(weight, "gx", axis=1, tiled=True)
    else:
        whole_weight = lax.all_gather(weight, "gx", axis=0, tiled=True)
    return (gathered, apply_weight(full_rows, whole_weight, backward))


def join(row_block, weight, backward):
    gathered = lax.all_gather(row_block, "gx", axis=0, tiled=True)
    full_rows = lax.all_to_all(gathered, "gy", split_axis=0, concat_axis=1, tiled=True)
    if backward:
        whole_weight = lax.all_gather(weight, "gy", axis=1, tiled=True)
    else:
        whole_weight = lax.all_gather(weight, "gy", axis=0, tiled=True)
    return (gathered, apply_weight(full_rows, whole_weight, backward))


def attend_image(packed):
    queries = packed[:, 0]
    key_rows = packed[:, 1]
    values = packed[:, 2]
    scaling = queries.shape[-1] ** (-0.5)
    scores = (
        jnp.einsum("qhd,khd->hqk", queries, key_rows, preferred_element_type=jnp.float32) * scaling
    )
    row_max = jnp.max(scores, axis=2, keepdims=True)
    exponent = jnp.exp(scores - row_max)
    row_total = jnp.sum(exponent, axis=2, keepdims=True)
    probability = (exponent / row_total).astype(jnp.bfloat16)
    mixture = jnp.einsum("hqk,khd->qhd", probability, values, preferred_element_type=jnp.float32)
    return (mixture.astype(jnp.bfloat16), (row_max + jnp.log(row_total))[:, :, 0])


def attend_backward(element):
    packed, log_total, grad_mixture = element
    queries = packed[:, 0]
    key_rows = packed[:, 1]
    values = packed[:, 2]
    scaling = queries.shape[-1] ** (-0.5)
    scores = (
        jnp.einsum("qhd,khd->hqk", queries, key_rows, preferred_element_type=jnp.float32) * scaling
    )
    probability = jnp.exp(scores - log_total[:, :, None])
    rounded = probability.astype(jnp.bfloat16)
    grad_values = jnp.einsum(
        "hqk,qhd->khd", rounded, grad_mixture, preferred_element_type=jnp.float32
    )
    grad_prob = jnp.einsum("qhd,khd->hqk", grad_mixture, values, preferred_element_type=jnp.float32)
    inner_sum = jnp.sum(probability * grad_prob, axis=2, keepdims=True)
    grad_scores = (probability * (grad_prob - inner_sum)).astype(jnp.bfloat16)
    grad_queries = (
        jnp.einsum("hqk,khd->qhd", grad_scores, key_rows, preferred_element_type=jnp.float32)
        * scaling
    )
    grad_keys = (
        jnp.einsum("hqk,qhd->khd", grad_scores, queries, preferred_element_type=jnp.float32)
        * scaling
    )
    return jnp.stack([grad_queries, grad_keys, grad_values], axis=1).astype(jnp.bfloat16)


def total_grads(mat_grads, row_grads):
    mat_summed = lax.psum(
        (
            mat_grads[0],
            mat_grads[1],
            mat_grads[2],
            mat_grads[3],
            mat_grads[4],
            mat_grads[5],
            mat_grads[6],
            mat_grads[7],
        ),
        "dp",
    )
    row_summed = lax.psum((row_grads[0], row_grads[1], row_grads[2], row_grads[3]), ("dp", "gy"))
    return (mat_summed, row_summed)


def on_device(
    tokens,
    cotangent,
    ln1_gain,
    ln1_bias,
    qkv_weight,
    qv_bias,
    out_weight,
    out_bias,
    ln2_gain,
    ln2_bias,
    fc1_weight,
    fc1_bias,
    fc2_weight,
    fc2_bias,
):
    width_local = qkv_weight.shape[0]
    head_cols = qkv_weight.shape[2]
    heads_here = head_cols // HEAD_DIM
    qkv_flat = qkv_weight.reshape(width_local, 3 * head_cols)
    bias_rows = (
        jnp.stack([qv_bias[0], jnp.zeros_like(qv_bias[0]), qv_bias[1]])
        .astype(jnp.float32)
        .reshape(1, 3 * head_cols)
    )
    gain_one = ln1_gain.astype(jnp.float32)
    shift_one = ln1_bias.astype(jnp.float32)
    gain_two = ln2_gain.astype(jnp.float32)
    shift_two = ln2_bias.astype(jnp.float32)
    bias_mix = out_bias.astype(jnp.float32)
    bias_first = fc1_bias.astype(jnp.float32)
    bias_second = fc2_bias.astype(jnp.float32)
    outputs = []
    grad_inputs = []
    mat_total = None
    row_total = None
    for batch_index in range(MICRO):
        current = tokens[batch_index].astype(jnp.float32)
        normed_one, inverse_one = norm_forward(current)
        ready_one = (normed_one * gain_one + shift_one).astype(jnp.bfloat16)
        gathered_one, projected = spread(ready_one, qkv_flat, False)
        projected = projected + bias_rows
        attn_rows = projected.shape[0]
        picture_count = attn_rows // SEQ
        packed = projected.astype(jnp.bfloat16).reshape(picture_count, SEQ, 3, heads_here, HEAD_DIM)
        mixture, log_total = lax.map(attend_image, packed)
        mixture = mixture.reshape(attn_rows, head_cols)
        gathered_mix, attn_out = join(mixture, out_weight, False)
        hidden = current + attn_out + bias_mix
        normed_two, inverse_two = norm_forward(hidden)
        ready_two = (normed_two * gain_two + shift_two).astype(jnp.bfloat16)
        gathered_two, first_out = spread(ready_two, fc1_weight, False)
        active, gelu_pull = jax.vjp(gelu_tanh, first_out + bias_first)
        gathered_act, second_out = join(active.astype(jnp.bfloat16), fc2_weight, False)
        outputs.append((hidden + second_out + bias_second).astype(jnp.bfloat16))
        grad_out = cotangent[batch_index]
        grad_out_all, grad_active = spread(grad_out, fc2_weight, True)
        grad_fc2 = contract_rows(gathered_act, grad_out_all)
        grad_fc2_bias = jnp.sum(grad_out_all, axis=0, dtype=jnp.float32)
        grad_first = gelu_pull(grad_active)[0].astype(jnp.bfloat16)
        grad_first_all, grad_ready_two = join(grad_first, fc1_weight, True)
        grad_fc1 = contract_rows(gathered_two, grad_first_all)
        grad_fc1_bias = jnp.sum(grad_first_all, axis=0, dtype=jnp.float32)
        grad_gain_two = jnp.sum(grad_ready_two * normed_two, axis=0)
        grad_shift_two = jnp.sum(grad_ready_two, axis=0)
        grad_hidden = grad_out.astype(jnp.float32) + norm_backward(
            grad_ready_two, normed_two, inverse_two, gain_two
        )
        grad_hidden_all, grad_mixture = spread(grad_hidden.astype(jnp.bfloat16), out_weight, True)
        grad_out_weight = contract_rows(gathered_mix, grad_hidden_all)
        grad_out_bias = jnp.sum(grad_hidden_all, axis=0, dtype=jnp.float32)
        grad_mix_low = grad_mixture.astype(jnp.bfloat16).reshape(
            picture_count, SEQ, heads_here, HEAD_DIM
        )
        grad_packed = lax.map(attend_backward, (packed, log_total, grad_mix_low))
        grad_packed = grad_packed.reshape(attn_rows, 3 * head_cols)
        grad_packed_all, grad_ready_one = join(grad_packed, qkv_flat, True)
        grad_qkv = contract_rows(gathered_one, grad_packed_all).reshape(width_local, 3, head_cols)
        col_sums = jnp.sum(grad_packed_all, axis=0, dtype=jnp.float32).reshape(3, head_cols)
        grad_qv = jnp.stack([col_sums[0], col_sums[2]])
        grad_gain_one = jnp.sum(grad_ready_one * normed_one, axis=0)
        grad_shift_one = jnp.sum(grad_ready_one, axis=0)
        grad_inputs.append(
            (grad_hidden + norm_backward(grad_ready_one, normed_one, inverse_one, gain_one)).astype(
                jnp.bfloat16
            )
        )
        mat_grads = (
            grad_qkv,
            grad_qv,
            grad_out_weight,
            grad_out_bias,
            grad_fc1,
            grad_fc1_bias,
            grad_fc2,
            grad_fc2_bias,
        )
        row_grads = (grad_gain_one, grad_shift_one, grad_gain_two, grad_shift_two)
        mat_grads, row_grads = total_grads(mat_grads, row_grads)
        if batch_index == 0:
            mat_total, row_total = (mat_grads, row_grads)
        else:
            mat_total = jax.tree.map(jnp.add, mat_total, mat_grads)
            row_total = jax.tree.map(jnp.add, row_total, row_grads)
    return (
        jnp.stack(outputs),
        jnp.stack(grad_inputs),
        row_total[0],
        row_total[1],
        mat_total[0],
        mat_total[1],
        mat_total[2],
        mat_total[3],
        row_total[2],
        row_total[3],
        mat_total[4],
        mat_total[5],
        mat_total[6],
        mat_total[7],
    )


def solution(mesh):
    return jax.shard_map(
        on_device,
        mesh=mesh,
        in_specs=(
            P(None, ("dp", "gy"), "gx"),
            P(None, ("dp", "gy"), "gx"),
            P("gx"),
            P("gx"),
            P("gx", None, "gy"),
            P(None, "gy"),
            P("gy", "gx"),
            P("gx"),
            P("gx"),
            P("gx"),
            P("gx", "gy"),
            P("gy"),
            P("gy", "gx"),
            P("gx"),
        ),
        out_specs=(
            P(None, ("dp", "gy"), "gx"),
            P(None, ("dp", "gy"), "gx"),
            P("gx"),
            P("gx"),
            P("gx", None, "gy"),
            P(None, "gy"),
            P("gy", "gx"),
            P("gx"),
            P("gx"),
            P("gx"),
            P("gx", "gy"),
            P("gy"),
            P("gy", "gx"),
            P("gx"),
        ),
        check_vma=False,
    )
```

profile of v0, /device:TPU:0, one launch (start us, length us, event | category | flops | bytes accessed | tf_op | source)
XLA Modules:
  0.0 3569.1 jit_solution(3430166739071463660)
XLA Ops:
  11.1 12.9 all-reduce.4
  28.3 68.2 %all-gather.52.cloned.1.call-done = bf16[4,1458,288]{1,2,0:T(8,128)(2,1)} async-done(((bf16[1,1458,288]{1,2,0:T(8,128)(2,1)}), bf16[4,1458,288]{1,2,0:T(8,128)(2,1)}) %all-gather.52.cloned.1.call-update) | async-done | bytes 3359248 | tf_op jit(solution)/shard_map/all_gather | solution.py:59
  101.5 65.8 %all-gather.62.cloned.1.call-done = bf16[4,1458,288]{1,2,0:T(8,128)(2,1)} async-done(((bf16[1,1458,288]{1,2,0:T(8,128)(2,1)}), bf16[4,1458,288]{1,2,0:T(8,128)(2,1)}) %all-gather.62.cloned.1.call-update) | async-done | bytes 3359248 | tf_op jit(solution)/shard_map/all_gather | solution.py:59
  172.0 29.6 all-gather.42.cloned.1.call-done
  285.7 26.1 all-gather.64.cloned.1.call-done
  311.8 53.7 %all-to-all-done.1 = bf16[4,1458,288]{1,2,0:T(8,128)(2,1)} async-done(((bf16[4,1458,288]{1,2,0:T(8,128)(2,1)}), bf16[4,1458,288]{1,2,0:T(8,128)(2,1)}, u32[]{:S(2)}, u32[]{:S(2)}) %all-to-all-start.1) | async-done | bytes 3359264 | tf_op jit(solution)/shard_map/all_to_all | solution.py:70
  379.5 187.2 %all_gather.83 = bf16[1152,288]{1,0:T(8,128)(2,1)S(1)} all-gather(bf16[288,288]{1,0:T(8,128)(2,1)} %param.28), channel_id=1, replica_groups=mesh['dp'=2,'gx'=4,'gy'=4] {'gy'}, dimensions={0}, use_global_device_ids=true | all-gather | bytes 829440 | tf_op jit(solution)/shard_map/all_gather | solution.py:74
  607.9 38.1 %reduce.2 = bf16[5832,288]{1,0:T(8,128)(2,1)} reduce(bf16[1,5832,288]{2,0,1:T(2,128)(2,1)} %all-gather.48.cloned.1.call-done, bf16[]{:T(256)} %constant.107), dimensions={0}, to_apply=%all-gather.reduce_sub_computation | reduce | bytes 6718466 | tf_op jit(solution)/shard_map/all_gather | solution.py:59
  663.8 54.7 %all-to-all-done.8 = bf16[4,1458,288]{1,2,0:T(8,128)(2,1)} async-done(((bf16[4,1458,288]{1,2,0:T(8,128)(2,1)}), bf16[4,1458,288]{1,2,0:T(8,128)(2,1)}, u32[]{:S(2)}, u32[]{:S(2)}) %all-to-all-start.8) | async-done | bytes 3359264 | tf_op jit(solution)/shard_map/all_to_all | solution.py:60
  733.6 26.0 all-gather.44.cloned.1.call-done
  759.6 19.1 all-to-all-done.2
  778.7 14.4 fusion.83
  793.1 126.9 %all-gather.50.cloned.1.call-done = bf16[1,5832,288]{2,0,1:T(2,128)(2,1)} async-done(((bf16[1,1458,288]{2,0,1:T(2,128)(2,1)}), bf16[1,5832,288]{2,0,1:T(2,128)(2,1)}) %all-gather.50.cloned.1.call-update) | async-done | bytes 3359248 | tf_op jit(solution)/shard_map/all_gather | solution.py:59
  920.0 38.1 %reduce.3 = bf16[5832,288]{1,0:T(8,128)(2,1)} reduce(bf16[1,5832,288]{2,0,1:T(2,128)(2,1)} %all-gather.50.cloned.1.call-done, bf16[]{:T(256)} %constant.107), dimensions={0}, to_apply=%all-gather.1.reduce_sub_computation | reduce | bytes 6718466 | tf_op jit(solution)/shard_map/all_gather | solution.py:59
  970.3 60.6 %all_to_all.304 = bf16[4,1458,288]{1,2,0:T(8,128)(2,1)} all-to-all(bf16[4,1458,288]{1,2,0:T(8,128)(2,1)} %copy.218), channel_id=1, replica_groups=mesh['dp'=2,'gx'=4,'gy'=4] {'gx'}, dimensions={0} | all-to-all | bytes 6718464 | tf_op jit(solution)/shard_map/all_to_all | solution.py:60
  1046.2 69.0 %all-to-all-done.6 = bf16[4,1458,288]{1,2,0:T(8,128)(2,1)} async-done(((bf16[4,1458,288]{1,2,0:T(8,128)(2,1)}), bf16[4,1458,288]{1,2,0:T(8,128)(2,1)}, u32[]{:S(2)}, u32[]{:S(2)}) %all-to-all-start.6) | async-done | bytes 3359264 | tf_op jit(solution)/shard_map/all_to_all | solution.py:60
  1115.2 14.1 fusion.82
  1136.2 76.6 %all-gather.80.cloned.1.call-done = bf16[4,1458,1076]{1,2,0:T(8,128)(2,1)} async-done(((bf16[1,1458,1076]{1,2,0:T(8,128)(2,1)}), bf16[4,1458,1076]{1,2,0:T(8,128)(2,1)}) %all-gather.80.cloned.1.call-update) | async-done | bytes 12550480 | tf_op jit(solution)/shard_map/all_gather | solution.py:69
  1212.8 210.8 %all-to-all-done.9 = bf16[4,1458,1076]{1,2,0:T(8,128)(2,1)} async-done(((bf16[4,1458,1076]{1,2,0:T(8,128)(2,1)}), bf16[4,1458,1076]{1,2,0:T(8,128)(2,1)}, u32[]{:S(2)}, u32[]{:S(2)}) %all-to-all-start.9) | async-done | bytes 12550496 | tf_op jit(solution)/shard_map/all_to_all | solution.py:70
  1430.9 138.4 %all-gather.72.cloned.1.call-done = bf16[4,1076,288]{1,2,0:T(8,128)(2,1)} async-done(((bf16[1,1076,288]{1,2,0:T(8,128)(2,1)}), bf16[4,1076,288]{1,2,0:T(8,128)(2,1)}) %all-gather.72.cloned.1.call-update) | async-done | bytes 2479120 | tf_op jit(solution)/shard_map/all_gather | solution.py:72
  1579.6 17.0 all_to_all.263
  1596.6 163.3 %all-to-all-done.13 = bf16[4,1458,1076]{1,2,0:T(8,128)(2,1)} async-done(((bf16[4,1458,1076]{1,2,0:T(8,128)(2,1)}), bf16[4,1458,1076]{1,2,0:T(8,128)(2,1)}, u32[]{:S(2)}, u32[]{:S(2)}) %all-to-all-start.13) | async-done | bytes 12550496 | tf_op jit(solution)/shard_map/all_to_all | solution.py:70
  1759.9 17.0 all_to_all.279
  1814.8 66.5 %all-gather.74.cloned.1.call-done = bf16[4,1458,288]{1,2,0:T(8,128)(2,1)} async-done(((bf16[1,1458,288]{1,2,0:T(8,128)(2,1)}), bf16[4,1458,288]{1,2,0:T(8,128)(2,1)}) %all-gather.74.cloned.1.call-update) | async-done | bytes 3359248 | tf_op jit(solution)/shard_map/all_gather | solution.py:59
  1885.1 114.2 %all-gather.58.cloned.1.call-done = bf16[4,1458,1076]{1,2,0:T(8,128)(2,1)} async-done(((bf16[1,1458,1076]{1,2,0:T(8,128)(2,1)}), bf16[4,1458,1076]{1,2,0:T(8,128)(2,1)}) %all-gather.58.cloned.1.call-update) | async-done | bytes 12550480 | tf_op jit(solution)/shard_map/all_gather | solution.py:69
  2025.3 59.5 %while.46 = (s32[]{:T(128)}, bf16[2,729,3,4,72]{1,4,3,2,0:T(8,128)(2,1)}, bf16[2,729,3,4,72]{1,4,3,2,0:T(8,128)(2,1)}, f32[2,4,729]{2,1,0:T(4,128)S(1)}, bf16[2,729,4,72]{1,3,2,0:T(8,128)(2,1)S(1)}, /*index=5*/s32[]{:T(128)}) while((s32[]{:T(128)}, bf16[2,729,3,4,72]{1,4,3,2,0:T(8,128)(2,1)}, bf16[2,729,3,4,72]{1,4,3,2,0:T(8,128)(2,1)}, ...), condition=%wide.region_30.31_spmd, body=%wide.region_28.30_spmd.sunk | while | flops 1560885248 | bytes 142425280 | solution.py:214
  2100.4 250.7 %all-to-all-done.3 = bf16[4,1458,1076]{1,2,0:T(8,128)(2,1)} async-done(((bf16[4,1458,1076]{1,2,0:T(8,128)(2,1)}), bf16[4,1458,1076]{1,2,0:T(8,128)(2,1)}, u32[]{:S(2)}, u32[]{:S(2)}) %all-to-all-start.3) | async-done | bytes 12550496 | tf_op jit(solution)/shard_map/all_to_all | solution.py:70
  2355.9 41.2 %all-to-all-done.14 = bf16[4,1458,288]{1,2,0:T(8,128)(2,1)} async-done(((bf16[4,1458,288]{1,2,0:T(8,128)(2,1)}), bf16[4,1458,288]{1,2,0:T(8,128)(2,1)}, u32[]{:S(2)}, u32[]{:S(2)}) %all-to-all-start.14) | async-done | bytes 3359264 | tf_op jit(solution)/shard_map/all_to_all | solution.py:60
  2411.6 59.4 %while.47 = (s32[]{:T(128)}, bf16[2,729,3,4,72]{1,4,3,2,0:T(8,128)(2,1)}, bf16[2,729,3,4,72]{1,4,3,2,0:T(8,128)(2,1)}, f32[2,4,729]{2,1,0:T(4,128)S(1)}, bf16[2,729,4,72]{1,3,2,0:T(8,128)(2,1)S(1)}, /*index=5*/s32[]{:T(128)}) while((s32[]{:T(128)}, bf16[2,729,3,4,72]{1,4,3,2,0:T(8,128)(2,1)}, bf16[2,729,3,4,72]{1,4,3,2,0:T(8,128)(2,1)}, ...), condition=%wide.region_41.42_spmd, body=%wide.region_39.41_spmd.sunk | while | flops 1560885248 | bytes 142425280 | solution.py:214
  2486.5 280.6 %all-to-all-done.7 = bf16[4,1458,1076]{1,2,0:T(8,128)(2,1)} async-done(((bf16[4,1458,1076]{1,2,0:T(8,128)(2,1)}), bf16[4,1458,1076]{1,2,0:T(8,128)(2,1)}, u32[]{:S(2)}, u32[]{:S(2)}) %all-to-all-start.7) | async-done | bytes 12550496 | tf_op jit(solution)/shard_map/all_to_all | solution.py:70
  2812.8 19.3 copy.238
  2832.1 20.9 copy.236
  2904.1 41.9 %copy.232 = bf16[4,1458,1076]{1,0,2:T(4,128)(2,1)} copy(bf16[4,1458,1076]{1,2,0:T(8,128)(2,1)} %all-gather.70.cloned.1.call-done) | data formatting | bytes 25100928 | tf_op jit(solution)/shard_map/all_gather | solution.py:69
  2946.0 25.3 reshape.342
  2971.3 41.8 %copy.234 = bf16[4,1458,1076]{1,0,2:T(4,128)(2,1)} copy(bf16[4,1458,1076]{1,2,0:T(8,128)(2,1)} %all-gather.80.cloned.1.call-done) | data formatting | bytes 25100928 | tf_op jit(solution)/shard_map/all_gather | solution.py:69
  3013.2 25.5 reshape.352
  3038.7 41.8 %copy.235 = bf16[4,1458,1076]{1,0,2:T(4,128)(2,1)} copy(bf16[4,1458,1076]{1,2,0:T(8,128)(2,1)} %all-gather.58.cloned.1.call-done) | data formatting | bytes 25100928 | tf_op jit(solution)/shard_map/all_gather | solution.py:69
  3080.5 25.3 reshape.330
  3105.8 41.8 %copy.237 = bf16[4,1458,1076]{1,0,2:T(4,128)(2,1)} copy(bf16[4,1458,1076]{1,2,0:T(8,128)(2,1)} %all-gather.68.cloned.1.call-done) | data formatting | bytes 25100928 | tf_op jit(solution)/shard_map/all_gather | solution.py:69
  3147.6 25.3 reshape.340
  3231.4 17.1 all_to_all.239
  3248.6 17.4 all_to_all.255
  3307.9 14.4 reshape.348
  3322.3 14.8 reshape.356
  3381.0 84.2 %all-reduce.9.cloned.1.call-done = (f32[288,3,288]{0,2,1:T(8,128)}, f32[288,288]{1,0:T(8,128)}, f32[288,1076]{1,0:T(8,128)}, f32[1076,288]{0,1:T(8,128)}) async-done(((f32[288,3,288]{0,2,1:T(8,128)}, f32[288,288]{1,0:T(8,128)}, f32[288,1076]{1,0:T(8,128)}, f32[1076,288]{0,1:T(8,128)}), (f32[288,3,288]{0,2,1:T(8,128)}, f32[288,288]{1,0:T(8,128)}, f32[288,1076]{1,0:T(8,128)}, ...) | async-done | bytes 3806224 | tf_op jit(solution)/shard_map/psum | solution.py:123
  3468.1 14.5 copy.213
  3482.6 14.5 copy.223
  3537.6 21.7 all-reduce
  (519 shorter events, 787.5 us)
Async XLA Ops:
  7.2 89.3 %all-gather.52.cloned.1.call-start = ((), (), s32[]{:S(2)}) async-start(), calls=%async_computation.21 | async-start | bytes 4423680 | tf_op jit(solution)/shard_map/all_gather | solution.py:59
  26.0 141.2 %all-gather.62.cloned.1.call-start = ((), (), s32[]{:S(2)}) async-start(), calls=%async_computation.26 | async-start | bytes 4423680 | tf_op jit(solution)/shard_map/all_gather | solution.py:59
  26.8 174.8 %all-gather.42.cloned.1.call-start = ((), (), s32[]{:S(2)}) async-start(), calls=%async_computation.16 | async-start | bytes 2580480 | tf_op jit(solution)/shard_map/all_gather | solution.py:64
  27.2 69.3 %copy-start.36 = (bf16[288,3,288]{0,2,1:T(8,128)(2,1)}, bf16[288,3,288]{0,2,1:T(8,128)(2,1)S(1)}, u32[]{:S(2)}) copy-start(bf16[288,3,288]{0,2,1:T(8,128)(2,1)S(1)} %copy.195) | copy-start | bytes 1492996
  28.3 73.0 %copy-start.96 = (bf16[2,288]{1,0:T(2,128)(2,1)S(1)}, bf16[2,288]{1,0:T(2,128)(2,1)}, u32[]{:S(2)}) copy-start(bf16[2,288]{1,0:T(2,128)(2,1)} %param.27) | copy-start | bytes 3460
  96.5 70.8 %all-to-all-start = ((bf16[4,1458,288]{1,2,0:T(8,128)(2,1)}), bf16[4,1458,288]{1,2,0:T(8,128)(2,1)}, u32[]{:S(2)}, u32[]{:S(2)}) async-start(bf16[4,1458,288]{1,2,0:T(8,128)(2,1)} %all-gather.52.cloned.1.call-done), calls=%async_computation | async-start | bytes 7077888 | tf_op jit(solution)/shard_map/all_to_all | solution.py:60
  167.3 71.7 %all-to-all-start.4 = ((bf16[4,1458,288]{1,2,0:T(8,128)(2,1)}), bf16[4,1458,288]{1,2,0:T(8,128)(2,1)}, u32[]{:S(2)}, u32[]{:S(2)}) async-start(bf16[4,1458,288]{1,2,0:T(8,128)(2,1)} %all-gather.62.cloned.1.call-done), calls=%async_computation.4 | async-start | bytes 7077888 | tf_op jit(solution)/shard_map/all_to_all | solution.py:60
  172.0 108.9 %all-gather.54.cloned.1.call-start = ((), (), s32[]{:S(2)}) async-start(), calls=%async_computation.22 | async-start | bytes 4423680 | tf_op jit(solution)/shard_map/all_gather | solution.py:69
  238.9 72.9 %all-gather.64.cloned.1.call-start = ((), (), s32[]{:S(2)}) async-start(), calls=%async_computation.27 | async-start | bytes 4423680 | tf_op jit(solution)/shard_map/all_gather | solution.py:69
  280.9 84.6 %all-to-all-start.1 = ((bf16[4,1458,288]{1,2,0:T(8,128)(2,1)}), bf16[4,1458,288]{1,2,0:T(8,128)(2,1)}, u32[]{:S(2)}, u32[]{:S(2)}) async-start(bf16[4,1458,288]{1,2,0:T(8,128)(2,1)} %all-gather.54.cloned.1.call-done), calls=%async_computation.1 | async-start | bytes 7077888 | tf_op jit(solution)/shard_map/all_to_all | solution.py:70
  285.7 84.6 %copy-start.10 = (bf16[2,1458,288]{1,2,0:T(8,128)(2,1)S(1)}, bf16[2,1458,288]{1,2,0:T(8,128)(2,1)}, u32[]{:S(2)}) copy-start(bf16[2,1458,288]{1,2,0:T(8,128)(2,1)} %param.23) | copy-start | bytes 5038852
  365.5 206.8 %all-to-all-start.5 = ((bf16[4,1458,288]{1,2,0:T(8,128)(2,1)}), bf16[4,1458,288]{1,2,0:T(8,128)(2,1)}, u32[]{:S(2)}, u32[]{:S(2)}) async-start(bf16[4,1458,288]{1,2,0:T(8,128)(2,1)} %all-gather.64.cloned.1.call-done), calls=%async_computation.5 | async-start | bytes 7077888 | tf_op jit(solution)/shard_map/all_to_all | solution.py:70
  370.2 237.6 %all-gather.48.cloned.1.call-start = ((), (), s32[]{:S(2)}) async-start(), calls=%async_computation.19 | async-start | bytes 11197440 | tf_op jit(solution)/shard_map/all_gather | solution.py:59
  371.6 195.9 %copy-start.8 = (bf16[2,1458,288]{1,2,0:T(8,128)(2,1)S(1)}, bf16[2,1458,288]{1,2,0:T(8,128)(2,1)}, u32[]{:S(2)}) copy-start(bf16[2,1458,288]{1,2,0:T(8,128)(2,1)} %param.22) | copy-start | bytes 5038852
  378.2 340.3 %all-gather.56.cloned.1.call-start = ((), (), s32[]{:S(2)}) async-start(), calls=%async_computation.23 | async-start | bytes 4423680 | tf_op jit(solution)/shard_map/all_gather | solution.py:59
  378.3 188.4 %copy-start.103 = (f32[288]{0:T(512)}, f32[288]{0:T(512)S(1)}, u32[]{:S(2)}) copy-start(f32[288]{0:T(512)S(1)} %convert_element_type.181) | copy-start | bytes 3460
  589.0 1219.0 %copy-start.60 = (f32[1458]{0:T(1024)}, f32[1458]{0:T(1024)S(1)}, u32[]{:S(2)}) copy-start(f32[1458]{0:T(1024)S(1)} %get-tuple-element.374) | copy-start | bytes 17500
  589.0 1219.0 %copy-start.62 = (f32[1458]{0:T(1024)}, f32[1458]{0:T(1024)S(1)}, u32[]{:S(2)}) copy-start(f32[1458]{0:T(1024)S(1)} %get-tuple-element.375) | copy-start | bytes 17500
  593.1 130.3 %all-gather.46.cloned.1.call-start = ((), (), s32[]{:S(2)}) async-start(), calls=%async_computation.18 | async-start | bytes 3317760 | tf_op jit(solution)/shard_map/all_gather | solution.py:62
  593.9 165.7 %all-gather.44.cloned.1.call-start = ((), (), s32[]{:S(2)}) async-start(), calls=%async_computation.17 | async-start | bytes 3317760 | tf_op jit(solution)/shard_map/all_gather | solution.py:64
  594.6 325.4 %all-gather.50.cloned.1.call-start = ((), (), s32[]{:S(2)}) async-start(), calls=%async_computation.20 | async-start | bytes 11197440 | tf_op jit(solution)/shard_map/all_gather | solution.py:59
  658.3 60.2 %all-to-all-start.8 = ((bf16[4,1458,288]{1,2,0:T(8,128)(2,1)}), bf16[4,1458,288]{1,2,0:T(8,128)(2,1)}, u32[]{:S(2)}, u32[]{:S(2)}) async-start(bf16[4,1458,288]{1,2,0:T(8,128)(2,1)} %copy.206), calls=%async_computation.8 | async-start | bytes 7077888 | tf_op jit(solution)/shard_map/all_to_all | solution.py:60
  663.0 367.9 %all-gather.66.cloned.1.call-start = ((), (), s32[]{:S(2)}) async-start(), calls=%async_computation.28 | async-start | bytes 4423680 | tf_op jit(solution)/shard_map/all_gather | solution.py:59
  663.8 59.5 %copy-start.97 = (bf16[1076]{0:T(1024)(128)(2,1)S(1)}, bf16[1076]{0:T(1024)(128)(2,1)}, u32[]{:S(2)}) copy-start(bf16[1076]{0:T(1024)(128)(2,1)} %param.33) | copy-start | bytes 6460
  718.5 60.2 %all-to-all-start.2 = ((bf16[4,1458,288]{1,2,0:T(8,128)(2,1)}), bf16[4,1458,288]{1,2,0:T(8,128)(2,1)}, u32[]{:S(2)}, u32[]{:S(2)}) async-start(bf16[4,1458,288]{1,2,0:T(8,128)(2,1)} %all-gather.56.cloned.1.call-done), calls=%async_computation.2 | async-start | bytes 7077888 | tf_op jit(solution)/shard_map/all_to_all | solution.py:60
  723.2 406.1 %all-gather.70.cloned.1.call-start = ((), (), s32[]{:S(2)}) async-start(), calls=%async_computation.30 | async-start | bytes 16588800 | tf_op jit(solution)/shard_map/all_gather | solution.py:69
  1030.9 84.2 %all-to-all-start.6 = ((bf16[4,1458,288]{1,2,0:T(8,128)(2,1)}), bf16[4,1458,288]{1,2,0:T(8,128)(2,1)}, u32[]{:S(2)}, u32[]{:S(2)}) async-start(bf16[4,1458,288]{1,2,0:T(8,128)(2,1)} %all-gather.66.cloned.1.call-done), calls=%async_computation.6 | async-start | bytes 7077888 | tf_op jit(solution)/shard_map/all_to_all | solution.py:60
  1035.7 177.1 %all-gather.80.cloned.1.call-start = ((), (), s32[]{:S(2)}) async-start(), calls=%async_computation.35 | async-start | bytes 16588800 | tf_op jit(solution)/shard_map/all_gather | solution.py:69
  1129.4 294.2 %all-to-all-start.9 = ((bf16[4,1458,1076]{1,2,0:T(8,128)(2,1)}), bf16[4,1458,1076]{1,2,0:T(8,128)(2,1)}, u32[]{:S(2)}, u32[]{:S(2)}) async-start(bf16[4,1458,1076]{1,2,0:T(8,128)(2,1)} %all-gather.70.cloned.1.call-done), calls=%async_computation.9 | async-start | bytes 26542080 | tf_op jit(solution)/shard_map/all_to_all | solution.py:70
  1423.6 336.3 %all-to-all-start.13 = ((bf16[4,1458,1076]{1,2,0:T(8,128)(2,1)}), bf16[4,1458,1076]{1,2,0:T(8,128)(2,1)}, u32[]{:S(2)}, u32[]{:S(2)}) async-start(bf16[4,1458,1076]{1,2,0:T(8,128)(2,1)} %all-gather.80.cloned.1.call-done), calls=%async_computation.13 | async-start | bytes 26542080 | tf_op jit(solution)/shard_map/all_to_all | solution.py:70
  1430.1 139.2 %all-gather.72.cloned.1.call-start = ((), (), s32[]{:S(2)}) async-start(), calls=%async_computation.31 | async-start | bytes 3317760 | tf_op jit(solution)/shard_map/all_gather | solution.py:72
  1430.6 450.7 %all-gather.74.cloned.1.call-start = ((), (), s32[]{:S(2)}) async-start(), calls=%async_computation.32 | async-start | bytes 4423680 | tf_op jit(solution)/shard_map/all_gather | solution.py:59
  1813.0 186.2 %all-gather.58.cloned.1.call-start = ((), (), s32[]{:S(2)}) async-start(), calls=%async_computation.24 | async-start | bytes 16588800 | tf_op jit(solution)/shard_map/all_gather | solution.py:69
  1813.6 537.5 %all-gather.82.cloned.1.call-start = ((), (), s32[]{:S(2)}) async-start(), calls=%async_computation.36 | async-start | bytes 4423680 | tf_op jit(solution)/shard_map/all_gather | solution.py:59
  1814.2 541.7 %all-gather.68.cloned.1.call-start = ((), (), s32[]{:S(2)}) async-start(), calls=%async_computation.29 | async-start | bytes 16588800 | tf_op jit(solution)/shard_map/all_gather | solution.py:69
  1881.3 118.0 %all-to-all-start.10 = ((bf16[4,1458,288]{1,2,0:T(8,128)(2,1)}), bf16[4,1458,288]{1,2,0:T(8,128)(2,1)S(1)}, u32[]{:S(2)}, u32[]{:S(2)}) async-start(bf16[4,1458,288]{1,2,0:T(8,128)(2,1)} %all-gather.74.cloned.1.call-done), calls=%async_computation.10 | async-start | bytes 7077888 | tf_op jit(solution)/shard_map/all_to_all | solution.py:60
  1999.3 351.8 %all-to-all-start.3 = ((bf16[4,1458,1076]{1,2,0:T(8,128)(2,1)}), bf16[4,1458,1076]{1,2,0:T(8,128)(2,1)}, u32[]{:S(2)}, u32[]{:S(2)}) async-start(bf16[4,1458,1076]{1,2,0:T(8,128)(2,1)} %all-gather.58.cloned.1.call-done), calls=%async_computation.3 | async-start | bytes 26542080 | tf_op jit(solution)/shard_map/all_to_all | solution.py:70
  2005.8 761.4 %all-gather.76.cloned.1.call-start = ((), (), s32[]{:S(2)}) async-start(), calls=%async_computation.33 | async-start | bytes 13117440 | tf_op jit(solution)/shard_map/all_gather | solution.py:69
  2351.1 46.0 %all-to-all-start.14 = ((bf16[4,1458,288]{1,2,0:T(8,128)(2,1)}), bf16[4,1458,288]{1,2,0:T(8,128)(2,1)}, u32[]{:S(2)}, u32[]{:S(2)}) async-start(bf16[4,1458,288]{1,2,0:T(8,128)(2,1)} %all-gather.82.cloned.1.call-done), calls=%async_computation.14 | async-start | bytes 7077888 | tf_op jit(solution)/shard_map/all_to_all | solution.py:60
  2355.9 49.8 %copy-start.50 = (bf16[288,1152]{0,1:T(8,128)(2,1)S(1)}, bf16[288,1152]{0,1:T(8,128)(2,1)}, u32[]{:S(2)}) copy-start(bf16[288,1152]{0,1:T(8,128)(2,1)} %copy-done.49) | copy-start | bytes 1990660
  2397.1 370.1 %all-to-all-start.7 = ((bf16[4,1458,1076]{1,2,0:T(8,128)(2,1)}), bf16[4,1458,1076]{1,2,0:T(8,128)(2,1)}, u32[]{:S(2)}, u32[]{:S(2)}) async-start(bf16[4,1458,1076]{1,2,0:T(8,128)(2,1)} %all-gather.68.cloned.1.call-done), calls=%async_computation.7 | async-start | bytes 26542080 | tf_op jit(solution)/shard_map/all_to_all | solution.py:70
  2403.5 370.5 %all-gather.78.cloned.1.call-start = ((), (), s32[]{:S(2)}) async-start(), calls=%async_computation.34 | async-start | bytes 2580480 | tf_op jit(solution)/shard_map/all_gather | solution.py:72
  2404.7 374.7 %all-gather.60.cloned.1.call-start = ((), (), s32[]{:S(2)}) async-start(), calls=%async_computation.25 | async-start | bytes 3317760 | tf_op jit(solution)/shard_map/all_gather | solution.py:74
  2405.4 767.5 %all-gather.84.cloned.1.call-start = ((), (), s32[]{:S(2)}) async-start(), calls=%async_computation.37 | async-start | bytes 13117440 | tf_op jit(solution)/shard_map/all_gather | solution.py:69
  2486.5 286.9 %copy-start.109 = (bf16[288]{0:T(512)(128)(2,1)S(1)}, bf16[288]{0:T(512)(128)(2,1)}, u32[]{:S(2)}) copy-start(bf16[288]{0:T(512)(128)(2,1)} %param.35) | copy-start | bytes 1732
  2767.2 405.8 %all-to-all-start.11 = ((bf16[4,1458,864]{2,1,0:T(8,128)(2,1)}), bf16[4,1458,864]{2,1,0:T(8,128)(2,1)}, u32[]{:S(2)}, u32[]{:S(2)}) async-start(bf16[4,1458,864]{2,1,0:T(8,128)(2,1)} %all-gather.76.cloned.1.call-done), calls=%async_computation.11 | async-start | bytes 20987904 | tf_op jit(solution)/shard_map/all_to_all | solution.py:70
  3172.9 309.7 %all-to-all-start.15 = ((bf16[4,1458,864]{2,1,0:T(8,128)(2,1)}), bf16[4,1458,864]{2,1,0:T(8,128)(2,1)}, u32[]{:S(2)}, u32[]{:S(2)}) async-start(bf16[4,1458,864]{2,1,0:T(8,128)(2,1)} %all-gather.84.cloned.1.call-done), calls=%async_computation.15 | async-start | bytes 20987904 | tf_op jit(solution)/shard_map/all_to_all | solution.py:70
  3179.0 286.2 %all-reduce.9.cloned.1.call-start = ((), (), s32[]{:S(2)}) async-start(), calls=%async_computation.38 | async-start | bytes 8847360 | tf_op jit(solution)/shard_map/psum | solution.py:123
  (111 other events, 916.3 us)
Sparse Core Ops, SparseCore 0:
  26.2 70.3 all-gather.51
  98.6 68.5 all-gather.61
  169.4 32.1 all-gather.41
  239.0 30.7 all-gather.53
  281.0 30.7 all-gather.63
  378.3 229.4 all-gather.47
  610.0 68.0 all-gather.55
  679.6 38.6 all-gather.45
  719.9 39.6 all-gather.43
  761.0 158.9 all-gather.49
  922.1 68.1 all-gather.65
  991.8 136.1 all-gather.69
  1129.5 83.2 all-gather.79
  1432.2 137.0 all-gather.71
  1813.2 68.1 all-gather.73
  1882.7 116.4 all-gather.57
  2001.3 166.1 all-gather.81
  2168.9 83.2 all-gather.67
  2253.8 70.2 all-gather.75
  2406.2 122.8 all-gather.77
  2530.7 91.3 all-gather.59
  2623.7 163.8 all-gather.83
  3350.5 114.6 all-reduce.8
where the time goes:
time: 3590 us; the launch traced here: 3570 us
  waiting for transfers between devices  1980 us (55%)
  local copies, waits for them, and re-layouts  705 us (20%)
  blocking collectives  336 us (9%)
  matrix products  263 us (7%)
  other arithmetic  187 us (5%)
  starting transfers between devices  82.3 us (2%)
    all_to_all x8, waiting for transfers between devices, join(): lax.all_to_all(gathered, 'gy', split_axis=0, concat_axis=1, tiled=True)  959 us
    all_gather x8, waiting for transfers between devices, spread(): gathered = lax.all_gather(row_block, 'gy', axis=0, tiled=True)  336 us
    unnamed x240, local copies, waits for them, and re-layouts  258 us
    all_gather x8, waiting for transfers between devices, join(): gathered = lax.all_gather(row_block, 'gx', axis=0, tiled=True)  217 us
    all_gather x1, blocking collectives, join(): whole_weight = lax.all_gather(weight, 'gy', axis=0, tiled=True)  187 us
    all_to_all x7, waiting for transfers between devices, spread(): lax.all_to_all(gathered, 'gx', split_axis=0, concat_axis=1, tiled=True)  184 us
    all_gather x6, local copies, waits for them, and re-layouts, join(): gathered = lax.all_gather(row_block, 'gx', axis=0, tiled=True)  176 us
    all_gather x2, waiting for transfers between devices, join(): whole_weight = lax.all_gather(weight, 'gy', axis=1, tiled=True)  138 us
  transfers between devices with their start and end apart: 38, of which 21 were waited for; matrix products, arithmetic and copies ran while one was open for 28% of the time, Pallas kernels for 0%

commit v1 on v0

v1 whole, which is shorter than its diff:
```python
import functools

import jax
import jax.numpy as jnp
from jax import lax
from jax.experimental import pallas as pl
from jax.experimental.pallas import tpu as pltpu
from jax.sharding import PartitionSpec as P

HEAD_DIM = 72
SEQ = 729
MICRO = 2
EPSILON = 1e-06
QUERY_ROWS = 384
BF16 = jnp.bfloat16
F32 = jnp.float32
VMEM_BYTES = 60 * 2**20


def contract(left, right, left_dim, right_dim):
    return lax.dot_general(
        left, right, (((left_dim,), (right_dim,)), ((), ())), preferred_element_type=F32
    )


def row_blocks(total, size):
    return [(low, min(low + size, total)) for low in range(0, total, size)]


def attend_kernel(heads, packed_ref, mix_ref, total_ref):
    seq = packed_ref.shape[1]
    width = heads * HEAD_DIM
    scaling = HEAD_DIM ** (-0.5)
    for head in range(heads):
        first = head * HEAD_DIM
        last = first + HEAD_DIM
        keys = packed_ref[0, :, width + first : width + last]
        values = packed_ref[0, :, 2 * width + first : 2 * width + last]
        for low, high in row_blocks(seq, QUERY_ROWS):
            queries = packed_ref[0, low:high, first:last]
            scores = contract(queries, keys, 1, 1) * scaling
            row_max = jnp.max(scores, axis=1, keepdims=True)
            exponent = jnp.exp(scores - row_max)
            row_total = jnp.sum(exponent, axis=1, keepdims=True)
            probability = (exponent * (1.0 / row_total)).astype(BF16)
            mix_ref[0, low:high, first:last] = contract(probability, values, 1, 0).astype(BF16)
            total_ref[0, low:high, head : head + 1] = row_max + jnp.log(row_total)


def attend(packed, heads):
    groups, seq, _ = packed.shape
    width = heads * HEAD_DIM
    return pl.pallas_call(
        functools.partial(attend_kernel, heads),
        grid=(groups,),
        in_specs=[pl.BlockSpec((1, seq, 3 * width), lambda i: (i, 0, 0))],
        out_specs=[
            pl.BlockSpec((1, seq, width), lambda i: (i, 0, 0)),
            pl.BlockSpec((1, seq, heads), lambda i: (i, 0, 0)),
        ],
        out_shape=[
            jax.ShapeDtypeStruct((groups, seq, width), BF16),
            jax.ShapeDtypeStruct((groups, seq, heads), F32),
        ],
        compiler_params=pltpu.CompilerParams(vmem_limit_bytes=VMEM_BYTES),
        cost_estimate=pl.CostEstimate(
            flops=12 * groups * heads * seq * seq * HEAD_DIM,
            bytes_accessed=8 * groups * seq * width,
            transcendentals=groups * heads * seq * seq,
        ),
        name="attend",
    )(packed)


def attend_back_kernel(heads, packed_ref, total_ref, grad_ref, out_ref, key_sum, value_sum):
    seq = packed_ref.shape[1]
    width = heads * HEAD_DIM
    scaling = HEAD_DIM ** (-0.5)
    for head in range(heads):
        first = head * HEAD_DIM
        last = first + HEAD_DIM
        keys = packed_ref[0, :, width + first : width + last]
        values = packed_ref[0, :, 2 * width + first : 2 * width + last]
        for low, high in row_blocks(seq, QUERY_ROWS):
            queries = packed_ref[0, low:high, first:last]
            grads = grad_ref[0, low:high, first:last]
            scores = contract(keys, queries, 1, 1) * scaling
            probability = jnp.exp(scores - total_ref[0, head : head + 1, low:high])
            grad_values = contract(probability.astype(BF16), grads, 1, 0)
            grad_prob = contract(values, grads, 1, 1)
            inner = jnp.sum(probability * grad_prob, axis=0, keepdims=True)
            grad_scores = (probability * (grad_prob - inner)).astype(BF16)
            grad_keys = contract(grad_scores, queries, 1, 0)
            grad_queries = contract(grad_scores, keys, 0, 0) * scaling
            out_ref[0, low:high, first:last] = grad_queries.astype(BF16)
            if low == 0:
                key_sum[...] = grad_keys
                value_sum[...] = grad_values
            else:
                key_sum[...] += grad_keys
                value_sum[...] += grad_values
        out_ref[0, :, width + first : width + last] = (key_sum[...] * scaling).astype(BF16)
        out_ref[0, :, 2 * width + first : 2 * width + last] = value_sum[...].astype(BF16)


def attend_back(packed, total, grads, heads):
    groups, seq, _ = packed.shape
    width = heads * HEAD_DIM
    return pl.pallas_call(
        functools.partial(attend_back_kernel, heads),
        grid=(groups,),
        in_specs=[
            pl.BlockSpec((1, seq, 3 * width), lambda i: (i, 0, 0)),
            pl.BlockSpec((1, heads, seq), lambda i: (i, 0, 0)),
            pl.BlockSpec((1, seq, width), lambda i: (i, 0, 0)),
        ],
        out_specs=pl.BlockSpec((1, seq, 3 * width), lambda i: (i, 0, 0)),
        out_shape=jax.ShapeDtypeStruct((groups, seq, 3 * width), BF16),
        scratch_shapes=[pltpu.VMEM((seq, HEAD_DIM), F32), pltpu.VMEM((seq, HEAD_DIM), F32)],
        compiler_params=pltpu.CompilerParams(vmem_limit_bytes=VMEM_BYTES),
        cost_estimate=pl.CostEstimate(
            flops=30 * groups * heads * seq * seq * HEAD_DIM,
            bytes_accessed=14 * groups * seq * width,
            transcendentals=groups * heads * seq * seq,
        ),
        name="attend_back",
    )(packed, total, grads)


def norm_forward(values):
    center = jnp.mean(values, axis=1, keepdims=True)
    shifted = values - center
    inverse = lax.rsqrt(jnp.mean(shifted * shifted, axis=1, keepdims=True) + EPSILON)
    return shifted * inverse, inverse


def norm_backward(grad_norm, normed, inverse, gain):
    grad_hat = grad_norm * gain
    return inverse * (
        grad_hat
        - jnp.mean(grad_hat, axis=1, keepdims=True)
        - normed * jnp.mean(grad_hat * normed, axis=1, keepdims=True)
    )


def gelu_pair(values):
    slope = 0.7978845608028654
    cubic = 0.044715
    bent = jnp.tanh(slope * (values + cubic * (values * values * values)))
    half = 0.5 * (1.0 + bent)
    result = values * half
    grad = half + 0.5 * values * (1.0 - bent * bent) * slope * (
        1.0 + (3.0 * cubic) * (values * values)
    )
    return result, grad


def images_here(block, copies):
    rows = block.shape[0] * block.shape[1]
    images = block.reshape(rows // SEQ, SEQ, block.shape[2])
    if copies > 1:
        images = jnp.repeat(images, copies, axis=0)
    whole = lax.all_to_all(images, "gx", split_axis=0, concat_axis=2, tiled=True)
    return whole.reshape(SEQ, whole.shape[2])


def images_back(image, copies, shape):
    parts = lax.all_to_all(image[None], "gx", split_axis=2, concat_axis=0, tiled=True)
    if copies > 1:
        parts = parts[::copies]
    return parts.reshape(shape)


def collect(block, order):
    return lax.all_gather(block, order, axis=0, tiled=True)


def shares(grads, order, extra):
    summed = lax.psum_scatter(grads.astype(BF16), order, scatter_dimension=0, tiled=True)
    return lax.psum(summed.astype(F32), "dp") * extra


def on_device(
    tokens,
    cotangent,
    ln1_gain,
    ln1_bias,
    qkv_weight,
    qv_bias,
    out_weight,
    out_bias,
    ln2_gain,
    ln2_bias,
    fc1_weight,
    fc1_bias,
    fc2_weight,
    fc2_bias,
):
    gx = lax.axis_size("gx")
    gy = lax.axis_size("gy")
    shape = tokens.shape
    part = shape[2]
    head_cols = qkv_weight.shape[2]
    heads = head_cols // HEAD_DIM
    hidden_cols = fc1_weight.shape[1]
    width = part * gx
    copies = gx // (MICRO * shape[1] // SEQ)
    extra = 1.0 / copies
    along = ("gy", "gx")

    image = images_here(tokens, copies).astype(F32)
    whole_qkv = collect(qkv_weight.reshape(part, 3 * head_cols), along)
    whole_qkv = whole_qkv.reshape(gy, width, 3 * head_cols)
    whole_out = collect(out_weight, ("gx", "gy")).reshape(gx, gy * head_cols, part)
    whole_out = jnp.concatenate([whole_out[i] for i in range(gx)], axis=1)
    whole_fc1 = collect(fc1_weight, along).reshape(gy, width, hidden_cols)
    whole_fc2 = collect(fc2_weight.T, along).reshape(gy, width, hidden_cols)

    wide = jnp.stack([ln1_gain, ln1_bias, out_bias, ln2_gain, ln2_bias, fc2_bias])
    wide = lax.all_gather(wide.astype(F32), "gx", axis=1, tiled=True)
    gain_one, shift_one, bias_mix, gain_two, shift_two, bias_second = [wide[i] for i in range(6)]
    deep = jnp.concatenate([qv_bias[0], qv_bias[1], fc1_bias]).astype(F32)
    deep = lax.all_gather(deep, "gy", axis=0, tiled=False)
    bias_qkv = jnp.concatenate(
        [deep[:, :head_cols], jnp.zeros((gy, head_cols), F32), deep[:, head_cols : 2 * head_cols]],
        axis=1,
    )
    bias_first = deep[:, 2 * head_cols :]

    normed_one, inverse_one = norm_forward(image)
    ready_one = (normed_one * gain_one + shift_one).astype(BF16)
    packed = jnp.stack(
        [
            (contract(ready_one, whole_qkv[j], 1, 0) + bias_qkv[j]).astype(BF16)
            for j in range(gy)
        ]
    )
    mixture, log_total = attend(packed, heads)
    mixture = jnp.concatenate([mixture[j] for j in range(gy)], axis=1)
    hidden = image + (contract(mixture, whole_out, 1, 0) + bias_mix)
    normed_two, inverse_two = norm_forward(hidden)
    ready_two = (normed_two * gain_two + shift_two).astype(BF16)
    active = []
    slopes = []
    second = bias_second
    for j in range(gy):
        result, slope = gelu_pair(contract(ready_two, whole_fc1[j], 1, 0) + bias_first[j])
        active.append(result.astype(BF16))
        slopes.append(slope)
        second = second + contract(active[j], whole_fc2[j], 1, 1)
    layer_out = images_back((hidden + second).astype(BF16), copies, shape)

    grad_low = images_here(cotangent, copies)
    grad_out = grad_low.astype(F32)
    grad_fc2 = jnp.stack([contract(grad_low, active[j], 0, 0).astype(BF16) for j in range(gy)])
    grad_fc2 = shares(grad_fc2.reshape(gy * width, hidden_cols), along, extra).T
    grad_first = []
    grad_ready_two = None
    for j in range(gy):
        grad_active = contract(grad_low, whole_fc2[j], 1, 0)
        grad_first.append((grad_active * slopes[j]).astype(BF16))
        term = contract(grad_first[j], whole_fc1[j], 1, 1)
        grad_ready_two = term if j == 0 else grad_ready_two + term
    grad_fc1 = jnp.stack([contract(ready_two, grad_first[j], 0, 0).astype(BF16) for j in range(gy)])
    grad_fc1 = shares(grad_fc1.reshape(gy * width, hidden_cols), along, extra)
    grad_hidden = grad_out + norm_backward(grad_ready_two, normed_two, inverse_two, gain_two)
    grad_hidden_low = grad_hidden.astype(BF16)
    grad_out_weight = contract(mixture, grad_hidden_low, 0, 0).astype(BF16)
    grad_out_weight = jnp.concatenate(
        [grad_out_weight[:, i * part : (i + 1) * part] for i in range(gx)], axis=0
    )
    grad_out_weight = shares(grad_out_weight, ("gx", "gy"), extra)
    grad_mixture = contract(grad_hidden_low, whole_out, 1, 1).astype(BF16)
    grad_mixture = jnp.stack(
        [grad_mixture[:, j * head_cols : (j + 1) * head_cols] for j in range(gy)]
    )
    grad_packed = attend_back(packed, jnp.swapaxes(log_total, 1, 2), grad_mixture, heads)
    grad_qkv = jnp.stack(
        [contract(ready_one, grad_packed[j], 0, 0).astype(BF16) for j in range(gy)]
    )
    grad_qkv = shares(grad_qkv.reshape(gy * width, 3 * head_cols), along, extra)
    grad_ready_one = None
    for j in range(gy):
        term = contract(grad_packed[j], whole_qkv[j], 1, 1)
        grad_ready_one = term if j == 0 else grad_ready_one + term
    tokens_grad = grad_hidden + norm_backward(grad_ready_one, normed_one, inverse_one, gain_one)
    tokens_grad = images_back(tokens_grad.astype(BF16), copies, shape)

    everywhere = ("dp", "gx", "gy")
    wide_sums = jnp.stack(
        [
            jnp.sum(grad_ready_one * normed_one, axis=0),
            jnp.sum(grad_ready_one, axis=0),
            jnp.sum(grad_hidden_low, axis=0, dtype=F32),
            jnp.sum(grad_ready_two * normed_two, axis=0),
            jnp.sum(grad_ready_two, axis=0),
            jnp.sum(grad_low, axis=0, dtype=F32),
        ]
    )
    packed_sums = jnp.sum(grad_packed, axis=1, dtype=F32)
    deep_sums = jnp.concatenate(
        [
            packed_sums[:, :head_cols],
            packed_sums[:, 2 * head_cols :],
            jnp.stack([jnp.sum(grad_first[j], axis=0, dtype=F32) for j in range(gy)]),
        ],
        axis=1,
    )
    wide_sums, deep_sums = lax.psum((wide_sums, deep_sums), everywhere)
    wide_sums = extra * lax.dynamic_slice_in_dim(wide_sums, lax.axis_index("gx") * part, part, 1)
    deep_sums = extra * lax.dynamic_index_in_dim(deep_sums, lax.axis_index("gy"), 0, False)
    return (
        layer_out,
        tokens_grad,
        wide_sums[0],
        wide_sums[1],
        grad_qkv.reshape(part, 3, head_cols),
        deep_sums[: 2 * head_cols].reshape(2, head_cols),
        grad_out_weight,
        wide_sums[2],
        wide_sums[3],
        wide_sums[4],
        grad_fc1,
        deep_sums[2 * head_cols :],
        grad_fc2,
        wide_sums[5],
    )


def solution(mesh):
    specs = (
        P(None, ("dp", "gy"), "gx"),
        P(None, ("dp", "gy"), "gx"),
        P("gx"),
        P("gx"),
        P("gx", None, "gy"),
        P(None, "gy"),
        P("gy", "gx"),
        P("gx"),
        P("gx"),
        P("gx"),
        P("gx", "gy"),
        P("gy"),
        P("gy", "gx"),
        P("gx"),
    )
    return jax.shard_map(
        on_device,
        mesh=mesh,
        in_specs=specs,
        out_specs=specs,
        check_vma=False,
    )
```

time: 3590 us -> 997 us (0.28)
  waiting for transfers between devices: 1980 us -> 303 us
  local copies, waits for them, and re-layouts: 705 us -> 179 us
  blocking collectives: 336 us -> 174 us
  other arithmetic: 187 us -> 71.3 us
  matrix products: 263 us -> 160 us
  Pallas kernels: 0 us -> 66.3 us
  starting transfers between devices: 82.3 us -> 17.2 us
    all_to_all x15 -> x4, waiting for transfers between devices: 1140 us -> 10.7 us  [the longest x2 10.7 us: images_here(): lax.all_to_all(images, 'gx', split_axis=0, concat_axis=2, tiled=True)]
    all_gather x22 -> x4, waiting for transfers between devices: 747 us -> 118 us  [collect(): return lax.all_gather(block, order, axis=0, tiled=True)]
    all_gather x17 -> x1, local copies, waits for them, and re-layouts: 256 us -> 0.63 us  [on_device(): wide = lax.all_gather(wide.astype(F32), 'gx', axis=1, tiled=True)]
    unnamed x240 -> x176, local copies, waits for them, and re-layouts: 258 us -> 90.6 us
    all_gather x2, blocking collectives: 197 us -> 38.2 us  [the longest x1 23.2 us: on_device(): wide = lax.all_gather(wide.astype(F32), 'gx', axis=1, tiled=True)]
    unnamed x23 -> x12, waiting for transfers between devices: 5.77 us -> 146 us
    all_to_all x10 -> x2, local copies, waits for them, and re-layouts: 122 us -> 2.74 us  [images_back(): lax.all_to_all(image[None], 'gx', split_axis=2, concat_axis=0, tiled=True)]
    dot_general x52 -> x39, matrix products: 263 us -> 160 us  [contract(): lax.dot_general(left, right, (((left_dim,), (right_dim,)), ((), ())), pre...]
  transfers between devices with their start and end apart: 38 -> 13, of which waited for: 21 -> 7; matrix products, arithmetic and copies ran while one was open for 28% -> 33% of each run, Pallas kernels for 0% -> 3%
where the time goes in v1:
time: 997 us; the launch traced here: 987 us
  waiting for transfers between devices  303 us (30%)
  local copies, waits for them, and re-layouts  179 us (18%)
  blocking collectives  174 us (17%)
  matrix products  160 us (16%)
  other arithmetic  71.3 us (7%)
  Pallas kernels  66.3 us (7%)
  starting transfers between devices  17.2 us (2%)
  between operations  15.3 us (2%)
    dot_general x39, matrix products, contract(): lax.dot_general(left, right, (((left_dim,), (right_dim,)), ((), ())), pre...  160 us
    unnamed x12, waiting for transfers between devices  146 us
    all_gather x4, waiting for transfers between devices, collect(): return lax.all_gather(block, order, axis=0, tiled=True)  118 us
    unnamed x176, local copies, waits for them, and re-layouts  90.6 us
    psum x1, blocking collectives, shares(): return lax.psum(summed.astype(F32), 'dp') * extra  83.6 us
    psum x1, blocking collectives, on_device(): wide_sums, deep_sums = lax.psum((wide_sums, deep_sums), everywhere)  52.5 us
    pallas_call x1, Pallas kernels, attend_back(): pl.pallas_call(functools.partial(attend_back_kernel, heads), grid=(groups...  37.1 us
    pallas_call x1, Pallas kernels, attend(): pl.pallas_call(functools.partial(attend_kernel, heads), grid=(groups,), i...  29.2 us
  transfers between devices with their start and end apart: 13, of which 7 were waited for; matrix products, arithmetic and copies ran while one was open for 33% of the time, Pallas kernels for 3%

profile of v1, /device:TPU:0, one launch (start us, length us, event | category | flops | bytes accessed | tf_op | source)
XLA Modules:
  0.0 987.1 jit_solution(14969209387332499127)
XLA Ops:
  29.9 5.4 reshape.308
  38.1 10.7 %all-to-all-done = bf16[4,729,288]{1,2,0:T(8,128)(2,1)S(1)} async-done(((bf16[4,729,288]{1,2,0:T(8,128)(2,1)}), bf16[4,729,288]{1,2,0:T(8,128)(2,1)S(1)}, u32[]{:S(2)}, u32[]{:S(2)}) %all-to-all-start) | async-done | bytes 1679648 | tf_op jit(solution)/shard_map/all_to_all | solution.py:163
  52.4 23.2 %all-gather = f32[4,288,6]{1,2,0:T(8,128)S(1)} all-gather(f32[1,288,6]{1,2,0:T(8,128)S(1)} %convert_bitcast_fusion.1), channel_id=1, replica_groups=mesh['dp'=2,'gx'=4,'gy'=4] {'gx'}, dimensions={0}, use_global_device_ids=true | all-gather | bytes 34560 | tf_op jit(solution)/shard_map/all_gather | solution.py:220
  79.2 15.0 %all-gather.1 = f32[4,1,1652]{2,1,0:T(1,128)S(1)} all-gather(f32[1,1,1652]{2,1,0:T(1,128)S(1)} %bitcast_convert_fusion), channel_id=1, replica_groups=mesh['dp'=2,'gx'=4,'gy'=4] {'gy'}, dimensions={0}, use_global_device_ids=true | all-gather | bytes 33040 | tf_op jit(solution)/shard_map/all_gather | solution.py:223
  104.0 5.2 copy.112
  122.4 18.6 %all-gather.7.cloned.1.call-done = bf16[4608,864]{1,0:T(8,128)(2,1)} async-done(((bf16[288,864]{1,0:T(8,128)(2,1)}), bf16[4608,864]{1,0:T(8,128)(2,1)}) %all-gather.7.cloned.1.call-update) | async-done | bytes 7962640 | tf_op jit(solution)/shard_map/all_gather | solution.py:175
  141.0 4.3 fusion.96
  156.1 29.2 %attend.1 = (bf16[4,729,288]{2,1,0:T(8,128)(2,1)}, f32[4,729,4]{2,1,0:T(8,128)}) custom-call(bf16[4,729,864]{2,1,0:T(8,128)(2,1)} %pad_maximum_fusion.3.packed_ref), custom_call_target="tpu_custom_call" | custom-call | flops 7346640384 | bytes 6718464 | tf_op jit(solution)/shard_map/attend/pallas_call | solution.py:53
  192.3 5.9 fusion.106
  200.8 29.5 %all-gather.11.cloned.1.call-done = bf16[4608,1076]{1,0:T(8,128)(2,1)} async-done(((bf16[288,1076]{1,0:T(8,128)(2,1)}), bf16[4608,1076]{1,0:T(8,128)(2,1)}) %all-gather.11.cloned.1.call-update) | async-done | bytes 9916432 | tf_op jit(solution)/shard_map/all_gather | solution.py:175
  230.3 6.6 convolution_add_fusion.3
  245.4 4.6 convolution_add_fusion
  249.9 69.4 %all-gather.13.cloned.1.call-done = bf16[4608,1076]{1,0:T(8,128)(2,1)} async-done(((bf16[288,1076]{1,0:T(8,128)(2,1)}), bf16[4608,1076]{1,0:T(8,128)(2,1)}) %all-gather.13.cloned.1.call-update) | async-done | bytes 9916432 | tf_op jit(solution)/shard_map/all_gather | solution.py:175
  319.4 8.1 convert_reduce_fusion.6
  328.6 4.6 fusion.62
  333.3 4.7 convert_reduce_fusion.5
  338.0 4.9 convert_reduce_fusion.4
  342.9 8.7 convert_reduce_fusion.3
  357.0 4.4 multiply_reduce_fusion.1
  368.9 37.1 %attend_back.1 = bf16[4,729,864]{2,1,0:T(8,128)(2,1)} custom-call(bf16[4,729,864]{2,1,0:T(8,128)(2,1)} %pad_maximum_fusion.3.packed_ref, f32[4,4,729]{2,1,0:T(4,128)} %bitcast.205, bf16[4,729,288]{2,1,0:T(8,128)(2,1)} %pad_maximum_fusion.5.grad_ref), custom_call_target="tpu_custom_call" | custom-call | flops 18366601216 | bytes 11757312 | tf_op jit(solution)/shard_map/attend_back/pallas_call | solution.py:109
  419.3 11.4 %copy.123 = bf16[4,1152,864]{2,1,0:T(8,128)(2,1)} copy(bf16[4,1152,864]{1,2,0:T(8,128)(2,1)} %pad_maximum_fusion.2) | data formatting | bytes 15925248 | tf_op jit(solution)/shard_map/stack | solution.py:278
  432.2 5.0 fusion.7
  446.4 6.0 pad_maximum_fusion.1
  452.4 14.7 %copy.140 = bf16[4,1152,1076]{2,1,0:T(8,128)(2,1)} copy(bf16[4,1152,1076]{1,2,0:T(8,128)(2,1)} %pad_maximum_fusion.1) | data formatting | bytes 19832832
  476.5 4.4 fusion.3
  492.4 9.7 pad_maximum_fusion
  502.2 14.7 %copy.139 = bf16[4,1152,1076]{2,1,0:T(8,128)(2,1)} copy(bf16[4,1152,1076]{1,2,0:T(8,128)(2,1)} %pad_maximum_fusion) | data formatting | bytes 19832832
  518.9 5.2 convolution_add_fusion.13
  524.1 5.3 convolution_add_fusion.12
  532.8 5.0 fusion.47
  537.7 9.0 copy.113
  547.3 11.9 %reduce.52 = bf16[1152,729]{1,0:T(8,128)(2,1)} reduce(bf16[1152,1,729]{2,1,0:T(2,128)(2,1)S(1)} %bitcast.188, bf16[]{:T(256)} %broadcast.273), dimensions={1}, to_apply=%bitcast.133.reduce_sub_computation | reduce | bytes 3359234
  559.2 6.9 reshape.352
  566.1 4.4 all-to-all-start.1
  578.8 4.3 convolution_add_fusion.5
  583.2 6.3 multiply_reduce_fusion.2
  591.9 70.8 %reduce-scatter.17.cloned.1.call-done = bf16[288,1076]{1,0:T(8,128)(2,1)} async-done(((bf16[4608,1076]{1,0:T(8,128)(2,1)}), bf16[288,1076]{1,0:T(8,128)(2,1)}) %reduce-scatter.17.cloned.1.call-update) | async-done | bytes 619792
  667.4 4.5 fusion.78
  671.9 8.9 copy.119
  680.9 11.9 %reduce.53 = bf16[1152,729]{1,0:T(8,128)(2,1)} reduce(bf16[1152,1,729]{2,1,0:T(2,128)(2,1)S(1)} %bitcast.189, bf16[]{:T(256)} %broadcast.273), dimensions={1}, to_apply=%bitcast.135.reduce_sub_computation | reduce | bytes 3359234
  692.8 7.1 reshape.354
  699.9 4.5 all-to-all-start.3
  708.6 52.5 %all-reduce = (f32[6,1152]{1,0:T(8,128)S(1)}, f32[4,1652]{1,0:T(4,128)S(1)}) all-reduce(f32[6,1152]{1,0:T(8,128)S(1)} %stack.155, f32[4,1652]{1,0:T(4,128)S(1)} %concatenate.32), channel_id=1, replica_groups=mesh['dp'=2,'gx'=4,'gy'=4] {'dp','gx','gy'}, use_global_device_ids=true, to_apply=%region_14.0 | all-reduce | flops 13520 | bytes 108160 | tf_op jit(solution)/shard_map/psum | solution.py:309
  763.2 5.5 reshape.353
  773.9 5.5 reshape.355
  785.7 73.6 %reduce-scatter.15.cloned.1.call-done = bf16[288,1076]{1,0:T(8,128)(2,1)} async-done(((bf16[4608,1076]{1,0:T(8,128)(2,1)}), bf16[288,1076]{1,0:T(8,128)(2,1)}) %reduce-scatter.15.cloned.1.call-update) | async-done | bytes 619792
  860.8 83.6 %all-reduce.7 = (f32[288,288]{0,1:T(8,128)S(1)}, f32[288,1076]{0,1:T(8,128)S(1)}) all-reduce(bf16[288,288]{0,1:T(8,128)(2,1)S(1)} %copy.134, bf16[288,1076]{0,1:T(8,128)(2,1)S(1)} %copy.136), channel_id=1, replica_groups=mesh['dp'=2,'gx'=4,'gy'=4] {'dp'}, use_global_device_ids=true, to_apply=%region_24.0 | all-reduce | flops 392832 | bytes 2356992 | tf_op jit(solution)/shard_map/psum | solution.py:180
  947.0 28.8 %all-reduce.6.cloned.1.call-done = (f32[288,3,288]{0,2,1:T(8,128)}, f32[1076,288]{1,0:T(8,128)}) async-done(((f32[288,3,288]{0,2,1:T(8,128)}, f32[1076,288]{1,0:T(8,128)}), (f32[288,3,288]{0,2,1:T(8,128)}, f32[1076,288]{1,0:T(8,128)})) %all-reduce.6.cloned.1.call-update) | async-done | bytes 2234896 | tf_op jit(solution)/shard_map/psum | solution.py:180
  (300 shorter events, 190.3 us)
Async XLA Ops:
  7.2 109.2 %all-gather.9.cloned.1.call-start = ((), (), s32[]{:S(2)}) async-start(), calls=%async_computation.9 | async-start | bytes 3760128 | tf_op jit(solution)/shard_map/all_gather | solution.py:175
  7.9 133.1 %all-gather.7.cloned.1.call-start = ((), (), s32[]{:S(2)}) async-start(), calls=%async_computation.8 | async-start | bytes 8773632 | tf_op jit(solution)/shard_map/all_gather | solution.py:175
  10.5 219.9 %all-gather.11.cloned.1.call-start = ((), (), s32[]{:S(2)}) async-start(), calls=%async_computation.10 | async-start | bytes 11280384 | tf_op jit(solution)/shard_map/all_gather | solution.py:175
  11.2 308.2 %all-gather.13.cloned.1.call-start = ((), (), s32[]{:S(2)}) async-start(), calls=%async_computation.11 | async-start | bytes 11280384 | tf_op jit(solution)/shard_map/all_gather | solution.py:175
  16.8 5.7 copy-start.47
  16.8 5.7 copy-start.48
  16.8 10.1 %copy-start.13 = (bf16[2,1458,288]{1,2,0:T(8,128)(2,1)S(1)}, bf16[2,1458,288]{1,2,0:T(8,128)(2,1)}, u32[]{:S(2)}) copy-start(bf16[2,1458,288]{1,2,0:T(8,128)(2,1)} %param.15) | copy-start | bytes 5038852
  18.2 30.5 %all-to-all-start = ((bf16[4,729,288]{1,2,0:T(8,128)(2,1)}), bf16[4,729,288]{1,2,0:T(8,128)(2,1)S(1)}, u32[]{:S(2)}, u32[]{:S(2)}) async-start(bf16[4,729,288]{1,2,0:T(8,128)(2,1)} %copy.107), calls=%async_computation | async-start | bytes 3538944 | tf_op jit(solution)/shard_map/all_to_all | solution.py:163
  29.9 7.6 copy-start.42
  48.7 60.5 %all-to-all-start.2 = ((bf16[4,729,288]{1,2,0:T(8,128)(2,1)}), bf16[4,729,288]{1,2,0:T(8,128)(2,1)S(1)}, u32[]{:S(2)}, u32[]{:S(2)}) async-start(bf16[4,729,288]{1,2,0:T(8,128)(2,1)} %copy.116), calls=%async_computation.2 | async-start | bytes 3538944 | tf_op jit(solution)/shard_map/all_to_all | solution.py:163
  52.3 537.2 %reduce-scatter.11.cloned.1.call-start = ((), (), s32[]{:S(2)}) async-start(), calls=%async_computation.12 | async-start | bytes 8773632 | tf_op jit(solution)/shard_map/reduce_scatter | solution.py:179
  96.6 18.0 %copy-start.19 = (f32[1152]{0:T(1024)}, f32[1152]{0:T(1024)S(1)}, u32[]{:S(2)}) copy-start(f32[1152]{0:T(1024)S(1)} %get-tuple-element.107) | copy-start | bytes 13828
  118.7 22.2 %copy-start.46 = (f32[864]{0:T(1024)S(1)}, f32[864]{0:T(1024)}, u32[]{:S(2)}) copy-start(f32[864]{0:T(1024)} %get-tuple-element.113) | copy-start | bytes 10372
  141.0 5.0 copy-start.50
  198.2 163.1 %copy-start = (f32[729,1152]{1,0:T(8,128)}, f32[729,1152]{1,0:T(8,128)S(1)}, u32[]{:S(2)}) copy-start(f32[729,1152]{1,0:T(8,128)S(1)} %get-tuple-element.147) | copy-start | bytes 10077700
  198.8 31.6 %copy-start.35 = (f32[1076]{0:T(1024)S(1)}, f32[1076]{0:T(1024)}, u32[]{:S(2)}) copy-start(f32[1076]{0:T(1024)} %get-tuple-element.111) | copy-start | bytes 12916
  230.3 6.6 copy-start.15
  230.3 6.6 copy-start.34
  230.3 6.6 copy-start.49
  319.4 13.8 %slice-start = ((s8[10616832]{0:T(1024)(128)(4,1)}), s8[4194304]{0:T(1024)(128)(4,1)S(1)}, s32[]{:S(2)}) async-start(s8[10616832]{0:T(1024)(128)(4,1)} %bitcast.206), calls=%async_computation.17 | async-start | bytes 8388608
  319.4 13.8 %slice-start.1 = ((s8[10616832]{0:T(1024)(128)(4,1)}), s8[4194304]{0:T(1024)(128)(4,1)S(1)}, s32[]{:S(2)}) async-start(s8[10616832]{0:T(1024)(128)(4,1)} %bitcast.206), calls=%async_computation.18 | async-start | bytes 8388608
  333.3 4.7 copy-start.51
  338.0 13.6 %copy-start.57 = (bf16[729,1076]{0,1:T(8,128)(2,1)}, bf16[729,1076]{0,1:T(8,128)(2,1)S(1)}, u32[]{:S(2)}) copy-start(bf16[729,1076]{0,1:T(8,128)(2,1)S(1)} %get-tuple-element.155) | copy-start | bytes 4706428
  338.0 13.6 %slice-start.6 = ((s8[10616832]{0:T(1024)(128)(4,1)}), s8[4194304]{0:T(1024)(128)(4,1)S(1)}, s32[]{:S(2)}) async-start(s8[10616832]{0:T(1024)(128)(4,1)} %bitcast.210), calls=%async_computation.23 | async-start | bytes 8388608
  338.0 13.6 %slice-start.7 = ((s8[10616832]{0:T(1024)(128)(4,1)}), s8[4194304]{0:T(1024)(128)(4,1)S(1)}, s32[]{:S(2)}) async-start(s8[10616832]{0:T(1024)(128)(4,1)} %bitcast.210), calls=%async_computation.24 | async-start | bytes 8388608
  342.9 11.4 %copy-start.59 = (bf16[729,1076]{0,1:T(8,128)(2,1)}, bf16[729,1076]{0,1:T(8,128)(2,1)S(1)}, u32[]{:S(2)}) copy-start(bf16[729,1076]{0,1:T(8,128)(2,1)S(1)} %get-tuple-element.153) | copy-start | bytes 4706428
  342.9 8.7 slice-start.8
  368.9 37.1 %copy-start.14 = (bf16[4,1,729,288]{2,3,0,1:T(8,128)(2,1)S(1)}, bf16[4,1,729,288]{2,3,0,1:T(8,128)(2,1)}, u32[]{:S(2)}) copy-start(bf16[4,1,729,288]{2,3,0,1:T(8,128)(2,1)} %add_convert_fusion) | copy-start | bytes 5038852
  430.8 231.9 %reduce-scatter.17.cloned.1.call-start = ((), (), s32[]{:S(2)}) async-start(), calls=%async_computation.15 | async-start | bytes 11280384
  432.2 5.0 copy-start.52
  467.1 317.5 %reduce-scatter.13.cloned.1.call-start = ((), (), s32[]{:S(2)}) async-start(), calls=%async_computation.13 | async-start | bytes 3760128
  492.4 367.0 %reduce-scatter.15.cloned.1.call-start = ((), (), s32[]{:S(2)}) async-start(), calls=%async_computation.14 | async-start | bytes 11280384
  518.9 5.2 copy-start.56
  518.9 10.5 %slice-start.3 = ((s8[10616832]{0:T(1024)(128)(4,1)}), s8[4194304]{0:T(1024)(128)(4,1)S(1)}, s32[]{:S(2)}) async-start(s8[10616832]{0:T(1024)(128)(4,1)} %bitcast.208), calls=%async_computation.20 | async-start | bytes 8388608
  518.9 10.5 %slice-start.4 = ((s8[10616832]{0:T(1024)(128)(4,1)}), s8[4194304]{0:T(1024)(128)(4,1)S(1)}, s32[]{:S(2)}) async-start(s8[10616832]{0:T(1024)(128)(4,1)} %bitcast.208), calls=%async_computation.21 | async-start | bytes 8388608
  524.1 5.3 slice-start.5
  524.1 5.3 copy-start.53
  566.1 133.8 %all-to-all-start.1 = ((bf16[4,2,104976]{2,1,0:T(2,128)(2,1)}), bf16[4,2,104976]{2,1,0:T(2,128)(2,1)}, u32[]{:S(2)}, u32[]{:S(2)}) async-start(bf16[4,2,104976]{2,1,0:T(2,128)(2,1)} %reshape.352), calls=%async_computation.1 | async-start | bytes 3362816 | tf_op jit(solution)/shard_map/all_to_all | solution.py:168
  570.5 405.3 %all-reduce.6.cloned.1.call-start = ((), (), s32[]{:S(2)}) async-start(), calls=%async_computation.16 | async-start | bytes 5971968 | tf_op jit(solution)/shard_map/psum | solution.py:180
  692.8 11.7 %copy-start.7 = (bf16[4,729,288]{1,2,0:T(8,128)(2,1)S(1)}, bf16[4,729,288]{1,2,0:T(8,128)(2,1)}, u32[]{:S(2)}) copy-start(bf16[4,729,288]{1,2,0:T(8,128)(2,1)} %copy-done.4) | copy-start | bytes 5038852
  699.9 5.0 copy-start.27
  699.9 5.1 copy-start.41
  699.9 5.1 copy-start.40
  699.9 5.1 copy-start.39
  699.9 5.1 copy-start.38
  699.9 5.1 copy-start.37
  699.9 5.2 copy-start.36
  699.9 74.0 %all-to-all-start.3 = ((bf16[4,2,104976]{2,1,0:T(2,128)(2,1)}), bf16[4,2,104976]{2,1,0:T(2,128)(2,1)}, u32[]{:S(2)}, u32[]{:S(2)}) async-start(bf16[4,2,104976]{2,1,0:T(2,128)(2,1)} %reshape.354), calls=%async_computation.3 | async-start | bytes 3362816 | tf_op jit(solution)/shard_map/all_to_all | solution.py:168
  (41 other events, 127.4 us)
Sparse Core Ops, SparseCore 0:
  10.3 54.2 all-gather.8
  67.5 73.4 all-gather.6
  143.3 87.0 all-gather.10
  232.5 86.8 all-gather.12
  430.9 102.0 reduce-scatter.10
  536.9 125.7 reduce-scatter.16
  666.6 69.6 reduce-scatter.12
  740.3 119.0 reduce-scatter.14
  862.4 113.3 all-reduce.5

commit v2 on v1

v2 whole, which is shorter than its diff:
```python
import functools

import jax
import jax.numpy as jnp
from jax import lax
from jax.experimental import pallas as pl
from jax.experimental.pallas import tpu as pltpu
from jax.sharding import PartitionSpec as P

HEAD_DIM = 72
SEQ = 729
MICRO = 2
EPSILON = 1e-06
QUERY_ROWS = 384
ROWS = 256
COLS = 256
BF16 = jnp.bfloat16
F32 = jnp.float32
VMEM_BYTES = 60 * 2**20


def contract(left, right, left_dim, right_dim):
    return lax.dot_general(
        left, right, (((left_dim,), (right_dim,)), ((), ())), preferred_element_type=F32
    )


def blocks_of(total, size):
    return [(low, min(low + size, total)) for low in range(0, total, size)]


def whole(shape):
    return pl.BlockSpec(shape, lambda i, *_: (0,) * len(shape))


def nth(shape):
    return pl.BlockSpec((1,) + tuple(shape[1:]), lambda i, *_: (i,) + (0,) * (len(shape) - 1))


def call(kernel, name, steps, ins, outs, flops, scratch=(), prefetch=()):
    moved = sum(a.size * a.dtype.itemsize for a, _ in list(ins) + list(outs))
    return pl.pallas_call(
        kernel,
        grid_spec=pltpu.PrefetchScalarGridSpec(
            num_scalar_prefetch=len(prefetch),
            grid=(steps,),
            in_specs=[spec for _, spec in ins],
            out_specs=[spec for _, spec in outs],
            scratch_shapes=list(scratch),
        ),
        out_shape=[shape for shape, _ in outs],
        compiler_params=pltpu.CompilerParams(vmem_limit_bytes=VMEM_BYTES),
        cost_estimate=pl.CostEstimate(flops=flops, bytes_accessed=moved, transcendentals=0),
        name=name,
    )(*prefetch, *[a for a, _ in ins])


def struct(shape, dtype):
    return jax.ShapeDtypeStruct(tuple(shape), dtype)


def attend_kernel(heads, packed_ref, mix_ref, total_ref):
    seq = packed_ref.shape[1]
    width = heads * HEAD_DIM
    scaling = HEAD_DIM ** (-0.5)
    for head in range(heads):
        first = head * HEAD_DIM
        last = first + HEAD_DIM
        keys = packed_ref[0, :, width + first : width + last]
        values = packed_ref[0, :, 2 * width + first : 2 * width + last]
        for low, high in blocks_of(seq, QUERY_ROWS):
            queries = packed_ref[0, low:high, first:last]
            scores = contract(queries, keys, 1, 1) * scaling
            row_max = jnp.max(scores, axis=1, keepdims=True)
            exponent = jnp.exp(scores - row_max)
            row_total = jnp.sum(exponent, axis=1, keepdims=True)
            probability = (exponent * (1.0 / row_total)).astype(BF16)
            mix_ref[0, low:high, first:last] = contract(probability, values, 1, 0).astype(BF16)
            total_ref[0, low:high, head : head + 1] = row_max + jnp.log(row_total)


def attend(packed, heads):
    groups, seq, _ = packed.shape
    mix = struct((groups, seq, heads * HEAD_DIM), BF16)
    total = struct((groups, seq, heads), F32)
    return call(
        functools.partial(attend_kernel, heads),
        "attend",
        groups,
        [(packed, nth(packed.shape))],
        [(mix, nth(mix.shape)), (total, nth(total.shape))],
        12 * groups * heads * seq * seq * HEAD_DIM,
    )


def attend_back_kernel(
    heads, packed_ref, total_ref, grad_ref, out_ref, sum_ref, key_sum, value_sum
):
    seq = packed_ref.shape[1]
    width = heads * HEAD_DIM
    scaling = HEAD_DIM ** (-0.5)
    for head in range(heads):
        first = head * HEAD_DIM
        last = first + HEAD_DIM
        keys = packed_ref[0, :, width + first : width + last]
        values = packed_ref[0, :, 2 * width + first : 2 * width + last]
        for low, high in blocks_of(seq, QUERY_ROWS):
            queries = packed_ref[0, low:high, first:last]
            grads = grad_ref[0, low:high, first:last]
            scores = contract(keys, queries, 1, 1) * scaling
            probability = jnp.exp(scores - total_ref[0, head : head + 1, low:high])
            grad_values = contract(probability.astype(BF16), grads, 1, 0)
            grad_prob = contract(values, grads, 1, 1)
            inner = jnp.sum(probability * grad_prob, axis=0, keepdims=True)
            grad_scores = (probability * (grad_prob - inner)).astype(BF16)
            grad_keys = contract(grad_scores, queries, 1, 0)
            grad_queries = contract(grad_scores, keys, 0, 0) * scaling
            out_ref[0, low:high, first:last] = grad_queries.astype(BF16)
            if low == 0:
                key_sum[...] = grad_keys
                value_sum[...] = grad_values
            else:
                key_sum[...] += grad_keys
                value_sum[...] += grad_values
        out_ref[0, :, width + first : width + last] = (key_sum[...] * scaling).astype(BF16)
        out_ref[0, :, 2 * width + first : 2 * width + last] = value_sum[...].astype(BF16)
    sum_ref[0] = jnp.sum(out_ref[0].astype(F32), axis=0, keepdims=True)


def attend_back(packed, total, grads, heads):
    groups, seq, triple = packed.shape
    out = struct(packed.shape, BF16)
    sums = struct((groups, 1, triple), F32)
    return call(
        functools.partial(attend_back_kernel, heads),
        "attend_back",
        groups,
        [(packed, nth(packed.shape)), (total, nth(total.shape)), (grads, nth(grads.shape))],
        [(out, nth(out.shape)), (sums, nth(sums.shape))],
        30 * groups * heads * seq * seq * HEAD_DIM,
        [pltpu.VMEM((seq, HEAD_DIM), F32), pltpu.VMEM((seq, HEAD_DIM), F32)],
    )


def norm(values):
    center = jnp.mean(values, axis=1, keepdims=True)
    shifted = values - center
    inverse = lax.rsqrt(jnp.mean(shifted * shifted, axis=1, keepdims=True) + EPSILON)
    return shifted * inverse, inverse


def norm_back(grad_norm, normed, inverse, gain):
    grad_hat = grad_norm * gain
    return inverse * (
        grad_hat
        - jnp.mean(grad_hat, axis=1, keepdims=True)
        - normed * jnp.mean(grad_hat * normed, axis=1, keepdims=True)
    )


def join_columns(parts_ref, whole_ref):
    count, _, part = parts_ref.shape
    for i in range(count):
        whole_ref[:, i * part : (i + 1) * part] = parts_ref[i]


def turned(rows, blocks_ref):
    flat = rows.T
    count, size, _ = blocks_ref.shape
    for i in range(count):
        blocks_ref[i] = flat[i * size : (i + 1) * size]


def spread_kernel(parts_ref, whole_ref, turned_ref, sum_ref):
    join_columns(parts_ref, whole_ref)
    turned(whole_ref[...], turned_ref)
    sum_ref[...] = jnp.sum(whole_ref[...].astype(F32), axis=0, keepdims=True)


def spread(parts, blocks):
    count, seq, part = parts.shape
    width = count * part
    outs = [
        struct((seq, width), BF16),
        struct((blocks, width // blocks, seq), BF16),
        struct((1, width), F32),
    ]
    return call(
        spread_kernel,
        "spread",
        1,
        [(parts, whole(parts.shape))],
        [(o, whole(o.shape)) for o in outs],
        seq * width,
    )


def project_kernel(
    triple, parts_ref, gain_ref, shift_ref, weight_ref, bias_ref, image_ref, ready_ref, turned_ref, packed_ref
):
    @pl.when(pl.program_id(0) == 0)
    def _():
        join_columns(parts_ref, image_ref)
        for low, high in blocks_of(image_ref.shape[0], ROWS):
            normed, _ = norm(image_ref[low:high].astype(F32))
            ready_ref[low:high] = (normed * gain_ref[...] + shift_ref[...]).astype(BF16)
        turned(ready_ref[...], turned_ref)

    packed = contract(ready_ref[...], weight_ref[0, :, :triple], 1, 0) + bias_ref[0]
    packed_ref[0] = packed.astype(BF16)


def project(parts, gain, shift, weight, bias, blocks):
    count, seq, part = parts.shape
    width = count * part
    groups, _, triple = bias.shape
    outs = [
        (struct((seq, width), BF16), whole((seq, width))),
        (struct((seq, width), BF16), whole((seq, width))),
        (struct((blocks, width // blocks, seq), BF16), whole((blocks, width // blocks, seq))),
        (struct((groups, seq, triple), BF16), nth((groups, seq, triple))),
    ]
    return call(
        functools.partial(project_kernel, triple),
        "project",
        groups,
        [
            (parts, whole(parts.shape)),
            (gain, whole(gain.shape)),
            (shift, whole(shift.shape)),
            (weight, nth(weight.shape)),
            (bias, nth(bias.shape)),
        ],
        outs,
        2 * groups * seq * width * triple,
    )


def mix_kernel(
    image_ref, parts_ref, weight_ref, bias_ref, gain_ref, shift_ref, hidden_ref, ready_ref, turned_ref, joined
):
    join_columns(parts_ref, joined)
    for low, high in blocks_of(image_ref.shape[0], ROWS):
        mixed = contract(joined[low:high], weight_ref[...], 1, 0) + bias_ref[...]
        hidden = image_ref[low:high].astype(F32) + mixed
        hidden_ref[low:high] = hidden
        normed, _ = norm(hidden)
        ready_ref[low:high] = (normed * gain_ref[...] + shift_ref[...]).astype(BF16)
    turned(ready_ref[...], turned_ref)


def mix(image, parts, weight, bias, gain, shift, blocks):
    seq, width = image.shape
    inner = weight.shape[0]
    outs = [
        struct((seq, width), F32),
        struct((seq, width), BF16),
        struct((blocks, width // blocks, seq), BF16),
    ]
    return call(
        mix_kernel,
        "mix",
        1,
        [(a, whole(a.shape)) for a in (image, parts, weight, bias, gain, shift)],
        [(o, whole(o.shape)) for o in outs],
        2 * seq * width * inner,
        [pltpu.VMEM((seq, inner), BF16)],
    )


def expand_kernel(ready_ref, weight_ref, bias_ref, active_ref, slope_ref):
    bend = 0.7978845608028654
    cubic = 0.044715
    for low, high in blocks_of(weight_ref.shape[2], COLS):
        first = contract(ready_ref[...], weight_ref[0, :, low:high], 1, 0) + bias_ref[0, :, low:high]
        square = first * first
        bent = jnp.tanh(bend * (first + cubic * (first * square)))
        half = 0.5 * (1.0 + bent)
        active_ref[0, :, low:high] = (first * half).astype(BF16)
        slope_ref[0, :, low:high] = half + (0.5 * bend) * first * (1.0 - bent * bent) * (
            1.0 + (3.0 * cubic) * square
        )


def expand(ready, weight, bias):
    seq, width = ready.shape
    groups, _, cols = weight.shape
    shape = (groups, seq, cols)
    return call(
        expand_kernel,
        "expand",
        groups,
        [(ready, whole(ready.shape)), (weight, nth(weight.shape)), (bias, nth(bias.shape))],
        [(struct(shape, BF16), nth(shape)), (struct(shape, F32), nth(shape))],
        2 * groups * seq * width * cols,
    )


def narrow_kernel(hidden_ref, active_ref, weight_ref, bias_ref, out_ref, total):
    step = pl.program_id(0)
    term = contract(active_ref[0], weight_ref[0], 1, 1)

    @pl.when(step == 0)
    def _():
        total[...] = hidden_ref[...] + bias_ref[...] + term

    @pl.when(step > 0)
    def _():
        total[...] += term

    @pl.when(step == pl.num_programs(0) - 1)
    def _():
        count, _, part = out_ref.shape
        for i in range(count):
            out_ref[i] = total[:, i * part : (i + 1) * part].astype(BF16)


def narrow(hidden, active, weight, bias, count):
    seq, width = hidden.shape
    groups, _, cols = weight.shape
    shape = (count, seq, width // count)
    return call(
        narrow_kernel,
        "narrow",
        groups,
        [
            (hidden, whole(hidden.shape)),
            (active, nth(active.shape)),
            (weight, nth(weight.shape)),
            (bias, whole(bias.shape)),
        ],
        [(struct(shape, BF16), whole(shape))],
        2 * groups * seq * width * cols,
        [pltpu.VMEM((seq, width), F32)],
    )[0]


def feed_back_kernel(
    grad_ref,
    hidden_ref,
    gain_ref,
    slope_ref,
    second_ref,
    first_ref,
    first_grad_ref,
    first_sum_ref,
    hidden_grad_ref,
    low_ref,
    turned_ref,
    gain_sum_ref,
    shift_sum_ref,
    low_sum_ref,
    total,
):
    step = pl.program_id(0)
    for low, high in blocks_of(second_ref.shape[2], COLS):
        active_grad = contract(grad_ref[...], second_ref[0, :, low:high], 1, 0)
        first_grad = (active_grad * slope_ref[0, :, low:high]).astype(BF16)
        first_grad_ref[0, :, low:high] = first_grad
        first_sum_ref[0, :, low:high] = jnp.sum(first_grad.astype(F32), axis=0, keepdims=True)
    term = contract(first_grad_ref[0], first_ref[0], 1, 1)

    @pl.when(step == 0)
    def _():
        total[...] = term

    @pl.when(step > 0)
    def _():
        total[...] += term

    @pl.when(step == pl.num_programs(0) - 1)
    def _():
        gain_sum = jnp.zeros(gain_sum_ref.shape, F32)
        shift_sum = jnp.zeros(gain_sum_ref.shape, F32)
        low_sum = jnp.zeros(gain_sum_ref.shape, F32)
        for low, high in blocks_of(total.shape[0], ROWS):
            normed, inverse = norm(hidden_ref[low:high])
            ready_grad = total[low:high]
            gain_sum += jnp.sum(ready_grad * normed, axis=0, keepdims=True)
            shift_sum += jnp.sum(ready_grad, axis=0, keepdims=True)
            hidden_grad = grad_ref[low:high].astype(F32) + norm_back(
                ready_grad, normed, inverse, gain_ref[...]
            )
            hidden_grad_ref[low:high] = hidden_grad
            rounded = hidden_grad.astype(BF16)
            low_ref[low:high] = rounded
            low_sum += jnp.sum(rounded.astype(F32), axis=0, keepdims=True)
        gain_sum_ref[...] = gain_sum
        shift_sum_ref[...] = shift_sum
        low_sum_ref[...] = low_sum
        turned(low_ref[...], turned_ref)


def feed_back(grad, hidden, gain, slope, second, first, blocks):
    seq, width = hidden.shape
    groups, _, cols = first.shape
    row = struct((1, width), F32)
    outs = [
        (struct(slope.shape, BF16), nth(slope.shape)),
        (struct((groups, 1, cols), F32), nth((groups, 1, cols))),
    ] + [
        (o, whole(o.shape))
        for o in (
            struct((seq, width), F32),
            struct((seq, width), BF16),
            struct((blocks, width // blocks, seq), BF16),
            row,
            row,
            row,
        )
    ]
    return call(
        feed_back_kernel,
        "feed_back",
        groups,
        [
            (grad, whole(grad.shape)),
            (hidden, whole(hidden.shape)),
            (gain, whole(gain.shape)),
            (slope, nth(slope.shape)),
            (second, nth(second.shape)),
            (first, nth(first.shape)),
        ],
        outs,
        4 * groups * seq * width * cols,
        [pltpu.VMEM((seq, width), F32)],
    )


def mix_back_kernel(grad_ref, weight_ref, out_ref):
    groups, _, part = out_ref.shape
    full = contract(grad_ref[...], weight_ref[...], 1, 1).astype(BF16)
    for j in range(groups):
        out_ref[j] = full[:, j * part : (j + 1) * part]


def mix_back(grad, weight, groups):
    seq, width = grad.shape
    shape = (groups, seq, weight.shape[0] // groups)
    return call(
        mix_back_kernel,
        "mix_back",
        1,
        [(grad, whole(grad.shape)), (weight, whole(weight.shape))],
        [(struct(shape, BF16), whole(shape))],
        2 * seq * width * weight.shape[0],
    )[0]


def project_back_kernel(
    triple, image_ref, gain_ref, hidden_grad_ref, packed_ref, weight_ref, out_ref, gain_sum_ref, shift_sum_ref, total
):
    step = pl.program_id(0)
    term = contract(packed_ref[0], weight_ref[0, :, :triple], 1, 1)

    @pl.when(step == 0)
    def _():
        total[...] = term

    @pl.when(step > 0)
    def _():
        total[...] += term

    @pl.when(step == pl.num_programs(0) - 1)
    def _():
        count, _, part = out_ref.shape
        gain_sum = jnp.zeros(gain_sum_ref.shape, F32)
        shift_sum = jnp.zeros(gain_sum_ref.shape, F32)
        for low, high in blocks_of(total.shape[0], ROWS):
            normed, inverse = norm(image_ref[low:high].astype(F32))
            ready_grad = total[low:high]
            gain_sum += jnp.sum(ready_grad * normed, axis=0, keepdims=True)
            shift_sum += jnp.sum(ready_grad, axis=0, keepdims=True)
            result = hidden_grad_ref[low:high] + norm_back(
                ready_grad, normed, inverse, gain_ref[...]
            )
            for i in range(count):
                out_ref[i, low:high] = result[:, i * part : (i + 1) * part].astype(BF16)
        gain_sum_ref[...] = gain_sum
        shift_sum_ref[...] = shift_sum


def project_back(image, gain, hidden_grad, packed_grad, weight, count):
    seq, width = image.shape
    groups, _, triple = packed_grad.shape
    shape = (count, seq, width // count)
    row = struct((1, width), F32)
    return call(
        functools.partial(project_back_kernel, triple),
        "project_back",
        groups,
        [
            (image, whole(image.shape)),
            (gain, whole(gain.shape)),
            (hidden_grad, whole(hidden_grad.shape)),
            (packed_grad, nth(packed_grad.shape)),
            (weight, nth(weight.shape)),
        ],
        [
            (struct(shape, BF16), whole(shape)),
            (row, whole(row.shape)),
            (row, whole(row.shape)),
        ],
        2 * groups * seq * width * triple,
        [pltpu.VMEM((seq, width), F32)],
    )


def share_kernel(half, added, pick_ref, turned_ref, right_ref, *rest):
    rows = turned_ref.shape[1]
    picked = rest[-1]
    count = picked.shape[0] // rows

    @pl.when(pl.program_id(0) == 0)
    def _():
        for i in range(count):
            picked[i * rows : (i + 1) * rows] = turned_ref[pick_ref[half * count + i]]

    product = contract(picked[...], right_ref[0], 1, 0)
    refs = rest[1:-1] if added else rest[:-1]
    for i in range(count):
        piece = product[i * rows : (i + 1) * rows]
        if added:
            piece = piece + rest[0][i, 0].astype(F32)
        out = refs[0] if len(refs) == 1 else refs[i // 2]
        out[i if len(refs) == 1 else i % 2, 0] = piece.astype(BF16)


def share(pick, turned_rows, right, received=None):
    total, rows, seq = turned_rows.shape
    groups, _, cols = right.shape
    count = total // 2
    spec = lambda n: pl.BlockSpec((n, 1, rows, cols), lambda i, *_: (0, i, 0, 0))
    ins = [(turned_rows, whole(turned_rows.shape)), (right, nth(right.shape))]
    if received is None:
        sizes = [count]
    else:
        ins.append((received, spec(count)))
        sizes = [2] * (count // 2)
    return call(
        functools.partial(share_kernel, 1 if received is None else 0, received is not None),
        "share",
        groups,
        ins,
        [(struct((n, groups, rows, cols), BF16), spec(n)) for n in sizes],
        2 * groups * count * rows * seq * cols,
        [pltpu.VMEM((count * rows, seq), BF16)],
        (pick,),
    )


def swap(array, axis, bit):
    size = lax.axis_size(axis)
    return lax.ppermute(array, axis, [(i, i ^ bit) for i in range(size)])


def shares(pick, turned_rows, right, extra):
    away = share(pick, turned_rows, right)[0]
    kept = share(pick, turned_rows, right, swap(away, "gx", 1))
    mine = [kept[0][0].astype(F32), kept[0][1].astype(F32)]
    if len(kept) == 2:
        arrived = swap(kept[1], "dp", 1)
        mine = [mine[0] + arrived[0].astype(F32), mine[1] + arrived[1].astype(F32)]
    arrived = swap(mine[1].astype(BF16), "gx", 2)
    total = (mine[0] + arrived.astype(F32)).astype(BF16)
    groups, rows, cols = total.shape
    own = lax.psum_scatter(
        total.reshape(groups * rows, cols), "gy", scatter_dimension=0, tiled=True
    )
    if len(kept) == 2:
        own = lax.all_gather(own, "dp", axis=0, tiled=True).astype(F32)
    else:
        own = lax.psum(own.astype(F32), "dp")
    return own if extra == 1.0 else own * extra


def images_here(block, copies):
    rows = block.shape[0] * block.shape[1]
    images = block.reshape(rows // SEQ, SEQ, block.shape[2])
    if copies > 1:
        images = jnp.repeat(images, copies, axis=0)
    return lax.all_to_all(images, "gx", split_axis=0, concat_axis=0, tiled=True)


def images_back(parts, copies, shape):
    parts = lax.all_to_all(parts, "gx", split_axis=0, concat_axis=0, tiled=True)
    if copies > 1:
        parts = parts[::copies]
    return parts.reshape(shape)


def collect(block, order):
    return lax.all_gather(block, order, axis=0, tiled=True)


def on_device(
    tokens,
    cotangent,
    ln1_gain,
    ln1_bias,
    qkv_weight,
    qv_bias,
    out_weight,
    out_bias,
    ln2_gain,
    ln2_bias,
    fc1_weight,
    fc1_bias,
    fc2_weight,
    fc2_bias,
):
    gx = lax.axis_size("gx")
    gy = lax.axis_size("gy")
    halves = 2 if lax.axis_size("dp") == 2 else 1
    blocks = gx * halves
    shape = tokens.shape
    part = shape[2]
    head_cols = qkv_weight.shape[2]
    heads = head_cols // HEAD_DIM
    triple = 3 * head_cols
    hidden_cols = fc1_weight.shape[1]
    width = part * gx
    copies = gx // (MICRO * shape[1] // SEQ)
    extra = 1.0 / copies
    along = ("gy", "gx")

    column = lax.axis_index("gx")
    half = lax.axis_index("dp")
    pick = jnp.stack(
        [
            (column ^ (2 * far + core)) * halves + (half ^ side if halves == 2 else 0)
            for core in range(2)
            for side in range(halves)
            for far in range(2)
        ]
    ).astype(jnp.int32)

    wide = jnp.stack([ln1_gain, ln1_bias, out_bias, ln2_gain, ln2_bias, fc2_bias], axis=1)
    deep = jnp.concatenate([qv_bias[0], qv_bias[1], fc1_bias])
    deep_cols = -(-deep.shape[0] // part)
    deep = jnp.pad(deep, (0, deep_cols * part - deep.shape[0])).reshape(deep_cols, part).T
    whole_qkv = collect(
        jnp.concatenate([qkv_weight.reshape(part, triple), wide, deep], axis=1), along
    ).reshape(gy, width, triple + 6 + deep_cols)
    whole_out = collect(out_weight, ("gx", "gy")).reshape(gx, gy * head_cols, part)
    whole_out = jnp.concatenate([whole_out[i] for i in range(gx)], axis=1)
    whole_fc1 = collect(fc1_weight, along).reshape(gy, width, hidden_cols)
    whole_fc2 = collect(fc2_weight.T, along).reshape(gy, width, hidden_cols)

    wide = whole_qkv[0, :, triple : triple + 6].T.astype(F32)
    gain_one, shift_one, bias_mix, gain_two, shift_two, bias_second = [
        wide[i : i + 1] for i in range(6)
    ]
    deep = whole_qkv[:, :part, triple + 6 :].astype(F32)
    deep = jnp.swapaxes(deep, 1, 2).reshape(gy, 1, deep_cols * part)
    bias_qkv = jnp.concatenate(
        [
            deep[:, :, :head_cols],
            jnp.zeros((gy, 1, head_cols), F32),
            deep[:, :, head_cols : 2 * head_cols],
        ],
        axis=2,
    )
    bias_first = deep[:, :, 2 * head_cols : 2 * head_cols + hidden_cols]

    token_parts = images_here(tokens, copies)
    grad_parts = images_here(cotangent, copies)
    grad_low, grad_turned, grad_sum = spread(grad_parts, blocks)
    image, ready_one, turned_one, packed = project(
        token_parts, gain_one, shift_one, whole_qkv, bias_qkv, blocks
    )
    mixture, log_total = attend(packed, heads)
    hidden, ready_two, turned_two = mix(
        image, mixture, whole_out, bias_mix, gain_two, shift_two, blocks
    )
    active, slope = expand(ready_two, whole_fc1, bias_first)
    grad_fc2 = shares(pick, grad_turned, active, extra).T
    layer_out = images_back(narrow(hidden, active, whole_fc2, bias_second, gx), copies, shape)
    (
        grad_first,
        first_sum,
        grad_hidden,
        grad_hidden_low,
        turned_hidden,
        gain_two_sum,
        shift_two_sum,
        low_sum,
    ) = feed_back(grad_low, hidden, gain_two, slope, whole_fc2, whole_fc1, blocks)
    grad_fc1 = shares(pick, turned_two, grad_first, extra)
    grad_out_weight = shares(pick, turned_hidden, mixture, extra).T
    grad_mixture = mix_back(grad_hidden_low, whole_out, gy)
    grad_packed, packed_sum = attend_back(
        packed, jnp.swapaxes(log_total, 1, 2), grad_mixture, heads
    )
    grad_qkv = shares(pick, turned_one, grad_packed, extra)
    tokens_grad, gain_one_sum, shift_one_sum = project_back(
        image, gain_one, grad_hidden, grad_packed, whole_qkv, gx
    )
    tokens_grad = images_back(tokens_grad, copies, shape)

    wide_sums = jnp.concatenate(
        [gain_one_sum, shift_one_sum, low_sum, gain_two_sum, shift_two_sum, grad_sum]
    )
    deep_sums = jnp.concatenate(
        [packed_sum[:, 0, :head_cols], packed_sum[:, 0, 2 * head_cols :], first_sum[:, 0]], axis=1
    )
    wide_sums, deep_sums = lax.psum((wide_sums, deep_sums), ("dp", "gx", "gy"))
    wide_sums = extra * lax.dynamic_slice_in_dim(wide_sums, column * part, part, 1)
    deep_sums = extra * lax.dynamic_index_in_dim(deep_sums, lax.axis_index("gy"), 0, False)
    return (
        layer_out,
        tokens_grad,
        wide_sums[0],
        wide_sums[1],
        grad_qkv.reshape(part, 3, head_cols),
        deep_sums[: 2 * head_cols].reshape(2, head_cols),
        grad_out_weight,
        wide_sums[2],
        wide_sums[3],
        wide_sums[4],
        grad_fc1,
        deep_sums[2 * head_cols :],
        grad_fc2,
        wide_sums[5],
    )


def solution(mesh):
    specs = (
        P(None, ("dp", "gy"), "gx"),
        P(None, ("dp", "gy"), "gx"),
        P("gx"),
        P("gx"),
        P("gx", None, "gy"),
        P(None, "gy"),
        P("gy", "gx"),
        P("gx"),
        P("gx"),
        P("gx"),
        P("gx", "gy"),
        P("gy"),
        P("gy", "gx"),
        P("gx"),
    )
    return jax.shard_map(
        on_device,
        mesh=mesh,
        in_specs=specs,
        out_specs=specs,
        check_vma=False,
    )
```

time: 997 us -> 834 us (0.84)
  Pallas kernels: 66.3 us -> 260 us
  matrix products: 160 us -> 0 us
  local copies, waits for them, and re-layouts: 179 us -> 78.5 us
  blocking collectives: 174 us -> 81.1 us
  other arithmetic: 71.3 us -> 21.8 us
  waiting for transfers between devices: 303 us -> 345 us
    pallas_call x2 -> x18, Pallas kernels: 66.3 us -> 260 us  [call(): pl.pallas_call(kernel, grid_spec=pltpu.PrefetchScalarGridSpec(num_scalar_...]
    dot_general x39 -> x0, matrix products: 160 us -> none  [contract(): lax.dot_general(left, right, (((left_dim,), (right_dim,)), ((), ())), pre...]
    ppermute x0 -> x12, waiting for transfers between devices: none -> 155 us  [swap(): return lax.ppermute(array, axis, [(i, i ^ bit) for i in range(size)])]
    unnamed x12 -> x8, waiting for transfers between devices: 146 us -> 1.97 us
    psum x2 -> x1, blocking collectives: 136 us -> 51.4 us  [on_device(): wide_sums, deep_sums = lax.psum((wide_sums, deep_sums), ('dp', 'gx', 'gy'))]
    unnamed x176 -> x25, local copies, waits for them, and re-layouts: 90.6 us -> 15 us
    all_to_all x4, waiting for transfers between devices: 10.7 us -> 48.5 us  [the longest x2 48.5 us: images_here(): return lax.all_to_all(images, 'gx', split_axis=0, concat_axis=0, tiled=True)]
    psum x1 -> x0, waiting for transfers between devices: 28.8 us -> none  [shares(): return lax.psum(summed.astype(F32), 'dp') * extra]
  transfers between devices with their start and end apart: 13 -> 24, of which waited for: 7 -> 11; matrix products, arithmetic and copies ran while one was open for 33% -> 12% of each run, Pallas kernels for 3% -> 21%
where the time goes in v2:
time: 834 us; the launch traced here: 826 us
  waiting for transfers between devices  345 us (41%)
  Pallas kernels  260 us (31%)
  blocking collectives  81.1 us (10%)
  local copies, waits for them, and re-layouts  78.5 us (9%)
  starting transfers between devices  24.4 us (3%)
  other arithmetic  21.8 us (3%)
  between operations  14.7 us (2%)
    pallas_call x18, Pallas kernels, call(): pl.pallas_call(kernel, grid_spec=pltpu.PrefetchScalarGridSpec(num_scalar_...  260 us
    ppermute x12, waiting for transfers between devices, swap(): return lax.ppermute(array, axis, [(i, i ^ bit) for i in range(size)])  155 us
    all_gather x4, waiting for transfers between devices, collect(): return lax.all_gather(block, order, axis=0, tiled=True)  140 us
    psum x1, blocking collectives, on_device(): wide_sums, deep_sums = lax.psum((wide_sums, deep_sums), ('dp', 'gx', 'gy'))  51.4 us
    all_to_all x2, waiting for transfers between devices, images_here(): return lax.all_to_all(images, 'gx', split_axis=0, concat_axis=0, tiled=True)  48.5 us
    all_gather x4, blocking collectives, shares(): own = lax.all_gather(own, 'dp', axis=0, tiled=True).astype(F32)  29.7 us
  transfers between devices with their start and end apart: 24, of which 11 were waited for; matrix products, arithmetic and copies ran while one was open for 12% of the time, Pallas kernels for 21%

profile of v2, /device:TPU:0, one launch (start us, length us, event | category | flops | bytes accessed | tf_op | source)
XLA Modules:
  0.0 825.8 jit_solution(16478441247133850283)
XLA Ops:
  18.0 3.3 copy.68
  24.4 4.5 all-to-all-start
  33.9 27.4 %all-to-all-done = bf16[4,729,288]{1,2,0:T(8,128)(2,1)} async-done(((bf16[4,729,288]{1,2,0:T(8,128)(2,1)}), bf16[4,729,288]{1,2,0:T(8,128)(2,1)}, u32[]{:S(2)}, u32[]{:S(2)}) %all-to-all-start) | async-done | bytes 1679648 | tf_op jit(solution)/shard_map/all_to_all | solution.py:582
  61.3 3.6 all-to-all-start.2
  66.1 4.0 copy.75.parts_ref
  70.2 21.1 %all-to-all-done.2 = bf16[4,729,288]{1,2,0:T(8,128)(2,1)S(1)} async-done(((bf16[4,729,288]{1,2,0:T(8,128)(2,1)}), bf16[4,729,288]{1,2,0:T(8,128)(2,1)S(1)}, u32[]{:S(2)}, u32[]{:S(2)}) %all-to-all-start.2) | async-done | bytes 1679648 | tf_op jit(solution)/shard_map/all_to_all | solution.py:582
  93.8 4.1 spread.1
  100.2 3.6 concatenate.21.weight_ref
  103.9 45.1 %all-gather.5.cloned.1.call-done = bf16[4608,876]{1,0:T(8,128)(2,1)} async-done(((bf16[288,876]{1,0:T(8,128)(2,1)}), bf16[4608,876]{1,0:T(8,128)(2,1)}) %all-gather.5.cloned.1.call-update) | async-done | bytes 8073232 | tf_op jit(solution)/shard_map/all_gather | solution.py:593
  158.8 14.0 %project.1 = (bf16[729,1152]{1,0:T(8,128)(2,1)}, bf16[729,1152]{1,0:T(8,128)(2,1)}, bf16[8,144,729]{2,1,0:T(8,128)(2,1)}, bf16[4,729,864]{2,1,0:T(8,128)(2,1)}) custom-call(bf16[4,729,288]{2,1,0:T(8,128)(2,1)} %copy.75.parts_ref, f32[1,1152]{1,0:T(1,128)} %copy.76.gain_ref, f32[1,1152]{1,0:T(1,128)} %copy.77.shift_ref, bf16[4,1152,876]{2,1,0:T(8,128)(2,1)} %bitcast.86, ...), custom_call_target="tpu_custom_call" | custom-call | flops 5804752896 | bytes 19853568 | tf_op jit(solution)/shard_map/project/pallas_call | solution.py:42
  172.7 29.2 %attend.1 = (bf16[4,729,288]{2,1,0:T(8,128)(2,1)}, f32[4,729,4]{2,1,0:T(8,128)}) custom-call(bf16[4,729,864]{2,1,0:T(8,128)(2,1)} %get-tuple-element.49.packed_ref), custom_call_target="tpu_custom_call" | custom-call | flops 7346640384 | bytes 6765120 | tf_op jit(solution)/shard_map/attend/pallas_call | solution.py:42
  204.4 8.8 %mix.1 = (f32[729,1152]{1,0:T(8,128)}, bf16[729,1152]{1,0:T(8,128)(2,1)}, bf16[8,144,729]{2,1,0:T(8,128)(2,1)}) custom-call(bf16[729,1152]{1,0:T(8,128)(2,1)} %get-tuple-element.48.image_ref, bf16[4,729,288]{2,1,0:T(8,128)(2,1)} %get-tuple-element.50.parts_ref.right_ref, bf16[1152,1152]{1,0:T(8,128)(2,1)} %concatenate.21.weight_ref, ...), custom_call_target="tpu_custom_call" | custom-call | flops 1934917632 | bytes 12745728 | tf_op jit(solution)/shard_map/mix/pallas_call | solution.py:42
  213.3 25.0 %all-gather.9.cloned.1.call-done = bf16[4608,1076]{1,0:T(8,128)(2,1)} async-done(((bf16[288,1076]{1,0:T(8,128)(2,1)}), bf16[4608,1076]{1,0:T(8,128)(2,1)}) %all-gather.9.cloned.1.call-update) | async-done | bytes 9916432 | tf_op jit(solution)/shard_map/all_gather | solution.py:593
  238.3 19.4 %expand.1 = (bf16[4,729,1076]{2,1,0:T(8,128)(2,1)}, f32[4,729,1076]{2,1,0:T(8,128)}) custom-call(bf16[729,1152]{1,0:T(8,128)(2,1)} %get-tuple-element.52.ready_ref, bf16[4,1152,1076]{2,1,0:T(8,128)(2,1)} %bitcast.91, f32[4,1,1076]{2,1,0:T(1,128)} %slice.194.bias_ref), custom_call_target="tpu_custom_call" | custom-call | flops 7229067264 | bytes 30438944 | tf_op jit(solution)/shard_map/expand/pallas_call | solution.py:42
  257.7 69.6 %all-gather.11.cloned.1.call-done = bf16[4608,1076]{1,0:T(8,128)(2,1)} async-done(((bf16[288,1076]{1,0:T(8,128)(2,1)}), bf16[4608,1076]{1,0:T(8,128)(2,1)}) %all-gather.11.cloned.1.call-update) | async-done | bytes 9916432 | tf_op jit(solution)/shard_map/all_gather | solution.py:593
  327.3 33.7 %feed_back.1 = (bf16[4,729,1076]{2,1,0:T(8,128)(2,1)}, f32[4,1,1076]{2,1,0:T(1,128)}, f32[729,1152]{1,0:T(8,128)}, bf16[729,1152]{1,0:T(8,128)(2,1)}, bf16[8,144...) custom-call(bf16[729,1152]{1,0:T(8,128)(2,1)} %get-tuple-element.54.grad_ref, ...), custom_call_target="tpu_custom_call" | custom-call | flops 14458134528 | bytes 50451488 | tf_op jit(solution)/shard_map/feed_back/pallas_call | solution.py:42
  361.0 6.4 mix_back.1.grad_ref
  367.4 36.9 %attend_back.1 = (bf16[4,729,864]{2,1,0:T(8,128)(2,1)}, f32[4,1,864]{2,1,0:T(1,128)}) custom-call(bf16[4,729,864]{2,1,0:T(8,128)(2,1)} %get-tuple-element.49.packed_ref, f32[4,4,729]{2,1,0:T(4,128)} %bitcast.83, bf16[4,729,288]{2,1,0:T(8,128)(2,1)} %mix_back.1.grad_ref), custom_call_target="tpu_custom_call" | custom-call | flops 18366601216 | bytes 11817792 | tf_op jit(solution)/shard_map/attend_back/pallas_call | solution.py:42
  404.3 8.7 %share.8 = bf16[4,4,144,864]{3,2,1,0:T(8,128)(2,1)} custom-call(s32[8]{0:T(128)} %stack.59.pick_ref, bf16[8,144,729]{2,1,0:T(8,128)(2,1)} %get-tuple-element.67.turned_ref, bf16[4,729,864]{2,1,0:T(8,128)(2,1)} %get-tuple-element.59.packed_ref.right_ref), custom_call_target="tpu_custom_call" | custom-call | flops 2902376448 | bytes 10699776 | tf_op jit(solution)/shard_map/share/pallas_call | solution.py:42
  413.3 10.0 %share.14 = bf16[4,4,144,1076]{3,2,1,0:T(8,128)(2,1)} custom-call(s32[8]{0:T(128)} %stack.59.pick_ref, bf16[8,144,729]{2,1,0:T(8,128)(2,1)} %get-tuple-element.79.turned_ref, bf16[4,729,1076]{2,1,0:T(8,128)(2,1)} %get-tuple-element.53.active_ref.right_ref), custom_call_target="tpu_custom_call" | custom-call | flops 3614533632 | bytes 12913056 | tf_op jit(solution)/shard_map/share/pallas_call | solution.py:42
  423.5 9.8 %share.12 = bf16[4,4,144,1076]{3,2,1,0:T(8,128)(2,1)} custom-call(s32[8]{0:T(128)} %stack.59.pick_ref, bf16[8,144,729]{2,1,0:T(8,128)(2,1)} %get-tuple-element.75.turned_ref, bf16[4,729,1076]{2,1,0:T(8,128)(2,1)} %get-tuple-element.76.right_ref), custom_call_target="tpu_custom_call" | custom-call | flops 3614533632 | bytes 12913056 | tf_op jit(solution)/shard_map/share/pallas_call | solution.py:42
  435.6 9.5 %share.9 = (bf16[2,4,144,864]{3,2,1,0:T(8,128)(2,1)}, bf16[2,4,144,864]{3,2,1,0:T(8,128)(2,1)}) custom-call(s32[8]{0:T(128)} %stack.59.pick_ref, bf16[8,144,729]{2,1,0:T(8,128)(2,1)} %get-tuple-element.67.turned_ref, bf16[4,729,864]{2,1,0:T(8,128)(2,1)} %get-tuple-element.59.packed_ref.right_ref, bf16[4,4,144,864]{3,2,1,0:T(8,128)(2,1)} %copy-done), custom_call_target="tpu_custom_call" | custom-call | flops 2902376448 | bytes 14681088 | tf_op jit(solution)/shard_map/share/pallas_call | solution.py:42
  446.5 6.3 share.10
  452.8 10.7 %share.15 = (bf16[2,4,144,1076]{3,2,1,0:T(8,128)(2,1)}, bf16[2,4,144,1076]{3,2,1,0:T(8,128)(2,1)}) custom-call(s32[8]{0:T(128)} %stack.59.pick_ref, bf16[8,144,729]{2,1,0:T(8,128)(2,1)} %get-tuple-element.79.turned_ref, bf16[4,729,1076]{2,1,0:T(8,128)(2,1)} %get-tuple-element.53.active_ref.right_ref, bf16[4,4,144,1076]{3,2,1,0:T(8,128)(2,1)} %collective-permute-done.9.rest_0_), custom_call_target="tpu_custom_call" | custom-call | flops 3614533632 | bytes 17871264 | tf_op jit(solution)/shard_map/share/pallas_call | solution.py:42
  464.2 6.8 share.11
  472.3 20.7 %collective-permute-done.1 = bf16[2,4,144,864]{3,2,1,0:T(8,128)(2,1)S(1)} collective-permute-done((bf16[2,4,144,864]{3,2,1,0:T(8,128)(2,1)}, bf16[2,4,144,864]{3,2,1,0:T(8,128)(2,1)S(1)}, u32[]{:S(2)}, u32[]{:S(2)}) %collective-permute-start.1) | collective-permute-done | bytes 1990688 | tf_op jit(solution)/shard_map/ppermute | solution.py:554
  494.9 73.3 %collective-permute-done.4 = bf16[2,4,144,288]{3,2,1,0:T(8,128)(2,1)S(1)} collective-permute-done((bf16[2,4,144,288]{3,2,1,0:T(8,128)(2,1)}, bf16[2,4,144,288]{3,2,1,0:T(8,128)(2,1)S(1)}, u32[]{:S(2)}, u32[]{:S(2)}) %collective-permute-start.4) | collective-permute-done | bytes 663584 | tf_op jit(solution)/shard_map/ppermute | solution.py:554
  568.9 10.9 %collective-permute-done.5 = bf16[4,144,288]{2,1,0:T(8,128)(2,1)S(1)} collective-permute-done((bf16[4,144,288]{2,1,0:T(8,128)(2,1)S(1)}, bf16[4,144,288]{2,1,0:T(8,128)(2,1)S(1)}, u32[]{:S(2)}, u32[]{:S(2)}) %collective-permute-start.5) | collective-permute-done | bytes 331808 | tf_op jit(solution)/shard_map/ppermute | solution.py:554
  580.8 10.8 %share.13 = (bf16[2,4,144,1076]{3,2,1,0:T(8,128)(2,1)}, bf16[2,4,144,1076]{3,2,1,0:T(8,128)(2,1)}) custom-call(s32[8]{0:T(128)} %stack.59.pick_ref, bf16[8,144,729]{2,1,0:T(8,128)(2,1)} %get-tuple-element.75.turned_ref, bf16[4,729,1076]{2,1,0:T(8,128)(2,1)} %get-tuple-element.76.right_ref, bf16[4,4,144,1076]{3,2,1,0:T(8,128)(2,1)} %collective-permute-done.6.rest_0_), custom_call_target="tpu_custom_call" | custom-call | flops 3614533632 | bytes 17871264 | tf_op jit(solution)/shard_map/share/pallas_call | solution.py:42
  593.1 3.2 fusion.2
  598.6 28.8 %collective-permute-done.11 = bf16[4,144,1076]{2,1,0:T(8,128)(2,1)S(1)} collective-permute-done((bf16[4,144,1076]{2,1,0:T(8,128)(2,1)S(1)}, bf16[4,144,1076]{2,1,0:T(8,128)(2,1)S(1)}, u32[]{:S(2)}, u32[]{:S(2)}) %collective-permute-start.11) | collective-permute-done | bytes 1239584 | tf_op jit(solution)/shard_map/ppermute | solution.py:554
  627.4 3.0 fusion
  630.4 19.5 %collective-permute-done.7 = bf16[2,4,144,1076]{3,2,1,0:T(8,128)(2,1)} collective-permute-done((bf16[2,4,144,1076]{3,2,1,0:T(8,128)(2,1)}, bf16[2,4,144,1076]{3,2,1,0:T(8,128)(2,1)}, u32[]{:S(2)}, u32[]{:S(2)}) %collective-permute-start.7) | collective-permute-done | bytes 2479136 | tf_op jit(solution)/shard_map/ppermute | solution.py:554
  650.0 3.1 fusion.3
  654.6 17.8 %project_back.1 = (bf16[4,729,288]{2,1,0:T(8,128)(2,1)}, f32[1,1152]{1,0:T(1,128)}, f32[1,1152]{1,0:T(1,128)}) custom-call(bf16[729,1152]{1,0:T(8,128)(2,1)} %get-tuple-element.48.image_ref, f32[1,1152]{1,0:T(1,128)} %copy.76.gain_ref, f32[729,1152]{1,0:T(8,128)} %get-tuple-element.56.hidden_grad_ref, ...), custom_call_target="tpu_custom_call" | custom-call | flops 5804752896 | bytes 19844352 | tf_op jit(solution)/shard_map/project_back/pallas_call | solution.py:42
  672.4 4.0 copy.91
  676.4 3.6 all-to-all-start.3
  682.0 3.3 fusion.1
  685.2 17.1 %narrow.1 = bf16[4,729,288]{2,1,0:T(8,128)(2,1)} custom-call(f32[729,1152]{1,0:T(8,128)} %get-tuple-element.51.hidden_ref, bf16[4,729,1076]{2,1,0:T(8,128)(2,1)} %get-tuple-element.53.active_ref.right_ref, bf16[4,1152,1076]{2,1,0:T(8,128)(2,1)} %bitcast.90, f32[1,1152]{1,0:T(1,128)} %copy.82.bias_ref), custom_call_target="tpu_custom_call" | custom-call | flops 7229067264 | bytes 21235104 | tf_op jit(solution)/shard_map/narrow/pallas_call | solution.py:42
  702.4 4.0 copy.83
  706.4 3.7 all-to-all-start.1
  714.4 51.4 %all-reduce.1 = (f32[6,1152]{1,0:T(8,128)}, f32[4,1652]{1,0:T(4,128)}) all-reduce(f32[6,1152]{1,0:T(8,128)} %concatenate.22, f32[4,1652]{1,0:T(4,128)} %concatenate.23), channel_id=1, replica_groups=mesh['dp'=2,'gx'=4,'gy'=4] {'dp','gx','gy'}, use_global_device_ids=true, to_apply=%region_0.1 | all-reduce | flops 13520 | bytes 108160 | tf_op jit(solution)/shard_map/psum | solution.py:707
  770.3 2.6 copy.92
  772.9 4.9 reshape.134
  784.0 5.8 all_gather.29
  790.9 7.2 all_gather.28
  799.8 8.2 all_gather.31
  809.2 8.4 %all_gather.30 = bf16[288,1076]{1,0:T(8,128)(2,1)S(1)} all-gather(bf16[144,1076]{1,0:T(8,128)(2,1)} %reduce-scatter.9.cloned.1.call-done), channel_id=1, replica_groups=mesh['dp'=2,'gx'=4,'gy'=4] {'dp'}, dimensions={0}, use_global_device_ids=true | all-gather | bytes 929664 | tf_op jit(solution)/shard_map/all_gather | solution.py:571
  (119 shorter events, 74.1 us)
Async XLA Ops:
  7.2 90.7 %all-gather.7.cloned.1.call-start = ((), (), s32[]{:S(2)}) async-start(), calls=%async_computation.9 | async-start | bytes 3760128 | tf_op jit(solution)/shard_map/all_gather | solution.py:593
  7.9 141.1 %all-gather.5.cloned.1.call-start = ((), (), s32[]{:S(2)}) async-start(), calls=%async_computation.8 | async-start | bytes 8773632 | tf_op jit(solution)/shard_map/all_gather | solution.py:593
  16.7 221.6 %all-gather.9.cloned.1.call-start = ((), (), s32[]{:S(2)}) async-start(), calls=%async_computation.10 | async-start | bytes 11280384 | tf_op jit(solution)/shard_map/all_gather | solution.py:593
  17.4 309.9 %all-gather.11.cloned.1.call-start = ((), (), s32[]{:S(2)}) async-start(), calls=%async_computation.11 | async-start | bytes 11280384 | tf_op jit(solution)/shard_map/all_gather | solution.py:593
  24.4 4.6 copy-start.5
  24.4 36.9 %all-to-all-start = ((bf16[4,729,288]{1,2,0:T(8,128)(2,1)}), bf16[4,729,288]{1,2,0:T(8,128)(2,1)}, u32[]{:S(2)}, u32[]{:S(2)}) async-start(bf16[4,729,288]{1,2,0:T(8,128)(2,1)} %copy.69), calls=%async_computation | async-start | bytes 3538944 | tf_op jit(solution)/shard_map/all_to_all | solution.py:582
  61.3 30.0 %all-to-all-start.2 = ((bf16[4,729,288]{1,2,0:T(8,128)(2,1)}), bf16[4,729,288]{1,2,0:T(8,128)(2,1)S(1)}, u32[]{:S(2)}, u32[]{:S(2)}) async-start(bf16[4,729,288]{1,2,0:T(8,128)(2,1)} %copy.86), calls=%async_computation.2 | async-start | bytes 3538944 | tf_op jit(solution)/shard_map/all_to_all | solution.py:582
  64.8 719.2 %reduce-scatter.15.cloned.1.call-start = ((), (), s32[]{:S(2)}) async-start(), calls=%async_computation.15 | async-start | bytes 552960 | tf_op jit(solution)/shard_map/reduce_scatter | solution.py:567
  413.0 20.6 %collective-permute-start = (bf16[4,4,144,864]{3,2,1,0:T(8,128)(2,1)}, bf16[4,4,144,864]{3,2,1,0:T(8,128)(2,1)S(1)}, u32[]{:S(2)}, u32[]{:S(2)}) collective-permute-start(bf16[4,4,144,864]{3,2,1,0:T(8,128)(2,1)} %share.8), channel_id=1, source_target_pairs={{0,4},{4,0},{8,12},{12,8},{1,5},{5,1},{9,13},{13,9},{2,6},{6,2},{1... | collective-permute-start | bytes 11943944 | tf_op jit(solution)/shard_map/ppermute | solution.py:554
  423.3 29.5 %collective-permute-start.9 = (bf16[4,4,144,1076]{3,2,1,0:T(8,128)(2,1)}, bf16[4,4,144,1076]{3,2,1,0:T(8,128)(2,1)}, u32[]{:S(2)}, u32[]{:S(2)}) collective-permute-start(bf16[4,4,144,1076]{3,2,1,0:T(8,128)(2,1)} %share.14), channel_id=1, source_target_pairs={{0,4},{4,0},{8,12},{12,8},{1,5},{5,1},{9,13},{13,9},{2,6},{6,2},{1... | collective-permute-start | bytes 14874632 | tf_op jit(solution)/shard_map/ppermute | solution.py:554
  433.3 147.5 %collective-permute-start.6 = (bf16[4,4,144,1076]{3,2,1,0:T(8,128)(2,1)}, bf16[4,4,144,1076]{3,2,1,0:T(8,128)(2,1)}, u32[]{:S(2)}, u32[]{:S(2)}) collective-permute-start(bf16[4,4,144,1076]{3,2,1,0:T(8,128)(2,1)} %share.12), channel_id=1, source_target_pairs={{0,4},{4,0},{8,12},{12,8},{1,5},{5,1},{9,13},{13,9},{2,6},{6,2},{1... | collective-permute-start | bytes 14874632 | tf_op jit(solution)/shard_map/ppermute | solution.py:554
  433.6 1.9 copy-start
  445.0 48.0 %collective-permute-start.1 = (bf16[2,4,144,864]{3,2,1,0:T(8,128)(2,1)}, bf16[2,4,144,864]{3,2,1,0:T(8,128)(2,1)S(1)}, u32[]{:S(2)}, u32[]{:S(2)}) collective-permute-start(bf16[2,4,144,864]{3,2,1,0:T(8,128)(2,1)} %get-tuple-element.69), channel_id=1, source_target_pairs={{0,16},{16,0},{1,17},{17,1},{2,18},{18,2},{3,19},{19,3},{4,20},{20... | collective-permute-start | bytes 5971976 | tf_op jit(solution)/shard_map/ppermute | solution.py:554
  452.8 11.3 %collective-permute-start.3 = (bf16[4,4,144,288]{3,2,1,0:T(8,128)(2,1)}, bf16[4,4,144,288]{3,2,1,0:T(8,128)(2,1)}, u32[]{:S(2)}, u32[]{:S(2)}) collective-permute-start(bf16[4,4,144,288]{3,2,1,0:T(8,128)(2,1)} %share.10), channel_id=1, source_target_pairs={{0,4},{4,0},{8,12},{12,8},{1,5},{5,1},{9,13},{13,9},{2,6},{6,2},{1... | collective-permute-start | bytes 3981320 | tf_op jit(solution)/shard_map/ppermute | solution.py:554
  463.6 29.4 %copy-start.3 = (bf16[2,4,144,864]{3,2,1,0:T(8,128)(2,1)S(1)}, bf16[2,4,144,864]{3,2,1,0:T(8,128)(2,1)}, u32[]{:S(2)}) copy-start(bf16[2,4,144,864]{3,2,1,0:T(8,128)(2,1)} %get-tuple-element.68) | copy-start | bytes 5971972
  463.6 132.8 %collective-permute-start.10 = (bf16[2,4,144,1076]{3,2,1,0:T(8,128)(2,1)}, bf16[2,4,144,1076]{3,2,1,0:T(8,128)(2,1)}, u32[]{:S(2)}, u32[]{:S(2)}) collective-permute-start(bf16[2,4,144,1076]{3,2,1,0:T(8,128)(2,1)} %get-tuple-element.81), channel_id=1, source_target_pairs={{0,16},{16,0},{1,17},{17,1},{2,18},{18,2},{3,19},{19,3},{4,20},{20... | collective-permute-start | bytes 7437320 | tf_op jit(solution)/shard_map/ppermute | solution.py:554
  471.0 97.2 %copy-start.6 = (bf16[2,4,144,288]{3,2,1,0:T(8,128)(2,1)S(1)}, bf16[2,4,144,288]{3,2,1,0:T(8,128)(2,1)}, u32[]{:S(2)}) copy-start(bf16[2,4,144,288]{3,2,1,0:T(8,128)(2,1)} %get-tuple-element.73) | copy-start | bytes 1990660
  471.0 97.2 %collective-permute-start.4 = (bf16[2,4,144,288]{3,2,1,0:T(8,128)(2,1)}, bf16[2,4,144,288]{3,2,1,0:T(8,128)(2,1)S(1)}, u32[]{:S(2)}, u32[]{:S(2)}) collective-permute-start(bf16[2,4,144,288]{3,2,1,0:T(8,128)(2,1)} %get-tuple-element.74), channel_id=1, source_target_pairs={{0,16},{16,0},{1,17},{17,1},{2,18},{18,2},{3,19},{19,3},{4,20},{20... | collective-permute-start | bytes 1990664 | tf_op jit(solution)/shard_map/ppermute | solution.py:554
  493.0 75.2 %copy-start.4 = (bf16[2,4,144,864]{3,2,1,0:T(8,128)(2,1)}, bf16[2,4,144,864]{3,2,1,0:T(8,128)(2,1)S(1)}, u32[]{:S(2)}) copy-start(bf16[2,4,144,864]{3,2,1,0:T(8,128)(2,1)S(1)} %collective-permute-done.1) | copy-start | bytes 5971972
  494.4 98.7 %collective-permute-start.2 = (bf16[4,144,864]{2,1,0:T(8,128)(2,1)}, bf16[4,144,864]{2,1,0:T(8,128)(2,1)}, u32[]{:S(2)}, u32[]{:S(2)}) collective-permute-start(bf16[4,144,864]{2,1,0:T(8,128)(2,1)} %fusion.5), channel_id=1, source_target_pairs={{0,8},{4,12},{8,0},{12,4},{1,9},{5,13},{9,1},{13,5},{2,10},{6,14},... | collective-permute-start | bytes 2985992 | tf_op jit(solution)/shard_map/ppermute | solution.py:554
  568.3 11.5 %collective-permute-start.5 = (bf16[4,144,288]{2,1,0:T(8,128)(2,1)S(1)}, bf16[4,144,288]{2,1,0:T(8,128)(2,1)S(1)}, u32[]{:S(2)}, u32[]{:S(2)}) collective-permute-start(bf16[4,144,288]{2,1,0:T(8,128)(2,1)S(1)} %fusion.7), channel_id=1, source_target_pairs={{0,8},{4,12},{8,0},{12,4},{1,9},{5,13},{9,1},{13,5},{2,10},{6,14},... | collective-permute-start | bytes 995336 | tf_op jit(solution)/shard_map/ppermute | solution.py:554
  580.8 210.1 %reduce-scatter.13.cloned.1.call-start = ((), (), s32[]{:S(2)}) async-start(), calls=%async_computation.14 | async-start | bytes 1290240 | tf_op jit(solution)/shard_map/reduce_scatter | solution.py:567
  591.6 4.8 copy-start.1
  591.6 58.4 %collective-permute-start.7 = (bf16[2,4,144,1076]{3,2,1,0:T(8,128)(2,1)}, bf16[2,4,144,1076]{3,2,1,0:T(8,128)(2,1)}, u32[]{:S(2)}, u32[]{:S(2)}) collective-permute-start(bf16[2,4,144,1076]{3,2,1,0:T(8,128)(2,1)} %get-tuple-element.78), channel_id=1, source_target_pairs={{0,16},{16,0},{1,17},{17,1},{2,18},{18,2},{3,19},{19,3},{4,20},{20... | collective-permute-start | bytes 7437320 | tf_op jit(solution)/shard_map/ppermute | solution.py:554
  596.3 203.5 %reduce-scatter.11.cloned.1.call-start = ((), (), s32[]{:S(2)}) async-start(), calls=%async_computation.13 | async-start | bytes 1658880 | tf_op jit(solution)/shard_map/reduce_scatter | solution.py:567
  598.0 29.4 %collective-permute-start.11 = (bf16[4,144,1076]{2,1,0:T(8,128)(2,1)S(1)}, bf16[4,144,1076]{2,1,0:T(8,128)(2,1)S(1)}, u32[]{:S(2)}, u32[]{:S(2)}) collective-permute-start(bf16[4,144,1076]{2,1,0:T(8,128)(2,1)S(1)} %fusion.4), channel_id=1, source_target_pairs={{0,8},{4,12},{8,0},{12,4},{1,9},{5,13},{9,1},{13,5},{2,10},{6,14},... | collective-permute-start | bytes 3718664 | tf_op jit(solution)/shard_map/ppermute | solution.py:554
  630.4 23.4 %copy-start.2 = (f32[1,1152]{0,1:T(8,128)S(1)}, f32[1,1152]{0,1:T(8,128)}, u32[]{:S(2)}) copy-start(f32[1,1152]{0,1:T(8,128)} %get-tuple-element.138) | copy-start | bytes 13828
  653.1 28.9 %collective-permute-start.8 = (bf16[4,144,1076]{2,1,0:T(8,128)(2,1)}, bf16[4,144,1076]{2,1,0:T(8,128)(2,1)S(1)}, u32[]{:S(2)}, u32[]{:S(2)}) collective-permute-start(bf16[4,144,1076]{2,1,0:T(8,128)(2,1)} %fusion.3), channel_id=1, source_target_pairs={{0,8},{4,12},{8,0},{12,4},{1,9},{5,13},{9,1},{13,5},{2,10},{6,14},... | collective-permute-start | bytes 3718664 | tf_op jit(solution)/shard_map/ppermute | solution.py:554
  676.4 30.0 %all-to-all-start.3 = ((bf16[4,729,288]{1,2,0:T(8,128)(2,1)}), bf16[4,729,288]{1,2,0:T(8,128)(2,1)S(1)}, u32[]{:S(2)}, u32[]{:S(2)}) async-start(bf16[4,729,288]{1,2,0:T(8,128)(2,1)} %copy.91), calls=%async_computation.3 | async-start | bytes 3538944 | tf_op jit(solution)/shard_map/all_to_all | solution.py:586
  680.0 129.1 %reduce-scatter.9.cloned.1.call-start = ((), (), s32[]{:S(2)}) async-start(), calls=%async_computation.12 | async-start | bytes 1658880 | tf_op jit(solution)/shard_map/reduce_scatter | solution.py:567
  706.4 5.1 copy-start.7
  706.4 72.7 %all-to-all-start.1 = ((bf16[4,729,288]{1,2,0:T(8,128)(2,1)}), bf16[4,729,288]{1,2,0:T(8,128)(2,1)S(1)}, u32[]{:S(2)}, u32[]{:S(2)}) async-start(bf16[4,729,288]{1,2,0:T(8,128)(2,1)} %copy.83), calls=%async_computation.1 | async-start | bytes 3538944 | tf_op jit(solution)/shard_map/all_to_all | solution.py:586
Sparse Core Ops, SparseCore 0:
  10.3 60.0 all-gather.6
  73.3 75.6 all-gather.4
  151.3 86.9 all-gather.8
  240.4 86.8 all-gather.10
  580.9 19.2 reduce-scatter.14
  603.0 25.3 reduce-scatter.12
  630.7 30.2 reduce-scatter.10
  685.4 29.7 reduce-scatter.8

commit v3 on v2

v3 whole, which is shorter than its diff:
```python
import functools

import jax
import jax.numpy as jnp
from jax import lax
from jax.experimental import pallas as pl
from jax.experimental.pallas import tpu as pltpu
from jax.sharding import PartitionSpec as P

HEAD_DIM = 72
SEQ = 729
MICRO = 2
EPSILON = 1e-06
QUERY_ROWS = 384
ROWS = 256
NEAR = 2
COST = 1
RING = False
COLS = 256
BF16 = jnp.bfloat16
F32 = jnp.float32
VMEM_BYTES = 60 * 2**20


def contract(left, right, left_dim, right_dim):
    return lax.dot_general(
        left, right, (((left_dim,), (right_dim,)), ((), ())), preferred_element_type=F32
    )


def blocks_of(total, size):
    return [(low, min(low + size, total)) for low in range(0, total, size)]


def whole(shape):
    return pl.BlockSpec(shape, lambda i, *_: (0,) * len(shape))


def nth(shape):
    return pl.BlockSpec((1,) + tuple(shape[1:]), lambda i, *_: (i,) + (0,) * (len(shape) - 1))


def call(kernel, name, steps, ins, outs, flops, scratch=(), prefetch=()):
    moved = sum(a.size * a.dtype.itemsize for a, _ in list(ins) + list(outs))
    return pl.pallas_call(
        kernel,
        grid_spec=pltpu.PrefetchScalarGridSpec(
            num_scalar_prefetch=len(prefetch),
            grid=(steps,),
            in_specs=[spec for _, spec in ins],
            out_specs=[spec for _, spec in outs],
            scratch_shapes=list(scratch),
        ),
        out_shape=[shape for shape, _ in outs],
        compiler_params=pltpu.CompilerParams(vmem_limit_bytes=VMEM_BYTES),
        cost_estimate=pl.CostEstimate(
            flops=flops * COST, bytes_accessed=moved * COST, transcendentals=0
        ),
        name=name,
    )(*prefetch, *[a for a, _ in ins])


def struct(shape, dtype):
    return jax.ShapeDtypeStruct(tuple(shape), dtype)


def attend_kernel(heads, packed_ref, mix_ref, total_ref):
    seq = packed_ref.shape[1]
    width = heads * HEAD_DIM
    scaling = HEAD_DIM ** (-0.5)
    for head in range(heads):
        first = head * HEAD_DIM
        last = first + HEAD_DIM
        keys = packed_ref[0, :, width + first : width + last]
        values = packed_ref[0, :, 2 * width + first : 2 * width + last]
        for low, high in blocks_of(seq, QUERY_ROWS):
            queries = packed_ref[0, low:high, first:last]
            scores = contract(queries, keys, 1, 1) * scaling
            row_max = jnp.max(scores, axis=1, keepdims=True)
            exponent = jnp.exp(scores - row_max)
            row_total = jnp.sum(exponent, axis=1, keepdims=True)
            probability = (exponent * (1.0 / row_total)).astype(BF16)
            mix_ref[0, low:high, first:last] = contract(probability, values, 1, 0).astype(BF16)
            total_ref[0, low:high, head : head + 1] = row_max + jnp.log(row_total)


def attend(packed, heads):
    groups, seq, _ = packed.shape
    mix = struct((groups, seq, heads * HEAD_DIM), BF16)
    total = struct((groups, seq, heads), F32)
    return call(
        functools.partial(attend_kernel, heads),
        "attend",
        groups,
        [(packed, nth(packed.shape))],
        [(mix, nth(mix.shape)), (total, nth(total.shape))],
        12 * groups * heads * seq * seq * HEAD_DIM,
    )


def attend_back_kernel(
    heads, some, packed_ref, total_ref, grad_ref, out_ref, sum_ref, key_sum, value_sum
):
    seq = packed_ref.shape[1]
    width = heads * HEAD_DIM
    part = len(some) * HEAD_DIM
    scaling = HEAD_DIM ** (-0.5)
    for place, head in enumerate(some):
        first = head * HEAD_DIM
        last = first + HEAD_DIM
        start = place * HEAD_DIM
        stop = start + HEAD_DIM
        keys = packed_ref[0, :, width + first : width + last]
        values = packed_ref[0, :, 2 * width + first : 2 * width + last]
        for low, high in blocks_of(seq, QUERY_ROWS):
            queries = packed_ref[0, low:high, first:last]
            grads = grad_ref[0, low:high, first:last]
            scores = contract(keys, queries, 1, 1) * scaling
            probability = jnp.exp(scores - total_ref[0, head : head + 1, low:high])
            grad_values = contract(probability.astype(BF16), grads, 1, 0)
            grad_prob = contract(values, grads, 1, 1)
            inner = jnp.sum(probability * grad_prob, axis=0, keepdims=True)
            grad_scores = (probability * (grad_prob - inner)).astype(BF16)
            grad_keys = contract(grad_scores, queries, 1, 0)
            grad_queries = contract(grad_scores, keys, 0, 0) * scaling
            out_ref[0, low:high, start:stop] = grad_queries.astype(BF16)
            if low == 0:
                key_sum[...] = grad_keys
                value_sum[...] = grad_values
            else:
                key_sum[...] += grad_keys
                value_sum[...] += grad_values
        out_ref[0, :, part + start : part + stop] = (key_sum[...] * scaling).astype(BF16)
        out_ref[0, :, 2 * part + start : 2 * part + stop] = value_sum[...].astype(BF16)
    sum_ref[0] = jnp.sum(out_ref[0].astype(F32), axis=0, keepdims=True)


def attend_back(packed, total, grads, heads, some):
    groups, seq, _ = packed.shape
    triple = 3 * len(some) * HEAD_DIM
    out = struct((groups, seq, triple), BF16)
    sums = struct((groups, 1, triple), F32)
    return call(
        functools.partial(attend_back_kernel, heads, some),
        "attend_back",
        groups,
        [(packed, nth(packed.shape)), (total, nth(total.shape)), (grads, nth(grads.shape))],
        [(out, nth(out.shape)), (sums, nth(sums.shape))],
        30 * groups * len(some) * seq * seq * HEAD_DIM,
        [pltpu.VMEM((seq, HEAD_DIM), F32), pltpu.VMEM((seq, HEAD_DIM), F32)],
    )


def norm(values):
    center = jnp.mean(values, axis=1, keepdims=True)
    shifted = values - center
    inverse = lax.rsqrt(jnp.mean(shifted * shifted, axis=1, keepdims=True) + EPSILON)
    return shifted * inverse, inverse


def norm_back(grad_norm, normed, inverse, gain):
    grad_hat = grad_norm * gain
    return inverse * (
        grad_hat
        - jnp.mean(grad_hat, axis=1, keepdims=True)
        - normed * jnp.mean(grad_hat * normed, axis=1, keepdims=True)
    )


def on_column(place_ref, count, body):
    for c in range(count):
        pl.when(place_ref[0] == c)(functools.partial(body, c))


def join_parts(place_ref, parts, blocks_ref):
    rows = blocks_ref.shape[1]
    each = parts[0].shape[0] // rows
    for r, ref in enumerate(parts):
        for i in range(each):
            blocks_ref[(place_ref[0] ^ r) * each + i] = ref[i * rows : (i + 1) * rows]


def flat(blocks_ref):
    count, rows, seq = blocks_ref.shape
    return blocks_ref[...].reshape(count * rows, seq)


def split_parts(place_ref, values, parts, blocks_ref):
    turned(values, blocks_ref)
    for r, ref in enumerate(parts):
        ref[...] = blocks_ref[place_ref[0] ^ r]


def join_columns(place_ref, groups, parts_ref, whole_ref):
    part = parts_ref.shape[2]
    for k in range(groups):
        whole_ref[:, k * part : (k + 1) * part] = parts_ref[order_of(place_ref, groups, k)]


def order_of(place_ref, groups, k):
    return place_ref[place_ref.shape[0] - groups + k]


def join_rows(place_ref, pieces, whole_ref, start, stop, k=0):
    for p, ref in enumerate(pieces):
        whole_ref[place_ref[1 + p], :, start:stop] = ref[k, :, : stop - start]


def turned(rows, blocks_ref):
    columns = rows.T
    count, size, _ = blocks_ref.shape
    for i in range(count):
        blocks_ref[i] = columns[i * size : (i + 1) * size]


def cut_kernel(copies, place_ref, rows_ref, *parts):
    seq = parts[0].shape[1]
    each = rows_ref.shape[2] // seq

    def body(c):
        for r, ref in enumerate(parts):
            image = (c ^ r) // copies
            start = (image % each) * seq
            ref[...] = rows_ref[image // each, :, start : start + seq]

    on_column(place_ref, len(parts), body)


def cut(spot, rows, count, copies):
    shape = struct((rows.shape[1], SEQ), BF16)
    return call(
        functools.partial(cut_kernel, copies),
        "cut",
        1,
        [(rows, whole(rows.shape))],
        [(shape, whole(shape.shape))] * count,
        0,
        prefetch=(spot,),
    )


def place_kernel(copies, place_ref, *refs):
    parts, rows_ref = refs[:-1], refs[-1]
    seq = parts[0].shape[1]
    each = rows_ref.shape[2] // seq

    def body(c):
        for image in range(len(parts) // copies):
            start = (image % each) * seq
            rows_ref[image // each, :, start : start + seq] = parts[c ^ (image * copies)][...]

    on_column(place_ref, len(parts), body)


def place(spot, parts, shape, copies):
    return call(
        functools.partial(place_kernel, copies),
        "place",
        1,
        [(a, whole(a.shape)) for a in parts],
        [(struct(shape, BF16), whole(shape))],
        0,
        prefetch=(spot,),
    )[0]


def spread_kernel(place_ref, *refs):
    parts = refs[:-3]
    whole_ref, turned_ref, sum_ref = refs[-3:]
    join_parts(place_ref, parts, turned_ref)
    whole_ref[...] = flat(turned_ref).T
    sum_ref[...] = jnp.sum(whole_ref[...].astype(F32), axis=0, keepdims=True)


def spread(spot, parts, blocks):
    part, seq = parts[0].shape
    width = len(parts) * part
    outs = [
        struct((seq, width), BF16),
        struct((blocks, width // blocks, seq), BF16),
        struct((1, width), F32),
    ]
    return call(
        spread_kernel,
        "spread",
        1,
        [(a, whole(a.shape)) for a in parts],
        [(o, whole(o.shape)) for o in outs],
        seq * width,
        prefetch=(spot,),
    )


def project_kernel(count, triple, place_ref, *refs):
    parts = refs[:count]
    gain_ref, shift_ref, weight_ref, bias_ref = refs[count : count + 4]
    image_ref, ready_ref, turned_ref, packed_ref = refs[count + 4 :]

    @pl.when(pl.program_id(0) == 0)
    def _():
        join_parts(place_ref, parts, turned_ref)
        image_ref[...] = flat(turned_ref).T
        for low, high in blocks_of(image_ref.shape[0], ROWS):
            normed, _ = norm(image_ref[low:high].astype(F32))
            ready_ref[low:high] = (normed * gain_ref[...] + shift_ref[...]).astype(BF16)
        turned(ready_ref[...], turned_ref)

    packed = contract(ready_ref[...], weight_ref[0, :, :triple], 1, 0) + bias_ref[0]
    packed_ref[0] = packed.astype(BF16)


def project(spot, parts, gain, shift, weight, bias, blocks):
    part, seq = parts[0].shape
    width = len(parts) * part
    groups, _, triple = bias.shape
    outs = [
        (struct((seq, width), BF16), whole((seq, width))),
        (struct((seq, width), BF16), whole((seq, width))),
        (struct((blocks, width // blocks, seq), BF16), whole((blocks, width // blocks, seq))),
        (struct((groups, seq, triple), BF16), nth((groups, seq, triple))),
    ]
    return call(
        functools.partial(project_kernel, len(parts), triple),
        "project",
        groups,
        [(a, whole(a.shape)) for a in parts]
        + [
            (gain, whole(gain.shape)),
            (shift, whole(shift.shape)),
            (weight, pl.BlockSpec((1, width, lanes(triple)), lambda i, *_: (i, 0, 0))),
            (bias, nth(bias.shape)),
        ],
        outs,
        2 * groups * seq * width * triple,
        prefetch=(spot,),
    )


def mix_kernel(count, groups, place_ref, image_ref, parts_ref, bias_ref, gain_ref, shift_ref, *refs):
    pieces = refs[:count]
    hidden_ref, ready_ref, turned_ref, weight_ref, joined, blocks = refs[count:]
    part = parts_ref.shape[2]
    join_columns(place_ref, groups, parts_ref, joined)
    for k in range(groups):
        join_rows(place_ref, pieces, blocks, k * part, (k + 1) * part, k)
    weight_ref[...] = flat(blocks)
    for low, high in blocks_of(image_ref.shape[0], ROWS):
        mixed = contract(joined[low:high], weight_ref[...], 1, 1) + bias_ref[...]
        hidden = image_ref[low:high].astype(F32) + mixed
        hidden_ref[low:high] = hidden
        normed, _ = norm(hidden)
        ready_ref[low:high] = (normed * gain_ref[...] + shift_ref[...]).astype(BF16)
    turned(ready_ref[...], turned_ref)


def mix(spot, image, parts, bias, gain, shift, pieces, blocks):
    seq, width = image.shape
    groups, _, part = parts.shape
    inner = groups * part
    size = lanes(part)
    spec = pl.BlockSpec(
        (groups, pieces[0].shape[1], size), lambda i, *_: (0, 0, pieces[0].shape[2] // size - 1)
    )
    outs = [
        struct((seq, width), F32),
        struct((seq, width), BF16),
        struct((blocks, width // blocks, seq), BF16),
        struct((width, inner), BF16),
    ]
    return call(
        functools.partial(mix_kernel, len(pieces), groups),
        "mix",
        1,
        [(a, whole(a.shape)) for a in (image, parts, bias, gain, shift)]
        + [(a, spec) for a in pieces],
        [(o, whole(o.shape)) for o in outs],
        2 * seq * width * inner,
        [pltpu.VMEM((seq, inner), BF16), pltpu.VMEM((blocks, width // blocks, inner), BF16)],
        (spot,),
    )


def expand_kernel(count, place_ref, ready_ref, bias_ref, *refs):
    pieces = refs[:count]
    active_ref, slope_ref, weight = refs[count:]
    bend = 0.7978845608028654
    cubic = 0.044715
    join_rows(place_ref, pieces, weight, 0, weight.shape[2])
    for low, high in blocks_of(active_ref.shape[2], COLS):
        right = weight[:, :, low:high].reshape(-1, high - low)
        first = contract(ready_ref[...], right, 1, 0) + bias_ref[0, :, low:high]
        square = first * first
        bent = jnp.tanh(bend * (first + cubic * (first * square)))
        half = 0.5 * (1.0 + bent)
        active_ref[0, :, low:high] = (first * half).astype(BF16)
        slope_ref[0, :, low:high] = half + (0.5 * bend) * first * (1.0 - bent * bent) * (
            1.0 + (3.0 * cubic) * square
        )


def near_piece(piece, size):
    return pl.BlockSpec((1, piece.shape[1], size), lambda i, *_: (i, 0, 0))


def ordered(groups, shape):
    zeros = (0,) * (len(shape) - 1)
    return pl.BlockSpec(
        (1,) + tuple(shape[1:]), lambda i, spot: (order_of(spot, groups, i),) + zeros
    )


def expand(spot, ready, bias, pieces, blocks):
    seq, width = ready.shape
    groups, _, cols = bias.shape
    shape = (groups, seq, cols)
    size = lanes(cols)
    return call(
        functools.partial(expand_kernel, len(pieces)),
        "expand",
        groups,
        [(ready, whole(ready.shape)), (bias, ordered(groups, bias.shape))]
        + [(a, near_piece(a, size)) for a in pieces],
        [(struct(shape, BF16), ordered(groups, shape)), (struct(shape, F32), ordered(groups, shape))],
        2 * groups * seq * width * cols,
        [pltpu.VMEM((blocks, width // blocks, size), BF16)],
        (spot,),
    )


def narrow_kernel(place_ref, hidden_ref, active_ref, weight_ref, bias_ref, *rest):
    parts = rest[:-2]
    total, blocks = rest[-2:]
    step = pl.program_id(0)
    term = contract(active_ref[0], weight_ref[0, :, : active_ref.shape[2]], 1, 1)

    @pl.when(step == 0)
    def _():
        total[...] = hidden_ref[...] + bias_ref[...] + term

    @pl.when(step > 0)
    def _():
        total[...] += term

    @pl.when(step == pl.num_programs(0) - 1)
    def _():
        split_parts(place_ref, total[...].astype(BF16), parts, blocks)


def narrow(spot, hidden, active, weight, bias, count):
    seq, width = hidden.shape
    groups, _, cols = active.shape
    shape = (width // count, seq)
    return call(
        narrow_kernel,
        "narrow",
        groups,
        [
            (hidden, whole(hidden.shape)),
            (active, nth(active.shape)),
            (weight, nth(weight.shape)),
            (bias, whole(bias.shape)),
        ],
        [(struct(shape, BF16), whole(shape))] * count,
        2 * groups * seq * width * cols,
        [pltpu.VMEM((seq, width), F32), pltpu.VMEM((count, width // count, seq), BF16)],
        (spot,),
    )


def feed_back_kernel(count, place_ref, grad_ref, hidden_ref, gain_ref, slope_ref, second_ref, *refs):
    pieces = refs[:count]
    (
        first_grad_ref,
        first_sum_ref,
        hidden_grad_ref,
        low_ref,
        turned_ref,
        gain_sum_ref,
        shift_sum_ref,
        low_sum_ref,
        total,
        weight,
    ) = refs[count:]
    step = pl.program_id(0)
    join_rows(place_ref, pieces, weight, 0, weight.shape[2])
    for low, high in blocks_of(slope_ref.shape[2], COLS):
        active_grad = contract(grad_ref[...], second_ref[0, :, low:high], 1, 0)
        first_grad = (active_grad * slope_ref[0, :, low:high]).astype(BF16)
        first_grad_ref[0, :, low:high] = first_grad
        first_sum_ref[0, :, low:high] = jnp.sum(first_grad.astype(F32), axis=0, keepdims=True)
    right = flat(weight)[:, : slope_ref.shape[2]]
    term = contract(first_grad_ref[0], right, 1, 1)

    @pl.when(step == 0)
    def _():
        total[...] = term

    @pl.when(step > 0)
    def _():
        total[...] += term

    @pl.when(step == pl.num_programs(0) - 1)
    def _():
        gain_sum = jnp.zeros(gain_sum_ref.shape, F32)
        shift_sum = jnp.zeros(gain_sum_ref.shape, F32)
        low_sum = jnp.zeros(gain_sum_ref.shape, F32)
        for low, high in blocks_of(total.shape[0], ROWS):
            normed, inverse = norm(hidden_ref[low:high])
            ready_grad = total[low:high]
            gain_sum += jnp.sum(ready_grad * normed, axis=0, keepdims=True)
            shift_sum += jnp.sum(ready_grad, axis=0, keepdims=True)
            hidden_grad = grad_ref[low:high].astype(F32) + norm_back(
                ready_grad, normed, inverse, gain_ref[...]
            )
            hidden_grad_ref[low:high] = hidden_grad
            rounded = hidden_grad.astype(BF16)
            low_ref[low:high] = rounded
            low_sum += jnp.sum(rounded.astype(F32), axis=0, keepdims=True)
        gain_sum_ref[...] = gain_sum
        shift_sum_ref[...] = shift_sum
        low_sum_ref[...] = low_sum
        turned(low_ref[...], turned_ref)


def feed_back(spot, grad, hidden, gain, slope, second, pieces, blocks):
    seq, width = hidden.shape
    groups, _, cols = slope.shape
    size = lanes(cols)
    row = struct((1, width), F32)
    outs = [
        (struct(slope.shape, BF16), ordered(groups, slope.shape)),
        (struct((groups, 1, cols), F32), ordered(groups, (groups, 1, cols))),
    ] + [
        (o, whole(o.shape))
        for o in (
            struct((seq, width), F32),
            struct((seq, width), BF16),
            struct((blocks, width // blocks, seq), BF16),
            row,
            row,
            row,
        )
    ]
    return call(
        functools.partial(feed_back_kernel, len(pieces)),
        "feed_back",
        groups,
        [
            (grad, whole(grad.shape)),
            (hidden, whole(hidden.shape)),
            (gain, whole(gain.shape)),
            (slope, ordered(groups, slope.shape)),
            (second, ordered(groups, second.shape)),
        ]
        + [(a, near_piece(a, size)) for a in pieces],
        outs,
        4 * groups * seq * width * cols,
        [pltpu.VMEM((seq, width), F32), pltpu.VMEM((blocks, width // blocks, size), BF16)],
        (spot,),
    )


def mix_back_kernel(groups, place_ref, grad_ref, weight_ref, out_ref):
    part = out_ref.shape[2]
    full = contract(grad_ref[...], weight_ref[...], 1, 0).astype(BF16)
    for k in range(groups):
        out_ref[order_of(place_ref, groups, k)] = full[:, k * part : (k + 1) * part]


def mix_back(spot, grad, weight, groups):
    seq, width = grad.shape
    shape = (groups, seq, weight.shape[1] // groups)
    return call(
        functools.partial(mix_back_kernel, groups),
        "mix_back",
        1,
        [(grad, whole(grad.shape)), (weight, whole(weight.shape))],
        [(struct(shape, BF16), whole(shape))],
        2 * seq * width * weight.shape[1],
        prefetch=(spot,),
    )[0]


def project_back_kernel(
    place_ref, image_ref, gain_ref, hidden_grad_ref, near_ref, far_ref, weight_ref, *rest
):
    parts = rest[:-5]
    gain_sum_ref, shift_sum_ref, total, joined, blocks = rest[-5:]
    step = pl.program_id(0)
    near = near_ref.shape[2] // 3
    far = far_ref.shape[2] // 3
    for i in range(3):
        start = i * (near + far)
        joined[:, start : start + near] = near_ref[0, :, i * near : (i + 1) * near]
        joined[:, start + near : start + near + far] = far_ref[0, :, i * far : (i + 1) * far]
    term = contract(joined[...], weight_ref[0, :, : joined.shape[1]], 1, 1)

    @pl.when(step == 0)
    def _():
        total[...] = term

    @pl.when(step > 0)
    def _():
        total[...] += term

    @pl.when(step == pl.num_programs(0) - 1)
    def _():
        gain_sum = jnp.zeros(gain_sum_ref.shape, F32)
        shift_sum = jnp.zeros(gain_sum_ref.shape, F32)
        for low, high in blocks_of(total.shape[0], ROWS):
            normed, inverse = norm(image_ref[low:high].astype(F32))
            ready_grad = total[low:high]
            gain_sum += jnp.sum(ready_grad * normed, axis=0, keepdims=True)
            shift_sum += jnp.sum(ready_grad, axis=0, keepdims=True)
            result = hidden_grad_ref[low:high] + norm_back(
                ready_grad, normed, inverse, gain_ref[...]
            )
            total[low:high] = result
        gain_sum_ref[...] = gain_sum
        shift_sum_ref[...] = shift_sum
        split_parts(place_ref, total[...].astype(BF16), parts, blocks)


def project_back(spot, image, gain, hidden_grad, near, far, weight, count):
    seq, width = image.shape
    groups = near.shape[0]
    triple = near.shape[2] + far.shape[2]
    shape = (width // count, seq)
    row = struct((1, width), F32)
    return call(
        project_back_kernel,
        "project_back",
        groups,
        [
            (image, whole(image.shape)),
            (gain, whole(gain.shape)),
            (hidden_grad, whole(hidden_grad.shape)),
            (near, nth(near.shape)),
            (far, nth(far.shape)),
            (weight, pl.BlockSpec((1, width, lanes(triple)), lambda i, *_: (i, 0, 0))),
        ],
        [(struct(shape, BF16), whole(shape))] * count
        + [(row, whole(row.shape)), (row, whole(row.shape))],
        2 * groups * seq * width * triple,
        [
            pltpu.VMEM((seq, width), F32),
            pltpu.VMEM((seq, triple), BF16),
            pltpu.VMEM((count, width // count, seq), BF16),
        ],
        (spot,),
    )


def share_kernel(half, added, pick_ref, turned_ref, right_ref, *rest):
    rows = turned_ref.shape[1]
    picked = rest[-1]
    count = picked.shape[0] // rows

    @pl.when(pl.program_id(0) == 0)
    def _():
        for i in range(count):
            picked[i * rows : (i + 1) * rows] = turned_ref[pick_ref[half * count + i]]

    product = contract(picked[...], right_ref[0], 1, 0)
    received = rest[:count] if added else ()
    outs = rest[len(received) : -1]
    for i in range(count):
        piece = product[i * rows : (i + 1) * rows]
        if added:
            piece = piece + received[i][0].astype(F32)
        if len(outs) == count:
            outs[i][0] = piece.astype(BF16)
        else:
            outs[i // 2][i % 2, 0] = piece.astype(BF16)


def share(pick, turned_rows, right, received=()):
    total, rows, seq = turned_rows.shape
    groups, _, cols = right.shape
    count = total // 2
    one = (struct((groups, rows, cols), BF16), nth((groups, rows, cols)))
    two = (
        struct((2, groups, rows, cols), BF16),
        pl.BlockSpec((2, 1, rows, cols), lambda i, *_: (0, i, 0, 0)),
    )
    return call(
        functools.partial(share_kernel, 0 if received else 1, bool(received)),
        "share",
        groups,
        [(turned_rows, whole(turned_rows.shape)), (right, nth(right.shape))]
        + [(a, nth(a.shape)) for a in received],
        [two] * (count // 2) if received else [one] * count,
        2 * groups * count * rows * seq * cols,
        [pltpu.VMEM((count * rows, seq), BF16)],
        (pick,),
    )


def swap(array, axis, bit):
    size = lax.axis_size(axis)
    return lax.ppermute(array, axis, [(i, i ^ bit) for i in range(size)])


def everyone(array):
    for axis in ("gx", "dp", "gy"):
        terms = [array] + [swap(array, axis, k) for k in range(1, lax.axis_size(axis))]
        while len(terms) > 1:
            terms = [a + b for a, b in zip(terms[::2], terms[1::2], strict=True)]
        array = terms[0]
    return array


class Sums:
    def __init__(self, line, pick, turned_rows, halves, half_first, ring=False):
        self.line = line
        self.pick = pick[half_first]
        self.rows = turned_rows
        self.halves = halves
        self.ring = ring
        steps = [("dp", 1), ("gx", 2)] if half_first else [("gx", 2), ("dp", 1)]
        self.steps = steps if halves == 2 else [None, ("gx", 2)]

    def away(self, right):
        self.right = right
        sent = self.line(lambda a: share(self.pick, a, right), self.rows)
        self.arrived = [swap(a, "gx", 1) for a in sent]

    def keep(self):
        kept = self.line(
            lambda a: share(self.pick, a, self.right, self.arrived), self.rows
        )
        self.kept = kept[0]
        if self.halves == 2:
            self.arrived = swap(kept[1], *self.steps[0])

    def mine(self, i, kept):
        value = kept[i].astype(F32)
        return value + self.arrived[i].astype(F32) if self.halves == 2 else value

    def send(self):
        sent = self.line(lambda a: self.mine(1, a).astype(BF16), self.kept)
        self.second = swap(sent, *self.steps[1])

    def total(self):
        total = self.line(
            lambda a: (self.mine(0, a) + self.second.astype(F32)).astype(BF16), self.kept
        )
        groups, rows, cols = total.shape
        if not self.ring:
            self.own = lax.psum_scatter(
                total.reshape(groups * rows, cols), "gy", scatter_dimension=0, tiled=True
            )
            return
        me = lax.axis_index("gy")
        up = [(i, (i + 1) % groups) for i in range(groups)]
        block = lambda k: lax.dynamic_index_in_dim(total, (me + groups - k) % groups, 0, False)
        running = block(1)
        for k in range(2, groups + 1):
            running = lax.ppermute(running, "gy", up)
            running = (running.astype(F32) + block(k % groups).astype(F32)).astype(BF16)
        self.own = running

    def trade(self):
        if self.halves == 2:
            self.own = self.line(lambda a: a, self.own)
            self.other = swap(self.own, "dp", 1)

    def end(self):
        if self.halves == 1:
            return lax.psum(self.own.astype(F32), "dp")
        other = self.other
        first = lax.axis_index("dp") == 0
        return jnp.concatenate(
            [jnp.where(first, self.own, other), jnp.where(first, other, self.own)], axis=0
        ).astype(F32)


class Line:
    def __init__(self):
        self.last = None

    def __call__(self, step, first):
        if self.last is not None:
            first = after(first, self.last)
        result = step(first)
        self.last = jax.tree.leaves(result)[0]
        return result


def after(value, *others):
    return lax.optimization_barrier((value,) + others)[0]


def traded(parts):
    return [part if r == 0 else swap(part, "gx", r) for r, part in enumerate(parts)]


class Pieces:
    def __init__(self, first, mixed, halves):
        rows = first.shape[0] // halves
        size = lanes(mixed.shape[1])
        start = -(-first.shape[1] // size) * size
        both = jnp.concatenate(
            [
                jnp.pad(first, ((0, 0), (0, start - first.shape[1]))),
                jnp.pad(mixed, ((0, 0), (0, size - mixed.shape[1]))),
            ],
            axis=1,
        )
        if halves == 2:
            both = lax.dynamic_slice_in_dim(both, lax.axis_index("dp") * rows, rows, 0)
        count = lax.axis_size("gy")
        up = [(i, (i + 1) % count) for i in range(count)]
        groups = [both]
        for _ in range(count - 1):
            groups.append(lax.ppermute(groups[-1], "gy", up))
        own = jnp.stack(groups)
        self.halves = halves
        self.near = [own, swap(own, "gx", 2)]
        if halves == 2:
            self.near.append(swap(own, "dp", 1))

    def middle(self, anchor):
        near = [after(piece, anchor) for piece in self.near]
        if self.halves == 2:
            self.near.append(swap(near[1], "dp", 1))
        self.far = [swap(piece, "gx", 1) for piece in near]

    def last(self, anchor):
        if self.halves == 2:
            self.far.append(swap(after(self.near[3], anchor), "gx", 1))
        return self.near + self.far


def lanes(cols):
    return -(-cols // 128) * 128


def collect(block, order):
    return lax.all_gather(block, order, axis=0, tiled=True)


def on_device(
    tokens,
    cotangent,
    ln1_gain,
    ln1_bias,
    qkv_weight,
    qv_bias,
    out_weight,
    out_bias,
    ln2_gain,
    ln2_bias,
    fc1_weight,
    fc1_bias,
    fc2_weight,
    fc2_bias,
):
    gx = lax.axis_size("gx")
    gy = lax.axis_size("gy")
    halves = 2 if lax.axis_size("dp") == 2 else 1
    blocks = gx * halves
    shape = tokens.shape
    turned_shape = (shape[0], shape[2], shape[1])
    part = shape[2]
    head_cols = qkv_weight.shape[2]
    heads = head_cols // HEAD_DIM
    triple = 3 * head_cols
    hidden_cols = fc1_weight.shape[1]
    width = part * gx
    copies = gx // (MICRO * shape[1] // SEQ)
    along = ("gy", "gx")

    column = lax.axis_index("gx")
    half = lax.axis_index("dp")

    def block(core, side, far):
        return (column ^ (2 * far + core)) * halves + (half ^ side if halves == 2 else 0)

    bits = range(halves)
    pick = {
        True: jnp.stack([block(c, s, f) for c in range(2) for s in bits for f in range(2)]),
        False: jnp.stack([block(c, s, f) for c in range(2) for f in range(2) for s in bits]),
    }
    here = lax.axis_index("gy")
    spot = jnp.concatenate(
        [
            jnp.reshape(column, (1,)),
            pick[True],
            (here + gy - jnp.arange(gy, dtype=jnp.int32)) % gy,
        ]
    ).astype(jnp.int32)
    line = Line()

    wide = jnp.stack([ln1_gain, ln1_bias, out_bias, ln2_gain, ln2_bias, fc2_bias], axis=1)
    deep = jnp.concatenate([qv_bias[0], qv_bias[1], fc1_bias])
    deep_cols = -(-deep.shape[0] // part)
    deep = jnp.pad(deep, (0, deep_cols * part - deep.shape[0])).reshape(deep_cols, part).T
    early = jnp.concatenate([qkv_weight.reshape(part, triple), wide, deep], axis=1)
    early_cols = lanes(early.shape[1])
    early = jnp.pad(early, ((0, 0), (0, early_cols - early.shape[1])))
    early = collect(early, along).reshape(gy, width, early_cols)
    second = jnp.pad(fc2_weight.T, ((0, 0), (0, lanes(hidden_cols) - hidden_cols)))
    second = collect(second, along).reshape(gy, width, lanes(hidden_cols))
    token_parts = cut(spot, jnp.swapaxes(tokens, 1, 2), gx, copies)
    gathered = Pieces(after(fc1_weight, token_parts[0]), out_weight.T, halves)
    token_parts = traded(token_parts)

    wide = early[0, :, triple : triple + 6].T.astype(F32)
    gain_one, shift_one, bias_mix, gain_two, shift_two, bias_second = [
        wide[i : i + 1] for i in range(6)
    ]
    deep = early[:, :part, triple + 6 : triple + 6 + deep_cols].astype(F32)
    deep = jnp.swapaxes(deep, 1, 2).reshape(gy, 1, deep_cols * part)
    bias_qkv = jnp.concatenate(
        [
            deep[:, :, :head_cols],
            jnp.zeros((gy, 1, head_cols), F32),
            deep[:, :, head_cols : 2 * head_cols],
        ],
        axis=2,
    )
    bias_first = deep[:, :, 2 * head_cols : 2 * head_cols + hidden_cols]

    image, ready_one, turned_one, packed = line(
        lambda a: project(spot, [a] + token_parts[1:], gain_one, shift_one, early, bias_qkv, blocks),
        token_parts[0],
    )
    grad_parts = line(lambda a: cut(spot, a, gx, copies), jnp.swapaxes(cotangent, 1, 2))
    grad_parts = traded(grad_parts)
    gathered.middle(packed)
    mixture, log_total = line(lambda a: attend(a, heads), packed)
    pieces = gathered.last(mixture)
    log_total = jnp.swapaxes(log_total, 1, 2)
    grad_low, grad_turned, grad_sum = line(
        lambda a: spread(spot, [a] + grad_parts[1:], blocks), grad_parts[0]
    )
    hidden, ready_two, turned_two, whole_out = line(
        lambda a: mix(spot, a, mixture, bias_mix, gain_two, shift_two, pieces, blocks), image
    )
    active, slope = line(lambda a: expand(spot, a, bias_first, pieces, blocks), ready_two)

    near = max(1, NEAR * heads // 4)
    fc2 = Sums(line, pick, grad_turned, halves, True)
    fc1 = Sums(line, pick, turned_two, halves, True)
    fc2.away(active)
    out_parts = line(lambda a: narrow(spot, a, active, second, bias_second, gx), hidden)
    out_parts = traded(out_parts)
    fc2.keep()
    (
        grad_first,
        first_sum,
        grad_hidden,
        grad_hidden_low,
        turned_hidden,
        gain_two_sum,
        shift_two_sum,
        low_sum,
    ) = line(
        lambda a: feed_back(spot, a, hidden, gain_two, slope, second, pieces, blocks), grad_low
    )
    out = Sums(line, pick, turned_hidden, halves, False)
    first_heads = Sums(line, pick, turned_one, halves, True)
    last_heads = Sums(line, pick, turned_one, halves, True, RING)
    fc1.away(grad_first)
    grad_mixture = line(lambda a: mix_back(spot, a, whole_out, gy), grad_hidden_low)
    fc1.keep()
    fc2.send()
    near_grad, near_sum = line(
        lambda a: attend_back(a, log_total, grad_mixture, heads, list(range(near))), packed
    )
    out.away(mixture)
    first_heads.away(near_grad)
    fc2.total()
    out.keep()
    first_heads.keep()
    fc1.send()
    fed_sums = everyone(
        line(
            lambda a: jnp.concatenate(
                [b.reshape(-1) for b in (a, gain_two_sum, shift_two_sum, grad_sum, first_sum)]
            ),
            low_sum,
        )
    )
    far_grad, far_sum = line(
        lambda a: attend_back(a, log_total, grad_mixture, heads, list(range(near, heads))), packed
    )
    out.send()
    last_heads.away(far_grad)
    first_heads.send()
    out.total()
    fc1.total()
    last_heads.keep()
    fc2.trade()
    first_heads.total()
    *grad_parts, gain_one_sum, shift_one_sum = line(
        lambda a: project_back(spot, a, gain_one, grad_hidden, near_grad, far_grad, early, gx), image
    )
    last_heads.send()
    grad_parts = traded(grad_parts)
    out.trade()
    fc1.trade()
    layer_out = line(
        lambda a: place(spot, [a] + out_parts[1:], turned_shape, copies), out_parts[0]
    )
    last_heads.total()
    first_heads.trade()
    tokens_grad = line(
        lambda a: place(spot, [a] + grad_parts[1:], turned_shape, copies), grad_parts[0]
    )
    last_heads.trade()
    grad_fc2 = fc2.end().T
    grad_fc1 = fc1.end()
    grad_out_weight = out.end().T
    grad_near = first_heads.end().reshape(part, 3, near * HEAD_DIM)
    grad_far = last_heads.end().reshape(part, 3, (heads - near) * HEAD_DIM)
    grad_qkv = jnp.concatenate([grad_near, grad_far], axis=2)

    near_sum = near_sum.reshape(gy, 3, near * HEAD_DIM)
    far_sum = far_sum.reshape(gy, 3, (heads - near) * HEAD_DIM)
    packed_sum = jnp.concatenate([near_sum, far_sum], axis=2)
    late_sums = everyone(
        jnp.concatenate(
            [a.reshape(-1) for a in (gain_one_sum, shift_one_sum, packed_sum[:, 0], packed_sum[:, 2])]
        )
    )
    wide_sums = jnp.concatenate([late_sums[: 2 * width], fed_sums[: 4 * width]]).reshape(6, width)
    wide_sums = lax.dynamic_slice_in_dim(wide_sums, column * part, part, 1)
    qv_sums = late_sums[2 * width :].reshape(2, gy, head_cols)
    qv_sums = lax.dynamic_index_in_dim(qv_sums, here, 1, False)
    first_sums = fed_sums[4 * width :].reshape(gy, hidden_cols)
    first_sums = lax.dynamic_index_in_dim(first_sums, here, 0, False)
    grads = (
        wide_sums[0],
        wide_sums[1],
        grad_qkv,
        qv_sums,
        grad_out_weight,
        wide_sums[2],
        wide_sums[3],
        wide_sums[4],
        grad_fc1,
        first_sums,
        grad_fc2,
        wide_sums[5],
    )
    if copies > 1:
        grads = tuple(grad * (1.0 / copies) for grad in grads)
    return (jnp.swapaxes(layer_out, 1, 2), jnp.swapaxes(tokens_grad, 1, 2)) + grads


def solution(mesh):
    specs = (
        P(None, ("dp", "gy"), "gx"),
        P(None, ("dp", "gy"), "gx"),
        P("gx"),
        P("gx"),
        P("gx", None, "gy"),
        P(None, "gy"),
        P("gy", "gx"),
        P("gx"),
        P("gx"),
        P("gx"),
        P("gx", "gy"),
        P("gy"),
        P("gy", "gx"),
        P("gx"),
    )
    return jax.shard_map(
        on_device,
        mesh=mesh,
        in_specs=specs,
        out_specs=specs,
        check_vma=False,
    )
```

time: 834 us -> 626 us (0.75)
  waiting for transfers between devices: 345 us -> 158 us
  blocking collectives: 81.1 us -> 0 us
  Pallas kernels: 260 us -> 299 us
  starting transfers between devices: 24.4 us -> 57.1 us
  local copies, waits for them, and re-layouts: 78.5 us -> 50.6 us
  other arithmetic: 21.8 us -> 35.8 us
    all_gather x4 -> x2, waiting for transfers between devices: 140 us -> 33.3 us  [collect(): return lax.all_gather(block, order, axis=0, tiled=True)]
    ppermute x12 -> x68, waiting for transfers between devices: 155 us -> 72.4 us  [swap(): return lax.ppermute(array, axis, [(i, i ^ bit) for i in range(size)])]
    ppermute x0 -> x3, waiting for transfers between devices: none -> 52.2 us  [__init__(): groups.append(lax.ppermute(groups[-1], 'gy', up))]
    psum x1 -> x0, blocking collectives: 51.4 us -> none  [on_device(): wide_sums, deep_sums = lax.psum((wide_sums, deep_sums), ('dp', 'gx', 'gy'))]
    all_to_all x4 -> x0, waiting for transfers between devices: 48.5 us -> none  [the longest x2 48.5 us: images_here(): return lax.all_to_all(images, 'gx', split_axis=0, concat_axis=0, tiled=True)]
    pallas_call x18 -> x25, Pallas kernels: 260 us -> 299 us  [call(): pl.pallas_call(kernel, grid_spec=pltpu.PrefetchScalarGridSpec(num_scalar_...]
    ppermute x12 -> x68, starting transfers between devices: 8.13 us -> 47.3 us  [swap(): return lax.ppermute(array, axis, [(i, i ^ bit) for i in range(size)])]
    all_gather x4 -> x0, blocking collectives: 29.7 us -> none  [shares(): own = lax.all_gather(own, 'dp', axis=0, tiled=True).astype(F32)]
  transfers between devices with their start and end apart: 24 -> 78, of which waited for: 11 -> 26; matrix products, arithmetic and copies ran while one was open for 12% -> 11% of each run, Pallas kernels for 21% -> 47%
where the time goes in v3:
time: 626 us; the launch traced here: 616 us
  Pallas kernels  299 us (48%)
  waiting for transfers between devices  158 us (25%)
  starting transfers between devices  57.1 us (9%)
  local copies, waits for them, and re-layouts  50.6 us (8%)
  other arithmetic  35.8 us (6%)
  between operations  15.2 us (2%)
    pallas_call x25, Pallas kernels, call(): pl.pallas_call(kernel, grid_spec=pltpu.PrefetchScalarGridSpec(num_scalar_...  299 us
    ppermute x68, waiting for transfers between devices, swap(): return lax.ppermute(array, axis, [(i, i ^ bit) for i in range(size)])  72.4 us
    ppermute x3, waiting for transfers between devices, __init__(): groups.append(lax.ppermute(groups[-1], 'gy', up))  52.2 us
    ppermute x68, starting transfers between devices, swap(): return lax.ppermute(array, axis, [(i, i ^ bit) for i in range(size)])  47.3 us
    all_gather x2, waiting for transfers between devices, collect(): return lax.all_gather(block, order, axis=0, tiled=True)  33.3 us
    unnamed x67, local copies, waits for them, and re-layouts  14.3 us
  transfers between devices with their start and end apart: 78, of which 26 were waited for; matrix products, arithmetic and copies ran while one was open for 11% of the time, Pallas kernels for 47%

profile of v3, /device:TPU:0, one launch (start us, length us, event | category | flops | bytes accessed | tf_op | source)
XLA Modules:
  0.0 616.0 jit_solution(10823683701383545840)
XLA Ops:
  18.0 3.7 cut.2
  21.8 3.1 collective-permute-start.6
  24.8 18.2 %collective-permute-done.6 = bf16[144,1536]{1,0:T(8,128)(2,1)S(1)} collective-permute-done((bf16[144,1536]{1,0:T(8,128)(2,1)S(1)}, bf16[144,1536]{1,0:T(8,128)(2,1)S(1)}, u32[]{:S(2)}, u32[]{:S(2)}) %collective-permute-start.6) | collective-permute-done | bytes 442400 | tf_op jit(solution)/shard_map/ppermute | solution.py:816
  43.0 6.4 %collective-permute-start.7 = (bf16[144,1536]{1,0:T(8,128)(2,1)S(1)}, bf16[144,1536]{1,0:T(8,128)(2,1)S(1)}, u32[]{:S(2)}, u32[]{:S(2)}) collective-permute-start(bf16[144,1536]{1,0:T(8,128)(2,1)S(1)} %collective-permute-done.6), channel_id=1, source_target_pairs={{0,1},{1,2},{2,3},{3,0},{4,5},{5,6},{6,7},{7,4},{8,9},{9,10},{10,1... | collective-permute-start | bytes 1327112 | tf_op jit(solution)/shard_map/ppermute | solution.py:816
  49.5 13.7 %collective-permute-done.7 = bf16[144,1536]{1,0:T(8,128)(2,1)S(1)} collective-permute-done((bf16[144,1536]{1,0:T(8,128)(2,1)S(1)}, bf16[144,1536]{1,0:T(8,128)(2,1)S(1)}, u32[]{:S(2)}, u32[]{:S(2)}) %collective-permute-start.7) | collective-permute-done | bytes 442400 | tf_op jit(solution)/shard_map/ppermute | solution.py:816
  65.2 20.3 %collective-permute-done.8 = bf16[144,1536]{1,0:T(8,128)(2,1)S(1)} collective-permute-done((bf16[144,1536]{1,0:T(8,128)(2,1)S(1)}, bf16[144,1536]{1,0:T(8,128)(2,1)S(1)}, u32[]{:S(2)}, u32[]{:S(2)}) %collective-permute-start.8) | collective-permute-done | bytes 442400 | tf_op jit(solution)/shard_map/ppermute | solution.py:816
  88.6 33.3 %all-gather.3.cloned.1.call-done = bf16[4608,896]{1,0:T(8,128)(2,1)} async-done(((bf16[288,896]{1,0:T(8,128)(2,1)}), bf16[4608,896]{1,0:T(8,128)(2,1)}) %all-gather.3.cloned.1.call-update) | async-done | bytes 8257552 | tf_op jit(solution)/shard_map/all_gather | solution.py:840
  132.7 14.9 %project.1 = (bf16[729,1152]{1,0:T(8,128)(2,1)}, bf16[729,1152]{1,0:T(8,128)(2,1)}, bf16[8,144,729]{2,1,0:T(8,128)(2,1)}, bf16[4,729,864]{2,1,0:T(8,128)(2,1)}) custom-call(s32[13]{0:T(128)} %concatenate.59.place_ref, bf16[288,729]{1,0:T(8,128)(2,1)} %get-tuple-element.132.refs_0_, bf16[288,729]{1,0:T(8,128)(2,1)} %collective-permute-done.refs_1_, ...), custom_call_target="tpu_custom_call" | custom-call | flops 5804752896 | bytes 20037888 | tf_op jit(solution)/shard_map/project/pallas_call | solution.py:45
  147.6 2.8 collective-permute-done.9.refs_1_
  151.9 3.9 cut.3
  156.5 29.0 %attend.1 = (bf16[4,729,288]{2,1,0:T(8,128)(2,1)}, f32[4,729,4]{2,1,0:T(8,128)}) custom-call(bf16[4,729,864]{2,1,0:T(8,128)(2,1)} %get-tuple-element.211.packed_ref), custom_call_target="tpu_custom_call" | custom-call | flops 7346640384 | bytes 6765120 | tf_op jit(solution)/shard_map/attend/pallas_call | solution.py:45
  185.5 5.7 collective-permute-done.11.refs_3_
  191.7 4.2 collective-permute-done.3.refs_1_
  196.2 12.0 %collective-permute-done.4.refs_2_ = bf16[288,729]{1,0:T(8,128)(2,1)} collective-permute-done((bf16[288,729]{1,0:T(8,128)(2,1)S(1)}, bf16[288,729]{1,0:T(8,128)(2,1)}, u32[]{:S(2)}, u32[]{:S(2)}) %collective-permute-start.4) | collective-permute-done | bytes 419936 | tf_op jit(solution)/shard_map/ppermute | solution.py:701
  213.8 6.7 %collective-permute-done.5.refs_3_ = bf16[288,729]{1,0:T(8,128)(2,1)} collective-permute-done((bf16[288,729]{1,0:T(8,128)(2,1)}, bf16[288,729]{1,0:T(8,128)(2,1)}, u32[]{:S(2)}, u32[]{:S(2)}) %collective-permute-start.5) | collective-permute-done | bytes 419936 | tf_op jit(solution)/shard_map/ppermute | solution.py:701
  220.5 3.9 spread.1
  224.5 11.6 %mix.1 = (f32[729,1152]{1,0:T(8,128)}, bf16[729,1152]{1,0:T(8,128)(2,1)}, bf16[8,144,729]{2,1,0:T(8,128)(2,1)}, bf16[1152,1152]{1,0:T(8,128)(2,1)}) custom-call(s32[13]{0:T(128)} %concatenate.59.place_ref, bf16[729,1152]{1,0:T(8,128)(2,1)} %get-tuple-element.228.image_ref, bf16[4,729,288]{2,1,0:T(8,128)(2,1)} %get-tuple-element.141.parts_ref.right_ref, ...), custom_call_target="tpu_custom_call" | custom-call | flops 1934917632 | bytes 26901504 | tf_op jit(solution)/shard_map/mix/pallas_call | solution.py:45
  236.1 21.3 %expand.1 = (bf16[4,729,1076]{2,1,0:T(8,128)(2,1)}, f32[4,729,1076]{2,1,0:T(8,128)}) custom-call(s32[13]{0:T(128)} %concatenate.59.place_ref, bf16[729,1152]{1,0:T(8,128)(2,1)} %get-tuple-element.156.ready_ref, f32[4,1,1076]{2,1,0:T(1,128)} %slice.200.bias_ref, bf16[4,144,1536]{2,1,0:T(8,128)(2,1)} %copy-done, ...), custom_call_target="tpu_custom_call" | custom-call | flops 7229067264 | bytes 34678304 | tf_op jit(solution)/shard_map/expand/pallas_call | solution.py:45
  257.4 9.7 %share.10 = (bf16[4,144,1076]{2,1,0:T(8,128)(2,1)}, bf16[4,144,1076]{2,1,0:T(8,128)(2,1)}, bf16[4,144,1076]{2,1,0:T(8,128)(2,1)}, bf16[4,144,1076]{2,1,0:T(8,128)(2,1)}) custom-call(s32[8]{0:T(128)} %stack.90.pick_ref, bf16[8,144,729]{2,1,0:T(8,128)(2,1)} %get-tuple-element.163.turned_ref, bf16[4,729,1076]{2,1,0:T(8,128)(2,1)} %get-tuple-element.157.right_ref.active_ref), custom_call_target="tpu_custom_call" | custom-call | flops 3614533632 | bytes 12913056 | tf_op jit(solution)/shard_map/share/pallas_call | solution.py:45
  268.9 17.6 %narrow.1 = (bf16[288,729]{1,0:T(8,128)(2,1)}, bf16[288,729]{1,0:T(8,128)(2,1)}, bf16[288,729]{1,0:T(8,128)(2,1)}, bf16[288,729]{1,0:T(8,128)(2,1)}) custom-call(s32[13]{0:T(128)} %concatenate.59.place_ref, f32[729,1152]{1,0:T(8,128)} %get-tuple-element.160.hidden_ref, bf16[4,729,1076]{2,1,0:T(8,128)(2,1)} %get-tuple-element.157.right_ref.active_ref, ...), custom_call_target="tpu_custom_call" | custom-call | flops 7229067264 | bytes 21935520 | tf_op jit(solution)/shard_map/narrow/pallas_call | solution.py:45
  288.0 10.9 %share.11 = (bf16[2,4,144,1076]{3,2,1,0:T(8,128)(2,1)}, bf16[2,4,144,1076]{3,2,1,0:T(8,128)(2,1)}) custom-call(s32[8]{0:T(128)} %stack.90.pick_ref, bf16[8,144,729]{2,1,0:T(8,128)(2,1)} %get-tuple-element.163.turned_ref, bf16[4,729,1076]{2,1,0:T(8,128)(2,1)} %get-tuple-element.157.right_ref.active_ref, ...), custom_call_target="tpu_custom_call" | custom-call | flops 3614533632 | bytes 17871264 | tf_op jit(solution)/shard_map/share/pallas_call | solution.py:45
  300.4 35.8 %feed_back.1 = (bf16[4,729,1076]{2,1,0:T(8,128)(2,1)}, f32[4,1,1076]{2,1,0:T(1,128)}, f32[729,1152]{1,0:T(8,128)}, bf16[729,1152]{1,0:T(8,128)(2,1)}, bf16[8,144...) custom-call(s32[13]{0:T(128)} %concatenate.59.place_ref, ...), custom_call_target="tpu_custom_call" | custom-call | flops 14458134528 | bytes 55391264 | tf_op jit(solution)/shard_map/feed_back/pallas_call | solution.py:45
  336.2 9.8 %share.12 = (bf16[4,144,1076]{2,1,0:T(8,128)(2,1)}, bf16[4,144,1076]{2,1,0:T(8,128)(2,1)}, bf16[4,144,1076]{2,1,0:T(8,128)(2,1)}, bf16[4,144,1076]{2,1,0:T(8,128)(2,1)}) custom-call(s32[8]{0:T(128)} %stack.90.pick_ref, bf16[8,144,729]{2,1,0:T(8,128)(2,1)} %get-tuple-element.176.turned_ref, bf16[4,729,1076]{2,1,0:T(8,128)(2,1)} %get-tuple-element.171.right_ref), custom_call_target="tpu_custom_call" | custom-call | flops 3614533632 | bytes 12913056 | tf_op jit(solution)/shard_map/share/pallas_call | solution.py:45
  348.7 7.1 %mix_back.1.grad_ref = bf16[4,729,288]{2,1,0:T(8,128)(2,1)} custom-call(s32[13]{0:T(128)} %concatenate.59.place_ref, bf16[729,1152]{1,0:T(8,128)(2,1)} %get-tuple-element.174.grad_ref, bf16[1152,1152]{1,0:T(8,128)(2,1)} %get-tuple-element.175.weight_ref), custom_call_target="tpu_custom_call" | custom-call | flops 1934917632 | bytes 6013440 | tf_op jit(solution)/shard_map/mix_back/pallas_call | solution.py:45
  355.9 11.3 %share.13 = (bf16[2,4,144,1076]{3,2,1,0:T(8,128)(2,1)}, bf16[2,4,144,1076]{3,2,1,0:T(8,128)(2,1)}) custom-call(s32[8]{0:T(128)} %stack.90.pick_ref, bf16[8,144,729]{2,1,0:T(8,128)(2,1)} %get-tuple-element.176.turned_ref, bf16[4,729,1076]{2,1,0:T(8,128)(2,1)} %get-tuple-element.171.right_ref, bf16[4,144,1076]{2,1,0:T(8,128)(2,1)} %collective-permute-done.20.rest_0_, ...), custom_call_target="tpu_custom_call" | custom-call | flops 3614533632 | bytes 17871264 | tf_op jit(solution)/shard_map/share/pallas_call | solution.py:45
  367.7 2.7 fusion.2
  370.9 20.4 %attend_back.2 = (bf16[4,729,432]{2,1,0:T(8,128)(2,1)}, f32[4,1,432]{2,1,0:T(1,128)}) custom-call(bf16[4,729,864]{2,1,0:T(8,128)(2,1)} %get-tuple-element.211.packed_ref, f32[4,4,729]{2,1,0:T(4,128)} %bitcast.102, bf16[4,729,288]{2,1,0:T(8,128)(2,1)} %mix_back.1.grad_ref), custom_call_target="tpu_custom_call" | custom-call | flops 9183300608 | bytes 9291456 | tf_op jit(solution)/shard_map/attend_back/pallas_call | solution.py:45
  391.3 6.3 %share.14 = (bf16[4,144,288]{2,1,0:T(8,128)(2,1)}, bf16[4,144,288]{2,1,0:T(8,128)(2,1)}, bf16[4,144,288]{2,1,0:T(8,128)(2,1)}, bf16[4,144,288]{2,1,0:T(8,128)(2,1)}) custom-call(s32[8]{0:T(128)} %stack.91.pick_ref, bf16[8,144,729]{2,1,0:T(8,128)(2,1)} %get-tuple-element.193.turned_ref, bf16[4,729,288]{2,1,0:T(8,128)(2,1)} %get-tuple-element.141.parts_ref.right_ref), custom_call_target="tpu_custom_call" | custom-call | flops 967458816 | bytes 4686336 | tf_op jit(solution)/shard_map/share/pallas_call | solution.py:45
  400.2 6.4 %share.15 = (bf16[4,144,432]{2,1,0:T(8,128)(2,1)}, bf16[4,144,432]{2,1,0:T(8,128)(2,1)}, bf16[4,144,432]{2,1,0:T(8,128)(2,1)}, bf16[4,144,432]{2,1,0:T(8,128)(2,1)}) custom-call(s32[8]{0:T(128)} %stack.90.pick_ref, bf16[8,144,729]{2,1,0:T(8,128)(2,1)} %get-tuple-element.221.turned_ref, bf16[4,729,432]{2,1,0:T(8,128)(2,1)} %get-tuple-element.187.right_ref.near_ref), custom_call_target="tpu_custom_call" | custom-call | flops 1451188224 | bytes 6189696 | tf_op jit(solution)/shard_map/share/pallas_call | solution.py:45
  407.6 3.3 fusion.1
  410.9 6.8 %share.16 = (bf16[2,4,144,288]{3,2,1,0:T(8,128)(2,1)}, bf16[2,4,144,288]{3,2,1,0:T(8,128)(2,1)}) custom-call(s32[8]{0:T(128)} %stack.91.pick_ref, bf16[8,144,729]{2,1,0:T(8,128)(2,1)} %get-tuple-element.193.turned_ref, bf16[4,729,288]{2,1,0:T(8,128)(2,1)} %get-tuple-element.141.parts_ref.right_ref, bf16[4,144,288]{2,1,0:T(8,128)(2,1)} %collective-permute-done.26.rest_0_, ...), custom_call_target="tpu_custom_call" | custom-call | flops 967458816 | bytes 6013440 | tf_op jit(solution)/shard_map/share/pallas_call | solution.py:45
  418.6 7.5 %share.17 = (bf16[2,4,144,432]{3,2,1,0:T(8,128)(2,1)}, bf16[2,4,144,432]{3,2,1,0:T(8,128)(2,1)}) custom-call(s32[8]{0:T(128)} %stack.90.pick_ref, bf16[8,144,729]{2,1,0:T(8,128)(2,1)} %get-tuple-element.221.turned_ref, bf16[4,729,432]{2,1,0:T(8,128)(2,1)} %get-tuple-element.187.right_ref.near_ref, bf16[4,144,432]{2,1,0:T(8,128)(2,1)} %copy-done.15, ...), custom_call_target="tpu_custom_call" | custom-call | flops 1451188224 | bytes 8180352 | tf_op jit(solution)/shard_map/share/pallas_call | solution.py:45
  429.1 2.7 fusion.3
  439.4 20.7 %attend_back.3 = (bf16[4,729,432]{2,1,0:T(8,128)(2,1)}, f32[4,1,432]{2,1,0:T(1,128)}) custom-call(bf16[4,729,864]{2,1,0:T(8,128)(2,1)} %get-tuple-element.211.packed_ref, f32[4,4,729]{2,1,0:T(4,128)} %bitcast.103, bf16[4,729,288]{2,1,0:T(8,128)(2,1)} %mix_back.1.grad_ref), custom_call_target="tpu_custom_call" | custom-call | flops 9183300608 | bytes 9291456 | tf_op jit(solution)/shard_map/attend_back/pallas_call | solution.py:45
  462.0 6.4 %share.18 = (bf16[4,144,432]{2,1,0:T(8,128)(2,1)}, bf16[4,144,432]{2,1,0:T(8,128)(2,1)}, bf16[4,144,432]{2,1,0:T(8,128)(2,1)}, bf16[4,144,432]{2,1,0:T(8,128)(2,1)}) custom-call(s32[8]{0:T(128)} %stack.90.pick_ref, bf16[8,144,729]{2,1,0:T(8,128)(2,1)} %get-tuple-element.221.turned_ref, bf16[4,729,432]{2,1,0:T(8,128)(2,1)} %get-tuple-element.212.right_ref.far_ref), custom_call_target="tpu_custom_call" | custom-call | flops 1451188224 | bytes 6189696 | tf_op jit(solution)/shard_map/share/pallas_call | solution.py:45
  468.5 2.2 fusion.9
  470.7 3.2 collective-permute-done.37
  476.8 3.3 fusion
  492.8 7.4 %share.19 = (bf16[2,4,144,432]{3,2,1,0:T(8,128)(2,1)}, bf16[2,4,144,432]{3,2,1,0:T(8,128)(2,1)}) custom-call(s32[8]{0:T(128)} %stack.90.pick_ref, bf16[8,144,729]{2,1,0:T(8,128)(2,1)} %get-tuple-element.221.turned_ref, bf16[4,729,432]{2,1,0:T(8,128)(2,1)} %get-tuple-element.212.right_ref.far_ref, bf16[4,144,432]{2,1,0:T(8,128)(2,1)} %copy-done.16, ...), custom_call_target="tpu_custom_call" | custom-call | flops 1451188224 | bytes 8180352 | tf_op jit(solution)/shard_map/share/pallas_call | solution.py:45
  502.6 2.4 fusion.5
  505.0 19.6 %project_back.1 = (bf16[288,729]{1,0:T(8,128)(2,1)}, bf16[288,729]{1,0:T(8,128)(2,1)}, bf16[288,729]{1,0:T(8,128)(2,1)}, bf16[288,729]{1,0:T(8,128)(2,1)}, f32[1,1152]{1,0:T(1,128)}, /*index=5*/f32[1,1152]{1,0:T(1,128)}) custom-call(s32[13]{0:T(128)} %concatenate.59.place_ref, bf16[729,1152]{1,0:T(8,128)(2,1)} %get-tuple-element.228.image_ref, ...), custom_call_target="tpu_custom_call" | custom-call | flops 5804752896 | bytes 20028672 | tf_op jit(solution)/shard_map/project_back/pallas_call | solution.py:45
  530.0 3.9 collective-permute-start.65
  545.2 2.6 collective-permute-start.56
  562.4 3.6 place.2
  566.0 6.6 %collective-permute-done.48 = bf16[4,144,432]{2,1,0:T(8,128)(2,1)S(1)} collective-permute-done((bf16[4,144,432]{2,1,0:T(8,128)(2,1)S(1)}, bf16[4,144,432]{2,1,0:T(8,128)(2,1)S(1)}, u32[]{:S(2)}, u32[]{:S(2)}) %collective-permute-start.48) | collective-permute-done | bytes 497696 | tf_op jit(solution)/shard_map/ppermute | solution.py:701
  582.2 10.2 %collective-permute-done.51.refs_3_ = bf16[288,729]{1,0:T(8,128)(2,1)S(1)} collective-permute-done((bf16[288,729]{1,0:T(8,128)(2,1)}, bf16[288,729]{1,0:T(8,128)(2,1)S(1)}, u32[]{:S(2)}, u32[]{:S(2)}) %collective-permute-start.51) | collective-permute-done | bytes 419936 | tf_op jit(solution)/shard_map/ppermute | solution.py:701
  593.2 3.6 place.3
  602.0 4.8 collective-permute-done.67
  (297 shorter events, 127.4 us)
Async XLA Ops:
  7.2 114.7 %all-gather.3.cloned.1.call-start = ((), (), s32[]{:S(2)}) async-start(), calls=%async_computation.5 | async-start | bytes 8773632 | tf_op jit(solution)/shard_map/all_gather | solution.py:840
  16.0 252.9 %all-gather.5.cloned.1.call-start = ((), (), s32[]{:S(2)}) async-start(), calls=%async_computation.6 | async-start | bytes 11280384 | tf_op jit(solution)/shard_map/all_gather | solution.py:840
  17.0 483.7 %reduce-scatter.14.cloned.1.call-start = ((), (), s32[]{:S(2)}) async-start(), calls=%async_computation.8 | async-start | bytes 1658880 | tf_op jit(solution)/shard_map/reduce_scatter | solution.py:750
  21.8 21.3 %collective-permute-start.6 = (bf16[144,1536]{1,0:T(8,128)(2,1)S(1)}, bf16[144,1536]{1,0:T(8,128)(2,1)S(1)}, u32[]{:S(2)}, u32[]{:S(2)}) collective-permute-start(bf16[144,1536]{1,0:T(8,128)(2,1)S(1)} %fusion.11), channel_id=1, source_target_pairs={{0,1},{1,2},{2,3},{3,0},{4,5},{5,6},{6,7},{7,4},{8,9},{9,10},{10,1... | collective-permute-start | bytes 1327112 | tf_op jit(solution)/shard_map/ppermute | solution.py:816
  43.0 20.2 %collective-permute-start.7 = (bf16[144,1536]{1,0:T(8,128)(2,1)S(1)}, bf16[144,1536]{1,0:T(8,128)(2,1)S(1)}, u32[]{:S(2)}, u32[]{:S(2)}) collective-permute-start(bf16[144,1536]{1,0:T(8,128)(2,1)S(1)} %collective-permute-done.6), channel_id=1, source_target_pairs={{0,1},{1,2},{2,3},{3,0},{4,5},{5,6},{6,7},{7,4},{8,9},{9,10},{10,1... | collective-permute-start | bytes 1327112 | tf_op jit(solution)/shard_map/ppermute | solution.py:816
  63.2 22.2 %collective-permute-start.8 = (bf16[144,1536]{1,0:T(8,128)(2,1)S(1)}, bf16[144,1536]{1,0:T(8,128)(2,1)S(1)}, u32[]{:S(2)}, u32[]{:S(2)}) collective-permute-start(bf16[144,1536]{1,0:T(8,128)(2,1)S(1)} %collective-permute-done.7), channel_id=1, source_target_pairs={{0,1},{1,2},{2,3},{3,0},{4,5},{5,6},{6,7},{7,4},{8,9},{9,10},{10,1... | collective-permute-start | bytes 1327112 | tf_op jit(solution)/shard_map/ppermute | solution.py:816
  63.2 69.4 %collective-permute-start = (bf16[288,729]{1,0:T(8,128)(2,1)}, bf16[288,729]{1,0:T(8,128)(2,1)}, u32[]{:S(2)}, u32[]{:S(2)}) collective-permute-start(bf16[288,729]{1,0:T(8,128)(2,1)} %get-tuple-element.133), channel_id=1, source_target_pairs={{0,4},{4,0},{8,12},{12,8},{1,5},{5,1},{9,13},{13,9},{2,6},{6,2},{1... | collective-permute-start | bytes 1259720 | tf_op jit(solution)/shard_map/ppermute | solution.py:701
  63.2 69.4 %collective-permute-start.1 = (bf16[288,729]{1,0:T(8,128)(2,1)}, bf16[288,729]{1,0:T(8,128)(2,1)}, u32[]{:S(2)}, u32[]{:S(2)}) collective-permute-start(bf16[288,729]{1,0:T(8,128)(2,1)} %get-tuple-element.134), channel_id=1, source_target_pairs={{0,8},{4,12},{8,0},{12,4},{1,9},{5,13},{9,1},{13,5},{2,10},{6,14},... | collective-permute-start | bytes 1259720 | tf_op jit(solution)/shard_map/ppermute | solution.py:701
  64.7 67.9 %collective-permute-start.2 = (bf16[288,729]{1,0:T(8,128)(2,1)}, bf16[288,729]{1,0:T(8,128)(2,1)}, u32[]{:S(2)}, u32[]{:S(2)}) collective-permute-start(bf16[288,729]{1,0:T(8,128)(2,1)} %get-tuple-element.135), channel_id=1, source_target_pairs={{0,12},{4,8},{8,4},{12,0},{1,13},{5,9},{9,5},{13,1},{2,14},{6,10},... | collective-permute-start | bytes 1259720 | tf_op jit(solution)/shard_map/ppermute | solution.py:701
  85.7 66.3 %collective-permute-start.10 = (bf16[4,144,1536]{2,1,0:T(8,128)(2,1)S(1)}, bf16[4,144,1536]{2,1,0:T(8,128)(2,1)}, u32[]{:S(2)}, u32[]{:S(2)}) collective-permute-start(bf16[4,144,1536]{2,1,0:T(8,128)(2,1)S(1)} %pad_maximum_fusion.refs_0_), channel_id=1, source_target_pairs={{0,16},{16,0},{1,17},{17,1},{2,18},{18,2},{3,19},{19,3},{4,20},{20... | collective-permute-start | bytes 5308424 | tf_op jit(solution)/shard_map/ppermute | solution.py:701
  87.3 63.2 %collective-permute-start.9 = (bf16[4,144,1536]{2,1,0:T(8,128)(2,1)S(1)}, bf16[4,144,1536]{2,1,0:T(8,128)(2,1)}, u32[]{:S(2)}, u32[]{:S(2)}) collective-permute-start(bf16[4,144,1536]{2,1,0:T(8,128)(2,1)S(1)} %pad_maximum_fusion.refs_0_), channel_id=1, source_target_pairs={{0,8},{4,12},{8,0},{12,4},{1,9},{5,13},{9,1},{13,5},{2,10},{6,14},... | collective-permute-start | bytes 5308424 | tf_op jit(solution)/shard_map/ppermute | solution.py:701
  150.4 40.8 %collective-permute-start.11 = (bf16[4,144,1536]{2,1,0:T(8,128)(2,1)}, bf16[4,144,1536]{2,1,0:T(8,128)(2,1)}, u32[]{:S(2)}, u32[]{:S(2)}) collective-permute-start(bf16[4,144,1536]{2,1,0:T(8,128)(2,1)} %collective-permute-done.9.refs_1_), channel_id=1, source_target_pairs={{0,16},{16,0},{1,17},{17,1},{2,18},{18,2},{3,19},{19,3},{4,20},{20... | collective-permute-start | bytes 5308424 | tf_op jit(solution)/shard_map/ppermute | solution.py:701
  151.9 72.5 %collective-permute-start.13 = (bf16[4,144,1536]{2,1,0:T(8,128)(2,1)}, bf16[4,144,1536]{2,1,0:T(8,128)(2,1)}, u32[]{:S(2)}, u32[]{:S(2)}) collective-permute-start(bf16[4,144,1536]{2,1,0:T(8,128)(2,1)} %collective-permute-done.9.refs_1_), channel_id=1, source_target_pairs={{0,4},{4,0},{8,12},{12,8},{1,5},{5,1},{9,13},{13,9},{2,6},{6,2},{1... | collective-permute-start | bytes 5308424 | tf_op jit(solution)/shard_map/ppermute | solution.py:701
  155.9 68.6 %collective-permute-start.12 = (bf16[4,144,1536]{2,1,0:T(8,128)(2,1)S(1)}, bf16[4,144,1536]{2,1,0:T(8,128)(2,1)}, u32[]{:S(2)}, u32[]{:S(2)}) collective-permute-start(bf16[4,144,1536]{2,1,0:T(8,128)(2,1)S(1)} %pad_maximum_fusion.refs_0_), channel_id=1, source_target_pairs={{0,4},{4,0},{8,12},{12,8},{1,5},{5,1},{9,13},{13,9},{2,6},{6,2},{1... | collective-permute-start | bytes 5308424 | tf_op jit(solution)/shard_map/ppermute | solution.py:701
  156.4 68.0 %collective-permute-start.14 = (bf16[4,144,1536]{2,1,0:T(8,128)(2,1)}, bf16[4,144,1536]{2,1,0:T(8,128)(2,1)}, u32[]{:S(2)}, u32[]{:S(2)}) collective-permute-start(bf16[4,144,1536]{2,1,0:T(8,128)(2,1)} %collective-permute-done.10.refs_2_), channel_id=1, source_target_pairs={{0,4},{4,0},{8,12},{12,8},{1,5},{5,1},{9,13},{13,9},{2,6},{6,2},{1... | collective-permute-start | bytes 5308424 | tf_op jit(solution)/shard_map/ppermute | solution.py:701
  191.2 33.2 %collective-permute-start.15 = (bf16[4,144,1536]{2,1,0:T(8,128)(2,1)}, bf16[4,144,1536]{2,1,0:T(8,128)(2,1)}, u32[]{:S(2)}, u32[]{:S(2)}) collective-permute-start(bf16[4,144,1536]{2,1,0:T(8,128)(2,1)} %collective-permute-done.11.refs_3_), channel_id=1, source_target_pairs={{0,4},{4,0},{8,12},{12,8},{1,5},{5,1},{9,13},{13,9},{2,6},{6,2},{1... | collective-permute-start | bytes 5308424 | tf_op jit(solution)/shard_map/ppermute | solution.py:701
  195.9 12.3 %collective-permute-start.4 = (bf16[288,729]{1,0:T(8,128)(2,1)S(1)}, bf16[288,729]{1,0:T(8,128)(2,1)}, u32[]{:S(2)}, u32[]{:S(2)}) collective-permute-start(bf16[288,729]{1,0:T(8,128)(2,1)S(1)} %copy-done.28), channel_id=1, source_target_pairs={{0,8},{4,12},{8,0},{12,4},{1,9},{5,13},{9,1},{13,5},{2,10},{6,14},... | collective-permute-start | bytes 1259720 | tf_op jit(solution)/shard_map/ppermute | solution.py:701
  208.2 12.3 %collective-permute-start.5 = (bf16[288,729]{1,0:T(8,128)(2,1)}, bf16[288,729]{1,0:T(8,128)(2,1)}, u32[]{:S(2)}, u32[]{:S(2)}) collective-permute-start(bf16[288,729]{1,0:T(8,128)(2,1)} %get-tuple-element.145), channel_id=1, source_target_pairs={{0,12},{4,8},{8,4},{12,0},{1,13},{5,9},{9,5},{13,1},{2,14},{6,10},... | collective-permute-start | bytes 1259720 | tf_op jit(solution)/shard_map/ppermute | solution.py:701
  267.1 19.5 %collective-permute-start.17 = (bf16[4,144,1076]{2,1,0:T(8,128)(2,1)}, bf16[4,144,1076]{2,1,0:T(8,128)(2,1)S(1)}, u32[]{:S(2)}, u32[]{:S(2)}) collective-permute-start(bf16[4,144,1076]{2,1,0:T(8,128)(2,1)} %get-tuple-element.164), channel_id=1, source_target_pairs={{0,4},{4,0},{8,12},{12,8},{1,5},{5,1},{9,13},{13,9},{2,6},{6,2},{1... | collective-permute-start | bytes 3718664 | tf_op jit(solution)/shard_map/ppermute | solution.py:701
  267.1 19.5 %collective-permute-start.18 = (bf16[4,144,1076]{2,1,0:T(8,128)(2,1)}, bf16[4,144,1076]{2,1,0:T(8,128)(2,1)S(1)}, u32[]{:S(2)}, u32[]{:S(2)}) collective-permute-start(bf16[4,144,1076]{2,1,0:T(8,128)(2,1)} %get-tuple-element.165), channel_id=1, source_target_pairs={{0,4},{4,0},{8,12},{12,8},{1,5},{5,1},{9,13},{13,9},{2,6},{6,2},{1... | collective-permute-start | bytes 3718664 | tf_op jit(solution)/shard_map/ppermute | solution.py:701
  267.6 19.0 %collective-permute-start.19 = (bf16[4,144,1076]{2,1,0:T(8,128)(2,1)}, bf16[4,144,1076]{2,1,0:T(8,128)(2,1)}, u32[]{:S(2)}, u32[]{:S(2)}) collective-permute-start(bf16[4,144,1076]{2,1,0:T(8,128)(2,1)} %get-tuple-element.166), channel_id=1, source_target_pairs={{0,4},{4,0},{8,12},{12,8},{1,5},{5,1},{9,13},{13,9},{2,6},{6,2},{1... | collective-permute-start | bytes 3718664 | tf_op jit(solution)/shard_map/ppermute | solution.py:701
  267.6 19.0 %collective-permute-start.16 = (bf16[4,144,1076]{2,1,0:T(8,128)(2,1)}, bf16[4,144,1076]{2,1,0:T(8,128)(2,1)}, u32[]{:S(2)}, u32[]{:S(2)}) collective-permute-start(bf16[4,144,1076]{2,1,0:T(8,128)(2,1)} %get-tuple-element.159), channel_id=1, source_target_pairs={{0,4},{4,0},{8,12},{12,8},{1,5},{5,1},{9,13},{13,9},{2,6},{6,2},{1... | collective-permute-start | bytes 3718664 | tf_op jit(solution)/shard_map/ppermute | solution.py:701
  298.9 68.7 %collective-permute-start.24 = (bf16[2,4,144,1076]{3,2,1,0:T(8,128)(2,1)}, bf16[2,4,144,1076]{3,2,1,0:T(8,128)(2,1)}, u32[]{:S(2)}, u32[]{:S(2)}) collective-permute-start(bf16[2,4,144,1076]{3,2,1,0:T(8,128)(2,1)} %get-tuple-element.184), channel_id=1, source_target_pairs={{0,16},{16,0},{1,17},{17,1},{2,18},{18,2},{3,19},{19,3},{4,20},{20... | collective-permute-start | bytes 7437320 | tf_op jit(solution)/shard_map/ppermute | solution.py:701
  367.1 62.0 %collective-permute-start.34 = (bf16[2,4,144,1076]{3,2,1,0:T(8,128)(2,1)}, bf16[2,4,144,1076]{3,2,1,0:T(8,128)(2,1)}, u32[]{:S(2)}, u32[]{:S(2)}) collective-permute-start(bf16[2,4,144,1076]{3,2,1,0:T(8,128)(2,1)} %get-tuple-element.205), channel_id=1, source_target_pairs={{0,16},{16,0},{1,17},{17,1},{2,18},{18,2},{3,19},{19,3},{4,20},{20... | collective-permute-start | bytes 7437320 | tf_op jit(solution)/shard_map/ppermute | solution.py:701
  370.4 37.1 %collective-permute-start.25 = (bf16[4,144,1076]{2,1,0:T(8,128)(2,1)}, bf16[4,144,1076]{2,1,0:T(8,128)(2,1)}, u32[]{:S(2)}, u32[]{:S(2)}) collective-permute-start(bf16[4,144,1076]{2,1,0:T(8,128)(2,1)} %fusion.2), channel_id=1, source_target_pairs={{0,8},{4,12},{8,0},{12,4},{1,9},{5,13},{9,1},{13,5},{2,10},{6,14},... | collective-permute-start | bytes 3718664 | tf_op jit(solution)/shard_map/ppermute | solution.py:701
  406.6 11.2 %collective-permute-start.30 = (bf16[4,144,432]{2,1,0:T(8,128)(2,1)}, bf16[4,144,432]{2,1,0:T(8,128)(2,1)S(1)}, u32[]{:S(2)}, u32[]{:S(2)}) collective-permute-start(bf16[4,144,432]{2,1,0:T(8,128)(2,1)} %get-tuple-element.191), channel_id=1, source_target_pairs={{0,4},{4,0},{8,12},{12,8},{1,5},{5,1},{9,13},{13,9},{2,6},{6,2},{1... | collective-permute-start | bytes 1493000 | tf_op jit(solution)/shard_map/ppermute | solution.py:701
  417.7 123.9 %reduce-scatter.16.cloned.1.call-start = ((), (), s32[]{:S(2)}) async-start(), calls=%async_computation.9 | async-start | bytes 552960
  426.1 34.0 %collective-permute-start.35 = (bf16[2,4,144,288]{3,2,1,0:T(8,128)(2,1)}, bf16[2,4,144,288]{3,2,1,0:T(8,128)(2,1)}, u32[]{:S(2)}, u32[]{:S(2)}) collective-permute-start(bf16[2,4,144,288]{3,2,1,0:T(8,128)(2,1)} %get-tuple-element.214), channel_id=1, source_target_pairs={{0,8},{4,12},{8,0},{12,4},{1,9},{5,13},{9,1},{13,5},{2,10},{6,14},... | collective-permute-start | bytes 1990664 | tf_op jit(solution)/shard_map/ppermute | solution.py:701
  427.6 40.9 %collective-permute-start.36 = (bf16[2,4,144,432]{3,2,1,0:T(8,128)(2,1)}, bf16[2,4,144,432]{3,2,1,0:T(8,128)(2,1)}, u32[]{:S(2)}, u32[]{:S(2)}) collective-permute-start(bf16[2,4,144,432]{3,2,1,0:T(8,128)(2,1)} %get-tuple-element.218), channel_id=1, source_target_pairs={{0,16},{16,0},{1,17},{17,1},{2,18},{18,2},{3,19},{19,3},{4,20},{20... | collective-permute-start | bytes 2985992 | tf_op jit(solution)/shard_map/ppermute | solution.py:701
  431.8 45.0 %collective-permute-start.38 = (bf16[4,144,1076]{2,1,0:T(8,128)(2,1)}, bf16[4,144,1076]{2,1,0:T(8,128)(2,1)}, u32[]{:S(2)}, u32[]{:S(2)}) collective-permute-start(bf16[4,144,1076]{2,1,0:T(8,128)(2,1)} %fusion.3), channel_id=1, source_target_pairs={{0,8},{4,12},{8,0},{12,4},{1,9},{5,13},{9,1},{13,5},{2,10},{6,14},... | collective-permute-start | bytes 3718664 | tf_op jit(solution)/shard_map/ppermute | solution.py:701
  462.0 11.9 %collective-permute-start.37 = (bf16[4,144,288]{2,1,0:T(8,128)(2,1)}, bf16[4,144,288]{2,1,0:T(8,128)(2,1)S(1)}, u32[]{:S(2)}, u32[]{:S(2)}) collective-permute-start(bf16[4,144,288]{2,1,0:T(8,128)(2,1)} %fusion.12), channel_id=1, source_target_pairs={{0,16},{16,0},{1,17},{17,1},{2,18},{18,2},{3,19},{19,3},{4,20},{20... | collective-permute-start | bytes 995336 | tf_op jit(solution)/shard_map/ppermute | solution.py:701
  475.9 82.9 %reduce-scatter.12.cloned.1.call-start = ((), (), s32[]{:S(2)}) async-start(), calls=%async_computation.7 | async-start | bytes 1658880 | tf_op jit(solution)/shard_map/reduce_scatter | solution.py:750
  480.1 98.2 %reduce-scatter.18.cloned.1.call-start = ((), (), s32[]{:S(2)}) async-start(), calls=%async_computation.10 | async-start | bytes 737280
  486.8 15.8 %collective-permute-start.43 = (bf16[4,144,432]{2,1,0:T(8,128)(2,1)}, bf16[4,144,432]{2,1,0:T(8,128)(2,1)}, u32[]{:S(2)}, u32[]{:S(2)}) collective-permute-start(bf16[4,144,432]{2,1,0:T(8,128)(2,1)} %fusion.9), channel_id=1, source_target_pairs={{0,8},{4,12},{8,0},{12,4},{1,9},{5,13},{9,1},{13,5},{2,10},{6,14},... | collective-permute-start | bytes 1493000 | tf_op jit(solution)/shard_map/ppermute | solution.py:701
  489.4 38.9 %collective-permute-start.62 = (f32[8912]{0:T(1024)}, f32[8912]{0:T(1024)}, u32[]{:S(2)}, u32[]{:S(2)}) collective-permute-start(f32[8912]{0:T(1024)} %add_add_fusion.1), channel_id=1, source_target_pairs={{0,16},{16,0},{1,17},{17,1},{2,18},{18,2},{3,19},{19,3},{4,20},{20... | collective-permute-start | bytes 106952 | tf_op jit(solution)/shard_map/ppermute | solution.py:701
  500.2 45.0 %collective-permute-start.44 = (bf16[2,4,144,432]{3,2,1,0:T(8,128)(2,1)}, bf16[2,4,144,432]{3,2,1,0:T(8,128)(2,1)S(1)}, u32[]{:S(2)}, u32[]{:S(2)}) collective-permute-start(bf16[2,4,144,432]{3,2,1,0:T(8,128)(2,1)} %get-tuple-element.232), channel_id=1, source_target_pairs={{0,16},{16,0},{1,17},{17,1},{2,18},{18,2},{3,19},{19,3},{4,20},{20... | collective-permute-start | bytes 2985992 | tf_op jit(solution)/shard_map/ppermute | solution.py:701
  528.3 30.4 %collective-permute-start.45 = (bf16[288,729]{1,0:T(8,128)(2,1)}, bf16[288,729]{1,0:T(8,128)(2,1)}, u32[]{:S(2)}, u32[]{:S(2)}) collective-permute-start(bf16[288,729]{1,0:T(8,128)(2,1)} %get-tuple-element.236), channel_id=1, source_target_pairs={{0,4},{4,0},{8,12},{12,8},{1,5},{5,1},{9,13},{13,9},{2,6},{6,2},{1... | collective-permute-start | bytes 1259720 | tf_op jit(solution)/shard_map/ppermute | solution.py:701
  535.9 24.3 %collective-permute-start.46 = (bf16[288,729]{1,0:T(8,128)(2,1)}, bf16[288,729]{1,0:T(8,128)(2,1)}, u32[]{:S(2)}, u32[]{:S(2)}) collective-permute-start(bf16[288,729]{1,0:T(8,128)(2,1)} %get-tuple-element.237), channel_id=1, source_target_pairs={{0,8},{4,12},{8,0},{12,4},{1,9},{5,13},{9,1},{13,5},{2,10},{6,14},... | collective-permute-start | bytes 1259720 | tf_op jit(solution)/shard_map/ppermute | solution.py:701
  543.3 55.9 %reduce-scatter.20.cloned.1.call-start = ((), (), s32[]{:S(2)}) async-start(), calls=%async_computation.11 | async-start | bytes 737280
  549.0 12.8 %collective-permute-start.47 = (bf16[288,729]{1,0:T(8,128)(2,1)}, bf16[288,729]{1,0:T(8,128)(2,1)}, u32[]{:S(2)}, u32[]{:S(2)}) collective-permute-start(bf16[288,729]{1,0:T(8,128)(2,1)} %get-tuple-element.238), channel_id=1, source_target_pairs={{0,12},{4,8},{8,4},{12,0},{1,13},{5,9},{9,5},{13,1},{2,14},{6,10},... | collective-permute-start | bytes 1259720 | tf_op jit(solution)/shard_map/ppermute | solution.py:701
  549.9 46.9 %collective-permute-start.70 = (bf16[144,1076]{1,0:T(8,128)(2,1)}, bf16[144,1076]{1,0:T(8,128)(2,1)}, u32[]{:S(2)}, u32[]{:S(2)}) collective-permute-start(bf16[144,1076]{1,0:T(8,128)(2,1)} %reduce-scatter.14.cloned.1.call-done), channel_id=1, source_target_pairs={{0,16},{16,0},{1,17},{17,1},{2,18},{18,2},{3,19},{19,3},{4,20},{20... | collective-permute-start | bytes 929672 | tf_op jit(solution)/shard_map/ppermute | solution.py:701
  550.5 22.1 %collective-permute-start.48 = (bf16[4,144,432]{2,1,0:T(8,128)(2,1)S(1)}, bf16[4,144,432]{2,1,0:T(8,128)(2,1)S(1)}, u32[]{:S(2)}, u32[]{:S(2)}) collective-permute-start(bf16[4,144,432]{2,1,0:T(8,128)(2,1)S(1)} %fusion.10), channel_id=1, source_target_pairs={{0,8},{4,12},{8,0},{12,4},{1,9},{5,13},{9,1},{13,5},{2,10},{6,14},... | collective-permute-start | bytes 1493000 | tf_op jit(solution)/shard_map/ppermute | solution.py:701
  558.7 17.1 %collective-permute-start.68 = (bf16[144,288]{0,1:T(8,128)(2,1)}, bf16[144,288]{0,1:T(8,128)(2,1)}, u32[]{:S(2)}, u32[]{:S(2)}) collective-permute-start(bf16[144,288]{0,1:T(8,128)(2,1)} %copy.80), channel_id=1, source_target_pairs={{0,16},{16,0},{1,17},{17,1},{2,18},{18,2},{3,19},{19,3},{4,20},{20... | collective-permute-start | bytes 248840 | tf_op jit(solution)/shard_map/ppermute | solution.py:701
  560.2 19.2 %collective-permute-start.49 = (bf16[288,729]{1,0:T(8,128)(2,1)}, bf16[288,729]{1,0:T(8,128)(2,1)}, u32[]{:S(2)}, u32[]{:S(2)}) collective-permute-start(bf16[288,729]{1,0:T(8,128)(2,1)} %get-tuple-element.242), channel_id=1, source_target_pairs={{0,4},{4,0},{8,12},{12,8},{1,5},{5,1},{9,13},{13,9},{2,6},{6,2},{1... | collective-permute-start | bytes 1259720 | tf_op jit(solution)/shard_map/ppermute | solution.py:701
  561.8 20.4 %collective-permute-start.50 = (bf16[288,729]{1,0:T(8,128)(2,1)}, bf16[288,729]{1,0:T(8,128)(2,1)}, u32[]{:S(2)}, u32[]{:S(2)}) collective-permute-start(bf16[288,729]{1,0:T(8,128)(2,1)} %get-tuple-element.243), channel_id=1, source_target_pairs={{0,8},{4,12},{8,0},{12,4},{1,9},{5,13},{9,1},{13,5},{2,10},{6,14},... | collective-permute-start | bytes 1259720 | tf_op jit(solution)/shard_map/ppermute | solution.py:701
  572.6 19.8 %collective-permute-start.51 = (bf16[288,729]{1,0:T(8,128)(2,1)}, bf16[288,729]{1,0:T(8,128)(2,1)S(1)}, u32[]{:S(2)}, u32[]{:S(2)}) collective-permute-start(bf16[288,729]{1,0:T(8,128)(2,1)} %get-tuple-element.244), channel_id=1, source_target_pairs={{0,12},{4,8},{8,4},{12,0},{1,13},{5,9},{9,5},{13,1},{2,14},{6,10},... | collective-permute-start | bytes 1259720 | tf_op jit(solution)/shard_map/ppermute | solution.py:701
  575.8 21.0 %collective-permute-start.69 = (bf16[144,1076]{1,0:T(8,128)(2,1)}, bf16[144,1076]{1,0:T(8,128)(2,1)S(1)}, u32[]{:S(2)}, u32[]{:S(2)}) collective-permute-start(bf16[144,1076]{1,0:T(8,128)(2,1)} %reduce-scatter.12.cloned.1.call-done), channel_id=1, source_target_pairs={{0,16},{16,0},{1,17},{17,1},{2,18},{18,2},{3,19},{19,3},{4,20},{20... | collective-permute-start | bytes 929672 | tf_op jit(solution)/shard_map/ppermute | solution.py:701
  579.4 22.7 %collective-permute-start.66 = (bf16[144,432]{0,1:T(8,128)(2,1)S(1)}, bf16[144,432]{0,1:T(8,128)(2,1)S(1)}, u32[]{:S(2)}, u32[]{:S(2)}) collective-permute-start(bf16[144,432]{0,1:T(8,128)(2,1)S(1)} %copy.82), channel_id=1, source_target_pairs={{0,16},{16,0},{1,17},{17,1},{2,18},{18,2},{3,19},{19,3},{4,20},{20... | collective-permute-start | bytes 373256 | tf_op jit(solution)/shard_map/ppermute | solution.py:701
  (59 other events, 550.8 us)
Sparse Core Ops, SparseCore 0:
  16.1 105.7 all-gather.2
  124.2 90.6 all-gather.4
  417.8 32.5 reduce-scatter.13
  476.0 20.4 reduce-scatter.15
  499.3 29.9 reduce-scatter.11
  543.4 20.2 reduce-scatter.17
  575.9 20.3 reduce-scatter.19

commit v4 on v3

--- a/solution.py
+++ b/solution.py
@@ -13,12 +13,13 @@
 EPSILON = 1e-06
 QUERY_ROWS = 384
 ROWS = 256
-NEAR = 2
+FC1 = True
+OUT = False
 COST = 1
-RING = False
 COLS = 256
 BF16 = jnp.bfloat16
 F32 = jnp.float32
+SLOPE = jnp.float32
 VMEM_BYTES = 60 * 2**20
 
 
@@ -191,19 +192,19 @@
         ref[...] = blocks_ref[place_ref[0] ^ r]
 
 
-def join_columns(place_ref, groups, parts_ref, whole_ref):
-    part = parts_ref.shape[2]
+def join_columns(parts_ref, whole_ref):
+    groups, _, part = parts_ref.shape
     for k in range(groups):
-        whole_ref[:, k * part : (k + 1) * part] = parts_ref[order_of(place_ref, groups, k)]
+        whole_ref[:, k * part : (k + 1) * part] = parts_ref[k]
 
 
 def order_of(place_ref, groups, k):
     return place_ref[place_ref.shape[0] - groups + k]
 
 
-def join_rows(place_ref, pieces, whole_ref, start, stop, k=0):
+def join_rows(place_ref, pieces, whole_ref):
     for p, ref in enumerate(pieces):
-        whole_ref[place_ref[1 + p], :, start:stop] = ref[k, :, : stop - start]
+        whole_ref[place_ref[1 + p]] = ref[0]
 
 
 def turned(rows, blocks_ref):
@@ -293,74 +294,80 @@
 
 def project_kernel(count, triple, place_ref, *refs):
     parts = refs[:count]
-    gain_ref, shift_ref, weight_ref, bias_ref = refs[count : count + 4]
-    image_ref, ready_ref, turned_ref, packed_ref = refs[count + 4 :]
+    weight_ref = refs[count]
+    image_ref, ready_ref, turned_ref, packed_ref, wide_ref, first_ref = refs[count + 1 :]
+    part = parts[0].shape[0]
+    third = triple // 3
+    start = triple // 128 * 128
+    notes = weight_ref[0, :, start:].astype(F32).T[triple - start :]
 
     @pl.when(pl.program_id(0) == 0)
     def _():
+        wide_ref[0:6] = notes[0:6]
         join_parts(place_ref, parts, turned_ref)
         image_ref[...] = flat(turned_ref).T
         for low, high in blocks_of(image_ref.shape[0], ROWS):
             normed, _ = norm(image_ref[low:high].astype(F32))
-            ready_ref[low:high] = (normed * gain_ref[...] + shift_ref[...]).astype(BF16)
+            ready_ref[low:high] = (normed * notes[0:1] + notes[1:2]).astype(BF16)
         turned(ready_ref[...], turned_ref)
 
-    packed = contract(ready_ref[...], weight_ref[0, :, :triple], 1, 0) + bias_ref[0]
-    packed_ref[0] = packed.astype(BF16)
-
-
-def project(spot, parts, gain, shift, weight, bias, blocks):
+    for i, (low, high) in enumerate(blocks_of(first_ref.shape[2], part)):
+        first_ref[0, :, low:high] = notes[8 + i : 9 + i, : high - low]
+    product = contract(ready_ref[...], weight_ref[0, :, :triple], 1, 0)
+    packed_ref[0, :, :third] = (product[:, :third] + notes[6:7, :third]).astype(BF16)
+    packed_ref[0, :, third : 2 * third] = product[:, third : 2 * third].astype(BF16)
+    packed_ref[0, :, 2 * third :] = (product[:, 2 * third :] + notes[7:8, :third]).astype(BF16)
+
+
+def project(spot, parts, weight, triple, cols, blocks):
     part, seq = parts[0].shape
     width = len(parts) * part
-    groups, _, triple = bias.shape
+    groups = weight.shape[0]
     outs = [
         (struct((seq, width), BF16), whole((seq, width))),
         (struct((seq, width), BF16), whole((seq, width))),
         (struct((blocks, width // blocks, seq), BF16), whole((blocks, width // blocks, seq))),
         (struct((groups, seq, triple), BF16), nth((groups, seq, triple))),
+        (struct((8, width), F32), whole((8, width))),
+        (struct((groups, 1, cols), F32), nth((groups, 1, cols))),
     ]
     return call(
         functools.partial(project_kernel, len(parts), triple),
         "project",
         groups,
         [(a, whole(a.shape)) for a in parts]
-        + [
-            (gain, whole(gain.shape)),
-            (shift, whole(shift.shape)),
-            (weight, pl.BlockSpec((1, width, lanes(triple)), lambda i, *_: (i, 0, 0))),
-            (bias, nth(bias.shape)),
-        ],
+        + [(weight, pl.BlockSpec((1, width, lanes(triple)), lambda i, *_: (i, 0, 0)))],
         outs,
         2 * groups * seq * width * triple,
         prefetch=(spot,),
     )
 
 
-def mix_kernel(count, groups, place_ref, image_ref, parts_ref, bias_ref, gain_ref, shift_ref, *refs):
-    pieces = refs[:count]
-    hidden_ref, ready_ref, turned_ref, weight_ref, joined, blocks = refs[count:]
-    part = parts_ref.shape[2]
-    join_columns(place_ref, groups, parts_ref, joined)
-    for k in range(groups):
-        join_rows(place_ref, pieces, blocks, k * part, (k + 1) * part, k)
-    weight_ref[...] = flat(blocks)
+def mix_kernel(count, image_ref, parts_ref, wide_ref, *refs):
+    strips = refs[:count]
+    hidden_ref, ready_ref, turned_ref, weight_ref, joined = refs[count:]
+    groups, _, part = parts_ref.shape
+    join_columns(parts_ref, joined)
+    for strip, (low, high) in zip(strips, blocks_of(part, 128), strict=True):
+        for k in range(groups):
+            weight_ref[:, k * part + low : k * part + high] = strip[k, :, : high - low]
     for low, high in blocks_of(image_ref.shape[0], ROWS):
-        mixed = contract(joined[low:high], weight_ref[...], 1, 1) + bias_ref[...]
+        mixed = contract(joined[low:high], weight_ref[...], 1, 1) + wide_ref[2:3]
         hidden = image_ref[low:high].astype(F32) + mixed
         hidden_ref[low:high] = hidden
         normed, _ = norm(hidden)
-        ready_ref[low:high] = (normed * gain_ref[...] + shift_ref[...]).astype(BF16)
+        ready_ref[low:high] = (normed * wide_ref[3:4] + wide_ref[4:5]).astype(BF16)
     turned(ready_ref[...], turned_ref)
 
 
-def mix(spot, image, parts, bias, gain, shift, pieces, blocks):
+def mix(image, parts, wide, weight, start, blocks):
     seq, width = image.shape
     groups, _, part = parts.shape
     inner = groups * part
-    size = lanes(part)
-    spec = pl.BlockSpec(
-        (groups, pieces[0].shape[1], size), lambda i, *_: (0, 0, pieces[0].shape[2] // size - 1)
-    )
+    strips = [
+        pl.BlockSpec((groups, width, 128), lambda i, *_, at=at: (0, 0, at))
+        for at in range(start // 128, start // 128 + len(blocks_of(part, 128)))
+    ]
     outs = [
         struct((seq, width), F32),
         struct((seq, width), BF16),
@@ -368,15 +375,13 @@
         struct((width, inner), BF16),
     ]
     return call(
-        functools.partial(mix_kernel, len(pieces), groups),
+        functools.partial(mix_kernel, len(strips)),
         "mix",
         1,
-        [(a, whole(a.shape)) for a in (image, parts, bias, gain, shift)]
-        + [(a, spec) for a in pieces],
+        [(a, whole(a.shape)) for a in (image, parts, wide)] + [(weight, strip) for strip in strips],
         [(o, whole(o.shape)) for o in outs],
         2 * seq * width * inner,
-        [pltpu.VMEM((seq, inner), BF16), pltpu.VMEM((blocks, width // blocks, inner), BF16)],
-        (spot,),
+        [pltpu.VMEM((seq, inner), BF16)],
     )
 
 
@@ -385,7 +390,7 @@
     active_ref, slope_ref, weight = refs[count:]
     bend = 0.7978845608028654
     cubic = 0.044715
-    join_rows(place_ref, pieces, weight, 0, weight.shape[2])
+    join_rows(place_ref, pieces, weight)
     for low, high in blocks_of(active_ref.shape[2], COLS):
         right = weight[:, :, low:high].reshape(-1, high - low)
         first = contract(ready_ref[...], right, 1, 0) + bias_ref[0, :, low:high]
@@ -393,9 +398,8 @@
         bent = jnp.tanh(bend * (first + cubic * (first * square)))
         half = 0.5 * (1.0 + bent)
         active_ref[0, :, low:high] = (first * half).astype(BF16)
-        slope_ref[0, :, low:high] = half + (0.5 * bend) * first * (1.0 - bent * bent) * (
-            1.0 + (3.0 * cubic) * square
-        )
+        slope = half + (0.5 * bend) * first * (1.0 - bent * bent) * (1.0 + (3.0 * cubic) * square)
+        slope_ref[0, :, low:high] = slope.astype(SLOPE)
 
 
 def near_piece(piece, size):
@@ -420,7 +424,7 @@
         groups,
         [(ready, whole(ready.shape)), (bias, ordered(groups, bias.shape))]
         + [(a, near_piece(a, size)) for a in pieces],
-        [(struct(shape, BF16), ordered(groups, shape)), (struct(shape, F32), ordered(groups, shape))],
+        [(struct(shape, BF16), ordered(groups, shape)), (struct(shape, SLOPE), ordered(groups, shape))],
         2 * groups * seq * width * cols,
         [pltpu.VMEM((blocks, width // blocks, size), BF16)],
         (spot,),
@@ -435,7 +439,7 @@
 
     @pl.when(step == 0)
     def _():
-        total[...] = hidden_ref[...] + bias_ref[...] + term
+        total[...] = hidden_ref[...] + bias_ref[5:6] + term
 
     @pl.when(step > 0)
     def _():
@@ -467,27 +471,29 @@
     )
 
 
-def feed_back_kernel(count, place_ref, grad_ref, hidden_ref, gain_ref, slope_ref, second_ref, *refs):
+def feed_back_kernel(
+    count, place_ref, grad_ref, sum_ref, hidden_ref, gain_ref, slope_ref, second_ref, *refs
+):
     pieces = refs[:count]
     (
         first_grad_ref,
-        first_sum_ref,
         hidden_grad_ref,
         low_ref,
         turned_ref,
-        gain_sum_ref,
-        shift_sum_ref,
-        low_sum_ref,
+        sums_ref,
         total,
         weight,
+        firsts,
     ) = refs[count:]
     step = pl.program_id(0)
-    join_rows(place_ref, pieces, weight, 0, weight.shape[2])
+    groups = place_ref.shape[0] - 1 - count
+    place = order_of(place_ref, groups, step)
+    join_rows(place_ref, pieces, weight)
     for low, high in blocks_of(slope_ref.shape[2], COLS):
         active_grad = contract(grad_ref[...], second_ref[0, :, low:high], 1, 0)
-        first_grad = (active_grad * slope_ref[0, :, low:high]).astype(BF16)
+        first_grad = (active_grad * slope_ref[0, :, low:high].astype(F32)).astype(BF16)
         first_grad_ref[0, :, low:high] = first_grad
-        first_sum_ref[0, :, low:high] = jnp.sum(first_grad.astype(F32), axis=0, keepdims=True)
+        firsts[place, :, low:high] = jnp.sum(first_grad.astype(F32), axis=0, keepdims=True)
     right = flat(weight)[:, : slope_ref.shape[2]]
     term = contract(first_grad_ref[0], right, 1, 1)
 
@@ -501,44 +507,43 @@
 
     @pl.when(step == pl.num_programs(0) - 1)
     def _():
-        gain_sum = jnp.zeros(gain_sum_ref.shape, F32)
-        shift_sum = jnp.zeros(gain_sum_ref.shape, F32)
-        low_sum = jnp.zeros(gain_sum_ref.shape, F32)
+        gain_sum = jnp.zeros((1, total.shape[1]), F32)
+        shift_sum = gain_sum
+        low_sum = gain_sum
         for low, high in blocks_of(total.shape[0], ROWS):
             normed, inverse = norm(hidden_ref[low:high])
             ready_grad = total[low:high]
             gain_sum += jnp.sum(ready_grad * normed, axis=0, keepdims=True)
             shift_sum += jnp.sum(ready_grad, axis=0, keepdims=True)
             hidden_grad = grad_ref[low:high].astype(F32) + norm_back(
-                ready_grad, normed, inverse, gain_ref[...]
+                ready_grad, normed, inverse, gain_ref[3:4]
             )
             hidden_grad_ref[low:high] = hidden_grad
             rounded = hidden_grad.astype(BF16)
             low_ref[low:high] = rounded
             low_sum += jnp.sum(rounded.astype(F32), axis=0, keepdims=True)
-        gain_sum_ref[...] = gain_sum
-        shift_sum_ref[...] = shift_sum
-        low_sum_ref[...] = low_sum
+        sums_ref[...] = jnp.zeros(sums_ref.shape, F32)
+        for k in range(groups):
+            sums_ref[4 + k : 5 + k, : firsts.shape[2]] = firsts[k]
+        sums_ref[0:1] = low_sum
+        sums_ref[1:2] = gain_sum
+        sums_ref[2:3] = shift_sum
+        sums_ref[3:4] = sum_ref[...]
         turned(low_ref[...], turned_ref)
 
 
-def feed_back(spot, grad, hidden, gain, slope, second, pieces, blocks):
+def feed_back(spot, grad, grad_sum, hidden, gain, slope, second, pieces, blocks):
     seq, width = hidden.shape
     groups, _, cols = slope.shape
     size = lanes(cols)
-    row = struct((1, width), F32)
-    outs = [
-        (struct(slope.shape, BF16), ordered(groups, slope.shape)),
-        (struct((groups, 1, cols), F32), ordered(groups, (groups, 1, cols))),
-    ] + [
+    rows = -(-(4 + groups) // 8) * 8
+    outs = [(struct(slope.shape, BF16), ordered(groups, slope.shape))] + [
         (o, whole(o.shape))
         for o in (
             struct((seq, width), F32),
             struct((seq, width), BF16),
             struct((blocks, width // blocks, seq), BF16),
-            row,
-            row,
-            row,
+            struct((rows, width), F32),
         )
     ]
     return call(
@@ -547,6 +552,7 @@
         groups,
         [
             (grad, whole(grad.shape)),
+            (grad_sum, whole(grad_sum.shape)),
             (hidden, whole(hidden.shape)),
             (gain, whole(gain.shape)),
             (slope, ordered(groups, slope.shape)),
@@ -555,45 +561,49 @@
         + [(a, near_piece(a, size)) for a in pieces],
         outs,
         4 * groups * seq * width * cols,
-        [pltpu.VMEM((seq, width), F32), pltpu.VMEM((blocks, width // blocks, size), BF16)],
+        [
+            pltpu.VMEM((seq, width), F32),
+            pltpu.VMEM((blocks, width // blocks, size), BF16),
+            pltpu.VMEM((groups, 1, cols), F32),
+        ],
         (spot,),
     )
 
 
-def mix_back_kernel(groups, place_ref, grad_ref, weight_ref, out_ref):
-    part = out_ref.shape[2]
+def mix_back_kernel(grad_ref, weight_ref, out_ref):
+    groups, _, part = out_ref.shape
     full = contract(grad_ref[...], weight_ref[...], 1, 0).astype(BF16)
     for k in range(groups):
-        out_ref[order_of(place_ref, groups, k)] = full[:, k * part : (k + 1) * part]
-
-
-def mix_back(spot, grad, weight, groups):
+        out_ref[k] = full[:, k * part : (k + 1) * part]
+
+
+def mix_back(grad, weight, groups):
     seq, width = grad.shape
     shape = (groups, seq, weight.shape[1] // groups)
     return call(
-        functools.partial(mix_back_kernel, groups),
+        mix_back_kernel,
         "mix_back",
         1,
         [(grad, whole(grad.shape)), (weight, whole(weight.shape))],
         [(struct(shape, BF16), whole(shape))],
         2 * seq * width * weight.shape[1],
-        prefetch=(spot,),
     )[0]
 
 
 def project_back_kernel(
-    place_ref, image_ref, gain_ref, hidden_grad_ref, near_ref, far_ref, weight_ref, *rest
+    place_ref,
+    image_ref,
+    gain_ref,
+    hidden_grad_ref,
+    packed_ref,
+    packed_sum_ref,
+    weight_ref,
+    *rest,
 ):
-    parts = rest[:-5]
-    gain_sum_ref, shift_sum_ref, total, joined, blocks = rest[-5:]
+    parts = rest[:-3]
+    sums_ref, total, blocks = rest[-3:]
     step = pl.program_id(0)
-    near = near_ref.shape[2] // 3
-    far = far_ref.shape[2] // 3
-    for i in range(3):
-        start = i * (near + far)
-        joined[:, start : start + near] = near_ref[0, :, i * near : (i + 1) * near]
-        joined[:, start + near : start + near + far] = far_ref[0, :, i * far : (i + 1) * far]
-    term = contract(joined[...], weight_ref[0, :, : joined.shape[1]], 1, 1)
+    term = contract(packed_ref[0], weight_ref[0, :, : packed_ref.shape[2]], 1, 1)
 
     @pl.when(step == 0)
     def _():
@@ -605,28 +615,30 @@
 
     @pl.when(step == pl.num_programs(0) - 1)
     def _():
-        gain_sum = jnp.zeros(gain_sum_ref.shape, F32)
-        shift_sum = jnp.zeros(gain_sum_ref.shape, F32)
+        sums_ref[...] = jnp.zeros(sums_ref.shape, F32)
+        gain_sum = jnp.zeros((1, total.shape[1]), F32)
+        shift_sum = gain_sum
         for low, high in blocks_of(total.shape[0], ROWS):
             normed, inverse = norm(image_ref[low:high].astype(F32))
             ready_grad = total[low:high]
             gain_sum += jnp.sum(ready_grad * normed, axis=0, keepdims=True)
             shift_sum += jnp.sum(ready_grad, axis=0, keepdims=True)
             result = hidden_grad_ref[low:high] + norm_back(
-                ready_grad, normed, inverse, gain_ref[...]
+                ready_grad, normed, inverse, gain_ref[0:1]
             )
             total[low:high] = result
-        gain_sum_ref[...] = gain_sum
-        shift_sum_ref[...] = shift_sum
+        sums_ref[0:1] = gain_sum
+        sums_ref[1:2] = shift_sum
+        for k in range(packed_sum_ref.shape[0]):
+            sums_ref[2 + k : 3 + k, : packed_ref.shape[2]] = packed_sum_ref[k]
         split_parts(place_ref, total[...].astype(BF16), parts, blocks)
 
 
-def project_back(spot, image, gain, hidden_grad, near, far, weight, count):
+def project_back(spot, image, gain, hidden_grad, packed_grad, packed_sum, weight, count):
     seq, width = image.shape
-    groups = near.shape[0]
-    triple = near.shape[2] + far.shape[2]
+    groups, _, triple = packed_grad.shape
     shape = (width // count, seq)
-    row = struct((1, width), F32)
+    sums = struct((-(-(2 + groups) // 8) * 8, width), F32)
     return call(
         project_back_kernel,
         "project_back",
@@ -635,23 +647,22 @@
             (image, whole(image.shape)),
             (gain, whole(gain.shape)),
             (hidden_grad, whole(hidden_grad.shape)),
-            (near, nth(near.shape)),
-            (far, nth(far.shape)),
+            (packed_grad, nth(packed_grad.shape)),
+            (packed_sum, whole(packed_sum.shape)),
             (weight, pl.BlockSpec((1, width, lanes(triple)), lambda i, *_: (i, 0, 0))),
         ],
         [(struct(shape, BF16), whole(shape))] * count
-        + [(row, whole(row.shape)), (row, whole(row.shape))],
+        + [(sums, whole(sums.shape))],
         2 * groups * seq * width * triple,
         [
             pltpu.VMEM((seq, width), F32),
-            pltpu.VMEM((seq, triple), BF16),
             pltpu.VMEM((count, width // count, seq), BF16),
         ],
         (spot,),
     )
 
 
-def share_kernel(half, added, pick_ref, turned_ref, right_ref, *rest):
+def share_kernel(half, cuts, pick_ref, turned_ref, right_ref, *rest):
     rows = turned_ref.shape[1]
     picked = rest[-1]
     count = picked.shape[0] // rows
@@ -659,40 +670,47 @@
     @pl.when(pl.program_id(0) == 0)
     def _():
         for i in range(count):
-            picked[i * rows : (i + 1) * rows] = turned_ref[pick_ref[half * count + i]]
+            picked[i * rows : (i + 1) * rows] = turned_ref[pick_ref[1 + half * count + i]]
 
     product = contract(picked[...], right_ref[0], 1, 0)
-    received = rest[:count] if added else ()
-    outs = rest[len(received) : -1]
+    if not cuts:
+        for i in range(count):
+            rest[i][0] = product[i * rows : (i + 1) * rows].astype(BF16)
+        return
+    received, outs = rest[:count], rest[count:-1]
+    each = len(outs) // len(cuts)
     for i in range(count):
-        piece = product[i * rows : (i + 1) * rows]
-        if added:
-            piece = piece + received[i][0].astype(F32)
-        if len(outs) == count:
-            outs[i][0] = piece.astype(BF16)
-        else:
-            outs[i // 2][i % 2, 0] = piece.astype(BF16)
-
-
-def share(pick, turned_rows, right, received=()):
+        piece = product[i * rows : (i + 1) * rows] + received[i][0].astype(F32)
+        for n, (low, high, side_first) in enumerate(cuts):
+            place = (i // 2, i % 2) if side_first else (i % 2, i // 2)
+            outs[n * each + place[0]][place[1], 0] = piece[:, low:high].astype(BF16)
+
+
+def share(spot, turned_rows, right, received=(), cuts=()):
     total, rows, seq = turned_rows.shape
     groups, _, cols = right.shape
     count = total // 2
-    one = (struct((groups, rows, cols), BF16), nth((groups, rows, cols)))
-    two = (
-        struct((2, groups, rows, cols), BF16),
-        pl.BlockSpec((2, 1, rows, cols), lambda i, *_: (0, i, 0, 0)),
-    )
-    return call(
-        functools.partial(share_kernel, 0 if received else 1, bool(received)),
+
+    def two(size):
+        return (
+            struct((2, groups, rows, size), BF16),
+            pl.BlockSpec((2, 1, rows, size), lambda i, *_: (0, i, 0, 0)),
+        )
+
+    if received:
+        outs = [two(high - low) for low, high, _ in cuts for _ in range(count // 2)]
+    else:
+        outs = [(struct((groups, rows, cols), BF16), nth((groups, rows, cols)))] * count
+    return call(
+        functools.partial(share_kernel, 0 if received else 1, cuts),
         "share",
         groups,
         [(turned_rows, whole(turned_rows.shape)), (right, nth(right.shape))]
         + [(a, nth(a.shape)) for a in received],
-        [two] * (count // 2) if received else [one] * count,
+        outs,
         2 * groups * count * rows * seq * cols,
         [pltpu.VMEM((count * rows, seq), BF16)],
-        (pick,),
+        (spot,),
     )
 
 
@@ -711,54 +729,77 @@
 
 
 class Sums:
-    def __init__(self, line, pick, turned_rows, halves, half_first, ring=False):
+    def __init__(self, line, spot, turned_rows, right, halves, *cuts):
         self.line = line
-        self.pick = pick[half_first]
+        self.spot = spot
         self.rows = turned_rows
+        self.right = right
         self.halves = halves
-        self.ring = ring
-        steps = [("dp", 1), ("gx", 2)] if half_first else [("gx", 2), ("dp", 1)]
+        if halves == 1:
+            cuts = [(0, right.shape[2], True)]
+        self.cuts = [Cut(line, halves, *cut) for cut in cuts]
+
+    def away(self):
+        sent = self.line(lambda a: share(self.spot, a, self.right), self.rows)
+        self.arrived = [swap(a, "gx", 1) for a in sent]
+
+    def keep(self):
+        cuts = [(cut.low, cut.high, cut.side_first) for cut in self.cuts]
+        kept = self.line(
+            lambda a: share(self.spot, a, self.right, self.arrived, cuts), self.rows
+        )
+        each = len(kept) // len(cuts)
+        for n, cut in enumerate(self.cuts):
+            cut.begin(kept[n * each : (n + 1) * each])
+
+    def send(self):
+        for cut in self.cuts:
+            cut.send()
+
+    def total(self):
+        for cut in self.cuts:
+            cut.total()
+
+
+class Cut:
+    def __init__(self, line, halves, low, high, side_first):
+        self.line = line
+        self.low = low
+        self.high = high
+        self.side_first = side_first
+        steps = [("dp", 1), ("gx", 2)] if side_first else [("gx", 2), ("dp", 1)]
         self.steps = steps if halves == 2 else [None, ("gx", 2)]
 
-    def away(self, right):
-        self.right = right
-        sent = self.line(lambda a: share(self.pick, a, right), self.rows)
-        self.arrived = [swap(a, "gx", 1) for a in sent]
-
-    def keep(self):
-        kept = self.line(
-            lambda a: share(self.pick, a, self.right, self.arrived), self.rows
-        )
+    def begin(self, kept):
         self.kept = kept[0]
-        if self.halves == 2:
-            self.arrived = swap(kept[1], *self.steps[0])
+        self.arrived = swap(kept[1], *self.steps[0]) if len(kept) == 2 else None
 
     def mine(self, i, kept):
         value = kept[i].astype(F32)
-        return value + self.arrived[i].astype(F32) if self.halves == 2 else value
+        return value if self.arrived is None else value + self.arrived[i].astype(F32)
 
     def send(self):
         sent = self.line(lambda a: self.mine(1, a).astype(BF16), self.kept)
         self.second = swap(sent, *self.steps[1])
 
     def total(self):
-        total = self.line(
+        self.sum = self.line(
             lambda a: (self.mine(0, a) + self.second.astype(F32)).astype(BF16), self.kept
         )
-        groups, rows, cols = total.shape
-        if not self.ring:
-            self.own = lax.psum_scatter(
-                total.reshape(groups * rows, cols), "gy", scatter_dimension=0, tiled=True
-            )
-            return
-        me = lax.axis_index("gy")
-        up = [(i, (i + 1) % groups) for i in range(groups)]
-        block = lambda k: lax.dynamic_index_in_dim(total, (me + groups - k) % groups, 0, False)
-        running = block(1)
-        for k in range(2, groups + 1):
-            running = lax.ppermute(running, "gy", up)
-            running = (running.astype(F32) + block(k % groups).astype(F32)).astype(BF16)
-        self.own = running
+
+
+class Shared:
+    def __init__(self, line, halves, *weights):
+        sums = [cut for weight in weights for cut in weight.cuts]
+        self.line = line
+        self.halves = halves
+        self.cols = [one.sum.shape[2] for one in sums]
+        groups, rows, _ = sums[0].sum.shape
+        wide = [jnp.pad(a.sum, ((0, 0), (0, 0), (0, lanes(c) - c))) for a, c in zip(sums, self.cols)]
+        wide = line(lambda a: jnp.concatenate([a] + wide[1:], axis=2), wide[0])
+        self.own = lax.psum_scatter(
+            wide.reshape(groups * rows, wide.shape[2]), "gy", scatter_dimension=0, tiled=True
+        )
 
     def trade(self):
         if self.halves == 2:
@@ -767,12 +808,14 @@
 
     def end(self):
         if self.halves == 1:
-            return lax.psum(self.own.astype(F32), "dp")
-        other = self.other
-        first = lax.axis_index("dp") == 0
-        return jnp.concatenate(
-            [jnp.where(first, self.own, other), jnp.where(first, other, self.own)], axis=0
-        ).astype(F32)
+            full = lax.psum(self.own.astype(F32), "dp")
+        else:
+            first = lax.axis_index("dp") == 0
+            low = jnp.where(first, self.own, self.other)
+            high = jnp.where(first, self.other, self.own)
+            full = jnp.concatenate([low, high], axis=0).astype(F32)
+        starts = [sum(lanes(c) for c in self.cols[:i]) for i in range(len(self.cols))]
+        return [full[:, start : start + c] for start, c in zip(starts, self.cols)]
 
 
 class Line:
@@ -796,17 +839,10 @@
 
 
 class Pieces:
-    def __init__(self, first, mixed, halves):
-        rows = first.shape[0] // halves
-        size = lanes(mixed.shape[1])
-        start = -(-first.shape[1] // size) * size
-        both = jnp.concatenate(
-            [
-                jnp.pad(first, ((0, 0), (0, start - first.shape[1]))),
-                jnp.pad(mixed, ((0, 0), (0, size - mixed.shape[1]))),
-            ],
-            axis=1,
-        )
+    def __init__(self, weight, halves):
+        rows = weight.shape[0] // halves
+        cols = weight.shape[1]
+        both = jnp.pad(weight, ((0, 0), (0, lanes(cols) - cols)))
         if halves == 2:
             both = lax.dynamic_slice_in_dim(both, lax.axis_index("dp") * rows, rows, 0)
         count = lax.axis_size("gy")
@@ -877,160 +913,126 @@
     def block(core, side, far):
         return (column ^ (2 * far + core)) * halves + (half ^ side if halves == 2 else 0)
 
-    bits = range(halves)
-    pick = {
-        True: jnp.stack([block(c, s, f) for c in range(2) for s in bits for f in range(2)]),
-        False: jnp.stack([block(c, s, f) for c in range(2) for f in range(2) for s in bits]),
-    }
+    pick = [block(c, s, f) for c in range(2) for s in range(halves) for f in range(2)]
     here = lax.axis_index("gy")
     spot = jnp.concatenate(
         [
             jnp.reshape(column, (1,)),
-            pick[True],
+            jnp.stack(pick),
             (here + gy - jnp.arange(gy, dtype=jnp.int32)) % gy,
         ]
     ).astype(jnp.int32)
     line = Line()
 
-    wide = jnp.stack([ln1_gain, ln1_bias, out_bias, ln2_gain, ln2_bias, fc2_bias], axis=1)
-    deep = jnp.concatenate([qv_bias[0], qv_bias[1], fc1_bias])
-    deep_cols = -(-deep.shape[0] // part)
-    deep = jnp.pad(deep, (0, deep_cols * part - deep.shape[0])).reshape(deep_cols, part).T
-    early = jnp.concatenate([qkv_weight.reshape(part, triple), wide, deep], axis=1)
+    early = [qkv_weight.reshape(part, triple)]
+    early += [a[:, None] for a in (ln1_gain, ln1_bias, out_bias, ln2_gain, ln2_bias, fc2_bias)]
+    for vector in (qv_bias[0], qv_bias[1], fc1_bias):
+        count = -(-vector.shape[0] // part)
+        vector = jnp.pad(vector, (0, count * part - vector.shape[0]))
+        early.append(vector.reshape(count, part).T)
+    early = jnp.concatenate(early, axis=1)
     early_cols = lanes(early.shape[1])
-    early = jnp.pad(early, ((0, 0), (0, early_cols - early.shape[1])))
-    early = collect(early, along).reshape(gy, width, early_cols)
+    early = jnp.concatenate(
+        [
+            jnp.pad(early, ((0, 0), (0, early_cols - early.shape[1]))),
+            jnp.pad(out_weight.T, ((0, 0), (0, lanes(head_cols) - head_cols))),
+        ],
+        axis=1,
+    )
+    early = collect(early, along).reshape(gy, width, early.shape[1])
     second = jnp.pad(fc2_weight.T, ((0, 0), (0, lanes(hidden_cols) - hidden_cols)))
     second = collect(second, along).reshape(gy, width, lanes(hidden_cols))
     token_parts = cut(spot, jnp.swapaxes(tokens, 1, 2), gx, copies)
-    gathered = Pieces(after(fc1_weight, token_parts[0]), out_weight.T, halves)
+    line.last = token_parts[0]
+    grad_parts = line(lambda a: cut(spot, a, gx, copies), jnp.swapaxes(cotangent, 1, 2))
+    gathered = Pieces(after(fc1_weight, token_parts[0]), halves)
     token_parts = traded(token_parts)
 
-    wide = early[0, :, triple : triple + 6].T.astype(F32)
-    gain_one, shift_one, bias_mix, gain_two, shift_two, bias_second = [
-        wide[i : i + 1] for i in range(6)
-    ]
-    deep = early[:, :part, triple + 6 : triple + 6 + deep_cols].astype(F32)
-    deep = jnp.swapaxes(deep, 1, 2).reshape(gy, 1, deep_cols * part)
-    bias_qkv = jnp.concatenate(
-        [
-            deep[:, :, :head_cols],
-            jnp.zeros((gy, 1, head_cols), F32),
-            deep[:, :, head_cols : 2 * head_cols],
-        ],
-        axis=2,
-    )
-    bias_first = deep[:, :, 2 * head_cols : 2 * head_cols + hidden_cols]
-
-    image, ready_one, turned_one, packed = line(
-        lambda a: project(spot, [a] + token_parts[1:], gain_one, shift_one, early, bias_qkv, blocks),
+    image, ready_one, turned_one, packed, wide, bias_first = line(
+        lambda a: project(spot, [a] + token_parts[1:], early, triple, hidden_cols, blocks),
         token_parts[0],
     )
-    grad_parts = line(lambda a: cut(spot, a, gx, copies), jnp.swapaxes(cotangent, 1, 2))
-    grad_parts = traded(grad_parts)
     gathered.middle(packed)
+    grad_parts = traded([after(a, packed) for a in grad_parts])
     mixture, log_total = line(lambda a: attend(a, heads), packed)
     pieces = gathered.last(mixture)
     log_total = jnp.swapaxes(log_total, 1, 2)
+    hidden, ready_two, turned_two, whole_out = line(
+        lambda a: mix(a, mixture, wide, early, early_cols, blocks), image
+    )
+    active, slope = line(lambda a: expand(spot, a, bias_first, pieces, blocks), ready_two)
     grad_low, grad_turned, grad_sum = line(
         lambda a: spread(spot, [a] + grad_parts[1:], blocks), grad_parts[0]
     )
-    hidden, ready_two, turned_two, whole_out = line(
-        lambda a: mix(spot, a, mixture, bias_mix, gain_two, shift_two, pieces, blocks), image
-    )
-    active, slope = line(lambda a: expand(spot, a, bias_first, pieces, blocks), ready_two)
-
-    near = max(1, NEAR * heads // 4)
-    fc2 = Sums(line, pick, grad_turned, halves, True)
-    fc1 = Sums(line, pick, turned_two, halves, True)
-    fc2.away(active)
-    out_parts = line(lambda a: narrow(spot, a, active, second, bias_second, gx), hidden)
+
+    fc2 = Sums(line, spot, grad_turned, active, halves, (0, hidden_cols, True))
+    fc2.away()
+    out_parts = line(lambda a: narrow(spot, a, active, second, wide, gx), hidden)
     out_parts = traded(out_parts)
     fc2.keep()
     (
         grad_first,
-        first_sum,
         grad_hidden,
         grad_hidden_low,
         turned_hidden,
-        gain_two_sum,
-        shift_two_sum,
-        low_sum,
+        fed_sums,
     ) = line(
-        lambda a: feed_back(spot, a, hidden, gain_two, slope, second, pieces, blocks), grad_low
-    )
-    out = Sums(line, pick, turned_hidden, halves, False)
-    first_heads = Sums(line, pick, turned_one, halves, True)
-    last_heads = Sums(line, pick, turned_one, halves, True, RING)
-    fc1.away(grad_first)
-    grad_mixture = line(lambda a: mix_back(spot, a, whole_out, gy), grad_hidden_low)
+        lambda a: feed_back(spot, a, grad_sum, hidden, wide, slope, second, pieces, blocks), grad_low
+    )
+    fc1 = Sums(line, spot, turned_two, grad_first, halves, (0, hidden_cols, FC1))
+    out = Sums(line, spot, turned_hidden, mixture, halves, (0, head_cols, OUT))
+    layer_out = line(
+        lambda a: place(spot, [a] + out_parts[1:], turned_shape, copies), out_parts[0]
+    )
+    fc1.away()
+    grad_mixture = line(lambda a: mix_back(a, whole_out, gy), grad_hidden_low)
     fc1.keep()
     fc2.send()
-    near_grad, near_sum = line(
-        lambda a: attend_back(a, log_total, grad_mixture, heads, list(range(near))), packed
-    )
-    out.away(mixture)
-    first_heads.away(near_grad)
+    packed_grad, packed_sum = line(
+        lambda a: attend_back(a, log_total, grad_mixture, heads, list(range(heads))), packed
+    )
+    middle = max(1, triple // 256) * 128
+    qkv = Sums(
+        line, spot, turned_one, packed_grad, halves, (0, middle, True), (middle, triple, False)
+    )
+    qkv.away()
+    out.away()
     fc2.total()
+    fc2_end = Shared(line, halves, fc2)
+    fc1.send()
+    qkv.keep()
     out.keep()
-    first_heads.keep()
-    fc1.send()
-    fed_sums = everyone(
-        line(
-            lambda a: jnp.concatenate(
-                [b.reshape(-1) for b in (a, gain_two_sum, shift_two_sum, grad_sum, first_sum)]
-            ),
-            low_sum,
-        )
-    )
-    far_grad, far_sum = line(
-        lambda a: attend_back(a, log_total, grad_mixture, heads, list(range(near, heads))), packed
-    )
+    fed_sums = everyone(line(lambda a: a, fed_sums))
+    fc1.total()
+    fc1_end = Shared(line, halves, fc1)
+    *grad_parts, late_sums = line(
+        lambda a: project_back(spot, a, wide, grad_hidden, packed_grad, packed_sum, early, gx),
+        image,
+    )
+    qkv.send()
     out.send()
-    last_heads.away(far_grad)
-    first_heads.send()
+    grad_parts = traded(grad_parts)
+    late_sums = everyone(line(lambda a: a, late_sums))
+    fc2_end.trade()
+    qkv.total()
     out.total()
-    fc1.total()
-    last_heads.keep()
-    fc2.trade()
-    first_heads.total()
-    *grad_parts, gain_one_sum, shift_one_sum = line(
-        lambda a: project_back(spot, a, gain_one, grad_hidden, near_grad, far_grad, early, gx), image
-    )
-    last_heads.send()
-    grad_parts = traded(grad_parts)
-    out.trade()
-    fc1.trade()
-    layer_out = line(
-        lambda a: place(spot, [a] + out_parts[1:], turned_shape, copies), out_parts[0]
-    )
-    last_heads.total()
-    first_heads.trade()
+    last_end = Shared(line, halves, out, qkv)
+    fc1_end.trade()
+    last_end.trade()
     tokens_grad = line(
         lambda a: place(spot, [a] + grad_parts[1:], turned_shape, copies), grad_parts[0]
     )
-    last_heads.trade()
-    grad_fc2 = fc2.end().T
-    grad_fc1 = fc1.end()
-    grad_out_weight = out.end().T
-    grad_near = first_heads.end().reshape(part, 3, near * HEAD_DIM)
-    grad_far = last_heads.end().reshape(part, 3, (heads - near) * HEAD_DIM)
-    grad_qkv = jnp.concatenate([grad_near, grad_far], axis=2)
-
-    near_sum = near_sum.reshape(gy, 3, near * HEAD_DIM)
-    far_sum = far_sum.reshape(gy, 3, (heads - near) * HEAD_DIM)
-    packed_sum = jnp.concatenate([near_sum, far_sum], axis=2)
-    late_sums = everyone(
-        jnp.concatenate(
-            [a.reshape(-1) for a in (gain_one_sum, shift_one_sum, packed_sum[:, 0], packed_sum[:, 2])]
-        )
-    )
-    wide_sums = jnp.concatenate([late_sums[: 2 * width], fed_sums[: 4 * width]]).reshape(6, width)
+    grad_fc2 = fc2_end.end()[0].T
+    grad_fc1 = fc1_end.end()[0]
+    grad_out_weight, *grad_qkv = last_end.end()
+    grad_out_weight = grad_out_weight.T
+    grad_qkv = jnp.concatenate(grad_qkv, axis=1).reshape(part, 3, head_cols)
+
+    first_sums = lax.dynamic_index_in_dim(fed_sums, 4 + here, 0, False)[:hidden_cols]
+    qv_sums = lax.dynamic_index_in_dim(late_sums, 2 + here, 0, False)
+    qv_sums = qv_sums[:triple].reshape(3, head_cols)[::2]
+    wide_sums = jnp.concatenate([late_sums[:2], fed_sums[:4]])
     wide_sums = lax.dynamic_slice_in_dim(wide_sums, column * part, part, 1)
-    qv_sums = late_sums[2 * width :].reshape(2, gy, head_cols)
-    qv_sums = lax.dynamic_index_in_dim(qv_sums, here, 1, False)
-    first_sums = fed_sums[4 * width :].reshape(gy, hidden_cols)
-    first_sums = lax.dynamic_index_in_dim(first_sums, here, 0, False)
     grads = (
         wide_sums[0],
         wide_sums[1],

time: 626 us -> 592 us (0.946)
  local copies, waits for them, and re-layouts: 50.6 us -> 27.2 us
  waiting for transfers between devices: 158 us -> 177 us
  Pallas kernels: 299 us -> 283 us
  other arithmetic: 35.8 us -> 25.2 us
    ppermute x68 -> x62, waiting for transfers between devices: 72.4 us -> 130 us  [swap(): return lax.ppermute(array, axis, [(i, i ^ bit) for i in range(size)])]
    all_gather x2, waiting for transfers between devices: 33.3 us -> 7.49 us  [collect(): return lax.all_gather(block, order, axis=0, tiled=True)]
    pallas_call x25 -> x22, Pallas kernels: 299 us -> 283 us  [call(): pl.pallas_call(kernel, grid_spec=pltpu.PrefetchScalarGridSpec(num_scalar_...]
    slice x14 -> x5, local copies, waits for them, and re-layouts: 15.2 us -> 1.26 us  [the longest x2 0.63 us: on_device(): qv_sums = qv_sums[:triple].reshape(3, head_cols)[::2]]
    ppermute x3, waiting for transfers between devices: 52.2 us -> 39.1 us  [__init__(): groups.append(lax.ppermute(groups[-1], 'gy', up))]
    unnamed x67 -> x68, local copies, waits for them, and re-layouts: 14.3 us -> 9.4 us
    ppermute x68 -> x62, starting transfers between devices: 47.3 us -> 47.5 us  [swap(): return lax.ppermute(array, axis, [(i, i ^ bit) for i in range(size)])]
  transfers between devices with their start and end apart: 78 -> 70, of which waited for: 26 -> 23; matrix products, arithmetic and copies ran while one was open for 11% -> 6% of each run, Pallas kernels for 47% -> 48%
where the time goes in v4:
time: 592 us; the launch traced here: 587 us
  Pallas kernels  283 us (48%)
  waiting for transfers between devices  177 us (30%)
  starting transfers between devices  59.7 us (10%)
  local copies, waits for them, and re-layouts  27.2 us (5%)
  other arithmetic  25.2 us (4%)
  between operations  14.8 us (2%)
    pallas_call x22, Pallas kernels, call(): pl.pallas_call(kernel, grid_spec=pltpu.PrefetchScalarGridSpec(num_scalar_...  283 us
    ppermute x62, waiting for transfers between devices, swap(): return lax.ppermute(array, axis, [(i, i ^ bit) for i in range(size)])  130 us
    ppermute x62, starting transfers between devices, swap(): return lax.ppermute(array, axis, [(i, i ^ bit) for i in range(size)])  47.5 us
    ppermute x3, waiting for transfers between devices, __init__(): groups.append(lax.ppermute(groups[-1], 'gy', up))  39.1 us
    ppermute x3, starting transfers between devices, __init__(): groups.append(lax.ppermute(groups[-1], 'gy', up))  11.9 us
  transfers between devices with their start and end apart: 70, of which 23 were waited for; matrix products, arithmetic and copies ran while one was open for 6% of the time, Pallas kernels for 48%

profile of v4, /device:TPU:0, one launch (start us, length us, event | category | flops | bytes accessed | tf_op | source)
XLA Modules:
  0.0 586.8 jit_solution(16267450933658160534)
XLA Ops:
  17.8 3.7 cut.2
  21.5 3.1 collective-permute-start.3
  24.6 13.0 %collective-permute-done.3 = bf16[144,1152]{1,0:T(8,128)(2,1)S(1)} collective-permute-done((bf16[144,1152]{1,0:T(8,128)(2,1)S(1)}, bf16[144,1152]{1,0:T(8,128)(2,1)S(1)}, u32[]{:S(2)}, u32[]{:S(2)}) %collective-permute-start.3) | collective-permute-done | bytes 331808 | tf_op jit(solution)/shard_map/ppermute | solution.py:852
  37.6 4.1 collective-permute-start.4
  41.7 18.1 %collective-permute-done.4 = bf16[144,1152]{1,0:T(8,128)(2,1)S(1)} collective-permute-done((bf16[144,1152]{1,0:T(8,128)(2,1)S(1)}, bf16[144,1152]{1,0:T(8,128)(2,1)S(1)}, u32[]{:S(2)}, u32[]{:S(2)}) %collective-permute-start.4) | collective-permute-done | bytes 331808 | tf_op jit(solution)/shard_map/ppermute | solution.py:852
  59.8 4.8 collective-permute-start.5
  64.7 8.0 %collective-permute-done.5 = bf16[144,1152]{1,0:T(8,128)(2,1)S(1)} collective-permute-done((bf16[144,1152]{1,0:T(8,128)(2,1)S(1)}, bf16[144,1152]{1,0:T(8,128)(2,1)S(1)}, u32[]{:S(2)}, u32[]{:S(2)}) %collective-permute-start.5) | collective-permute-done | bytes 331808 | tf_op jit(solution)/shard_map/ppermute | solution.py:852
  77.7 4.0 cut.3
  81.7 61.9 %collective-permute-done.1.refs_2_ = bf16[288,729]{1,0:T(8,128)(2,1)} collective-permute-done((bf16[288,729]{1,0:T(8,128)(2,1)S(1)}, bf16[288,729]{1,0:T(8,128)(2,1)}, u32[]{:S(2)}, u32[]{:S(2)}) %collective-permute-start.1) | collective-permute-done | bytes 419936 | tf_op jit(solution)/shard_map/ppermute | solution.py:719
  143.6 6.0 %collective-permute-done.2.refs_3_ = bf16[288,729]{1,0:T(8,128)(2,1)} collective-permute-done((bf16[288,729]{1,0:T(8,128)(2,1)S(1)}, bf16[288,729]{1,0:T(8,128)(2,1)}, u32[]{:S(2)}, u32[]{:S(2)}) %collective-permute-start.2) | collective-permute-done | bytes 419936 | tf_op jit(solution)/shard_map/ppermute | solution.py:719
  149.6 7.5 %all-gather.3.cloned.1.call-done = bf16[4608,1280]{1,0:T(8,128)(2,1)} async-done(((bf16[288,1280]{1,0:T(8,128)(2,1)}), bf16[4608,1280]{1,0:T(8,128)(2,1)}) %all-gather.3.cloned.1.call-update) | async-done | bytes 11796496 | tf_op jit(solution)/shard_map/all_gather | solution.py:876
  157.1 14.8 %project.1 = (bf16[729,1152]{1,0:T(8,128)(2,1)}, bf16[729,1152]{1,0:T(8,128)(2,1)}, bf16[8,144,729]{2,1,0:T(8,128)(2,1)}, bf16[4,729,864]{2,1,0:T(8,128)(2,1)}, ...) custom-call(s32[13]{0:T(128)} %concatenate.27.place_ref.pick_ref, bf16[288,729]{1,0:T(8,128)(2,1)} %get-tuple-element.131.refs_0_, ...), custom_call_target="tpu_custom_call" | custom-call | flops 5804752896 | bytes 23607872 | tf_op jit(solution)/shard_map/project/pallas_call | solution.py:46
  174.1 29.2 %attend.1 = (bf16[4,729,288]{2,1,0:T(8,128)(2,1)}, f32[4,729,4]{2,1,0:T(8,128)}) custom-call(bf16[4,729,864]{2,1,0:T(8,128)(2,1)} %get-tuple-element.194.packed_ref), custom_call_target="tpu_custom_call" | custom-call | flops 7346640384 | bytes 6765120 | tf_op jit(solution)/shard_map/attend/pallas_call | solution.py:46
  203.9 11.3 %mix.1 = (f32[729,1152]{1,0:T(8,128)}, bf16[729,1152]{1,0:T(8,128)(2,1)}, bf16[8,144,729]{2,1,0:T(8,128)(2,1)}, bf16[1152,1152]{1,0:T(8,128)(2,1)}) custom-call(bf16[729,1152]{1,0:T(8,128)(2,1)} %get-tuple-element.218.image_ref, bf16[4,729,288]{2,1,0:T(8,128)(2,1)} %get-tuple-element.138.parts_ref.right_ref, ...), custom_call_target="tpu_custom_call" | custom-call | flops 1934917632 | bytes 48158208 | tf_op jit(solution)/shard_map/mix/pallas_call | solution.py:46
  217.0 21.1 %expand.1 = (bf16[4,729,1076]{2,1,0:T(8,128)(2,1)}, f32[4,729,1076]{2,1,0:T(8,128)}) custom-call(s32[13]{0:T(128)} %concatenate.27.place_ref.pick_ref, bf16[729,1152]{1,0:T(8,128)(2,1)} %get-tuple-element.144.ready_ref, f32[4,1,1076]{2,1,0:T(1,128)} %get-tuple-element.145.bias_ref, bf16[4,144,1152]{2,1,0:T(8,128)(2,1)} %copy-done.4, ...), custom_call_target="tpu_custom_call" | custom-call | flops 7229067264 | bytes 31139360 | tf_op jit(solution)/shard_map/expand/pallas_call | solution.py:46
  238.2 7.1 %collective-permute-done.15.refs_3_ = bf16[288,729]{1,0:T(8,128)(2,1)S(1)} collective-permute-done((bf16[288,729]{1,0:T(8,128)(2,1)S(1)}, bf16[288,729]{1,0:T(8,128)(2,1)S(1)}, u32[]{:S(2)}, u32[]{:S(2)}) %collective-permute-start.15) | collective-permute-done | bytes 419936 | tf_op jit(solution)/shard_map/ppermute | solution.py:719
  246.1 4.0 spread.1
  250.1 9.8 %share.8 = (bf16[4,144,1076]{2,1,0:T(8,128)(2,1)}, bf16[4,144,1076]{2,1,0:T(8,128)(2,1)}, bf16[4,144,1076]{2,1,0:T(8,128)(2,1)}, bf16[4,144,1076]{2,1,0:T(8,128)(2,1)}) custom-call(s32[13]{0:T(128)} %concatenate.27.place_ref.pick_ref, bf16[8,144,729]{2,1,0:T(8,128)(2,1)} %get-tuple-element.165.turned_ref, ...), custom_call_target="tpu_custom_call" | custom-call | flops 3614533632 | bytes 12913056 | tf_op jit(solution)/shard_map/share/pallas_call | solution.py:46
  260.9 18.0 %narrow.1 = (bf16[288,729]{1,0:T(8,128)(2,1)}, bf16[288,729]{1,0:T(8,128)(2,1)}, bf16[288,729]{1,0:T(8,128)(2,1)}, bf16[288,729]{1,0:T(8,128)(2,1)}) custom-call(s32[13]{0:T(128)} %concatenate.27.place_ref.pick_ref, f32[729,1152]{1,0:T(8,128)} %get-tuple-element.163.hidden_ref, bf16[4,729,1076]{2,1,0:T(8,128)(2,1)} %get-tuple-element.151.right_ref.active_ref, ...), custom_call_target="tpu_custom_call" | custom-call | flops 7229067264 | bytes 21967776 | tf_op jit(solution)/shard_map/narrow/pallas_call | solution.py:46
  280.8 11.0 %share.9 = (bf16[2,4,144,1076]{3,2,1,0:T(8,128)(2,1)}, bf16[2,4,144,1076]{3,2,1,0:T(8,128)(2,1)}) custom-call(s32[13]{0:T(128)} %concatenate.27.place_ref.pick_ref, bf16[8,144,729]{2,1,0:T(8,128)(2,1)} %get-tuple-element.165.turned_ref, bf16[4,729,1076]{2,1,0:T(8,128)(2,1)} %get-tuple-element.151.right_ref.active_ref, ...), custom_call_target="tpu_custom_call" | custom-call | flops 3614533632 | bytes 17871264 | tf_op jit(solution)/shard_map/share/pallas_call | solution.py:46
  293.2 35.2 %feed_back.1 = (bf16[4,729,1076]{2,1,0:T(8,128)(2,1)}, f32[729,1152]{1,0:T(8,128)}, bf16[729,1152]{1,0:T(8,128)(2,1)}, bf16[8,144,729]{2,1,0:T(8,128)(2,1)}, f32[8,1152]{1,0:T(8,128)}) custom-call(s32[13]{0:T(128)} %concatenate.27.place_ref.pick_ref, bf16[729,1152]{1,0:T(8,128)(2,1)} %get-tuple-element.170.grad_ref, f32[1,1152]{1,0:T(1,128)} %get-tuple-element.171.sum_ref, ...), custom_call_target="tpu_custom_call" | custom-call | flops 14458134528 | bytes 51895008 | tf_op jit(solution)/shard_map/feed_back/pallas_call | solution.py:46
  330.1 3.8 place.2
  333.9 9.8 %share.10 = (bf16[4,144,1076]{2,1,0:T(8,128)(2,1)}, bf16[4,144,1076]{2,1,0:T(8,128)(2,1)}, bf16[4,144,1076]{2,1,0:T(8,128)(2,1)}, bf16[4,144,1076]{2,1,0:T(8,128)(2,1)}) custom-call(s32[13]{0:T(128)} %concatenate.27.place_ref.pick_ref, bf16[8,144,729]{2,1,0:T(8,128)(2,1)} %get-tuple-element.184.turned_ref, bf16[4,729,1076]{2,1,0:T(8,128)(2,1)} %get-tuple-element.173.right_ref), custom_call_target="tpu_custom_call" | custom-call | flops 3614533632 | bytes 12913056 | tf_op jit(solution)/shard_map/share/pallas_call | solution.py:46
  345.8 6.3 %mix_back.1.grad_ref = bf16[4,729,288]{2,1,0:T(8,128)(2,1)} custom-call(bf16[729,1152]{1,0:T(8,128)(2,1)} %get-tuple-element.182.grad_ref, bf16[1152,1152]{1,0:T(8,128)(2,1)} %get-tuple-element.183.weight_ref), custom_call_target="tpu_custom_call" | custom-call | flops 1934917632 | bytes 6013440 | tf_op jit(solution)/shard_map/mix_back/pallas_call | solution.py:46
  353.2 11.1 %share.11 = (bf16[2,4,144,1076]{3,2,1,0:T(8,128)(2,1)}, bf16[2,4,144,1076]{3,2,1,0:T(8,128)(2,1)}) custom-call(s32[13]{0:T(128)} %concatenate.27.place_ref.pick_ref, bf16[8,144,729]{2,1,0:T(8,128)(2,1)} %get-tuple-element.184.turned_ref, bf16[4,729,1076]{2,1,0:T(8,128)(2,1)} %get-tuple-element.173.right_ref, ...), custom_call_target="tpu_custom_call" | custom-call | flops 3614533632 | bytes 17871264 | tf_op jit(solution)/shard_map/share/pallas_call | solution.py:46
  364.9 2.7 fusion.6
  369.0 37.1 %attend_back.1 = (bf16[4,729,864]{2,1,0:T(8,128)(2,1)}, f32[4,1,864]{2,1,0:T(1,128)}) custom-call(bf16[4,729,864]{2,1,0:T(8,128)(2,1)} %get-tuple-element.194.packed_ref, f32[4,4,729]{2,1,0:T(4,128)} %bitcast.87, bf16[4,729,288]{2,1,0:T(8,128)(2,1)} %mix_back.1.grad_ref), custom_call_target="tpu_custom_call" | custom-call | flops 18366601216 | bytes 11817792 | tf_op jit(solution)/shard_map/attend_back/pallas_call | solution.py:46
  406.0 8.5 %share.12 = (bf16[4,144,864]{2,1,0:T(8,128)(2,1)}, bf16[4,144,864]{2,1,0:T(8,128)(2,1)}, bf16[4,144,864]{2,1,0:T(8,128)(2,1)}, bf16[4,144,864]{2,1,0:T(8,128)(2,1)}) custom-call(s32[13]{0:T(128)} %concatenate.27.place_ref.pick_ref, bf16[8,144,729]{2,1,0:T(8,128)(2,1)} %get-tuple-element.205.turned_ref, ...), custom_call_target="tpu_custom_call" | custom-call | flops 2902376448 | bytes 10699776 | tf_op jit(solution)/shard_map/share/pallas_call | solution.py:46
  414.5 6.2 %share.13 = (bf16[4,144,288]{2,1,0:T(8,128)(2,1)}, bf16[4,144,288]{2,1,0:T(8,128)(2,1)}, bf16[4,144,288]{2,1,0:T(8,128)(2,1)}, bf16[4,144,288]{2,1,0:T(8,128)(2,1)}) custom-call(s32[13]{0:T(128)} %concatenate.27.place_ref.pick_ref, bf16[8,144,729]{2,1,0:T(8,128)(2,1)} %get-tuple-element.210.turned_ref, ...), custom_call_target="tpu_custom_call" | custom-call | flops 967458816 | bytes 4686336 | tf_op jit(solution)/shard_map/share/pallas_call | solution.py:46
  420.7 1.8 fusion.2
  424.9 2.7 fusion.7
  431.8 9.9 %share.14 = (bf16[2,4,144,384]{3,2,1,0:T(8,128)(2,1)}, bf16[2,4,144,384]{3,2,1,0:T(8,128)(2,1)}, bf16[2,4,144,480]{3,2,1,0:T(8,128)(2,1)}, bf16[2,4,144,480]{3,2,1,0:T(8,128)(2,1)}) custom-call(s32[13]{0:T(128)} %concatenate.27.place_ref.pick_ref, bf16[8,144,729]{2,1,0:T(8,128)(2,1)} %get-tuple-element.205.turned_ref, ...), custom_call_target="tpu_custom_call" | custom-call | flops 2902376448 | bytes 14681088 | tf_op jit(solution)/shard_map/share/pallas_call | solution.py:46
  442.8 6.8 %share.15 = (bf16[2,4,144,288]{3,2,1,0:T(8,128)(2,1)}, bf16[2,4,144,288]{3,2,1,0:T(8,128)(2,1)}) custom-call(s32[13]{0:T(128)} %concatenate.27.place_ref.pick_ref, bf16[8,144,729]{2,1,0:T(8,128)(2,1)} %get-tuple-element.210.turned_ref, bf16[4,729,288]{2,1,0:T(8,128)(2,1)} %get-tuple-element.138.parts_ref.right_ref, ...), custom_call_target="tpu_custom_call" | custom-call | flops 967458816 | bytes 6013440 | tf_op jit(solution)/shard_map/share/pallas_call | solution.py:46
  451.7 8.2 %collective-permute-done.38 = bf16[4,144,1076]{2,1,0:T(8,128)(2,1)} collective-permute-done((bf16[4,144,1076]{2,1,0:T(8,128)(2,1)}, bf16[4,144,1076]{2,1,0:T(8,128)(2,1)}, u32[]{:S(2)}, u32[]{:S(2)}) %collective-permute-start.38) | collective-permute-done | bytes 1239584 | tf_op jit(solution)/shard_map/ppermute | solution.py:719
  459.9 2.2 fusion.1
  464.1 18.2 %project_back.1 = (bf16[288,729]{1,0:T(8,128)(2,1)}, bf16[288,729]{1,0:T(8,128)(2,1)}, bf16[288,729]{1,0:T(8,128)(2,1)}, bf16[288,729]{1,0:T(8,128)(2,1)}, f32[8,1152]{1,0:T(8,128)}) custom-call(s32[13]{0:T(128)} %concatenate.27.place_ref.pick_ref, bf16[729,1152]{1,0:T(8,128)(2,1)} %get-tuple-element.218.image_ref, ...), custom_call_target="tpu_custom_call" | custom-call | flops 5804752896 | bytes 23641344 | tf_op jit(solution)/shard_map/project_back/pallas_call | solution.py:46
  482.3 2.0 fusion.14
  488.5 15.6 %collective-permute-done.41 = bf16[2,4,144,288]{3,2,1,0:T(8,128)(2,1)} collective-permute-done((bf16[2,4,144,288]{3,2,1,0:T(8,128)(2,1)}, bf16[2,4,144,288]{3,2,1,0:T(8,128)(2,1)}, u32[]{:S(2)}, u32[]{:S(2)}) %collective-permute-start.41) | collective-permute-done | bytes 663584 | tf_op jit(solution)/shard_map/ppermute | solution.py:719
  504.1 1.9 fusion.15
  507.5 5.2 collective-permute-done.42
  528.4 3.4 collective-permute-start.61
  532.8 3.4 collective-permute-start.54
  537.5 3.1 collective-permute-done.60
  543.1 3.1 collective-permute-done.53
  549.7 7.4 %collective-permute-done.64 = bf16[144,1152]{1,0:T(8,128)(2,1)} collective-permute-done((bf16[144,1152]{1,0:T(8,128)(2,1)S(1)}, bf16[144,1152]{1,0:T(8,128)(2,1)}, u32[]{:S(2)}, u32[]{:S(2)}) %collective-permute-start.64) | collective-permute-done | bytes 331808 | tf_op jit(solution)/shard_map/ppermute | solution.py:719
  557.1 5.6 collective-permute-done.63
  571.5 3.6 place.3
  578.2 1.6 copy.43
  (244 shorter events, 85.1 us)
Async XLA Ops:
  7.2 149.9 %all-gather.3.cloned.1.call-start = ((), (), s32[]{:S(2)}) async-start(), calls=%async_computation.3 | async-start | bytes 12533760 | tf_op jit(solution)/shard_map/all_gather | solution.py:876
  16.1 244.8 %all-gather.5.cloned.1.call-start = ((), (), s32[]{:S(2)}) async-start(), calls=%async_computation.4 | async-start | bytes 11280384 | tf_op jit(solution)/shard_map/all_gather | solution.py:876
  17.1 490.4 %reduce-scatter.6.cloned.1.call-start = ((), (), s32[]{:S(2)}) async-start(), calls=%async_computation.5 | async-start | bytes 1658880 | tf_op jit(solution)/shard_map/reduce_scatter | solution.py:800
  21.5 16.1 %collective-permute-start.3 = (bf16[144,1152]{1,0:T(8,128)(2,1)S(1)}, bf16[144,1152]{1,0:T(8,128)(2,1)S(1)}, u32[]{:S(2)}, u32[]{:S(2)}) collective-permute-start(bf16[144,1152]{1,0:T(8,128)(2,1)S(1)} %pad_dynamic-slice_fusion), channel_id=1, source_target_pairs={{0,1},{1,2},{2,3},{3,0},{4,5},{5,6},{6,7},{7,4},{8,9},{9,10},{10,1... | collective-permute-start | bytes 995336 | tf_op jit(solution)/shard_map/ppermute | solution.py:852
  37.6 22.2 %collective-permute-start.4 = (bf16[144,1152]{1,0:T(8,128)(2,1)S(1)}, bf16[144,1152]{1,0:T(8,128)(2,1)S(1)}, u32[]{:S(2)}, u32[]{:S(2)}) collective-permute-start(bf16[144,1152]{1,0:T(8,128)(2,1)S(1)} %collective-permute-done.3), channel_id=1, source_target_pairs={{0,1},{1,2},{2,3},{3,0},{4,5},{5,6},{6,7},{7,4},{8,9},{9,10},{10,1... | collective-permute-start | bytes 995336 | tf_op jit(solution)/shard_map/ppermute | solution.py:852
  59.8 12.8 %collective-permute-start.5 = (bf16[144,1152]{1,0:T(8,128)(2,1)S(1)}, bf16[144,1152]{1,0:T(8,128)(2,1)S(1)}, u32[]{:S(2)}, u32[]{:S(2)}) collective-permute-start(bf16[144,1152]{1,0:T(8,128)(2,1)S(1)} %collective-permute-done.4), channel_id=1, source_target_pairs={{0,1},{1,2},{2,3},{3,0},{4,5},{5,6},{6,7},{7,4},{8,9},{9,10},{10,1... | collective-permute-start | bytes 995336 | tf_op jit(solution)/shard_map/ppermute | solution.py:852
  72.9 99.0 %collective-permute-start.6 = (bf16[4,144,1152]{2,1,0:T(8,128)(2,1)S(1)}, bf16[4,144,1152]{2,1,0:T(8,128)(2,1)S(1)}, u32[]{:S(2)}, u32[]{:S(2)}) collective-permute-start(bf16[4,144,1152]{2,1,0:T(8,128)(2,1)S(1)} %pad_maximum_fusion.refs_0_), channel_id=1, source_target_pairs={{0,8},{4,12},{8,0},{12,4},{1,9},{5,13},{9,1},{13,5},{2,10},{6,14},... | collective-permute-start | bytes 3981320 | tf_op jit(solution)/shard_map/ppermute | solution.py:719
  74.3 69.3 %collective-permute-start.1 = (bf16[288,729]{1,0:T(8,128)(2,1)S(1)}, bf16[288,729]{1,0:T(8,128)(2,1)}, u32[]{:S(2)}, u32[]{:S(2)}) collective-permute-start(bf16[288,729]{1,0:T(8,128)(2,1)S(1)} %copy-done.31), channel_id=1, source_target_pairs={{0,8},{4,12},{8,0},{12,4},{1,9},{5,13},{9,1},{13,5},{2,10},{6,14},... | collective-permute-start | bytes 1259720 | tf_op jit(solution)/shard_map/ppermute | solution.py:719
  75.0 74.6 %collective-permute-start.2 = (bf16[288,729]{1,0:T(8,128)(2,1)S(1)}, bf16[288,729]{1,0:T(8,128)(2,1)}, u32[]{:S(2)}, u32[]{:S(2)}) collective-permute-start(bf16[288,729]{1,0:T(8,128)(2,1)S(1)} %copy-done.30), channel_id=1, source_target_pairs={{0,12},{4,8},{8,4},{12,0},{1,13},{5,9},{9,5},{13,1},{2,14},{6,10},... | collective-permute-start | bytes 1259720 | tf_op jit(solution)/shard_map/ppermute | solution.py:719
  76.2 97.3 %collective-permute-start.7 = (bf16[4,144,1152]{2,1,0:T(8,128)(2,1)S(1)}, bf16[4,144,1152]{2,1,0:T(8,128)(2,1)}, u32[]{:S(2)}, u32[]{:S(2)}) collective-permute-start(bf16[4,144,1152]{2,1,0:T(8,128)(2,1)S(1)} %pad_maximum_fusion.refs_0_), channel_id=1, source_target_pairs={{0,16},{16,0},{1,17},{17,1},{2,18},{18,2},{3,19},{19,3},{4,20},{20... | collective-permute-start | bytes 3981320 | tf_op jit(solution)/shard_map/ppermute | solution.py:719
  171.9 31.5 %collective-permute-start.8 = (bf16[4,144,1152]{2,1,0:T(8,128)(2,1)S(1)}, bf16[4,144,1152]{2,1,0:T(8,128)(2,1)}, u32[]{:S(2)}, u32[]{:S(2)}) collective-permute-start(bf16[4,144,1152]{2,1,0:T(8,128)(2,1)S(1)} %collective-permute-done.6.refs_1_), channel_id=1, source_target_pairs={{0,16},{16,0},{1,17},{17,1},{2,18},{18,2},{3,19},{19,3},{4,20},{20... | collective-permute-start | bytes 3981320 | tf_op jit(solution)/shard_map/ppermute | solution.py:719
  173.5 41.7 %collective-permute-start.10 = (bf16[4,144,1152]{2,1,0:T(8,128)(2,1)S(1)}, bf16[4,144,1152]{2,1,0:T(8,128)(2,1)}, u32[]{:S(2)}, u32[]{:S(2)}) collective-permute-start(bf16[4,144,1152]{2,1,0:T(8,128)(2,1)S(1)} %collective-permute-done.6.refs_1_), channel_id=1, source_target_pairs={{0,4},{4,0},{8,12},{12,8},{1,5},{5,1},{9,13},{13,9},{2,6},{6,2},{1... | collective-permute-start | bytes 3981320 | tf_op jit(solution)/shard_map/ppermute | solution.py:719
  173.5 42.0 %collective-permute-start.9 = (bf16[4,144,1152]{2,1,0:T(8,128)(2,1)S(1)}, bf16[4,144,1152]{2,1,0:T(8,128)(2,1)}, u32[]{:S(2)}, u32[]{:S(2)}) collective-permute-start(bf16[4,144,1152]{2,1,0:T(8,128)(2,1)S(1)} %pad_maximum_fusion.refs_0_), channel_id=1, source_target_pairs={{0,4},{4,0},{8,12},{12,8},{1,5},{5,1},{9,13},{13,9},{2,6},{6,2},{1... | collective-permute-start | bytes 3981320 | tf_op jit(solution)/shard_map/ppermute | solution.py:719
  174.0 43.0 %collective-permute-start.11 = (bf16[4,144,1152]{2,1,0:T(8,128)(2,1)}, bf16[4,144,1152]{2,1,0:T(8,128)(2,1)}, u32[]{:S(2)}, u32[]{:S(2)}) collective-permute-start(bf16[4,144,1152]{2,1,0:T(8,128)(2,1)} %collective-permute-done.7.refs_2_), channel_id=1, source_target_pairs={{0,4},{4,0},{8,12},{12,8},{1,5},{5,1},{9,13},{13,9},{2,6},{6,2},{1... | collective-permute-start | bytes 3981320 | tf_op jit(solution)/shard_map/ppermute | solution.py:719
  203.4 13.6 %collective-permute-start.12 = (bf16[4,144,1152]{2,1,0:T(8,128)(2,1)}, bf16[4,144,1152]{2,1,0:T(8,128)(2,1)}, u32[]{:S(2)}, u32[]{:S(2)}) collective-permute-start(bf16[4,144,1152]{2,1,0:T(8,128)(2,1)} %collective-permute-done.8.refs_3_), channel_id=1, source_target_pairs={{0,4},{4,0},{8,12},{12,8},{1,5},{5,1},{9,13},{13,9},{2,6},{6,2},{1... | collective-permute-start | bytes 3981320 | tf_op jit(solution)/shard_map/ppermute | solution.py:719
  203.8 34.3 %collective-permute-start.13 = (bf16[288,729]{1,0:T(8,128)(2,1)}, bf16[288,729]{1,0:T(8,128)(2,1)S(1)}, u32[]{:S(2)}, u32[]{:S(2)}) collective-permute-start(bf16[288,729]{1,0:T(8,128)(2,1)} %get-tuple-element.154), channel_id=1, source_target_pairs={{0,4},{4,0},{8,12},{12,8},{1,5},{5,1},{9,13},{13,9},{2,6},{6,2},{1... | collective-permute-start | bytes 1259720 | tf_op jit(solution)/shard_map/ppermute | solution.py:719
  215.1 23.0 %collective-permute-start.14 = (bf16[288,729]{1,0:T(8,128)(2,1)}, bf16[288,729]{1,0:T(8,128)(2,1)S(1)}, u32[]{:S(2)}, u32[]{:S(2)}) collective-permute-start(bf16[288,729]{1,0:T(8,128)(2,1)} %get-tuple-element.156), channel_id=1, source_target_pairs={{0,8},{4,12},{8,0},{12,4},{1,9},{5,13},{9,1},{13,5},{2,10},{6,14},... | collective-permute-start | bytes 1259720 | tf_op jit(solution)/shard_map/ppermute | solution.py:719
  215.5 29.8 %collective-permute-start.15 = (bf16[288,729]{1,0:T(8,128)(2,1)S(1)}, bf16[288,729]{1,0:T(8,128)(2,1)S(1)}, u32[]{:S(2)}, u32[]{:S(2)}) collective-permute-start(bf16[288,729]{1,0:T(8,128)(2,1)S(1)} %copy-done.29), channel_id=1, source_target_pairs={{0,12},{4,8},{8,4},{12,0},{1,13},{5,9},{9,5},{13,1},{2,14},{6,10},... | collective-permute-start | bytes 1259720 | tf_op jit(solution)/shard_map/ppermute | solution.py:719
  259.9 19.3 %collective-permute-start.17 = (bf16[4,144,1076]{2,1,0:T(8,128)(2,1)}, bf16[4,144,1076]{2,1,0:T(8,128)(2,1)S(1)}, u32[]{:S(2)}, u32[]{:S(2)}) collective-permute-start(bf16[4,144,1076]{2,1,0:T(8,128)(2,1)} %get-tuple-element.166), channel_id=1, source_target_pairs={{0,4},{4,0},{8,12},{12,8},{1,5},{5,1},{9,13},{13,9},{2,6},{6,2},{1... | collective-permute-start | bytes 3718664 | tf_op jit(solution)/shard_map/ppermute | solution.py:719
  260.1 19.4 %collective-permute-start.18 = (bf16[4,144,1076]{2,1,0:T(8,128)(2,1)}, bf16[4,144,1076]{2,1,0:T(8,128)(2,1)S(1)}, u32[]{:S(2)}, u32[]{:S(2)}) collective-permute-start(bf16[4,144,1076]{2,1,0:T(8,128)(2,1)} %get-tuple-element.167), channel_id=1, source_target_pairs={{0,4},{4,0},{8,12},{12,8},{1,5},{5,1},{9,13},{13,9},{2,6},{6,2},{1... | collective-permute-start | bytes 3718664 | tf_op jit(solution)/shard_map/ppermute | solution.py:719
  260.4 20.4 %collective-permute-start.19 = (bf16[4,144,1076]{2,1,0:T(8,128)(2,1)}, bf16[4,144,1076]{2,1,0:T(8,128)(2,1)}, u32[]{:S(2)}, u32[]{:S(2)}) collective-permute-start(bf16[4,144,1076]{2,1,0:T(8,128)(2,1)} %get-tuple-element.168), channel_id=1, source_target_pairs={{0,4},{4,0},{8,12},{12,8},{1,5},{5,1},{9,13},{13,9},{2,6},{6,2},{1... | collective-permute-start | bytes 3718664 | tf_op jit(solution)/shard_map/ppermute | solution.py:719
  260.6 20.2 %collective-permute-start.16 = (bf16[4,144,1076]{2,1,0:T(8,128)(2,1)}, bf16[4,144,1076]{2,1,0:T(8,128)(2,1)}, u32[]{:S(2)}, u32[]{:S(2)}) collective-permute-start(bf16[4,144,1076]{2,1,0:T(8,128)(2,1)} %get-tuple-element.162), channel_id=1, source_target_pairs={{0,4},{4,0},{8,12},{12,8},{1,5},{5,1},{9,13},{13,9},{2,6},{6,2},{1... | collective-permute-start | bytes 3718664 | tf_op jit(solution)/shard_map/ppermute | solution.py:719
  278.9 49.5 %collective-permute-start.20 = (bf16[288,729]{1,0:T(8,128)(2,1)}, bf16[288,729]{1,0:T(8,128)(2,1)S(1)}, u32[]{:S(2)}, u32[]{:S(2)}) collective-permute-start(bf16[288,729]{1,0:T(8,128)(2,1)} %get-tuple-element.175), channel_id=1, source_target_pairs={{0,4},{4,0},{8,12},{12,8},{1,5},{5,1},{9,13},{13,9},{2,6},{6,2},{1... | collective-permute-start | bytes 1259720 | tf_op jit(solution)/shard_map/ppermute | solution.py:719
  279.2 49.3 %collective-permute-start.21 = (bf16[288,729]{1,0:T(8,128)(2,1)}, bf16[288,729]{1,0:T(8,128)(2,1)S(1)}, u32[]{:S(2)}, u32[]{:S(2)}) collective-permute-start(bf16[288,729]{1,0:T(8,128)(2,1)} %get-tuple-element.176), channel_id=1, source_target_pairs={{0,8},{4,12},{8,0},{12,4},{1,9},{5,13},{9,1},{13,5},{2,10},{6,14},... | collective-permute-start | bytes 1259720 | tf_op jit(solution)/shard_map/ppermute | solution.py:719
  279.5 49.0 %collective-permute-start.22 = (bf16[288,729]{1,0:T(8,128)(2,1)}, bf16[288,729]{1,0:T(8,128)(2,1)S(1)}, u32[]{:S(2)}, u32[]{:S(2)}) collective-permute-start(bf16[288,729]{1,0:T(8,128)(2,1)} %get-tuple-element.177), channel_id=1, source_target_pairs={{0,12},{4,8},{8,4},{12,0},{1,13},{5,9},{9,5},{13,1},{2,14},{6,10},... | collective-permute-start | bytes 1259720 | tf_op jit(solution)/shard_map/ppermute | solution.py:719
  291.8 73.1 %collective-permute-start.27 = (bf16[2,4,144,1076]{3,2,1,0:T(8,128)(2,1)}, bf16[2,4,144,1076]{3,2,1,0:T(8,128)(2,1)}, u32[]{:S(2)}, u32[]{:S(2)}) collective-permute-start(bf16[2,4,144,1076]{3,2,1,0:T(8,128)(2,1)} %get-tuple-element.193), channel_id=1, source_target_pairs={{0,16},{16,0},{1,17},{17,1},{2,18},{18,2},{3,19},{19,3},{4,20},{20... | collective-permute-start | bytes 7437320 | tf_op jit(solution)/shard_map/ppermute | solution.py:719
  364.3 60.6 %collective-permute-start.29 = (bf16[2,4,144,1076]{3,2,1,0:T(8,128)(2,1)}, bf16[2,4,144,1076]{3,2,1,0:T(8,128)(2,1)}, u32[]{:S(2)}, u32[]{:S(2)}) collective-permute-start(bf16[2,4,144,1076]{3,2,1,0:T(8,128)(2,1)} %get-tuple-element.204), channel_id=1, source_target_pairs={{0,16},{16,0},{1,17},{17,1},{2,18},{18,2},{3,19},{19,3},{4,20},{20... | collective-permute-start | bytes 7437320 | tf_op jit(solution)/shard_map/ppermute | solution.py:719
  367.6 53.1 %collective-permute-start.28 = (bf16[4,144,1076]{2,1,0:T(8,128)(2,1)}, bf16[4,144,1076]{2,1,0:T(8,128)(2,1)S(1)}, u32[]{:S(2)}, u32[]{:S(2)}) collective-permute-start(bf16[4,144,1076]{2,1,0:T(8,128)(2,1)} %fusion.6), channel_id=1, source_target_pairs={{0,8},{4,12},{8,0},{12,4},{1,9},{5,13},{9,1},{13,5},{2,10},{6,14},... | collective-permute-start | bytes 3718664 | tf_op jit(solution)/shard_map/ppermute | solution.py:719
  423.7 118.6 %reduce-scatter.8.cloned.1.call-start = ((), (), s32[]{:S(2)}) async-start(), calls=%async_computation.6 | async-start | bytes 1658880 | tf_op jit(solution)/shard_map/reduce_scatter | solution.py:800
  427.6 32.3 %collective-permute-start.38 = (bf16[4,144,1076]{2,1,0:T(8,128)(2,1)}, bf16[4,144,1076]{2,1,0:T(8,128)(2,1)}, u32[]{:S(2)}, u32[]{:S(2)}) collective-permute-start(bf16[4,144,1076]{2,1,0:T(8,128)(2,1)} %fusion.7), channel_id=1, source_target_pairs={{0,8},{4,12},{8,0},{12,4},{1,9},{5,13},{9,1},{13,5},{2,10},{6,14},... | collective-permute-start | bytes 3718664 | tf_op jit(solution)/shard_map/ppermute | solution.py:719
  428.3 13.4 %collective-permute-start.35 = (bf16[4,144,288]{2,1,0:T(8,128)(2,1)}, bf16[4,144,288]{2,1,0:T(8,128)(2,1)S(1)}, u32[]{:S(2)}, u32[]{:S(2)}) collective-permute-start(bf16[4,144,288]{2,1,0:T(8,128)(2,1)} %get-tuple-element.211), channel_id=1, source_target_pairs={{0,4},{4,0},{8,12},{12,8},{1,5},{5,1},{9,13},{13,9},{2,6},{6,2},{1... | collective-permute-start | bytes 995336 | tf_op jit(solution)/shard_map/ppermute | solution.py:719
  429.8 11.9 %collective-permute-start.36 = (bf16[4,144,288]{2,1,0:T(8,128)(2,1)}, bf16[4,144,288]{2,1,0:T(8,128)(2,1)S(1)}, u32[]{:S(2)}, u32[]{:S(2)}) collective-permute-start(bf16[4,144,288]{2,1,0:T(8,128)(2,1)} %get-tuple-element.212), channel_id=1, source_target_pairs={{0,4},{4,0},{8,12},{12,8},{1,5},{5,1},{9,13},{13,9},{2,6},{6,2},{1... | collective-permute-start | bytes 995336 | tf_op jit(solution)/shard_map/ppermute | solution.py:719
  431.2 10.5 %collective-permute-start.37 = (bf16[4,144,288]{2,1,0:T(8,128)(2,1)}, bf16[4,144,288]{2,1,0:T(8,128)(2,1)S(1)}, u32[]{:S(2)}, u32[]{:S(2)}) collective-permute-start(bf16[4,144,288]{2,1,0:T(8,128)(2,1)} %get-tuple-element.213), channel_id=1, source_target_pairs={{0,4},{4,0},{8,12},{12,8},{1,5},{5,1},{9,13},{13,9},{2,6},{6,2},{1... | collective-permute-start | bytes 995336 | tf_op jit(solution)/shard_map/ppermute | solution.py:719
  431.4 10.4 %collective-permute-start.34 = (bf16[4,144,288]{2,1,0:T(8,128)(2,1)}, bf16[4,144,288]{2,1,0:T(8,128)(2,1)}, u32[]{:S(2)}, u32[]{:S(2)}) collective-permute-start(bf16[4,144,288]{2,1,0:T(8,128)(2,1)} %get-tuple-element.200), channel_id=1, source_target_pairs={{0,4},{4,0},{8,12},{12,8},{1,5},{5,1},{9,13},{13,9},{2,6},{6,2},{1... | collective-permute-start | bytes 995336 | tf_op jit(solution)/shard_map/ppermute | solution.py:719
  449.6 32.7 %collective-permute-start.39 = (bf16[2,4,144,384]{3,2,1,0:T(8,128)(2,1)}, bf16[2,4,144,384]{3,2,1,0:T(8,128)(2,1)}, u32[]{:S(2)}, u32[]{:S(2)}) collective-permute-start(bf16[2,4,144,384]{3,2,1,0:T(8,128)(2,1)} %get-tuple-element.225), channel_id=1, source_target_pairs={{0,16},{16,0},{1,17},{17,1},{2,18},{18,2},{3,19},{19,3},{4,20},{20... | collective-permute-start | bytes 2654216 | tf_op jit(solution)/shard_map/ppermute | solution.py:719
  451.1 34.6 %collective-permute-start.40 = (bf16[2,4,144,480]{3,2,1,0:T(8,128)(2,1)}, bf16[2,4,144,480]{3,2,1,0:T(8,128)(2,1)}, u32[]{:S(2)}, u32[]{:S(2)}) collective-permute-start(bf16[2,4,144,480]{3,2,1,0:T(8,128)(2,1)} %get-tuple-element.227), channel_id=1, source_target_pairs={{0,8},{4,12},{8,0},{12,4},{1,9},{5,13},{9,1},{13,5},{2,10},{6,14},... | collective-permute-start | bytes 3317768 | tf_op jit(solution)/shard_map/ppermute | solution.py:719
  463.3 100.7 %reduce-scatter.10.cloned.1.call-start = ((), (), s32[]{:S(2)}) async-start(), calls=%async_computation.7 | async-start | bytes 1843200
  463.3 40.8 %collective-permute-start.41 = (bf16[2,4,144,288]{3,2,1,0:T(8,128)(2,1)}, bf16[2,4,144,288]{3,2,1,0:T(8,128)(2,1)}, u32[]{:S(2)}, u32[]{:S(2)}) collective-permute-start(bf16[2,4,144,288]{3,2,1,0:T(8,128)(2,1)} %get-tuple-element.229), channel_id=1, source_target_pairs={{0,8},{4,12},{8,0},{12,4},{1,9},{5,13},{9,1},{13,5},{2,10},{6,14},... | collective-permute-start | bytes 1990664 | tf_op jit(solution)/shard_map/ppermute | solution.py:719
  484.4 28.3 %collective-permute-start.42 = (bf16[4,144,384]{2,1,0:T(8,128)(2,1)}, bf16[4,144,384]{2,1,0:T(8,128)(2,1)}, u32[]{:S(2)}, u32[]{:S(2)}) collective-permute-start(bf16[4,144,384]{2,1,0:T(8,128)(2,1)} %fusion.14), channel_id=1, source_target_pairs={{0,8},{4,12},{8,0},{12,4},{1,9},{5,13},{9,1},{13,5},{2,10},{6,14},... | collective-permute-start | bytes 1327112 | tf_op jit(solution)/shard_map/ppermute | solution.py:719
  486.9 27.1 %collective-permute-start.43 = (bf16[4,144,480]{2,1,0:T(8,128)(2,1)S(1)}, bf16[4,144,480]{2,1,0:T(8,128)(2,1)}, u32[]{:S(2)}, u32[]{:S(2)}) collective-permute-start(bf16[4,144,480]{2,1,0:T(8,128)(2,1)S(1)} %fusion.13), channel_id=1, source_target_pairs={{0,16},{16,0},{1,17},{17,1},{2,18},{18,2},{3,19},{19,3},{4,20},{20... | collective-permute-start | bytes 1658888 | tf_op jit(solution)/shard_map/ppermute | solution.py:719
  506.0 10.8 %collective-permute-start.44 = (bf16[4,144,288]{2,1,0:T(8,128)(2,1)}, bf16[4,144,288]{2,1,0:T(8,128)(2,1)}, u32[]{:S(2)}, u32[]{:S(2)}) collective-permute-start(bf16[4,144,288]{2,1,0:T(8,128)(2,1)} %fusion.15), channel_id=1, source_target_pairs={{0,16},{16,0},{1,17},{17,1},{2,18},{18,2},{3,19},{19,3},{4,20},{20... | collective-permute-start | bytes 995336 | tf_op jit(solution)/shard_map/ppermute | solution.py:719
  536.2 10.1 %collective-permute-start.53 = (f32[8,1152]{1,0:T(8,128)S(1)}, f32[8,1152]{1,0:T(8,128)S(1)}, u32[]{:S(2)}, u32[]{:S(2)}) collective-permute-start(f32[8,1152]{1,0:T(8,128)S(1)} %add.219), channel_id=1, source_target_pairs={{0,2},{1,3},{2,0},{3,1},{4,6},{5,7},{6,4},{7,5},{8,10},{9,11},{10,... | collective-permute-start | bytes 110600 | tf_op jit(solution)/shard_map/ppermute | solution.py:719
  536.2 11.3 %collective-permute-start.52 = (f32[8,1152]{1,0:T(8,128)S(1)}, f32[8,1152]{1,0:T(8,128)S(1)}, u32[]{:S(2)}, u32[]{:S(2)}) collective-permute-start(f32[8,1152]{1,0:T(8,128)S(1)} %add.219), channel_id=1, source_target_pairs={{0,1},{1,0},{2,3},{3,2},{4,5},{5,4},{6,7},{7,6},{8,9},{9,8},{10,11... | collective-permute-start | bytes 110600 | tf_op jit(solution)/shard_map/ppermute | solution.py:719
  541.2 28.6 %collective-permute-start.45 = (bf16[288,729]{1,0:T(8,128)(2,1)}, bf16[288,729]{1,0:T(8,128)(2,1)S(1)}, u32[]{:S(2)}, u32[]{:S(2)}) collective-permute-start(bf16[288,729]{1,0:T(8,128)(2,1)} %get-tuple-element.239), channel_id=1, source_target_pairs={{0,4},{4,0},{8,12},{12,8},{1,5},{5,1},{9,13},{13,9},{2,6},{6,2},{1... | collective-permute-start | bytes 1259720 | tf_op jit(solution)/shard_map/ppermute | solution.py:719
  541.2 28.6 %collective-permute-start.46 = (bf16[288,729]{1,0:T(8,128)(2,1)}, bf16[288,729]{1,0:T(8,128)(2,1)S(1)}, u32[]{:S(2)}, u32[]{:S(2)}) collective-permute-start(bf16[288,729]{1,0:T(8,128)(2,1)} %get-tuple-element.240), channel_id=1, source_target_pairs={{0,8},{4,12},{8,0},{12,4},{1,9},{5,13},{9,1},{13,5},{2,10},{6,14},... | collective-permute-start | bytes 1259720 | tf_op jit(solution)/shard_map/ppermute | solution.py:719
  542.3 27.5 %collective-permute-start.47 = (bf16[288,729]{1,0:T(8,128)(2,1)}, bf16[288,729]{1,0:T(8,128)(2,1)S(1)}, u32[]{:S(2)}, u32[]{:S(2)}) collective-permute-start(bf16[288,729]{1,0:T(8,128)(2,1)} %get-tuple-element.241), channel_id=1, source_target_pairs={{0,12},{4,8},{8,4},{12,0},{1,13},{5,9},{9,5},{13,1},{2,14},{6,10},... | collective-permute-start | bytes 1259720 | tf_op jit(solution)/shard_map/ppermute | solution.py:719
  546.3 10.8 %collective-permute-start.64 = (bf16[144,1152]{1,0:T(8,128)(2,1)S(1)}, bf16[144,1152]{1,0:T(8,128)(2,1)}, u32[]{:S(2)}, u32[]{:S(2)}) collective-permute-start(bf16[144,1152]{1,0:T(8,128)(2,1)S(1)} %copy-done.24), channel_id=1, source_target_pairs={{0,16},{16,0},{1,17},{17,1},{2,18},{18,2},{3,19},{19,3},{4,20},{20... | collective-permute-start | bytes 995336 | tf_op jit(solution)/shard_map/ppermute | solution.py:719
  547.5 15.2 %collective-permute-start.63 = (bf16[144,1152]{1,0:T(8,128)(2,1)}, bf16[144,1152]{1,0:T(8,128)(2,1)}, u32[]{:S(2)}, u32[]{:S(2)}) collective-permute-start(bf16[144,1152]{1,0:T(8,128)(2,1)} %reduce-scatter.8.cloned.1.call-done), channel_id=1, source_target_pairs={{0,16},{16,0},{1,17},{17,1},{2,18},{18,2},{3,19},{19,3},{4,20},{20... | collective-permute-start | bytes 995336 | tf_op jit(solution)/shard_map/ppermute | solution.py:719
  (55 other events, 454.8 us)
Sparse Core Ops, SparseCore 0:
  16.2 140.8 all-gather.2
  159.4 95.2 all-gather.4
  423.8 31.7 reduce-scatter.5
  463.4 31.7 reduce-scatter.7
  519.5 38.5 reduce-scatter.9

commit v5 on v4

--- a/solution.py
+++ b/solution.py
@@ -13,9 +13,8 @@
 EPSILON = 1e-06
 QUERY_ROWS = 384
 ROWS = 256
-FC1 = True
-OUT = False
 COST = 1
+CUT = 8
 COLS = 256
 BF16 = jnp.bfloat16
 F32 = jnp.float32
@@ -662,33 +661,54 @@
     )
 
 
-def share_kernel(half, cuts, pick_ref, turned_ref, right_ref, *rest):
-    rows = turned_ref.shape[1]
-    picked = rest[-1]
-    count = picked.shape[0] // rows
+def share_kernel(half, cuts, starts, pick_ref, *refs):
+    pairs = len(starts)
+    turned_refs, right_refs = refs[:pairs], refs[pairs : 2 * pairs]
+    rest, picked = refs[2 * pairs : -pairs], refs[-pairs:]
+    rows = turned_refs[0].shape[1]
+    count = picked[0].shape[0] // rows
 
     @pl.when(pl.program_id(0) == 0)
     def _():
+        for turned_ref, chosen in zip(turned_refs, picked, strict=True):
+            for i in range(count):
+                chosen[i * rows : (i + 1) * rows] = turned_ref[pick_ref[1 + half * count + i]]
+
+    received, outs = (rest[: pairs * count], rest[pairs * count :]) if cuts else ((), rest)
+    each = len(outs) // max(1, len(cuts))
+    for p, (start, right_ref, chosen) in enumerate(zip(starts, right_refs, picked, strict=True)):
+        product = contract(chosen[...], right_ref[0], 1, 0)
+        stop = start + product.shape[1]
         for i in range(count):
-            picked[i * rows : (i + 1) * rows] = turned_ref[pick_ref[1 + half * count + i]]
-
-    product = contract(picked[...], right_ref[0], 1, 0)
-    if not cuts:
-        for i in range(count):
-            rest[i][0] = product[i * rows : (i + 1) * rows].astype(BF16)
-        return
-    received, outs = rest[:count], rest[count:-1]
-    each = len(outs) // len(cuts)
-    for i in range(count):
-        piece = product[i * rows : (i + 1) * rows] + received[i][0].astype(F32)
-        for n, (low, high, side_first) in enumerate(cuts):
-            place = (i // 2, i % 2) if side_first else (i % 2, i // 2)
-            outs[n * each + place[0]][place[1], 0] = piece[:, low:high].astype(BF16)
-
-
-def share(spot, turned_rows, right, received=(), cuts=()):
-    total, rows, seq = turned_rows.shape
-    groups, _, cols = right.shape
+            piece = product[i * rows : (i + 1) * rows]
+            if not cuts:
+                outs[p * count + i][0] = piece.astype(BF16)
+            else:
+                piece = piece + received[p * count + i][0].astype(F32)
+            for n, (low, high, side_first) in enumerate(cuts):
+                place = (i // 2, i % 2) if side_first else (i % 2, i // 2)
+                first, last = max(low, start), min(high, stop)
+                if first < last:
+                    outs[n * each + place[0]][place[1], 0, :, first - low : last - low] = piece[
+                        :, first - start : last - start
+                    ].astype(BF16)
+
+
+def side_by_side(pairs):
+    starts = []
+    cols = 0
+    for _, right in pairs:
+        starts.append(lanes(cols))
+        cols = starts[-1] + right.shape[2]
+    return starts, cols
+
+
+def share(spot, first, pairs, received=(), cuts=()):
+    turned_rows = [first] + [a for a, _ in pairs[1:]]
+    rights = [b for _, b in pairs]
+    total, rows, seq = first.shape
+    groups = rights[0].shape[0]
+    starts, cols = side_by_side(pairs)
     count = total // 2
 
     def two(size):
@@ -700,16 +720,21 @@
     if received:
         outs = [two(high - low) for low, high, _ in cuts for _ in range(count // 2)]
     else:
-        outs = [(struct((groups, rows, cols), BF16), nth((groups, rows, cols)))] * count
-    return call(
-        functools.partial(share_kernel, 0 if received else 1, cuts),
+        outs = [
+            (struct((groups, rows, b.shape[2]), BF16), nth((groups, rows, b.shape[2])))
+            for b in rights
+            for _ in range(count)
+        ]
+    return call(
+        functools.partial(share_kernel, 0 if received else 1, cuts, starts),
         "share",
         groups,
-        [(turned_rows, whole(turned_rows.shape)), (right, nth(right.shape))]
+        [(a, whole(a.shape)) for a in turned_rows]
+        + [(a, nth(a.shape)) for a in rights]
         + [(a, nth(a.shape)) for a in received],
         outs,
         2 * groups * count * rows * seq * cols,
-        [pltpu.VMEM((count * rows, seq), BF16)],
+        [pltpu.VMEM((count * rows, seq), BF16)] * len(pairs),
         (spot,),
     )
 
@@ -729,24 +754,22 @@
 
 
 class Sums:
-    def __init__(self, line, spot, turned_rows, right, halves, *cuts):
+    def __init__(self, line, spot, pairs, halves, *cuts):
         self.line = line
         self.spot = spot
-        self.rows = turned_rows
-        self.right = right
-        self.halves = halves
-        if halves == 1:
-            cuts = [(0, right.shape[2], True)]
+        self.pairs = pairs
+        if halves == 1 or not cuts:
+            cuts = [(0, side_by_side(pairs)[1], True)]
         self.cuts = [Cut(line, halves, *cut) for cut in cuts]
 
     def away(self):
-        sent = self.line(lambda a: share(self.spot, a, self.right), self.rows)
+        sent = self.line(lambda a: share(self.spot, a, self.pairs), self.pairs[0][0])
         self.arrived = [swap(a, "gx", 1) for a in sent]
 
     def keep(self):
         cuts = [(cut.low, cut.high, cut.side_first) for cut in self.cuts]
         kept = self.line(
-            lambda a: share(self.spot, a, self.right, self.arrived, cuts), self.rows
+            lambda a: share(self.spot, a, self.pairs, self.arrived, cuts), self.pairs[0][0]
         )
         each = len(kept) // len(cuts)
         for n, cut in enumerate(self.cuts):
@@ -965,7 +988,7 @@
         lambda a: spread(spot, [a] + grad_parts[1:], blocks), grad_parts[0]
     )
 
-    fc2 = Sums(line, spot, grad_turned, active, halves, (0, hidden_cols, True))
+    fc2 = Sums(line, spot, [(grad_turned, active)], halves)
     fc2.away()
     out_parts = line(lambda a: narrow(spot, a, active, second, wide, gx), hidden)
     out_parts = traded(out_parts)
@@ -979,29 +1002,29 @@
     ) = line(
         lambda a: feed_back(spot, a, grad_sum, hidden, wide, slope, second, pieces, blocks), grad_low
     )
-    fc1 = Sums(line, spot, turned_two, grad_first, halves, (0, hidden_cols, FC1))
-    out = Sums(line, spot, turned_hidden, mixture, halves, (0, head_cols, OUT))
+    fc1_pairs = [(turned_two, grad_first), (turned_hidden, mixture)]
+    fc1_cols = side_by_side(fc1_pairs)[1]
+    cut_at = fc1_cols * CUT // 1280 * 128
+    fc1 = Sums(line, spot, fc1_pairs, halves, (0, cut_at, True), (cut_at, fc1_cols, False))
     layer_out = line(
         lambda a: place(spot, [a] + out_parts[1:], turned_shape, copies), out_parts[0]
     )
     fc1.away()
     grad_mixture = line(lambda a: mix_back(a, whole_out, gy), grad_hidden_low)
+    fc2.send()
     fc1.keep()
-    fc2.send()
     packed_grad, packed_sum = line(
         lambda a: attend_back(a, log_total, grad_mixture, heads, list(range(heads))), packed
     )
     middle = max(1, triple // 256) * 128
     qkv = Sums(
-        line, spot, turned_one, packed_grad, halves, (0, middle, True), (middle, triple, False)
+        line, spot, [(turned_one, packed_grad)], halves, (0, middle, True), (middle, triple, False)
     )
     qkv.away()
-    out.away()
     fc2.total()
     fc2_end = Shared(line, halves, fc2)
     fc1.send()
     qkv.keep()
-    out.keep()
     fed_sums = everyone(line(lambda a: a, fed_sums))
     fc1.total()
     fc1_end = Shared(line, halves, fc1)
@@ -1010,22 +1033,21 @@
         image,
     )
     qkv.send()
-    out.send()
     grad_parts = traded(grad_parts)
+    fc2_end.trade()
+    fc1_end.trade()
+    qkv.total()
+    last_end = Shared(line, halves, qkv)
     late_sums = everyone(line(lambda a: a, late_sums))
-    fc2_end.trade()
-    qkv.total()
-    out.total()
-    last_end = Shared(line, halves, out, qkv)
-    fc1_end.trade()
     last_end.trade()
     tokens_grad = line(
         lambda a: place(spot, [a] + grad_parts[1:], turned_shape, copies), grad_parts[0]
     )
     grad_fc2 = fc2_end.end()[0].T
-    grad_fc1 = fc1_end.end()[0]
-    grad_out_weight, *grad_qkv = last_end.end()
-    grad_out_weight = grad_out_weight.T
+    grad_fc1 = jnp.concatenate(fc1_end.end(), axis=1)
+    grad_out_weight = grad_fc1[:, lanes(hidden_cols) :].T
+    grad_fc1 = grad_fc1[:, :hidden_cols]
+    grad_qkv = last_end.end()
     grad_qkv = jnp.concatenate(grad_qkv, axis=1).reshape(part, 3, head_cols)
 
     first_sums = lax.dynamic_index_in_dim(fed_sums, 4 + here, 0, False)[:hidden_cols]

time: 592 us -> 584 us (0.986)
  waiting for transfers between devices: 177 us -> 185 us
  Pallas kernels: 283 us -> 276 us
    ppermute x62, waiting for transfers between devices: 130 us -> 139 us  [swap(): return lax.ppermute(array, axis, [(i, i ^ bit) for i in range(size)])]
    pallas_call x22 -> x20, Pallas kernels: 283 us -> 276 us  [call(): pl.pallas_call(kernel, grid_spec=pltpu.PrefetchScalarGridSpec(num_scalar_...]
  transfers between devices with their start and end apart: 70 -> 70, of which waited for: 23 -> 23; matrix products, arithmetic and copies ran while one was open for 6% -> 5% of each run, Pallas kernels for 48% -> 48%
where the time goes in v5:
time: 584 us; the launch traced here: 578 us
  Pallas kernels  276 us (47%)
  waiting for transfers between devices  185 us (32%)
  starting transfers between devices  57.9 us (10%)
  other arithmetic  23 us (4%)
  local copies, waits for them, and re-layouts  22.2 us (4%)
  between operations  14.6 us (2%)
    pallas_call x20, Pallas kernels, call(): pl.pallas_call(kernel, grid_spec=pltpu.PrefetchScalarGridSpec(num_scalar_...  276 us
    ppermute x62, waiting for transfers between devices, swap(): return lax.ppermute(array, axis, [(i, i ^ bit) for i in range(size)])  139 us
    ppermute x62, starting transfers between devices, swap(): return lax.ppermute(array, axis, [(i, i ^ bit) for i in range(size)])  45.9 us
    ppermute x3, waiting for transfers between devices, __init__(): groups.append(lax.ppermute(groups[-1], 'gy', up))  39.2 us
    ppermute x3, starting transfers between devices, __init__(): groups.append(lax.ppermute(groups[-1], 'gy', up))  11.8 us
  transfers between devices with their start and end apart: 70, of which 23 were waited for; matrix products, arithmetic and copies ran while one was open for 5% of the time, Pallas kernels for 48%

profile of v5, /device:TPU:0, one launch (start us, length us, event | category | flops | bytes accessed | tf_op | source)
XLA Modules:
  0.0 578.4 jit_solution(14721381177001355060)
XLA Ops:
  17.8 3.7 cut.2
  21.6 3.1 collective-permute-start.3
  24.7 13.1 %collective-permute-done.3 = bf16[144,1152]{1,0:T(8,128)(2,1)S(1)} collective-permute-done((bf16[144,1152]{1,0:T(8,128)(2,1)S(1)}, bf16[144,1152]{1,0:T(8,128)(2,1)S(1)}, u32[]{:S(2)}, u32[]{:S(2)}) %collective-permute-start.3) | collective-permute-done | bytes 331808 | tf_op jit(solution)/shard_map/ppermute | solution.py:875
  37.8 4.1 collective-permute-start.4
  41.8 18.1 %collective-permute-done.4 = bf16[144,1152]{1,0:T(8,128)(2,1)S(1)} collective-permute-done((bf16[144,1152]{1,0:T(8,128)(2,1)S(1)}, bf16[144,1152]{1,0:T(8,128)(2,1)S(1)}, u32[]{:S(2)}, u32[]{:S(2)}) %collective-permute-start.4) | collective-permute-done | bytes 331808 | tf_op jit(solution)/shard_map/ppermute | solution.py:875
  60.0 4.7 collective-permute-start.5
  64.7 7.9 %collective-permute-done.5 = bf16[144,1152]{1,0:T(8,128)(2,1)S(1)} collective-permute-done((bf16[144,1152]{1,0:T(8,128)(2,1)S(1)}, bf16[144,1152]{1,0:T(8,128)(2,1)S(1)}, u32[]{:S(2)}, u32[]{:S(2)}) %collective-permute-start.5) | collective-permute-done | bytes 331808 | tf_op jit(solution)/shard_map/ppermute | solution.py:875
  77.8 3.9 cut.3
  81.7 61.7 %collective-permute-done.1.refs_2_ = bf16[288,729]{1,0:T(8,128)(2,1)} collective-permute-done((bf16[288,729]{1,0:T(8,128)(2,1)S(1)}, bf16[288,729]{1,0:T(8,128)(2,1)}, u32[]{:S(2)}, u32[]{:S(2)}) %collective-permute-start.1) | collective-permute-done | bytes 419936 | tf_op jit(solution)/shard_map/ppermute | solution.py:744
  143.4 6.0 %collective-permute-done.2.refs_3_ = bf16[288,729]{1,0:T(8,128)(2,1)} collective-permute-done((bf16[288,729]{1,0:T(8,128)(2,1)S(1)}, bf16[288,729]{1,0:T(8,128)(2,1)}, u32[]{:S(2)}, u32[]{:S(2)}) %collective-permute-start.2) | collective-permute-done | bytes 419936 | tf_op jit(solution)/shard_map/ppermute | solution.py:744
  149.4 6.7 %all-gather.3.cloned.1.call-done = bf16[4608,1280]{1,0:T(8,128)(2,1)} async-done(((bf16[288,1280]{1,0:T(8,128)(2,1)}), bf16[4608,1280]{1,0:T(8,128)(2,1)}) %all-gather.3.cloned.1.call-update) | async-done | bytes 11796496 | tf_op jit(solution)/shard_map/all_gather | solution.py:899
  156.1 14.8 %project.1 = (bf16[729,1152]{1,0:T(8,128)(2,1)}, bf16[729,1152]{1,0:T(8,128)(2,1)}, bf16[8,144,729]{2,1,0:T(8,128)(2,1)}, bf16[4,729,864]{2,1,0:T(8,128)(2,1)}, ...) custom-call(s32[13]{0:T(128)} %concatenate.30.place_ref.pick_ref, bf16[288,729]{1,0:T(8,128)(2,1)} %get-tuple-element.129.refs_0_, ...), custom_call_target="tpu_custom_call" | custom-call | flops 5804752896 | bytes 23607872 | tf_op jit(solution)/shard_map/project/pallas_call | solution.py:45
  170.9 2.3 collective-permute-start.8
  173.8 29.2 %attend.1 = (bf16[4,729,288]{2,1,0:T(8,128)(2,1)}, f32[4,729,4]{2,1,0:T(8,128)}) custom-call(bf16[4,729,864]{2,1,0:T(8,128)(2,1)} %get-tuple-element.197.packed_ref), custom_call_target="tpu_custom_call" | custom-call | flops 7346640384 | bytes 6765120 | tf_op jit(solution)/shard_map/attend/pallas_call | solution.py:45
  203.6 11.3 %mix.1 = (f32[729,1152]{1,0:T(8,128)}, bf16[729,1152]{1,0:T(8,128)(2,1)}, bf16[8,144,729]{2,1,0:T(8,128)(2,1)}, bf16[1152,1152]{1,0:T(8,128)(2,1)}) custom-call(bf16[729,1152]{1,0:T(8,128)(2,1)} %get-tuple-element.217.image_ref, bf16[4,729,288]{2,1,0:T(8,128)(2,1)} %get-tuple-element.136.parts_ref.refs_3_, ...), custom_call_target="tpu_custom_call" | custom-call | flops 1934917632 | bytes 48158208 | tf_op jit(solution)/shard_map/mix/pallas_call | solution.py:45
  215.1 1.6 collective-permute-start.15
  216.7 21.1 %expand.1 = (bf16[4,729,1076]{2,1,0:T(8,128)(2,1)}, f32[4,729,1076]{2,1,0:T(8,128)}) custom-call(s32[13]{0:T(128)} %concatenate.30.place_ref.pick_ref, bf16[729,1152]{1,0:T(8,128)(2,1)} %get-tuple-element.142.ready_ref, f32[4,1,1076]{2,1,0:T(1,128)} %get-tuple-element.143.bias_ref, bf16[4,144,1152]{2,1,0:T(8,128)(2,1)} %copy-done.4, ...), custom_call_target="tpu_custom_call" | custom-call | flops 7229067264 | bytes 31139360 | tf_op jit(solution)/shard_map/expand/pallas_call | solution.py:45
  237.9 7.1 %collective-permute-done.15.refs_3_ = bf16[288,729]{1,0:T(8,128)(2,1)S(1)} collective-permute-done((bf16[288,729]{1,0:T(8,128)(2,1)S(1)}, bf16[288,729]{1,0:T(8,128)(2,1)S(1)}, u32[]{:S(2)}, u32[]{:S(2)}) %collective-permute-start.15) | collective-permute-done | bytes 419936 | tf_op jit(solution)/shard_map/ppermute | solution.py:744
  245.8 4.0 spread.1
  249.8 9.8 %share.6 = (bf16[4,144,1076]{2,1,0:T(8,128)(2,1)}, bf16[4,144,1076]{2,1,0:T(8,128)(2,1)}, bf16[4,144,1076]{2,1,0:T(8,128)(2,1)}, bf16[4,144,1076]{2,1,0:T(8,128)(2,1)}) custom-call(s32[13]{0:T(128)} %concatenate.30.place_ref.pick_ref, bf16[8,144,729]{2,1,0:T(8,128)(2,1)} %get-tuple-element.163.refs_0_, ...), custom_call_target="tpu_custom_call" | custom-call | flops 3614533632 | bytes 12913056 | tf_op jit(solution)/shard_map/share/pallas_call | solution.py:45
  260.6 18.0 %narrow.1 = (bf16[288,729]{1,0:T(8,128)(2,1)}, bf16[288,729]{1,0:T(8,128)(2,1)}, bf16[288,729]{1,0:T(8,128)(2,1)}, bf16[288,729]{1,0:T(8,128)(2,1)}) custom-call(s32[13]{0:T(128)} %concatenate.30.place_ref.pick_ref, f32[729,1152]{1,0:T(8,128)} %get-tuple-element.161.hidden_ref, bf16[4,729,1076]{2,1,0:T(8,128)(2,1)} %get-tuple-element.149.refs_1_.active_ref, ...), custom_call_target="tpu_custom_call" | custom-call | flops 7229067264 | bytes 21967776 | tf_op jit(solution)/shard_map/narrow/pallas_call | solution.py:45
  280.6 10.9 %share.7 = (bf16[2,4,144,1076]{3,2,1,0:T(8,128)(2,1)}, bf16[2,4,144,1076]{3,2,1,0:T(8,128)(2,1)}) custom-call(s32[13]{0:T(128)} %concatenate.30.place_ref.pick_ref, bf16[8,144,729]{2,1,0:T(8,128)(2,1)} %get-tuple-element.163.refs_0_, bf16[4,729,1076]{2,1,0:T(8,128)(2,1)} %get-tuple-element.149.refs_1_.active_ref, ...), custom_call_target="tpu_custom_call" | custom-call | flops 3614533632 | bytes 17871264 | tf_op jit(solution)/shard_map/share/pallas_call | solution.py:45
  293.0 35.1 %feed_back.1 = (bf16[4,729,1076]{2,1,0:T(8,128)(2,1)}, f32[729,1152]{1,0:T(8,128)}, bf16[729,1152]{1,0:T(8,128)(2,1)}, bf16[8,144,729]{2,1,0:T(8,128)(2,1)}, f32[8,1152]{1,0:T(8,128)}) custom-call(s32[13]{0:T(128)} %concatenate.30.place_ref.pick_ref, bf16[729,1152]{1,0:T(8,128)(2,1)} %get-tuple-element.168.grad_ref, f32[1,1152]{1,0:T(1,128)} %get-tuple-element.169.sum_ref, ...), custom_call_target="tpu_custom_call" | custom-call | flops 14458134528 | bytes 51895008 | tf_op jit(solution)/shard_map/feed_back/pallas_call | solution.py:45
  329.8 3.8 place.2
  333.6 11.7 %share.8 = (bf16[4,144,1076]{2,1,0:T(8,128)(2,1)}, bf16[4,144,1076]{2,1,0:T(8,128)(2,1)}, bf16[4,144,1076]{2,1,0:T(8,128)(2,1)}, bf16[4,144,1076]{2,1,0:T(8,128)...) custom-call(s32[13]{0:T(128)} %concatenate.30.place_ref.pick_ref, ...), custom_call_target="tpu_custom_call" | custom-call | flops 4837294080 | bytes 17599392 | tf_op jit(solution)/shard_map/share/pallas_call | solution.py:45
  350.1 6.5 %mix_back.1.grad_ref = bf16[4,729,288]{2,1,0:T(8,128)(2,1)} custom-call(bf16[729,1152]{1,0:T(8,128)(2,1)} %get-tuple-element.181.grad_ref, bf16[1152,1152]{1,0:T(8,128)(2,1)} %get-tuple-element.182.weight_ref), custom_call_target="tpu_custom_call" | custom-call | flops 1934917632 | bytes 6013440 | tf_op jit(solution)/shard_map/mix_back/pallas_call | solution.py:45
  356.9 1.6 fusion.7
  360.1 14.1 %share.9 = (bf16[2,4,144,1152]{3,2,1,0:T(8,128)(2,1)}, bf16[2,4,144,1152]{3,2,1,0:T(8,128)(2,1)}, bf16[2,4,144,288]{3,2,1,0:T(8,128)(2,1)}, bf16[2,4,144,288]{3,2,1,0:T(8,128)(2,1)}) custom-call(s32[13]{0:T(128)} %concatenate.30.place_ref.pick_ref, bf16[8,144,729]{2,1,0:T(8,128)(2,1)} %get-tuple-element.185.refs_0_, ...), custom_call_target="tpu_custom_call" | custom-call | flops 4837294080 | bytes 24234912 | tf_op jit(solution)/shard_map/share/pallas_call | solution.py:45
  374.8 37.0 %attend_back.1 = (bf16[4,729,864]{2,1,0:T(8,128)(2,1)}, f32[4,1,864]{2,1,0:T(1,128)}) custom-call(bf16[4,729,864]{2,1,0:T(8,128)(2,1)} %get-tuple-element.197.packed_ref, f32[4,4,729]{2,1,0:T(4,128)} %bitcast.88, bf16[4,729,288]{2,1,0:T(8,128)(2,1)} %mix_back.1.grad_ref), custom_call_target="tpu_custom_call" | custom-call | flops 18366601216 | bytes 11817792 | tf_op jit(solution)/shard_map/attend_back/pallas_call | solution.py:45
  412.6 8.5 %share.10 = (bf16[4,144,864]{2,1,0:T(8,128)(2,1)}, bf16[4,144,864]{2,1,0:T(8,128)(2,1)}, bf16[4,144,864]{2,1,0:T(8,128)(2,1)}, bf16[4,144,864]{2,1,0:T(8,128)(2,1)}) custom-call(s32[13]{0:T(128)} %concatenate.30.place_ref.pick_ref, bf16[8,144,729]{2,1,0:T(8,128)(2,1)} %get-tuple-element.208.refs_0_, bf16[4,729,864]{2,1,0:T(8,128)(2,1)} %get-tuple-element.199.refs_1_.packed_ref), custom_call_target="tpu_custom_call" | custom-call | flops 2902376448 | bytes 10699776 | tf_op jit(solution)/shard_map/share/pallas_call | solution.py:45
  421.1 2.2 fusion.2
  424.6 9.5 %collective-permute-done.33 = bf16[2,4,144,1152]{3,2,1,0:T(8,128)(2,1)} collective-permute-done((bf16[2,4,144,1152]{3,2,1,0:T(8,128)(2,1)}, bf16[2,4,144,1152]{3,2,1,0:T(8,128)(2,1)}, u32[]{:S(2)}, u32[]{:S(2)}) %collective-permute-start.33) | collective-permute-done | bytes 2654240 | tf_op jit(solution)/shard_map/ppermute | solution.py:744
  434.0 2.7 fusion.8
  438.8 1.9 fusion.16
  444.9 10.0 %share.11 = (bf16[2,4,144,384]{3,2,1,0:T(8,128)(2,1)}, bf16[2,4,144,384]{3,2,1,0:T(8,128)(2,1)}, bf16[2,4,144,480]{3,2,1,0:T(8,128)(2,1)}, bf16[2,4,144,480]{3,2,1,0:T(8,128)(2,1)}) custom-call(s32[13]{0:T(128)} %concatenate.30.place_ref.pick_ref, bf16[8,144,729]{2,1,0:T(8,128)(2,1)} %get-tuple-element.208.refs_0_, ...), custom_call_target="tpu_custom_call" | custom-call | flops 2902376448 | bytes 14681088 | tf_op jit(solution)/shard_map/share/pallas_call | solution.py:45
  454.9 12.3 %collective-permute-done.39 = bf16[4,144,1152]{2,1,0:T(8,128)(2,1)} collective-permute-done((bf16[4,144,1152]{2,1,0:T(8,128)(2,1)}, bf16[4,144,1152]{2,1,0:T(8,128)(2,1)}, u32[]{:S(2)}, u32[]{:S(2)}) %collective-permute-start.39) | collective-permute-done | bytes 1327136 | tf_op jit(solution)/shard_map/ppermute | solution.py:744
  467.2 2.2 fusion.1
  476.1 18.5 %project_back.1 = (bf16[288,729]{1,0:T(8,128)(2,1)}, bf16[288,729]{1,0:T(8,128)(2,1)}, bf16[288,729]{1,0:T(8,128)(2,1)}, bf16[288,729]{1,0:T(8,128)(2,1)}, f32[8,1152]{1,0:T(8,128)}) custom-call(s32[13]{0:T(128)} %concatenate.30.place_ref.pick_ref, bf16[729,1152]{1,0:T(8,128)(2,1)} %get-tuple-element.217.image_ref, ...), custom_call_target="tpu_custom_call" | custom-call | flops 5804752896 | bytes 23641344 | tf_op jit(solution)/shard_map/project_back/pallas_call | solution.py:45
  494.6 2.0 fusion.17
  497.2 3.1 collective-permute-done.42
  503.4 10.8 %collective-permute-done.58 = f32[8,1152]{1,0:T(8,128)S(1)} collective-permute-done((f32[8,1152]{1,0:T(8,128)S(1)}, f32[8,1152]{1,0:T(8,128)S(1)}, u32[]{:S(2)}, u32[]{:S(2)}) %collective-permute-start.58) | collective-permute-done | bytes 36896 | tf_op jit(solution)/shard_map/ppermute | solution.py:744
  514.2 3.3 collective-permute-start.61
  528.6 6.4 %collective-permute-done.64 = bf16[144,1152]{1,0:T(8,128)(2,1)S(1)} collective-permute-done((bf16[144,1152]{1,0:T(8,128)(2,1)S(1)}, bf16[144,1152]{1,0:T(8,128)(2,1)S(1)}, u32[]{:S(2)}, u32[]{:S(2)}) %collective-permute-start.64) | collective-permute-done | bytes 331808 | tf_op jit(solution)/shard_map/ppermute | solution.py:744
  535.4 3.4 collective-permute-start.54
  542.2 3.7 collective-permute-done.53
  548.8 8.3 %collective-permute-done.63 = bf16[144,1536]{1,0:T(8,128)(2,1)S(1)} collective-permute-done((bf16[144,1536]{1,0:T(8,128)(2,1)S(1)}, bf16[144,1536]{1,0:T(8,128)(2,1)S(1)}, u32[]{:S(2)}, u32[]{:S(2)}) %collective-permute-start.63) | collective-permute-done | bytes 442400 | tf_op jit(solution)/shard_map/ppermute | solution.py:744
  563.7 3.6 place.3
  567.3 2.7 collective-permute-done.62
  (247 shorter events, 75.6 us)
Async XLA Ops:
  7.2 148.9 %all-gather.3.cloned.1.call-start = ((), (), s32[]{:S(2)}) async-start(), calls=%async_computation.3 | async-start | bytes 12533760 | tf_op jit(solution)/shard_map/all_gather | solution.py:899
  16.1 244.6 %all-gather.5.cloned.1.call-start = ((), (), s32[]{:S(2)}) async-start(), calls=%async_computation.4 | async-start | bytes 11280384 | tf_op jit(solution)/shard_map/all_gather | solution.py:899
  17.1 501.6 %reduce-scatter.8.cloned.1.call-start = ((), (), s32[]{:S(2)}) async-start(), calls=%async_computation.6 | async-start | bytes 1658880 | tf_op jit(solution)/shard_map/reduce_scatter | solution.py:823
  21.6 16.2 %collective-permute-start.3 = (bf16[144,1152]{1,0:T(8,128)(2,1)S(1)}, bf16[144,1152]{1,0:T(8,128)(2,1)S(1)}, u32[]{:S(2)}, u32[]{:S(2)}) collective-permute-start(bf16[144,1152]{1,0:T(8,128)(2,1)S(1)} %pad_dynamic-slice_fusion), channel_id=1, source_target_pairs={{0,1},{1,2},{2,3},{3,0},{4,5},{5,6},{6,7},{7,4},{8,9},{9,10},{10,1... | collective-permute-start | bytes 995336 | tf_op jit(solution)/shard_map/ppermute | solution.py:875
  37.8 22.2 %collective-permute-start.4 = (bf16[144,1152]{1,0:T(8,128)(2,1)S(1)}, bf16[144,1152]{1,0:T(8,128)(2,1)S(1)}, u32[]{:S(2)}, u32[]{:S(2)}) collective-permute-start(bf16[144,1152]{1,0:T(8,128)(2,1)S(1)} %collective-permute-done.3), channel_id=1, source_target_pairs={{0,1},{1,2},{2,3},{3,0},{4,5},{5,6},{6,7},{7,4},{8,9},{9,10},{10,1... | collective-permute-start | bytes 995336 | tf_op jit(solution)/shard_map/ppermute | solution.py:875
  60.0 12.6 %collective-permute-start.5 = (bf16[144,1152]{1,0:T(8,128)(2,1)S(1)}, bf16[144,1152]{1,0:T(8,128)(2,1)S(1)}, u32[]{:S(2)}, u32[]{:S(2)}) collective-permute-start(bf16[144,1152]{1,0:T(8,128)(2,1)S(1)} %collective-permute-done.4), channel_id=1, source_target_pairs={{0,1},{1,2},{2,3},{3,0},{4,5},{5,6},{6,7},{7,4},{8,9},{9,10},{10,1... | collective-permute-start | bytes 995336 | tf_op jit(solution)/shard_map/ppermute | solution.py:875
  72.8 98.0 %collective-permute-start.6 = (bf16[4,144,1152]{2,1,0:T(8,128)(2,1)S(1)}, bf16[4,144,1152]{2,1,0:T(8,128)(2,1)S(1)}, u32[]{:S(2)}, u32[]{:S(2)}) collective-permute-start(bf16[4,144,1152]{2,1,0:T(8,128)(2,1)S(1)} %pad_maximum_fusion.refs_0_), channel_id=1, source_target_pairs={{0,8},{4,12},{8,0},{12,4},{1,9},{5,13},{9,1},{13,5},{2,10},{6,14},... | collective-permute-start | bytes 3981320 | tf_op jit(solution)/shard_map/ppermute | solution.py:744
  74.4 69.0 %collective-permute-start.1 = (bf16[288,729]{1,0:T(8,128)(2,1)S(1)}, bf16[288,729]{1,0:T(8,128)(2,1)}, u32[]{:S(2)}, u32[]{:S(2)}) collective-permute-start(bf16[288,729]{1,0:T(8,128)(2,1)S(1)} %copy-done.34), channel_id=1, source_target_pairs={{0,8},{4,12},{8,0},{12,4},{1,9},{5,13},{9,1},{13,5},{2,10},{6,14},... | collective-permute-start | bytes 1259720 | tf_op jit(solution)/shard_map/ppermute | solution.py:744
  75.3 74.1 %collective-permute-start.2 = (bf16[288,729]{1,0:T(8,128)(2,1)S(1)}, bf16[288,729]{1,0:T(8,128)(2,1)}, u32[]{:S(2)}, u32[]{:S(2)}) collective-permute-start(bf16[288,729]{1,0:T(8,128)(2,1)S(1)} %copy-done.33), channel_id=1, source_target_pairs={{0,12},{4,8},{8,4},{12,0},{1,13},{5,9},{9,5},{13,1},{2,14},{6,10},... | collective-permute-start | bytes 1259720 | tf_op jit(solution)/shard_map/ppermute | solution.py:744
  76.3 96.9 %collective-permute-start.7 = (bf16[4,144,1152]{2,1,0:T(8,128)(2,1)S(1)}, bf16[4,144,1152]{2,1,0:T(8,128)(2,1)}, u32[]{:S(2)}, u32[]{:S(2)}) collective-permute-start(bf16[4,144,1152]{2,1,0:T(8,128)(2,1)S(1)} %pad_maximum_fusion.refs_0_), channel_id=1, source_target_pairs={{0,16},{16,0},{1,17},{17,1},{2,18},{18,2},{3,19},{19,3},{4,20},{20... | collective-permute-start | bytes 3981320 | tf_op jit(solution)/shard_map/ppermute | solution.py:744
  170.9 32.1 %collective-permute-start.8 = (bf16[4,144,1152]{2,1,0:T(8,128)(2,1)S(1)}, bf16[4,144,1152]{2,1,0:T(8,128)(2,1)}, u32[]{:S(2)}, u32[]{:S(2)}) collective-permute-start(bf16[4,144,1152]{2,1,0:T(8,128)(2,1)S(1)} %collective-permute-done.6.refs_1_), channel_id=1, source_target_pairs={{0,16},{16,0},{1,17},{17,1},{2,18},{18,2},{3,19},{19,3},{4,20},{20... | collective-permute-start | bytes 3981320 | tf_op jit(solution)/shard_map/ppermute | solution.py:744
  173.2 41.7 %collective-permute-start.10 = (bf16[4,144,1152]{2,1,0:T(8,128)(2,1)S(1)}, bf16[4,144,1152]{2,1,0:T(8,128)(2,1)}, u32[]{:S(2)}, u32[]{:S(2)}) collective-permute-start(bf16[4,144,1152]{2,1,0:T(8,128)(2,1)S(1)} %collective-permute-done.6.refs_1_), channel_id=1, source_target_pairs={{0,4},{4,0},{8,12},{12,8},{1,5},{5,1},{9,13},{13,9},{2,6},{6,2},{1... | collective-permute-start | bytes 3981320 | tf_op jit(solution)/shard_map/ppermute | solution.py:744
  173.2 41.9 %collective-permute-start.9 = (bf16[4,144,1152]{2,1,0:T(8,128)(2,1)S(1)}, bf16[4,144,1152]{2,1,0:T(8,128)(2,1)}, u32[]{:S(2)}, u32[]{:S(2)}) collective-permute-start(bf16[4,144,1152]{2,1,0:T(8,128)(2,1)S(1)} %pad_maximum_fusion.refs_0_), channel_id=1, source_target_pairs={{0,4},{4,0},{8,12},{12,8},{1,5},{5,1},{9,13},{13,9},{2,6},{6,2},{1... | collective-permute-start | bytes 3981320 | tf_op jit(solution)/shard_map/ppermute | solution.py:744
  173.7 43.0 %collective-permute-start.11 = (bf16[4,144,1152]{2,1,0:T(8,128)(2,1)}, bf16[4,144,1152]{2,1,0:T(8,128)(2,1)}, u32[]{:S(2)}, u32[]{:S(2)}) collective-permute-start(bf16[4,144,1152]{2,1,0:T(8,128)(2,1)} %collective-permute-done.7.refs_2_), channel_id=1, source_target_pairs={{0,4},{4,0},{8,12},{12,8},{1,5},{5,1},{9,13},{13,9},{2,6},{6,2},{1... | collective-permute-start | bytes 3981320 | tf_op jit(solution)/shard_map/ppermute | solution.py:744
  203.0 13.7 %collective-permute-start.12 = (bf16[4,144,1152]{2,1,0:T(8,128)(2,1)}, bf16[4,144,1152]{2,1,0:T(8,128)(2,1)}, u32[]{:S(2)}, u32[]{:S(2)}) collective-permute-start(bf16[4,144,1152]{2,1,0:T(8,128)(2,1)} %collective-permute-done.8.refs_3_), channel_id=1, source_target_pairs={{0,4},{4,0},{8,12},{12,8},{1,5},{5,1},{9,13},{13,9},{2,6},{6,2},{1... | collective-permute-start | bytes 3981320 | tf_op jit(solution)/shard_map/ppermute | solution.py:744
  203.5 34.3 %collective-permute-start.13 = (bf16[288,729]{1,0:T(8,128)(2,1)}, bf16[288,729]{1,0:T(8,128)(2,1)S(1)}, u32[]{:S(2)}, u32[]{:S(2)}) collective-permute-start(bf16[288,729]{1,0:T(8,128)(2,1)} %get-tuple-element.152), channel_id=1, source_target_pairs={{0,4},{4,0},{8,12},{12,8},{1,5},{5,1},{9,13},{13,9},{2,6},{6,2},{1... | collective-permute-start | bytes 1259720 | tf_op jit(solution)/shard_map/ppermute | solution.py:744
  214.9 23.0 %collective-permute-start.14 = (bf16[288,729]{1,0:T(8,128)(2,1)}, bf16[288,729]{1,0:T(8,128)(2,1)S(1)}, u32[]{:S(2)}, u32[]{:S(2)}) collective-permute-start(bf16[288,729]{1,0:T(8,128)(2,1)} %get-tuple-element.154), channel_id=1, source_target_pairs={{0,8},{4,12},{8,0},{12,4},{1,9},{5,13},{9,1},{13,5},{2,10},{6,14},... | collective-permute-start | bytes 1259720 | tf_op jit(solution)/shard_map/ppermute | solution.py:744
  215.1 29.9 %collective-permute-start.15 = (bf16[288,729]{1,0:T(8,128)(2,1)S(1)}, bf16[288,729]{1,0:T(8,128)(2,1)S(1)}, u32[]{:S(2)}, u32[]{:S(2)}) collective-permute-start(bf16[288,729]{1,0:T(8,128)(2,1)S(1)} %copy-done.32), channel_id=1, source_target_pairs={{0,12},{4,8},{8,4},{12,0},{1,13},{5,9},{9,5},{13,1},{2,14},{6,10},... | collective-permute-start | bytes 1259720 | tf_op jit(solution)/shard_map/ppermute | solution.py:744
  259.6 19.3 %collective-permute-start.17 = (bf16[4,144,1076]{2,1,0:T(8,128)(2,1)}, bf16[4,144,1076]{2,1,0:T(8,128)(2,1)S(1)}, u32[]{:S(2)}, u32[]{:S(2)}) collective-permute-start(bf16[4,144,1076]{2,1,0:T(8,128)(2,1)} %get-tuple-element.164), channel_id=1, source_target_pairs={{0,4},{4,0},{8,12},{12,8},{1,5},{5,1},{9,13},{13,9},{2,6},{6,2},{1... | collective-permute-start | bytes 3718664 | tf_op jit(solution)/shard_map/ppermute | solution.py:744
  259.9 19.4 %collective-permute-start.18 = (bf16[4,144,1076]{2,1,0:T(8,128)(2,1)}, bf16[4,144,1076]{2,1,0:T(8,128)(2,1)S(1)}, u32[]{:S(2)}, u32[]{:S(2)}) collective-permute-start(bf16[4,144,1076]{2,1,0:T(8,128)(2,1)} %get-tuple-element.165), channel_id=1, source_target_pairs={{0,4},{4,0},{8,12},{12,8},{1,5},{5,1},{9,13},{13,9},{2,6},{6,2},{1... | collective-permute-start | bytes 3718664 | tf_op jit(solution)/shard_map/ppermute | solution.py:744
  260.1 20.4 %collective-permute-start.19 = (bf16[4,144,1076]{2,1,0:T(8,128)(2,1)}, bf16[4,144,1076]{2,1,0:T(8,128)(2,1)}, u32[]{:S(2)}, u32[]{:S(2)}) collective-permute-start(bf16[4,144,1076]{2,1,0:T(8,128)(2,1)} %get-tuple-element.166), channel_id=1, source_target_pairs={{0,4},{4,0},{8,12},{12,8},{1,5},{5,1},{9,13},{13,9},{2,6},{6,2},{1... | collective-permute-start | bytes 3718664 | tf_op jit(solution)/shard_map/ppermute | solution.py:744
  260.4 20.2 %collective-permute-start.16 = (bf16[4,144,1076]{2,1,0:T(8,128)(2,1)}, bf16[4,144,1076]{2,1,0:T(8,128)(2,1)}, u32[]{:S(2)}, u32[]{:S(2)}) collective-permute-start(bf16[4,144,1076]{2,1,0:T(8,128)(2,1)} %get-tuple-element.160), channel_id=1, source_target_pairs={{0,4},{4,0},{8,12},{12,8},{1,5},{5,1},{9,13},{13,9},{2,6},{6,2},{1... | collective-permute-start | bytes 3718664 | tf_op jit(solution)/shard_map/ppermute | solution.py:744
  278.7 49.4 %collective-permute-start.20 = (bf16[288,729]{1,0:T(8,128)(2,1)}, bf16[288,729]{1,0:T(8,128)(2,1)S(1)}, u32[]{:S(2)}, u32[]{:S(2)}) collective-permute-start(bf16[288,729]{1,0:T(8,128)(2,1)} %get-tuple-element.173), channel_id=1, source_target_pairs={{0,4},{4,0},{8,12},{12,8},{1,5},{5,1},{9,13},{13,9},{2,6},{6,2},{1... | collective-permute-start | bytes 1259720 | tf_op jit(solution)/shard_map/ppermute | solution.py:744
  278.9 49.2 %collective-permute-start.21 = (bf16[288,729]{1,0:T(8,128)(2,1)}, bf16[288,729]{1,0:T(8,128)(2,1)S(1)}, u32[]{:S(2)}, u32[]{:S(2)}) collective-permute-start(bf16[288,729]{1,0:T(8,128)(2,1)} %get-tuple-element.174), channel_id=1, source_target_pairs={{0,8},{4,12},{8,0},{12,4},{1,9},{5,13},{9,1},{13,5},{2,10},{6,14},... | collective-permute-start | bytes 1259720 | tf_op jit(solution)/shard_map/ppermute | solution.py:744
  279.2 48.9 %collective-permute-start.22 = (bf16[288,729]{1,0:T(8,128)(2,1)}, bf16[288,729]{1,0:T(8,128)(2,1)S(1)}, u32[]{:S(2)}, u32[]{:S(2)}) collective-permute-start(bf16[288,729]{1,0:T(8,128)(2,1)} %get-tuple-element.175), channel_id=1, source_target_pairs={{0,12},{4,8},{8,4},{12,0},{1,13},{5,9},{9,5},{13,1},{2,14},{6,10},... | collective-permute-start | bytes 1259720 | tf_op jit(solution)/shard_map/ppermute | solution.py:744
  291.5 65.0 %collective-permute-start.23 = (bf16[2,4,144,1076]{3,2,1,0:T(8,128)(2,1)}, bf16[2,4,144,1076]{3,2,1,0:T(8,128)(2,1)}, u32[]{:S(2)}, u32[]{:S(2)}) collective-permute-start(bf16[2,4,144,1076]{3,2,1,0:T(8,128)(2,1)} %get-tuple-element.184), channel_id=1, source_target_pairs={{0,16},{16,0},{1,17},{17,1},{2,18},{18,2},{3,19},{19,3},{4,20},{20... | collective-permute-start | bytes 7437320 | tf_op jit(solution)/shard_map/ppermute | solution.py:744
  346.1 14.0 %collective-permute-start.25 = (bf16[4,144,1076]{2,1,0:T(8,128)(2,1)}, bf16[4,144,1076]{2,1,0:T(8,128)(2,1)}, u32[]{:S(2)}, u32[]{:S(2)}) collective-permute-start(bf16[4,144,1076]{2,1,0:T(8,128)(2,1)} %get-tuple-element.186), channel_id=1, source_target_pairs={{0,4},{4,0},{8,12},{12,8},{1,5},{5,1},{9,13},{13,9},{2,6},{6,2},{1... | collective-permute-start | bytes 3718664 | tf_op jit(solution)/shard_map/ppermute | solution.py:744
  347.5 12.5 %collective-permute-start.26 = (bf16[4,144,1076]{2,1,0:T(8,128)(2,1)}, bf16[4,144,1076]{2,1,0:T(8,128)(2,1)}, u32[]{:S(2)}, u32[]{:S(2)}) collective-permute-start(bf16[4,144,1076]{2,1,0:T(8,128)(2,1)} %get-tuple-element.187), channel_id=1, source_target_pairs={{0,4},{4,0},{8,12},{12,8},{1,5},{5,1},{9,13},{13,9},{2,6},{6,2},{1... | collective-permute-start | bytes 3718664 | tf_op jit(solution)/shard_map/ppermute | solution.py:744
  348.1 11.9 %collective-permute-start.27 = (bf16[4,144,1076]{2,1,0:T(8,128)(2,1)}, bf16[4,144,1076]{2,1,0:T(8,128)(2,1)}, u32[]{:S(2)}, u32[]{:S(2)}) collective-permute-start(bf16[4,144,1076]{2,1,0:T(8,128)(2,1)} %get-tuple-element.188), channel_id=1, source_target_pairs={{0,4},{4,0},{8,12},{12,8},{1,5},{5,1},{9,13},{13,9},{2,6},{6,2},{1... | collective-permute-start | bytes 3718664 | tf_op jit(solution)/shard_map/ppermute | solution.py:744
  348.8 11.3 %collective-permute-start.24 = (bf16[4,144,1076]{2,1,0:T(8,128)(2,1)}, bf16[4,144,1076]{2,1,0:T(8,128)(2,1)}, u32[]{:S(2)}, u32[]{:S(2)}) collective-permute-start(bf16[4,144,1076]{2,1,0:T(8,128)(2,1)} %get-tuple-element.180), channel_id=1, source_target_pairs={{0,4},{4,0},{8,12},{12,8},{1,5},{5,1},{9,13},{13,9},{2,6},{6,2},{1... | collective-permute-start | bytes 3718664 | tf_op jit(solution)/shard_map/ppermute | solution.py:744
  358.6 62.5 %collective-permute-start.32 = (bf16[4,144,1076]{2,1,0:T(8,128)(2,1)S(1)}, bf16[4,144,1076]{2,1,0:T(8,128)(2,1)}, u32[]{:S(2)}, u32[]{:S(2)}) collective-permute-start(bf16[4,144,1076]{2,1,0:T(8,128)(2,1)S(1)} %fusion.7), channel_id=1, source_target_pairs={{0,8},{4,12},{8,0},{12,4},{1,9},{5,13},{9,1},{13,5},{2,10},{6,14},... | collective-permute-start | bytes 3718664 | tf_op jit(solution)/shard_map/ppermute | solution.py:744
  374.2 59.9 %collective-permute-start.33 = (bf16[2,4,144,1152]{3,2,1,0:T(8,128)(2,1)}, bf16[2,4,144,1152]{3,2,1,0:T(8,128)(2,1)}, u32[]{:S(2)}, u32[]{:S(2)}) collective-permute-start(bf16[2,4,144,1152]{3,2,1,0:T(8,128)(2,1)} %get-tuple-element.205), channel_id=1, source_target_pairs={{0,16},{16,0},{1,17},{17,1},{2,18},{18,2},{3,19},{19,3},{4,20},{20... | collective-permute-start | bytes 7962632 | tf_op jit(solution)/shard_map/ppermute | solution.py:744
  411.9 26.5 %collective-permute-start.34 = (bf16[2,4,144,288]{3,2,1,0:T(8,128)(2,1)}, bf16[2,4,144,288]{3,2,1,0:T(8,128)(2,1)}, u32[]{:S(2)}, u32[]{:S(2)}) collective-permute-start(bf16[2,4,144,288]{3,2,1,0:T(8,128)(2,1)} %get-tuple-element.207), channel_id=1, source_target_pairs={{0,8},{4,12},{8,0},{12,4},{1,9},{5,13},{9,1},{13,5},{2,10},{6,14},... | collective-permute-start | bytes 1990664 | tf_op jit(solution)/shard_map/ppermute | solution.py:744
  424.5 94.1 %reduce-scatter.6.cloned.1.call-start = ((), (), s32[]{:S(2)}) async-start(), calls=%async_computation.5 | async-start | bytes 2211840 | tf_op jit(solution)/shard_map/reduce_scatter | solution.py:823
  436.7 30.5 %collective-permute-start.39 = (bf16[4,144,1152]{2,1,0:T(8,128)(2,1)}, bf16[4,144,1152]{2,1,0:T(8,128)(2,1)}, u32[]{:S(2)}, u32[]{:S(2)}) collective-permute-start(bf16[4,144,1152]{2,1,0:T(8,128)(2,1)} %fusion.8), channel_id=1, source_target_pairs={{0,8},{4,12},{8,0},{12,4},{1,9},{5,13},{9,1},{13,5},{2,10},{6,14},... | collective-permute-start | bytes 3981320 | tf_op jit(solution)/shard_map/ppermute | solution.py:744
  442.1 27.3 %collective-permute-start.40 = (bf16[4,144,288]{2,1,0:T(8,128)(2,1)}, bf16[4,144,288]{2,1,0:T(8,128)(2,1)S(1)}, u32[]{:S(2)}, u32[]{:S(2)}) collective-permute-start(bf16[4,144,288]{2,1,0:T(8,128)(2,1)} %fusion.16), channel_id=1, source_target_pairs={{0,16},{16,0},{1,17},{17,1},{2,18},{18,2},{3,19},{19,3},{4,20},{20... | collective-permute-start | bytes 995336 | tf_op jit(solution)/shard_map/ppermute | solution.py:744
  472.0 86.1 %reduce-scatter.10.cloned.1.call-start = ((), (), s32[]{:S(2)}) async-start(), calls=%async_computation.7 | async-start | bytes 1290240
  472.1 22.5 %collective-permute-start.41 = (bf16[2,4,144,384]{3,2,1,0:T(8,128)(2,1)}, bf16[2,4,144,384]{3,2,1,0:T(8,128)(2,1)}, u32[]{:S(2)}, u32[]{:S(2)}) collective-permute-start(bf16[2,4,144,384]{3,2,1,0:T(8,128)(2,1)} %get-tuple-element.223), channel_id=1, source_target_pairs={{0,16},{16,0},{1,17},{17,1},{2,18},{18,2},{3,19},{19,3},{4,20},{20... | collective-permute-start | bytes 2654216 | tf_op jit(solution)/shard_map/ppermute | solution.py:744
  472.8 27.6 %collective-permute-start.42 = (bf16[2,4,144,480]{3,2,1,0:T(8,128)(2,1)}, bf16[2,4,144,480]{3,2,1,0:T(8,128)(2,1)S(1)}, u32[]{:S(2)}, u32[]{:S(2)}) collective-permute-start(bf16[2,4,144,480]{3,2,1,0:T(8,128)(2,1)} %get-tuple-element.225), channel_id=1, source_target_pairs={{0,8},{4,12},{8,0},{12,4},{1,9},{5,13},{9,1},{13,5},{2,10},{6,14},... | collective-permute-start | bytes 3317768 | tf_op jit(solution)/shard_map/ppermute | solution.py:744
  474.2 28.5 %collective-permute-start.57 = (f32[8,1152]{1,0:T(8,128)S(1)}, f32[8,1152]{1,0:T(8,128)S(1)}, u32[]{:S(2)}, u32[]{:S(2)}) collective-permute-start(f32[8,1152]{1,0:T(8,128)S(1)} %copy-done.25), channel_id=1, source_target_pairs={{0,12},{4,8},{8,4},{12,0},{1,13},{5,9},{9,5},{13,1},{2,14},{6,10},... | collective-permute-start | bytes 110600 | tf_op jit(solution)/shard_map/ppermute | solution.py:744
  474.2 28.5 %collective-permute-start.56 = (f32[8,1152]{1,0:T(8,128)S(1)}, f32[8,1152]{1,0:T(8,128)S(1)}, u32[]{:S(2)}, u32[]{:S(2)}) collective-permute-start(f32[8,1152]{1,0:T(8,128)S(1)} %copy-done.25), channel_id=1, source_target_pairs={{0,8},{4,12},{8,0},{12,4},{1,9},{5,13},{9,1},{13,5},{2,10},{6,14},... | collective-permute-start | bytes 110600 | tf_op jit(solution)/shard_map/ppermute | solution.py:744
  474.8 27.9 %collective-permute-start.55 = (f32[8,1152]{1,0:T(8,128)S(1)}, f32[8,1152]{1,0:T(8,128)S(1)}, u32[]{:S(2)}, u32[]{:S(2)}) collective-permute-start(f32[8,1152]{1,0:T(8,128)S(1)} %copy-done.25), channel_id=1, source_target_pairs={{0,4},{4,0},{8,12},{12,8},{1,5},{5,1},{9,13},{13,9},{2,6},{6,2},{1... | collective-permute-start | bytes 110600 | tf_op jit(solution)/shard_map/ppermute | solution.py:744
  496.6 22.0 %collective-permute-start.43 = (bf16[4,144,384]{2,1,0:T(8,128)(2,1)}, bf16[4,144,384]{2,1,0:T(8,128)(2,1)}, u32[]{:S(2)}, u32[]{:S(2)}) collective-permute-start(bf16[4,144,384]{2,1,0:T(8,128)(2,1)} %fusion.17), channel_id=1, source_target_pairs={{0,8},{4,12},{8,0},{12,4},{1,9},{5,13},{9,1},{13,5},{2,10},{6,14},... | collective-permute-start | bytes 1327112 | tf_op jit(solution)/shard_map/ppermute | solution.py:744
  501.3 18.7 %collective-permute-start.44 = (bf16[4,144,480]{2,1,0:T(8,128)(2,1)}, bf16[4,144,480]{2,1,0:T(8,128)(2,1)}, u32[]{:S(2)}, u32[]{:S(2)}) collective-permute-start(bf16[4,144,480]{2,1,0:T(8,128)(2,1)} %fusion.15), channel_id=1, source_target_pairs={{0,16},{16,0},{1,17},{17,1},{2,18},{18,2},{3,19},{19,3},{4,20},{20... | collective-permute-start | bytes 1658888 | tf_op jit(solution)/shard_map/ppermute | solution.py:744
  502.7 11.5 %collective-permute-start.58 = (f32[8,1152]{1,0:T(8,128)S(1)}, f32[8,1152]{1,0:T(8,128)S(1)}, u32[]{:S(2)}, u32[]{:S(2)}) collective-permute-start(f32[8,1152]{1,0:T(8,128)S(1)} %add_add_fusion.1), channel_id=1, source_target_pairs={{0,16},{16,0},{1,17},{17,1},{2,18},{18,2},{3,19},{19,3},{4,20},{20... | collective-permute-start | bytes 110600 | tf_op jit(solution)/shard_map/ppermute | solution.py:744
  526.3 35.7 %collective-permute-start.45 = (bf16[288,729]{1,0:T(8,128)(2,1)}, bf16[288,729]{1,0:T(8,128)(2,1)S(1)}, u32[]{:S(2)}, u32[]{:S(2)}) collective-permute-start(bf16[288,729]{1,0:T(8,128)(2,1)} %get-tuple-element.235), channel_id=1, source_target_pairs={{0,4},{4,0},{8,12},{12,8},{1,5},{5,1},{9,13},{13,9},{2,6},{6,2},{1... | collective-permute-start | bytes 1259720 | tf_op jit(solution)/shard_map/ppermute | solution.py:744
  526.3 35.7 %collective-permute-start.46 = (bf16[288,729]{1,0:T(8,128)(2,1)}, bf16[288,729]{1,0:T(8,128)(2,1)S(1)}, u32[]{:S(2)}, u32[]{:S(2)}) collective-permute-start(bf16[288,729]{1,0:T(8,128)(2,1)} %get-tuple-element.236), channel_id=1, source_target_pairs={{0,8},{4,12},{8,0},{12,4},{1,9},{5,13},{9,1},{13,5},{2,10},{6,14},... | collective-permute-start | bytes 1259720 | tf_op jit(solution)/shard_map/ppermute | solution.py:744
  542.2 19.8 %collective-permute-start.47 = (bf16[288,729]{1,0:T(8,128)(2,1)S(1)}, bf16[288,729]{1,0:T(8,128)(2,1)S(1)}, u32[]{:S(2)}, u32[]{:S(2)}) collective-permute-start(bf16[288,729]{1,0:T(8,128)(2,1)S(1)} %copy-done.31), channel_id=1, source_target_pairs={{0,12},{4,8},{8,4},{12,0},{1,13},{5,9},{9,5},{13,1},{2,14},{6,10},... | collective-permute-start | bytes 1259720 | tf_op jit(solution)/shard_map/ppermute | solution.py:744
  (59 other events, 476.3 us)
Sparse Core Ops, SparseCore 0:
  16.2 139.8 all-gather.2
  158.4 95.9 all-gather.4
  424.6 32.3 reduce-scatter.7
  472.1 38.3 reduce-scatter.5
  526.4 29.4 reduce-scatter.9

commit v6 on v5

--- a/solution.py
+++ b/solution.py
@@ -12,6 +12,7 @@
 MICRO = 2
 EPSILON = 1e-06
 QUERY_ROWS = 384
+BACK_ROWS = 768
 ROWS = 256
 COST = 1
 CUT = 8
@@ -112,7 +113,7 @@
         stop = start + HEAD_DIM
         keys = packed_ref[0, :, width + first : width + last]
         values = packed_ref[0, :, 2 * width + first : 2 * width + last]
-        for low, high in blocks_of(seq, QUERY_ROWS):
+        for low, high in blocks_of(seq, BACK_ROWS):
             queries = packed_ref[0, low:high, first:last]
             grads = grad_ref[0, low:high, first:last]
             scores = contract(keys, queries, 1, 1) * scaling
@@ -1025,7 +1026,6 @@
     fc2_end = Shared(line, halves, fc2)
     fc1.send()
     qkv.keep()
-    fed_sums = everyone(line(lambda a: a, fed_sums))
     fc1.total()
     fc1_end = Shared(line, halves, fc1)
     *grad_parts, late_sums = line(
@@ -1038,7 +1038,9 @@
     fc1_end.trade()
     qkv.total()
     last_end = Shared(line, halves, qkv)
-    late_sums = everyone(line(lambda a: a, late_sums))
+    top = fed_sums.shape[0]
+    sums = everyone(line(lambda a: jnp.concatenate([fed_sums, a]), late_sums))
+    fed_sums, late_sums = sums[:top], sums[top:]
     last_end.trade()
     tokens_grad = line(
         lambda a: place(spot, [a] + grad_parts[1:], turned_shape, copies), grad_parts[0]

time: 584 us -> 584 us (level)
  waiting for transfers between devices: 185 us -> 196 us
    reduce_scatter x2, waiting for transfers between devices: 0.01 us -> 6.18 us  [__init__(): lax.psum_scatter(wide.reshape(groups * rows, wide.shape[2]), 'gy', scatte...]
    ppermute x62 -> x55, starting transfers between devices: 45.9 us -> 40.4 us  [swap(): return lax.ppermute(array, axis, [(i, i ^ bit) for i in range(size)])]
    ppermute x62 -> x55, waiting for transfers between devices: 139 us -> 144 us  [swap(): return lax.ppermute(array, axis, [(i, i ^ bit) for i in range(size)])]
  transfers between devices with their start and end apart: 70 -> 63, of which waited for: 23 -> 27; matrix products, arithmetic and copies ran while one was open for 5% -> 5% of each run, Pallas kernels for 48% -> 47%
where the time goes in v6:
time: 584 us; the launch traced here: 579 us
  Pallas kernels  271 us (46%)
  waiting for transfers between devices  196 us (34%)
  starting transfers between devices  52.5 us (9%)
  other arithmetic  23 us (4%)
  local copies, waits for them, and re-layouts  22.2 us (4%)
  between operations  14.5 us (2%)
    pallas_call x20, Pallas kernels, call(): pl.pallas_call(kernel, grid_spec=pltpu.PrefetchScalarGridSpec(num_scalar_...  271 us
    ppermute x55, waiting for transfers between devices, swap(): return lax.ppermute(array, axis, [(i, i ^ bit) for i in range(size)])  144 us
    ppermute x55, starting transfers between devices, swap(): return lax.ppermute(array, axis, [(i, i ^ bit) for i in range(size)])  40.4 us
    ppermute x3, waiting for transfers between devices, __init__(): groups.append(lax.ppermute(groups[-1], 'gy', up))  39.2 us
    ppermute x3, starting transfers between devices, __init__(): groups.append(lax.ppermute(groups[-1], 'gy', up))  11.8 us
  transfers between devices with their start and end apart: 63, of which 27 were waited for; matrix products, arithmetic and copies ran while one was open for 5% of the time, Pallas kernels for 47%

profile of v6, /device:TPU:0, one launch (start us, length us, event | category | flops | bytes accessed | tf_op | source)
XLA Modules:
  0.0 578.9 jit_solution(13899343412149258731)
XLA Ops:
  17.8 3.7 cut.2
  21.6 3.1 collective-permute-start.3
  24.7 13.1 %collective-permute-done.3 = bf16[144,1152]{1,0:T(8,128)(2,1)S(1)} collective-permute-done((bf16[144,1152]{1,0:T(8,128)(2,1)S(1)}, bf16[144,1152]{1,0:T(8,128)(2,1)S(1)}, u32[]{:S(2)}, u32[]{:S(2)}) %collective-permute-start.3) | collective-permute-done | bytes 331808 | tf_op jit(solution)/shard_map/ppermute | solution.py:876
  37.8 4.1 collective-permute-start.4
  41.8 18.1 %collective-permute-done.4 = bf16[144,1152]{1,0:T(8,128)(2,1)S(1)} collective-permute-done((bf16[144,1152]{1,0:T(8,128)(2,1)S(1)}, bf16[144,1152]{1,0:T(8,128)(2,1)S(1)}, u32[]{:S(2)}, u32[]{:S(2)}) %collective-permute-start.4) | collective-permute-done | bytes 331808 | tf_op jit(solution)/shard_map/ppermute | solution.py:876
  60.0 4.7 collective-permute-start.5
  64.7 7.9 %collective-permute-done.5 = bf16[144,1152]{1,0:T(8,128)(2,1)S(1)} collective-permute-done((bf16[144,1152]{1,0:T(8,128)(2,1)S(1)}, bf16[144,1152]{1,0:T(8,128)(2,1)S(1)}, u32[]{:S(2)}, u32[]{:S(2)}) %collective-permute-start.5) | collective-permute-done | bytes 331808 | tf_op jit(solution)/shard_map/ppermute | solution.py:876
  77.8 4.0 cut.3
  81.8 61.6 %collective-permute-done.1.refs_2_ = bf16[288,729]{1,0:T(8,128)(2,1)} collective-permute-done((bf16[288,729]{1,0:T(8,128)(2,1)S(1)}, bf16[288,729]{1,0:T(8,128)(2,1)}, u32[]{:S(2)}, u32[]{:S(2)}) %collective-permute-start.1) | collective-permute-done | bytes 419936 | tf_op jit(solution)/shard_map/ppermute | solution.py:745
  143.4 6.0 %collective-permute-done.2.refs_3_ = bf16[288,729]{1,0:T(8,128)(2,1)} collective-permute-done((bf16[288,729]{1,0:T(8,128)(2,1)S(1)}, bf16[288,729]{1,0:T(8,128)(2,1)}, u32[]{:S(2)}, u32[]{:S(2)}) %collective-permute-start.2) | collective-permute-done | bytes 419936 | tf_op jit(solution)/shard_map/ppermute | solution.py:745
  149.4 6.7 %all-gather.3.cloned.1.call-done = bf16[4608,1280]{1,0:T(8,128)(2,1)} async-done(((bf16[288,1280]{1,0:T(8,128)(2,1)}), bf16[4608,1280]{1,0:T(8,128)(2,1)}) %all-gather.3.cloned.1.call-update) | async-done | bytes 11796496 | tf_op jit(solution)/shard_map/all_gather | solution.py:900
  156.1 14.8 %project.1 = (bf16[729,1152]{1,0:T(8,128)(2,1)}, bf16[729,1152]{1,0:T(8,128)(2,1)}, bf16[8,144,729]{2,1,0:T(8,128)(2,1)}, bf16[4,729,864]{2,1,0:T(8,128)(2,1)}, ...) custom-call(s32[13]{0:T(128)} %concatenate.33.place_ref.pick_ref, bf16[288,729]{1,0:T(8,128)(2,1)} %get-tuple-element.128.refs_0_, ...), custom_call_target="tpu_custom_call" | custom-call | flops 5804752896 | bytes 23607872 | tf_op jit(solution)/shard_map/project/pallas_call | solution.py:46
  170.9 2.3 collective-permute-start.8
  173.8 29.5 %attend.1 = (bf16[4,729,288]{2,1,0:T(8,128)(2,1)}, f32[4,729,4]{2,1,0:T(8,128)}) custom-call(bf16[4,729,864]{2,1,0:T(8,128)(2,1)} %get-tuple-element.195.packed_ref), custom_call_target="tpu_custom_call" | custom-call | flops 7346640384 | bytes 6765120 | tf_op jit(solution)/shard_map/attend/pallas_call | solution.py:46
  203.9 11.3 %mix.1 = (f32[729,1152]{1,0:T(8,128)}, bf16[729,1152]{1,0:T(8,128)(2,1)}, bf16[8,144,729]{2,1,0:T(8,128)(2,1)}, bf16[1152,1152]{1,0:T(8,128)(2,1)}) custom-call(bf16[729,1152]{1,0:T(8,128)(2,1)} %get-tuple-element.214.image_ref, bf16[4,729,288]{2,1,0:T(8,128)(2,1)} %get-tuple-element.135.parts_ref.refs_3_, ...), custom_call_target="tpu_custom_call" | custom-call | flops 1934917632 | bytes 48158208 | tf_op jit(solution)/shard_map/mix/pallas_call | solution.py:46
  217.1 21.1 %expand.1 = (bf16[4,729,1076]{2,1,0:T(8,128)(2,1)}, f32[4,729,1076]{2,1,0:T(8,128)}) custom-call(s32[13]{0:T(128)} %concatenate.33.place_ref.pick_ref, bf16[729,1152]{1,0:T(8,128)(2,1)} %get-tuple-element.141.ready_ref, f32[4,1,1076]{2,1,0:T(1,128)} %get-tuple-element.142.bias_ref, bf16[4,144,1152]{2,1,0:T(8,128)(2,1)} %copy-done.4, ...), custom_call_target="tpu_custom_call" | custom-call | flops 7229067264 | bytes 31139360 | tf_op jit(solution)/shard_map/expand/pallas_call | solution.py:46
  238.2 6.8 %collective-permute-done.15.refs_3_ = bf16[288,729]{1,0:T(8,128)(2,1)S(1)} collective-permute-done((bf16[288,729]{1,0:T(8,128)(2,1)S(1)}, bf16[288,729]{1,0:T(8,128)(2,1)S(1)}, u32[]{:S(2)}, u32[]{:S(2)}) %collective-permute-start.15) | collective-permute-done | bytes 419936 | tf_op jit(solution)/shard_map/ppermute | solution.py:745
  245.8 4.0 spread.1
  249.8 9.8 %share.6 = (bf16[4,144,1076]{2,1,0:T(8,128)(2,1)}, bf16[4,144,1076]{2,1,0:T(8,128)(2,1)}, bf16[4,144,1076]{2,1,0:T(8,128)(2,1)}, bf16[4,144,1076]{2,1,0:T(8,128)(2,1)}) custom-call(s32[13]{0:T(128)} %concatenate.33.place_ref.pick_ref, bf16[8,144,729]{2,1,0:T(8,128)(2,1)} %get-tuple-element.162.refs_0_, ...), custom_call_target="tpu_custom_call" | custom-call | flops 3614533632 | bytes 12913056 | tf_op jit(solution)/shard_map/share/pallas_call | solution.py:46
  260.6 17.8 %narrow.1 = (bf16[288,729]{1,0:T(8,128)(2,1)}, bf16[288,729]{1,0:T(8,128)(2,1)}, bf16[288,729]{1,0:T(8,128)(2,1)}, bf16[288,729]{1,0:T(8,128)(2,1)}) custom-call(s32[13]{0:T(128)} %concatenate.33.place_ref.pick_ref, f32[729,1152]{1,0:T(8,128)} %get-tuple-element.160.hidden_ref, bf16[4,729,1076]{2,1,0:T(8,128)(2,1)} %get-tuple-element.148.refs_1_.active_ref, ...), custom_call_target="tpu_custom_call" | custom-call | flops 7229067264 | bytes 21967776 | tf_op jit(solution)/shard_map/narrow/pallas_call | solution.py:46
  280.3 10.9 %share.7 = (bf16[2,4,144,1076]{3,2,1,0:T(8,128)(2,1)}, bf16[2,4,144,1076]{3,2,1,0:T(8,128)(2,1)}) custom-call(s32[13]{0:T(128)} %concatenate.33.place_ref.pick_ref, bf16[8,144,729]{2,1,0:T(8,128)(2,1)} %get-tuple-element.162.refs_0_, bf16[4,729,1076]{2,1,0:T(8,128)(2,1)} %get-tuple-element.148.refs_1_.active_ref, ...), custom_call_target="tpu_custom_call" | custom-call | flops 3614533632 | bytes 17871264 | tf_op jit(solution)/shard_map/share/pallas_call | solution.py:46
  292.6 35.2 %feed_back.1 = (bf16[4,729,1076]{2,1,0:T(8,128)(2,1)}, f32[729,1152]{1,0:T(8,128)}, bf16[729,1152]{1,0:T(8,128)(2,1)}, bf16[8,144,729]{2,1,0:T(8,128)(2,1)}, f32[8,1152]{1,0:T(8,128)}) custom-call(s32[13]{0:T(128)} %concatenate.33.place_ref.pick_ref, bf16[729,1152]{1,0:T(8,128)(2,1)} %get-tuple-element.167.grad_ref, f32[1,1152]{1,0:T(1,128)} %get-tuple-element.168.sum_ref, ...), custom_call_target="tpu_custom_call" | custom-call | flops 14458134528 | bytes 51895008 | tf_op jit(solution)/shard_map/feed_back/pallas_call | solution.py:46
  329.5 3.8 place.2
  333.4 11.7 %share.8 = (bf16[4,144,1076]{2,1,0:T(8,128)(2,1)}, bf16[4,144,1076]{2,1,0:T(8,128)(2,1)}, bf16[4,144,1076]{2,1,0:T(8,128)(2,1)}, bf16[4,144,1076]{2,1,0:T(8,128)...) custom-call(s32[13]{0:T(128)} %concatenate.33.place_ref.pick_ref, ...), custom_call_target="tpu_custom_call" | custom-call | flops 4837294080 | bytes 17599392 | tf_op jit(solution)/shard_map/share/pallas_call | solution.py:46
  349.9 6.5 %mix_back.1.grad_ref = bf16[4,729,288]{2,1,0:T(8,128)(2,1)} custom-call(bf16[729,1152]{1,0:T(8,128)(2,1)} %get-tuple-element.180.grad_ref, bf16[1152,1152]{1,0:T(8,128)(2,1)} %get-tuple-element.181.weight_ref), custom_call_target="tpu_custom_call" | custom-call | flops 1934917632 | bytes 6013440 | tf_op jit(solution)/shard_map/mix_back/pallas_call | solution.py:46
  356.7 1.6 fusion.7
  359.9 14.1 %share.9 = (bf16[2,4,144,1152]{3,2,1,0:T(8,128)(2,1)}, bf16[2,4,144,1152]{3,2,1,0:T(8,128)(2,1)}, bf16[2,4,144,288]{3,2,1,0:T(8,128)(2,1)}, bf16[2,4,144,288]{3,2,1,0:T(8,128)(2,1)}) custom-call(s32[13]{0:T(128)} %concatenate.33.place_ref.pick_ref, bf16[8,144,729]{2,1,0:T(8,128)(2,1)} %get-tuple-element.184.refs_0_, ...), custom_call_target="tpu_custom_call" | custom-call | flops 4837294080 | bytes 24234912 | tf_op jit(solution)/shard_map/share/pallas_call | solution.py:46
  374.6 31.8 %attend_back.1 = (bf16[4,729,864]{2,1,0:T(8,128)(2,1)}, f32[4,1,864]{2,1,0:T(1,128)}) custom-call(bf16[4,729,864]{2,1,0:T(8,128)(2,1)} %get-tuple-element.195.packed_ref, f32[4,4,729]{2,1,0:T(4,128)} %bitcast.88, bf16[4,729,288]{2,1,0:T(8,128)(2,1)} %mix_back.1.grad_ref), custom_call_target="tpu_custom_call" | custom-call | flops 18366601216 | bytes 11817792 | tf_op jit(solution)/shard_map/attend_back/pallas_call | solution.py:46
  407.1 8.5 %share.10 = (bf16[4,144,864]{2,1,0:T(8,128)(2,1)}, bf16[4,144,864]{2,1,0:T(8,128)(2,1)}, bf16[4,144,864]{2,1,0:T(8,128)(2,1)}, bf16[4,144,864]{2,1,0:T(8,128)(2,1)}) custom-call(s32[13]{0:T(128)} %concatenate.33.place_ref.pick_ref, bf16[8,144,729]{2,1,0:T(8,128)(2,1)} %get-tuple-element.206.refs_0_, bf16[4,729,864]{2,1,0:T(8,128)(2,1)} %get-tuple-element.197.refs_1_.packed_ref), custom_call_target="tpu_custom_call" | custom-call | flops 2902376448 | bytes 10699776 | tf_op jit(solution)/shard_map/share/pallas_call | solution.py:46
  415.6 2.2 fusion.2
  419.1 14.7 %collective-permute-done.33 = bf16[2,4,144,1152]{3,2,1,0:T(8,128)(2,1)} collective-permute-done((bf16[2,4,144,1152]{3,2,1,0:T(8,128)(2,1)}, bf16[2,4,144,1152]{3,2,1,0:T(8,128)(2,1)}, u32[]{:S(2)}, u32[]{:S(2)}) %collective-permute-start.33) | collective-permute-done | bytes 2654240 | tf_op jit(solution)/shard_map/ppermute | solution.py:745
  433.8 2.7 fusion.8
  438.6 1.9 fusion.16
  444.8 9.7 %share.11 = (bf16[2,4,144,384]{3,2,1,0:T(8,128)(2,1)}, bf16[2,4,144,384]{3,2,1,0:T(8,128)(2,1)}, bf16[2,4,144,480]{3,2,1,0:T(8,128)(2,1)}, bf16[2,4,144,480]{3,2,1,0:T(8,128)(2,1)}) custom-call(s32[13]{0:T(128)} %concatenate.33.place_ref.pick_ref, bf16[8,144,729]{2,1,0:T(8,128)(2,1)} %get-tuple-element.206.refs_0_, ...), custom_call_target="tpu_custom_call" | custom-call | flops 2902376448 | bytes 14681088 | tf_op jit(solution)/shard_map/share/pallas_call | solution.py:46
  454.5 12.5 %collective-permute-done.39 = bf16[4,144,1152]{2,1,0:T(8,128)(2,1)} collective-permute-done((bf16[4,144,1152]{2,1,0:T(8,128)(2,1)}, bf16[4,144,1152]{2,1,0:T(8,128)(2,1)}, u32[]{:S(2)}, u32[]{:S(2)}) %collective-permute-start.39) | collective-permute-done | bytes 1327136 | tf_op jit(solution)/shard_map/ppermute | solution.py:745
  467.0 2.2 fusion.1
  473.9 18.7 %project_back.1 = (bf16[288,729]{1,0:T(8,128)(2,1)}, bf16[288,729]{1,0:T(8,128)(2,1)}, bf16[288,729]{1,0:T(8,128)(2,1)}, bf16[288,729]{1,0:T(8,128)(2,1)}, f32[8,1152]{1,0:T(8,128)}) custom-call(s32[13]{0:T(128)} %concatenate.33.place_ref.pick_ref, bf16[729,1152]{1,0:T(8,128)(2,1)} %get-tuple-element.214.image_ref, ...), custom_call_target="tpu_custom_call" | custom-call | flops 5804752896 | bytes 23641344 | tf_op jit(solution)/shard_map/project_back/pallas_call | solution.py:46
  492.6 2.0 fusion.17
  495.8 5.8 %collective-permute-done.42 = bf16[2,4,144,480]{3,2,1,0:T(8,128)(2,1)S(1)} collective-permute-done((bf16[2,4,144,480]{3,2,1,0:T(8,128)(2,1)}, bf16[2,4,144,480]{3,2,1,0:T(8,128)(2,1)S(1)}, u32[]{:S(2)}, u32[]{:S(2)}) %collective-permute-start.42) | collective-permute-done | bytes 1105952 | tf_op jit(solution)/shard_map/ppermute | solution.py:745
  504.1 6.2 %reduce-scatter.6.cloned.1.call-done = bf16[144,1536]{1,0:T(8,128)(2,1)} async-done(((bf16[576,1536]{1,0:T(8,128)(2,1)}), bf16[144,1536]{1,0:T(8,128)(2,1)}) %reduce-scatter.6.cloned.1.call-update) | async-done | bytes 442384 | tf_op jit(solution)/shard_map/reduce_scatter | solution.py:824
  515.2 1.7 collective-permute-start.49
  522.9 4.8 collective-permute-done.57
  528.7 3.3 collective-permute-start.54
  534.3 2.9 collective-permute-done.54
  537.3 9.8 %collective-permute-done.53 = f32[16,1152]{1,0:T(8,128)S(1)} collective-permute-done((f32[16,1152]{1,0:T(8,128)S(1)}, f32[16,1152]{1,0:T(8,128)S(1)}, u32[]{:S(2)}, u32[]{:S(2)}) %collective-permute-start.53) | collective-permute-done | bytes 73760 | tf_op jit(solution)/shard_map/ppermute | solution.py:745
  550.6 7.3 %collective-permute-done.56 = bf16[144,1536]{1,0:T(8,128)(2,1)S(1)} collective-permute-done((bf16[144,1536]{1,0:T(8,128)(2,1)S(1)}, bf16[144,1536]{1,0:T(8,128)(2,1)S(1)}, u32[]{:S(2)}, u32[]{:S(2)}) %collective-permute-start.56) | collective-permute-done | bytes 442400 | tf_op jit(solution)/shard_map/ppermute | solution.py:745
  564.6 3.6 place.3
  568.2 2.4 collective-permute-done.55
  (232 shorter events, 75.4 us)
Async XLA Ops:
  7.2 148.9 %all-gather.3.cloned.1.call-start = ((), (), s32[]{:S(2)}) async-start(), calls=%async_computation.3 | async-start | bytes 12533760 | tf_op jit(solution)/shard_map/all_gather | solution.py:900
  16.1 244.6 %all-gather.5.cloned.1.call-start = ((), (), s32[]{:S(2)}) async-start(), calls=%async_computation.4 | async-start | bytes 11280384 | tf_op jit(solution)/shard_map/all_gather | solution.py:900
  17.1 487.0 %reduce-scatter.8.cloned.1.call-start = ((), (), s32[]{:S(2)}) async-start(), calls=%async_computation.6 | async-start | bytes 1658880 | tf_op jit(solution)/shard_map/reduce_scatter | solution.py:824
  21.6 16.2 %collective-permute-start.3 = (bf16[144,1152]{1,0:T(8,128)(2,1)S(1)}, bf16[144,1152]{1,0:T(8,128)(2,1)S(1)}, u32[]{:S(2)}, u32[]{:S(2)}) collective-permute-start(bf16[144,1152]{1,0:T(8,128)(2,1)S(1)} %pad_dynamic-slice_fusion), channel_id=1, source_target_pairs={{0,1},{1,2},{2,3},{3,0},{4,5},{5,6},{6,7},{7,4},{8,9},{9,10},{10,1... | collective-permute-start | bytes 995336 | tf_op jit(solution)/shard_map/ppermute | solution.py:876
  37.8 22.2 %collective-permute-start.4 = (bf16[144,1152]{1,0:T(8,128)(2,1)S(1)}, bf16[144,1152]{1,0:T(8,128)(2,1)S(1)}, u32[]{:S(2)}, u32[]{:S(2)}) collective-permute-start(bf16[144,1152]{1,0:T(8,128)(2,1)S(1)} %collective-permute-done.3), channel_id=1, source_target_pairs={{0,1},{1,2},{2,3},{3,0},{4,5},{5,6},{6,7},{7,4},{8,9},{9,10},{10,1... | collective-permute-start | bytes 995336 | tf_op jit(solution)/shard_map/ppermute | solution.py:876
  60.0 12.6 %collective-permute-start.5 = (bf16[144,1152]{1,0:T(8,128)(2,1)S(1)}, bf16[144,1152]{1,0:T(8,128)(2,1)S(1)}, u32[]{:S(2)}, u32[]{:S(2)}) collective-permute-start(bf16[144,1152]{1,0:T(8,128)(2,1)S(1)} %collective-permute-done.4), channel_id=1, source_target_pairs={{0,1},{1,2},{2,3},{3,0},{4,5},{5,6},{6,7},{7,4},{8,9},{9,10},{10,1... | collective-permute-start | bytes 995336 | tf_op jit(solution)/shard_map/ppermute | solution.py:876
  72.8 98.0 %collective-permute-start.6 = (bf16[4,144,1152]{2,1,0:T(8,128)(2,1)S(1)}, bf16[4,144,1152]{2,1,0:T(8,128)(2,1)S(1)}, u32[]{:S(2)}, u32[]{:S(2)}) collective-permute-start(bf16[4,144,1152]{2,1,0:T(8,128)(2,1)S(1)} %pad_maximum_fusion.refs_0_), channel_id=1, source_target_pairs={{0,8},{4,12},{8,0},{12,4},{1,9},{5,13},{9,1},{13,5},{2,10},{6,14},... | collective-permute-start | bytes 3981320 | tf_op jit(solution)/shard_map/ppermute | solution.py:745
  74.4 69.0 %collective-permute-start.1 = (bf16[288,729]{1,0:T(8,128)(2,1)S(1)}, bf16[288,729]{1,0:T(8,128)(2,1)}, u32[]{:S(2)}, u32[]{:S(2)}) collective-permute-start(bf16[288,729]{1,0:T(8,128)(2,1)S(1)} %copy-done.34), channel_id=1, source_target_pairs={{0,8},{4,12},{8,0},{12,4},{1,9},{5,13},{9,1},{13,5},{2,10},{6,14},... | collective-permute-start | bytes 1259720 | tf_op jit(solution)/shard_map/ppermute | solution.py:745
  75.3 74.1 %collective-permute-start.2 = (bf16[288,729]{1,0:T(8,128)(2,1)S(1)}, bf16[288,729]{1,0:T(8,128)(2,1)}, u32[]{:S(2)}, u32[]{:S(2)}) collective-permute-start(bf16[288,729]{1,0:T(8,128)(2,1)S(1)} %copy-done.33), channel_id=1, source_target_pairs={{0,12},{4,8},{8,4},{12,0},{1,13},{5,9},{9,5},{13,1},{2,14},{6,10},... | collective-permute-start | bytes 1259720 | tf_op jit(solution)/shard_map/ppermute | solution.py:745
  76.3 96.9 %collective-permute-start.7 = (bf16[4,144,1152]{2,1,0:T(8,128)(2,1)S(1)}, bf16[4,144,1152]{2,1,0:T(8,128)(2,1)}, u32[]{:S(2)}, u32[]{:S(2)}) collective-permute-start(bf16[4,144,1152]{2,1,0:T(8,128)(2,1)S(1)} %pad_maximum_fusion.refs_0_), channel_id=1, source_target_pairs={{0,16},{16,0},{1,17},{17,1},{2,18},{18,2},{3,19},{19,3},{4,20},{20... | collective-permute-start | bytes 3981320 | tf_op jit(solution)/shard_map/ppermute | solution.py:745
  170.9 32.4 %collective-permute-start.8 = (bf16[4,144,1152]{2,1,0:T(8,128)(2,1)S(1)}, bf16[4,144,1152]{2,1,0:T(8,128)(2,1)}, u32[]{:S(2)}, u32[]{:S(2)}) collective-permute-start(bf16[4,144,1152]{2,1,0:T(8,128)(2,1)S(1)} %collective-permute-done.6.refs_1_), channel_id=1, source_target_pairs={{0,16},{16,0},{1,17},{17,1},{2,18},{18,2},{3,19},{19,3},{4,20},{20... | collective-permute-start | bytes 3981320 | tf_op jit(solution)/shard_map/ppermute | solution.py:745
  173.2 42.0 %collective-permute-start.10 = (bf16[4,144,1152]{2,1,0:T(8,128)(2,1)S(1)}, bf16[4,144,1152]{2,1,0:T(8,128)(2,1)}, u32[]{:S(2)}, u32[]{:S(2)}) collective-permute-start(bf16[4,144,1152]{2,1,0:T(8,128)(2,1)S(1)} %collective-permute-done.6.refs_1_), channel_id=1, source_target_pairs={{0,4},{4,0},{8,12},{12,8},{1,5},{5,1},{9,13},{13,9},{2,6},{6,2},{1... | collective-permute-start | bytes 3981320 | tf_op jit(solution)/shard_map/ppermute | solution.py:745
  173.2 42.4 %collective-permute-start.9 = (bf16[4,144,1152]{2,1,0:T(8,128)(2,1)S(1)}, bf16[4,144,1152]{2,1,0:T(8,128)(2,1)}, u32[]{:S(2)}, u32[]{:S(2)}) collective-permute-start(bf16[4,144,1152]{2,1,0:T(8,128)(2,1)S(1)} %pad_maximum_fusion.refs_0_), channel_id=1, source_target_pairs={{0,4},{4,0},{8,12},{12,8},{1,5},{5,1},{9,13},{13,9},{2,6},{6,2},{1... | collective-permute-start | bytes 3981320 | tf_op jit(solution)/shard_map/ppermute | solution.py:745
  173.7 43.4 %collective-permute-start.11 = (bf16[4,144,1152]{2,1,0:T(8,128)(2,1)}, bf16[4,144,1152]{2,1,0:T(8,128)(2,1)}, u32[]{:S(2)}, u32[]{:S(2)}) collective-permute-start(bf16[4,144,1152]{2,1,0:T(8,128)(2,1)} %collective-permute-done.7.refs_2_), channel_id=1, source_target_pairs={{0,4},{4,0},{8,12},{12,8},{1,5},{5,1},{9,13},{13,9},{2,6},{6,2},{1... | collective-permute-start | bytes 3981320 | tf_op jit(solution)/shard_map/ppermute | solution.py:745
  203.3 13.8 %collective-permute-start.12 = (bf16[4,144,1152]{2,1,0:T(8,128)(2,1)}, bf16[4,144,1152]{2,1,0:T(8,128)(2,1)}, u32[]{:S(2)}, u32[]{:S(2)}) collective-permute-start(bf16[4,144,1152]{2,1,0:T(8,128)(2,1)} %collective-permute-done.8.refs_3_), channel_id=1, source_target_pairs={{0,4},{4,0},{8,12},{12,8},{1,5},{5,1},{9,13},{13,9},{2,6},{6,2},{1... | collective-permute-start | bytes 3981320 | tf_op jit(solution)/shard_map/ppermute | solution.py:745
  203.8 34.3 %collective-permute-start.13 = (bf16[288,729]{1,0:T(8,128)(2,1)}, bf16[288,729]{1,0:T(8,128)(2,1)S(1)}, u32[]{:S(2)}, u32[]{:S(2)}) collective-permute-start(bf16[288,729]{1,0:T(8,128)(2,1)} %get-tuple-element.151), channel_id=1, source_target_pairs={{0,4},{4,0},{8,12},{12,8},{1,5},{5,1},{9,13},{13,9},{2,6},{6,2},{1... | collective-permute-start | bytes 1259720 | tf_op jit(solution)/shard_map/ppermute | solution.py:745
  215.2 23.0 %collective-permute-start.14 = (bf16[288,729]{1,0:T(8,128)(2,1)S(1)}, bf16[288,729]{1,0:T(8,128)(2,1)S(1)}, u32[]{:S(2)}, u32[]{:S(2)}) collective-permute-start(bf16[288,729]{1,0:T(8,128)(2,1)S(1)} %copy-done.32), channel_id=1, source_target_pairs={{0,8},{4,12},{8,0},{12,4},{1,9},{5,13},{9,1},{13,5},{2,10},{6,14},... | collective-permute-start | bytes 1259720 | tf_op jit(solution)/shard_map/ppermute | solution.py:745
  215.6 29.4 %collective-permute-start.15 = (bf16[288,729]{1,0:T(8,128)(2,1)S(1)}, bf16[288,729]{1,0:T(8,128)(2,1)S(1)}, u32[]{:S(2)}, u32[]{:S(2)}) collective-permute-start(bf16[288,729]{1,0:T(8,128)(2,1)S(1)} %copy-done.31), channel_id=1, source_target_pairs={{0,12},{4,8},{8,4},{12,0},{1,13},{5,9},{9,5},{13,1},{2,14},{6,10},... | collective-permute-start | bytes 1259720 | tf_op jit(solution)/shard_map/ppermute | solution.py:745
  259.6 19.1 %collective-permute-start.17 = (bf16[4,144,1076]{2,1,0:T(8,128)(2,1)}, bf16[4,144,1076]{2,1,0:T(8,128)(2,1)S(1)}, u32[]{:S(2)}, u32[]{:S(2)}) collective-permute-start(bf16[4,144,1076]{2,1,0:T(8,128)(2,1)} %get-tuple-element.163), channel_id=1, source_target_pairs={{0,4},{4,0},{8,12},{12,8},{1,5},{5,1},{9,13},{13,9},{2,6},{6,2},{1... | collective-permute-start | bytes 3718664 | tf_op jit(solution)/shard_map/ppermute | solution.py:745
  259.8 19.2 %collective-permute-start.18 = (bf16[4,144,1076]{2,1,0:T(8,128)(2,1)}, bf16[4,144,1076]{2,1,0:T(8,128)(2,1)S(1)}, u32[]{:S(2)}, u32[]{:S(2)}) collective-permute-start(bf16[4,144,1076]{2,1,0:T(8,128)(2,1)} %get-tuple-element.164), channel_id=1, source_target_pairs={{0,4},{4,0},{8,12},{12,8},{1,5},{5,1},{9,13},{13,9},{2,6},{6,2},{1... | collective-permute-start | bytes 3718664 | tf_op jit(solution)/shard_map/ppermute | solution.py:745
  260.1 20.2 %collective-permute-start.19 = (bf16[4,144,1076]{2,1,0:T(8,128)(2,1)}, bf16[4,144,1076]{2,1,0:T(8,128)(2,1)}, u32[]{:S(2)}, u32[]{:S(2)}) collective-permute-start(bf16[4,144,1076]{2,1,0:T(8,128)(2,1)} %get-tuple-element.165), channel_id=1, source_target_pairs={{0,4},{4,0},{8,12},{12,8},{1,5},{5,1},{9,13},{13,9},{2,6},{6,2},{1... | collective-permute-start | bytes 3718664 | tf_op jit(solution)/shard_map/ppermute | solution.py:745
  260.3 20.0 %collective-permute-start.16 = (bf16[4,144,1076]{2,1,0:T(8,128)(2,1)}, bf16[4,144,1076]{2,1,0:T(8,128)(2,1)}, u32[]{:S(2)}, u32[]{:S(2)}) collective-permute-start(bf16[4,144,1076]{2,1,0:T(8,128)(2,1)} %get-tuple-element.159), channel_id=1, source_target_pairs={{0,4},{4,0},{8,12},{12,8},{1,5},{5,1},{9,13},{13,9},{2,6},{6,2},{1... | collective-permute-start | bytes 3718664 | tf_op jit(solution)/shard_map/ppermute | solution.py:745
  278.4 49.4 %collective-permute-start.20 = (bf16[288,729]{1,0:T(8,128)(2,1)}, bf16[288,729]{1,0:T(8,128)(2,1)S(1)}, u32[]{:S(2)}, u32[]{:S(2)}) collective-permute-start(bf16[288,729]{1,0:T(8,128)(2,1)} %get-tuple-element.172), channel_id=1, source_target_pairs={{0,4},{4,0},{8,12},{12,8},{1,5},{5,1},{9,13},{13,9},{2,6},{6,2},{1... | collective-permute-start | bytes 1259720 | tf_op jit(solution)/shard_map/ppermute | solution.py:745
  278.7 49.2 %collective-permute-start.21 = (bf16[288,729]{1,0:T(8,128)(2,1)}, bf16[288,729]{1,0:T(8,128)(2,1)S(1)}, u32[]{:S(2)}, u32[]{:S(2)}) collective-permute-start(bf16[288,729]{1,0:T(8,128)(2,1)} %get-tuple-element.173), channel_id=1, source_target_pairs={{0,8},{4,12},{8,0},{12,4},{1,9},{5,13},{9,1},{13,5},{2,10},{6,14},... | collective-permute-start | bytes 1259720 | tf_op jit(solution)/shard_map/ppermute | solution.py:745
  279.0 48.9 %collective-permute-start.22 = (bf16[288,729]{1,0:T(8,128)(2,1)}, bf16[288,729]{1,0:T(8,128)(2,1)S(1)}, u32[]{:S(2)}, u32[]{:S(2)}) collective-permute-start(bf16[288,729]{1,0:T(8,128)(2,1)} %get-tuple-element.174), channel_id=1, source_target_pairs={{0,12},{4,8},{8,4},{12,0},{1,13},{5,9},{9,5},{13,1},{2,14},{6,10},... | collective-permute-start | bytes 1259720 | tf_op jit(solution)/shard_map/ppermute | solution.py:745
  291.2 65.2 %collective-permute-start.23 = (bf16[2,4,144,1076]{3,2,1,0:T(8,128)(2,1)}, bf16[2,4,144,1076]{3,2,1,0:T(8,128)(2,1)}, u32[]{:S(2)}, u32[]{:S(2)}) collective-permute-start(bf16[2,4,144,1076]{3,2,1,0:T(8,128)(2,1)} %get-tuple-element.183), channel_id=1, source_target_pairs={{0,16},{16,0},{1,17},{17,1},{2,18},{18,2},{3,19},{19,3},{4,20},{20... | collective-permute-start | bytes 7437320 | tf_op jit(solution)/shard_map/ppermute | solution.py:745
  345.9 13.9 %collective-permute-start.25 = (bf16[4,144,1076]{2,1,0:T(8,128)(2,1)}, bf16[4,144,1076]{2,1,0:T(8,128)(2,1)}, u32[]{:S(2)}, u32[]{:S(2)}) collective-permute-start(bf16[4,144,1076]{2,1,0:T(8,128)(2,1)} %get-tuple-element.185), channel_id=1, source_target_pairs={{0,4},{4,0},{8,12},{12,8},{1,5},{5,1},{9,13},{13,9},{2,6},{6,2},{1... | collective-permute-start | bytes 3718664 | tf_op jit(solution)/shard_map/ppermute | solution.py:745
  347.3 12.6 %collective-permute-start.26 = (bf16[4,144,1076]{2,1,0:T(8,128)(2,1)}, bf16[4,144,1076]{2,1,0:T(8,128)(2,1)}, u32[]{:S(2)}, u32[]{:S(2)}) collective-permute-start(bf16[4,144,1076]{2,1,0:T(8,128)(2,1)} %get-tuple-element.186), channel_id=1, source_target_pairs={{0,4},{4,0},{8,12},{12,8},{1,5},{5,1},{9,13},{13,9},{2,6},{6,2},{1... | collective-permute-start | bytes 3718664 | tf_op jit(solution)/shard_map/ppermute | solution.py:745
  347.9 12.0 %collective-permute-start.27 = (bf16[4,144,1076]{2,1,0:T(8,128)(2,1)}, bf16[4,144,1076]{2,1,0:T(8,128)(2,1)}, u32[]{:S(2)}, u32[]{:S(2)}) collective-permute-start(bf16[4,144,1076]{2,1,0:T(8,128)(2,1)} %get-tuple-element.187), channel_id=1, source_target_pairs={{0,4},{4,0},{8,12},{12,8},{1,5},{5,1},{9,13},{13,9},{2,6},{6,2},{1... | collective-permute-start | bytes 3718664 | tf_op jit(solution)/shard_map/ppermute | solution.py:745
  348.5 11.3 %collective-permute-start.24 = (bf16[4,144,1076]{2,1,0:T(8,128)(2,1)}, bf16[4,144,1076]{2,1,0:T(8,128)(2,1)}, u32[]{:S(2)}, u32[]{:S(2)}) collective-permute-start(bf16[4,144,1076]{2,1,0:T(8,128)(2,1)} %get-tuple-element.179), channel_id=1, source_target_pairs={{0,4},{4,0},{8,12},{12,8},{1,5},{5,1},{9,13},{13,9},{2,6},{6,2},{1... | collective-permute-start | bytes 3718664 | tf_op jit(solution)/shard_map/ppermute | solution.py:745
  358.4 57.2 %collective-permute-start.32 = (bf16[4,144,1076]{2,1,0:T(8,128)(2,1)S(1)}, bf16[4,144,1076]{2,1,0:T(8,128)(2,1)}, u32[]{:S(2)}, u32[]{:S(2)}) collective-permute-start(bf16[4,144,1076]{2,1,0:T(8,128)(2,1)S(1)} %fusion.7), channel_id=1, source_target_pairs={{0,8},{4,12},{8,0},{12,4},{1,9},{5,13},{9,1},{13,5},{2,10},{6,14},... | collective-permute-start | bytes 3718664 | tf_op jit(solution)/shard_map/ppermute | solution.py:745
  374.0 59.9 %collective-permute-start.33 = (bf16[2,4,144,1152]{3,2,1,0:T(8,128)(2,1)}, bf16[2,4,144,1152]{3,2,1,0:T(8,128)(2,1)}, u32[]{:S(2)}, u32[]{:S(2)}) collective-permute-start(bf16[2,4,144,1152]{3,2,1,0:T(8,128)(2,1)} %get-tuple-element.203), channel_id=1, source_target_pairs={{0,16},{16,0},{1,17},{17,1},{2,18},{18,2},{3,19},{19,3},{4,20},{20... | collective-permute-start | bytes 7962632 | tf_op jit(solution)/shard_map/ppermute | solution.py:745
  406.4 31.8 %collective-permute-start.34 = (bf16[2,4,144,288]{3,2,1,0:T(8,128)(2,1)}, bf16[2,4,144,288]{3,2,1,0:T(8,128)(2,1)}, u32[]{:S(2)}, u32[]{:S(2)}) collective-permute-start(bf16[2,4,144,288]{3,2,1,0:T(8,128)(2,1)} %get-tuple-element.205), channel_id=1, source_target_pairs={{0,8},{4,12},{8,0},{12,4},{1,9},{5,13},{9,1},{13,5},{2,10},{6,14},... | collective-permute-start | bytes 1990664 | tf_op jit(solution)/shard_map/ppermute | solution.py:745
  419.0 91.3 %reduce-scatter.6.cloned.1.call-start = ((), (), s32[]{:S(2)}) async-start(), calls=%async_computation.5 | async-start | bytes 2211840 | tf_op jit(solution)/shard_map/reduce_scatter | solution.py:824
  436.5 30.5 %collective-permute-start.39 = (bf16[4,144,1152]{2,1,0:T(8,128)(2,1)}, bf16[4,144,1152]{2,1,0:T(8,128)(2,1)}, u32[]{:S(2)}, u32[]{:S(2)}) collective-permute-start(bf16[4,144,1152]{2,1,0:T(8,128)(2,1)} %fusion.8), channel_id=1, source_target_pairs={{0,8},{4,12},{8,0},{12,4},{1,9},{5,13},{9,1},{13,5},{2,10},{6,14},... | collective-permute-start | bytes 3981320 | tf_op jit(solution)/shard_map/ppermute | solution.py:745
  442.0 27.3 %collective-permute-start.40 = (bf16[4,144,288]{2,1,0:T(8,128)(2,1)}, bf16[4,144,288]{2,1,0:T(8,128)(2,1)S(1)}, u32[]{:S(2)}, u32[]{:S(2)}) collective-permute-start(bf16[4,144,288]{2,1,0:T(8,128)(2,1)} %fusion.16), channel_id=1, source_target_pairs={{0,16},{16,0},{1,17},{17,1},{2,18},{18,2},{3,19},{19,3},{4,20},{20... | collective-permute-start | bytes 995336 | tf_op jit(solution)/shard_map/ppermute | solution.py:745
  471.8 87.2 %reduce-scatter.10.cloned.1.call-start = ((), (), s32[]{:S(2)}) async-start(), calls=%async_computation.7 | async-start | bytes 1290240
  471.9 20.7 %collective-permute-start.41 = (bf16[2,4,144,384]{3,2,1,0:T(8,128)(2,1)}, bf16[2,4,144,384]{3,2,1,0:T(8,128)(2,1)}, u32[]{:S(2)}, u32[]{:S(2)}) collective-permute-start(bf16[2,4,144,384]{3,2,1,0:T(8,128)(2,1)} %get-tuple-element.220), channel_id=1, source_target_pairs={{0,16},{16,0},{1,17},{17,1},{2,18},{18,2},{3,19},{19,3},{4,20},{20... | collective-permute-start | bytes 2654216 | tf_op jit(solution)/shard_map/ppermute | solution.py:745
  472.5 29.1 %collective-permute-start.42 = (bf16[2,4,144,480]{3,2,1,0:T(8,128)(2,1)}, bf16[2,4,144,480]{3,2,1,0:T(8,128)(2,1)S(1)}, u32[]{:S(2)}, u32[]{:S(2)}) collective-permute-start(bf16[2,4,144,480]{3,2,1,0:T(8,128)(2,1)} %get-tuple-element.222), channel_id=1, source_target_pairs={{0,8},{4,12},{8,0},{12,4},{1,9},{5,13},{9,1},{13,5},{2,10},{6,14},... | collective-permute-start | bytes 3317768 | tf_op jit(solution)/shard_map/ppermute | solution.py:745
  494.6 15.7 %collective-permute-start.43 = (bf16[4,144,384]{2,1,0:T(8,128)(2,1)}, bf16[4,144,384]{2,1,0:T(8,128)(2,1)}, u32[]{:S(2)}, u32[]{:S(2)}) collective-permute-start(bf16[4,144,384]{2,1,0:T(8,128)(2,1)} %fusion.17), channel_id=1, source_target_pairs={{0,8},{4,12},{8,0},{12,4},{1,9},{5,13},{9,1},{13,5},{2,10},{6,14},... | collective-permute-start | bytes 1327112 | tf_op jit(solution)/shard_map/ppermute | solution.py:745
  517.0 10.6 %collective-permute-start.57 = (bf16[144,1152]{1,0:T(8,128)(2,1)S(1)}, bf16[144,1152]{1,0:T(8,128)(2,1)S(1)}, u32[]{:S(2)}, u32[]{:S(2)}) collective-permute-start(bf16[144,1152]{1,0:T(8,128)(2,1)S(1)} %copy-done.22), channel_id=1, source_target_pairs={{0,16},{16,0},{1,17},{17,1},{2,18},{18,2},{3,19},{19,3},{4,20},{20... | collective-permute-start | bytes 995336 | tf_op jit(solution)/shard_map/ppermute | solution.py:745
  518.5 44.3 %collective-permute-start.45 = (bf16[288,729]{1,0:T(8,128)(2,1)}, bf16[288,729]{1,0:T(8,128)(2,1)S(1)}, u32[]{:S(2)}, u32[]{:S(2)}) collective-permute-start(bf16[288,729]{1,0:T(8,128)(2,1)} %get-tuple-element.233), channel_id=1, source_target_pairs={{0,4},{4,0},{8,12},{12,8},{1,5},{5,1},{9,13},{13,9},{2,6},{6,2},{1... | collective-permute-start | bytes 1259720 | tf_op jit(solution)/shard_map/ppermute | solution.py:745
  519.5 43.3 %collective-permute-start.46 = (bf16[288,729]{1,0:T(8,128)(2,1)}, bf16[288,729]{1,0:T(8,128)(2,1)S(1)}, u32[]{:S(2)}, u32[]{:S(2)}) collective-permute-start(bf16[288,729]{1,0:T(8,128)(2,1)} %get-tuple-element.234), channel_id=1, source_target_pairs={{0,8},{4,12},{8,0},{12,4},{1,9},{5,13},{9,1},{13,5},{2,10},{6,14},... | collective-permute-start | bytes 1259720 | tf_op jit(solution)/shard_map/ppermute | solution.py:745
  532.0 15.0 %collective-permute-start.53 = (f32[16,1152]{1,0:T(8,128)S(1)}, f32[16,1152]{1,0:T(8,128)S(1)}, u32[]{:S(2)}, u32[]{:S(2)}) collective-permute-start(f32[16,1152]{1,0:T(8,128)S(1)} %add.196), channel_id=1, source_target_pairs={{0,2},{1,3},{2,0},{3,1},{4,6},{5,7},{6,4},{7,5},{8,10},{9,11},{10,... | collective-permute-start | bytes 221192 | tf_op jit(solution)/shard_map/ppermute | solution.py:745
  532.0 16.5 %collective-permute-start.52 = (f32[16,1152]{1,0:T(8,128)S(1)}, f32[16,1152]{1,0:T(8,128)S(1)}, u32[]{:S(2)}, u32[]{:S(2)}) collective-permute-start(f32[16,1152]{1,0:T(8,128)S(1)} %add.196), channel_id=1, source_target_pairs={{0,1},{1,0},{2,3},{3,2},{4,5},{5,4},{6,7},{7,6},{8,9},{9,8},{10,11... | collective-permute-start | bytes 221192 | tf_op jit(solution)/shard_map/ppermute | solution.py:745
  537.3 25.6 %collective-permute-start.47 = (bf16[288,729]{1,0:T(8,128)(2,1)S(1)}, bf16[288,729]{1,0:T(8,128)(2,1)S(1)}, u32[]{:S(2)}, u32[]{:S(2)}) collective-permute-start(bf16[288,729]{1,0:T(8,128)(2,1)S(1)} %copy-done.30), channel_id=1, source_target_pairs={{0,12},{4,8},{8,4},{12,0},{1,13},{5,9},{9,5},{13,1},{2,14},{6,10},... | collective-permute-start | bytes 1259720 | tf_op jit(solution)/shard_map/ppermute | solution.py:745
  547.1 10.9 %collective-permute-start.56 = (bf16[144,1536]{1,0:T(8,128)(2,1)S(1)}, bf16[144,1536]{1,0:T(8,128)(2,1)S(1)}, u32[]{:S(2)}, u32[]{:S(2)}) collective-permute-start(bf16[144,1536]{1,0:T(8,128)(2,1)S(1)} %copy-done.11), channel_id=1, source_target_pairs={{0,16},{16,0},{1,17},{17,1},{2,18},{18,2},{3,19},{19,3},{4,20},{20... | collective-permute-start | bytes 1327112 | tf_op jit(solution)/shard_map/ppermute | solution.py:745
  560.2 10.3 %collective-permute-start.55 = (bf16[144,896]{0,1:T(8,128)(2,1)S(1)}, bf16[144,896]{0,1:T(8,128)(2,1)S(1)}, u32[]{:S(2)}, u32[]{:S(2)}) collective-permute-start(bf16[144,896]{0,1:T(8,128)(2,1)S(1)} %copy.44), channel_id=1, source_target_pairs={{0,16},{16,0},{1,17},{17,1},{2,18},{18,2},{3,19},{19,3},{4,20},{20... | collective-permute-start | bytes 774152 | tf_op jit(solution)/shard_map/ppermute | solution.py:745
  (51 other events, 459.1 us)
Sparse Core Ops, SparseCore 0:
  16.2 139.8 all-gather.2
  158.4 95.7 all-gather.4
  419.1 32.3 reduce-scatter.7
  472.0 38.2 reduce-scatter.5
  518.7 32.0 reduce-scatter.9
